TPU v7x, 32 devices: a whole 2x2x4 slice. The times are simulated.
32 devices in a mesh: dp: 4 (over z), seqhi: 2 (over x), seqlo: 4 (over y, core).
Axes of the slice: x: 2, y: 2, z: 4, core: 2. Of those that a mesh axis runs over, the one named last changes fastest.
Arguments:
- queries: bfloat16 [4, 2048, 384], P('dp', ('seqhi', 'seqlo')), may hold values from -2 to 2
- key_rows: bfloat16 [4, 2048, 384], P('dp', ('seqhi', 'seqlo')), may hold values from -2 to 2
- value_rows: bfloat16 [4, 2048, 384], P('dp', ('seqhi', 'seqlo')), may hold values from -3 to 3
- head_scale: float32 [6], replicated, may hold values from 0.15 to 1
- out_weight: bfloat16 [384, 384], replicated, may hold values from -0.3125 to 0.3125
- cotangent: bfloat16 [4, 2048, 384], P('dp', ('seqhi', 'seqlo')), may hold values from -6 to 6
Outputs:
- queries_gradient: bfloat16 [4, 2048, 384], P('dp', ('seqhi', 'seqlo'))
- keys_gradient: bfloat16 [4, 2048, 384], P('dp', ('seqhi', 'seqlo'))
- values_gradient: bfloat16 [4, 2048, 384], P('dp', ('seqhi', 'seqlo'))
- weight_gradient: float32 [384, 384], P('dp')
All inputs are finite; a program needn't handle non-finite values.
Results may differ from a plain program's by a relative error of at most 0.025.
Values may be sent and summed in bfloat16 or wider, within the bound.
No kernel may reach another device: no remote copies, remote signals or barrier semaphores. Data moves between devices by JAX's collectives and lax.ppermute only.
A program may use at most 64 MiB of HBM per device.

v0:
```python
import jax
import jax.numpy as jnp
from jax import lax
from jax.sharding import PartitionSpec as P


def swapped(value, axis, stride):
    mask = 2**stride
    pairs = [(source, source ^ mask) for source in range(lax.axis_size(axis))]
    return lax.ppermute(value, axis, pairs)


def split_heads(matrix, head_count):
    return matrix.reshape(matrix.shape[0], head_count, matrix.shape[1] // head_count)


def pair_mean(matrix):
    paired = matrix.astype(jnp.float32).reshape(matrix.shape[0] // 2, 2, matrix.shape[1])
    return (0.5 * (paired[:, 0] + paired[:, 1])).astype(jnp.bfloat16)


def pair_total(matrix):
    paired = matrix.astype(jnp.float32).reshape(matrix.shape[0] // 2, 2, matrix.shape[1])
    return (paired[:, 0] + paired[:, 1]).astype(jnp.bfloat16)


def spread_rows(matrix, factor):
    widened = jnp.broadcast_to(matrix[:, None], (matrix.shape[0], factor) + matrix.shape[1:])
    return widened.reshape((matrix.shape[0] * factor,) + matrix.shape[1:])


def group_sum(matrix, factor):
    return jnp.sum(matrix.reshape((matrix.shape[0] // factor, factor) + matrix.shape[1:]), axis=1)


def score_terms(queries, key_block, scales):
    head_count = scales.shape[0]
    factor = scales / jnp.sqrt(jnp.float32(queries.shape[1] // head_count))
    logits = jnp.einsum(
        "rhe,che->hrc",
        split_heads(queries, head_count),
        split_heads(key_block, head_count),
        preferred_element_type=jnp.float32,
    )
    return (jnp.exp(logits * factor[:, None, None]), factor)


def attend(queries, key_block, value_block, scales, multiplicity):
    head_count = scales.shape[0]
    weights, factor = score_terms(queries, key_block, scales)
    probabilities = weights.astype(jnp.bfloat16)
    numerator = jnp.einsum(
        "hrc,che->rhe",
        probabilities,
        split_heads(value_block, head_count),
        preferred_element_type=jnp.float32,
    )
    numerator = numerator.reshape(queries.shape[0], queries.shape[1])
    denominator = multiplicity * jnp.sum(weights, axis=2).T
    return (numerator, denominator)


def attend_back(queries, key_block, value_block, scales, multiplicity, numer_grad, denom_grad):
    head_count = scales.shape[0]
    weights, factor = score_terms(queries, key_block, scales)
    probabilities = weights.astype(jnp.bfloat16)
    grad_heads = split_heads(numer_grad, head_count)
    prob_grad = jnp.einsum(
        "rhe,che->hrc",
        grad_heads,
        split_heads(value_block, head_count),
        preferred_element_type=jnp.float32,
    )
    logit_grad = (
        weights * (prob_grad + multiplicity * denom_grad.T[:, :, None]) * factor[:, None, None]
    ).astype(jnp.bfloat16)
    query_piece = jnp.einsum(
        "hrc,che->rhe",
        logit_grad,
        split_heads(key_block, head_count),
        preferred_element_type=jnp.float32,
    ).reshape(queries.shape)
    key_piece = jnp.einsum(
        "hrc,rhe->che",
        logit_grad,
        split_heads(queries, head_count),
        preferred_element_type=jnp.float32,
    ).reshape(key_block.shape)
    value_piece = jnp.einsum(
        "hrc,rhe->che", probabilities, grad_heads, preferred_element_type=jnp.float32
    ).reshape(value_block.shape)
    return (query_piece, key_piece, value_piece)


def shards(queries, key_rows, value_rows, head_scale, out_weight, cotangent):
    query_local = queries[0]
    key_local = key_rows[0]
    value_local = value_rows[0]
    cotan_local = cotangent[0]
    head_count = head_scale.shape[0]
    feature_width = query_local.shape[1]
    block_rows = key_local.shape[0] // 2
    top_level = lax.axis_size(("seqhi", "seqlo")).bit_length() - 1
    position = lax.axis_index(("seqhi", "seqlo"))
    numerator, denominator = attend(query_local, key_local, value_local, head_scale, 1.0)
    coarse_queries = [query_local]
    sibling_pairs = [None]
    level_numers = [None]
    level_denoms = [None]
    own_keys = pair_mean(key_local)
    own_values = pair_total(value_local)
    for height in range(1, top_level + 1):
        coarse_queries.append(pair_mean(coarse_queries[-1]))
        if height > 1:
            lower_first = position // 2 ** (height - 2) % 2 == 0
            sib_keys, sib_values = sibling_pairs[-1]
            own_keys = pair_mean(
                jnp.concatenate(
                    [
                        jnp.where(lower_first, own_keys, sib_keys),
                        jnp.where(lower_first, sib_keys, own_keys),
                    ],
                    axis=0,
                )
            )
            own_values = pair_total(
                jnp.concatenate(
                    [
                        jnp.where(lower_first, own_values, sib_values),
                        jnp.where(lower_first, sib_values, own_values),
                    ],
                    axis=0,
                )
            )
        arrived = swapped((own_keys, own_values), ("seqhi", "seqlo"), height - 1)
        sibling_pairs.append(arrived)
        level_numer, level_denom = attend(
            coarse_queries[height], arrived[0], arrived[1], head_scale, float(2**height)
        )
        level_numers.append(level_numer)
        level_denoms.append(level_denom)
    numer_acc = level_numers[top_level]
    denom_acc = level_denoms[top_level]
    for height in range(top_level - 1, 0, -1):
        numer_acc = level_numers[height] + spread_rows(numer_acc, 2)
        denom_acc = level_denoms[height] + spread_rows(denom_acc, 2)
    numerator = numerator + spread_rows(numer_acc, 2)
    denominator = denominator + spread_rows(denom_acc, 2)
    attended_heads = split_heads(numerator, head_count) / denominator[:, :, None]
    attended = attended_heads.reshape(numerator.shape).astype(jnp.bfloat16)
    own_rows = feature_width // lax.axis_size("dp")
    weight_term = lax.dot_general(
        attended, cotan_local, (((0,), (0,)), ((), ())), preferred_element_type=jnp.float32
    )
    summed = lax.psum(weight_term, ("dp", "seqhi", "seqlo"))
    weight_gradient = lax.dynamic_slice_in_dim(summed, lax.axis_index("dp") * own_rows, own_rows, 0)
    backward = lax.dot_general(
        cotan_local, out_weight, (((1,), (1,)), ((), ())), preferred_element_type=jnp.float32
    ).astype(jnp.bfloat16)
    back_heads = split_heads(backward, head_count).astype(jnp.float32)
    numer_grad = (back_heads / denominator[:, :, None]).reshape(numerator.shape)
    denom_grad = -jnp.sum(back_heads * attended_heads, axis=2) / denominator
    query_grad, key_grad, value_grad = attend_back(
        query_local,
        key_local,
        value_local,
        head_scale,
        1.0,
        numer_grad.astype(jnp.bfloat16),
        denom_grad,
    )
    level_query_grads = [None]
    level_key_sends = [None]
    numer_group = numer_grad
    denom_group = denom_grad
    for height in range(1, top_level + 1):
        numer_group = group_sum(numer_group, 2)
        denom_group = group_sum(denom_group, 2)
        query_piece, key_piece, value_piece = attend_back(
            coarse_queries[height],
            sibling_pairs[height][0],
            sibling_pairs[height][1],
            head_scale,
            float(2**height),
            numer_group.astype(jnp.bfloat16),
            denom_group,
        )
        level_query_grads.append(query_piece)
        level_key_sends.append((key_piece, value_piece))
    chain_query = level_query_grads[top_level]
    for height in range(top_level - 1, 0, -1):
        chain_query = level_query_grads[height] + spread_rows(0.5 * chain_query, 2)
    query_total = query_grad + spread_rows(0.5 * chain_query, 2)
    returned = [None]
    for height in range(1, top_level + 1):
        returned.append(swapped(level_key_sends[height], ("seqhi", "seqlo"), height - 1))
    carry_pair = returned[top_level]
    for height in range(top_level - 1, 0, -1):
        up_keys = spread_rows(0.5 * carry_pair[0], 2)
        up_values = spread_rows(carry_pair[1], 2)
        split_lower_first = position // 2 ** (height - 1) % 2 == 0
        own_pair = (
            jnp.where(split_lower_first, up_keys[:block_rows], up_keys[block_rows:]),
            jnp.where(split_lower_first, up_values[:block_rows], up_values[block_rows:]),
        )
        other_pair = (
            jnp.where(split_lower_first, up_keys[block_rows:], up_keys[:block_rows]),
            jnp.where(split_lower_first, up_values[block_rows:], up_values[:block_rows]),
        )
        own_pair, other_pair = (own_pair, other_pair)
        parent = swapped((other_pair[0], other_pair[1]), ("seqhi", "seqlo"), height - 1)
        carry_pair = (
            own_pair[0] + parent[0] + returned[height][0],
            own_pair[1] + parent[1] + returned[height][1],
        )
    key_total = key_grad + spread_rows(0.5 * carry_pair[0], 2)
    value_total = value_grad + spread_rows(carry_pair[1], 2)
    return (
        query_total.astype(jnp.bfloat16)[None],
        key_total.astype(jnp.bfloat16)[None],
        value_total.astype(jnp.bfloat16)[None],
        weight_gradient,
    )


def solution(mesh):
    in_specs = (
        P("dp", ("seqhi", "seqlo"), None),
        P("dp", ("seqhi", "seqlo"), None),
        P("dp", ("seqhi", "seqlo"), None),
        P(),
        P(),
        P("dp", ("seqhi", "seqlo"), None),
    )
    out_specs = (
        P("dp", ("seqhi", "seqlo"), None),
        P("dp", ("seqhi", "seqlo"), None),
        P("dp", ("seqhi", "seqlo"), None),
        P("dp", None),
    )
    return jax.shard_map(shards, mesh=mesh, in_specs=in_specs, out_specs=out_specs, check_vma=False)
```

profile of v0, /device:TPU:0, one launch (start us, length us, event | category | flops | bytes accessed | tf_op | source)
XLA Modules:
  0.0 210.4 jit_solution(2963989376022502578)
XLA Ops:
  7.2 1.2 reshape.433
  10.2 0.8 copy.316
  13.5 0.7 convert_element_type.251
  14.9 0.7 fusion.37
  15.5 3.0 %collective-permute-start.4 = (bf16[128,384]{1,0:T(8,128)(2,1)}, bf16[128,384]{1,0:T(8,128)(2,1)S(1)}, u32[]{:S(2)}, u32[]{:S(2)}) collective-permute-start(bf16[128,384]{1,0:T(8,128)(2,1)} %fusion.37), channel_id=1, source_target_pairs={{0,2},{1,3},{2,0},{3,1},{4,6},{5,7},{6,4},{7,5},{8,10},{9,11},{10,... | collective-permute-start | bytes 294920 | tf_op jit(solution)/shard_map/ppermute | solution.py:10
  19.1 0.7 fusion.34
  20.6 1.3 collective-permute-done.4
  21.9 1.0 broadcast_select_fusion.1
  24.1 1.5 collective-permute-start.5
  25.6 1.0 broadcast_select_fusion.3
  27.8 1.0 copy.302
  29.2 1.0 copy.325
  30.4 0.8 copy.328
  31.2 0.7 collective-permute-done.2
  33.2 1.9 divide_convert_fusion
  35.1 0.8 copy.388
  35.9 0.9 copy.317
  36.8 1.0 reshape.442
  37.8 1.0 copy.326
  39.5 0.9 broadcast_in_dim.46
  40.4 1.5 reshape.410
  41.9 1.0 copy.330
  43.0 1.1 copy.315
  44.1 1.1 fusion.16
  45.2 0.9 fusion.57
  46.2 0.8 copy.335
  48.7 1.4 div.55
  50.1 1.6 divide_reduce_fusion
  55.3 0.9 fusion.68
  56.3 0.9 copy.390
  57.2 0.8 fusion.44
  59.1 2.1 %fusion.30 = f32[384,384]{1,0:T(8,128)} fusion(bf16[256,384]{0,1:T(8,128)(2,1)} %bitcast.190, bf16[1,256,384]{2,1,0:T(8,128)(2,1)} %param.11), kind=kOutput, calls=%fused_computation.59 | convolution fusion | flops 75497472 | bytes 983040 | tf_op jit(solution)/shard_map/dot_general | solution.py:152
  61.5 0.8 copy.357
  62.5 0.8 copy.349
  64.7 2.3 %collective-permute-start.8 = (f32[128,384]{1,0:T(8,128)S(1)}, f32[128,384]{1,0:T(8,128)}, u32[]{:S(2)}, u32[]{:S(2)}) collective-permute-start(f32[128,384]{1,0:T(8,128)S(1)} %copy.351), channel_id=1, source_target_pairs={{0,2},{1,3},{2,0},{3,1},{4,6},{5,7},{6,4},{7,5},{8,10},{9,11},{10,... | collective-permute-start | bytes 589832 | tf_op jit(solution)/shard_map/ppermute | solution.py:10
  67.5 0.7 collective-permute-start.6
  68.3 0.7 add_convert_fusion.2
  69.0 6.1 %collective-permute-done.6 = f32[128,384]{1,0:T(8,128)S(1)} collective-permute-done((f32[128,384]{1,0:T(8,128)}, f32[128,384]{1,0:T(8,128)S(1)}, u32[]{:S(2)}, u32[]{:S(2)}) %collective-permute-start.6) | collective-permute-done | bytes 196640 | tf_op jit(solution)/shard_map/ppermute | solution.py:10
  75.9 5.9 %collective-permute-done.11 = f32[128,384]{1,0:T(8,128)S(1)} collective-permute-done((f32[128,384]{1,0:T(8,128)S(1)}, f32[128,384]{1,0:T(8,128)S(1)}, u32[]{:S(2)}, u32[]{:S(2)}) %collective-permute-start.11) | collective-permute-done | bytes 196640 | tf_op jit(solution)/shard_map/ppermute | solution.py:10
  82.4 107.4 %all-reduce.2.cloned.1.call-done = f32[384,384]{1,0:T(8,128)} async-done(((f32[384,384]{1,0:T(8,128)}), f32[384,384]{1,0:T(8,128)}) %all-reduce.2.cloned.1.call-update) | async-done | bytes 589840 | tf_op jit(solution)/shard_map/psum | solution.py:155
  189.9 1.6 constant_dynamic-slice_fusion
  191.4 1.4 collective-permute-start.12
  192.9 1.0 add_multiply_fusion.1
  194.4 4.2 %collective-permute-done.12 = f32[128,384]{1,0:T(8,128)} collective-permute-done((f32[128,384]{1,0:T(8,128)S(1)}, f32[128,384]{1,0:T(8,128)}, u32[]{:S(2)}, u32[]{:S(2)}) %collective-permute-start.12) | collective-permute-done | bytes 196640 | tf_op jit(solution)/shard_map/ppermute | solution.py:10
  198.6 1.1 add_add_fusion.1
  200.2 1.0 add_multiply_fusion
  202.1 0.7 add_convert_fusion.1
  202.8 0.7 add_convert_fusion
  (254 shorter events, 22.5 us)
Async XLA Ops:
  7.2 26.0 %copy-start = (bf16[384,384]{1,0:T(8,128)(2,1)S(1)}, bf16[384,384]{1,0:T(8,128)(2,1)}, u32[]{:S(2)}) copy-start(bf16[384,384]{1,0:T(8,128)(2,1)} %param.10) | copy-start | bytes 884740
  7.2 2.2 %copy-start.29 = (bf16[1,256,384]{2,1,0:T(8,128)(2,1)S(1)}, bf16[1,256,384]{2,1,0:T(8,128)(2,1)}, u32[]{:S(2)}) copy-start(bf16[1,256,384]{2,1,0:T(8,128)(2,1)} %param.8) | copy-start | bytes 589828
  7.2 182.7 %all-reduce.2.cloned.1.call-start = ((), (), s32[]{:S(2)}) async-start(), calls=%async_computation | async-start | bytes 1179648 | tf_op jit(solution)/shard_map/psum | solution.py:155
  8.8 2.2 %copy-start.30 = (bf16[1,256,384]{2,1,0:T(8,128)(2,1)S(1)}, bf16[1,256,384]{2,1,0:T(8,128)(2,1)}, u32[]{:S(2)}) copy-start(bf16[1,256,384]{2,1,0:T(8,128)(2,1)} %param.6) | copy-start | bytes 589828
  8.8 5.4 %collective-permute-start = (bf16[128,384]{1,0:T(8,128)(2,1)S(1)}, bf16[128,384]{1,0:T(8,128)(2,1)S(1)}, u32[]{:S(2)}, u32[]{:S(2)}) collective-permute-start(bf16[128,384]{1,0:T(8,128)(2,1)S(1)} %fusion.33), channel_id=1, source_target_pairs={{0,1},{1,0},{2,3},{3,2},{4,5},{5,4},{6,7},{7,6},{8,9},{9,8},{10,11... | collective-permute-start | bytes 294920 | tf_op jit(solution)/shard_map/ppermute | solution.py:10
  9.9 4.3 %collective-permute-start.3 = (bf16[128,384]{1,0:T(8,128)(2,1)S(1)}, bf16[128,384]{1,0:T(8,128)(2,1)S(1)}, u32[]{:S(2)}, u32[]{:S(2)}) collective-permute-start(bf16[128,384]{1,0:T(8,128)(2,1)S(1)} %fusion.36), channel_id=1, source_target_pairs={{0,1},{1,0},{2,3},{3,2},{4,5},{5,4},{6,7},{7,6},{8,9},{9,8},{10,11... | collective-permute-start | bytes 294920 | tf_op jit(solution)/shard_map/ppermute | solution.py:10
  10.2 2.7 %copy-start.1 = (bf16[1,256,384]{1,2,0:T(8,128)(2,1)}, bf16[1,256,384]{1,2,0:T(8,128)(2,1)S(1)}, u32[]{:S(2)}) copy-start(bf16[1,256,384]{1,2,0:T(8,128)(2,1)S(1)} %copy.293) | copy-start | bytes 589828
  10.2 1.8 copy-start.42
  11.8 8.0 %copy-start.22 = (bf16[128,1,384]{0,2,1:T(8,128)(2,1)}, bf16[128,1,384]{0,2,1:T(8,128)(2,1)S(1)}, u32[]{:S(2)}) copy-start(bf16[128,1,384]{0,2,1:T(8,128)(2,1)S(1)} %copy.296) | copy-start | bytes 294916
  12.0 20.0 %copy-start.40 = (f32[6]{0:T(128)}, f32[6]{0:T(128)S(1)}, u32[]{:S(2)}) copy-start(f32[6]{0:T(128)S(1)} %broadcast_multiply_fusion.1) | copy-start | bytes 76
  12.5 16.3 %copy-start.12 = (bf16[64,384]{0,1:T(8,128)(2,1)}, bf16[64,384]{0,1:T(8,128)(2,1)S(1)}, u32[]{:S(2)}) copy-start(bf16[64,384]{0,1:T(8,128)(2,1)S(1)} %copy.389) | copy-start | bytes 147460
  15.5 6.4 %collective-permute-start.4 = (bf16[128,384]{1,0:T(8,128)(2,1)}, bf16[128,384]{1,0:T(8,128)(2,1)S(1)}, u32[]{:S(2)}, u32[]{:S(2)}) collective-permute-start(bf16[128,384]{1,0:T(8,128)(2,1)} %fusion.37), channel_id=1, source_target_pairs={{0,2},{1,3},{2,0},{3,1},{4,6},{5,7},{6,4},{7,5},{8,10},{9,11},{10,... | collective-permute-start | bytes 294920 | tf_op jit(solution)/shard_map/ppermute | solution.py:10
  19.7 5.8 %collective-permute-start.1 = (bf16[128,384]{1,0:T(8,128)(2,1)}, bf16[128,384]{1,0:T(8,128)(2,1)}, u32[]{:S(2)}, u32[]{:S(2)}) collective-permute-start(bf16[128,384]{1,0:T(8,128)(2,1)} %fusion.34), channel_id=1, source_target_pairs={{0,2},{1,3},{2,0},{3,1},{4,6},{5,7},{6,4},{7,5},{8,10},{9,11},{10,... | collective-permute-start | bytes 294920 | tf_op jit(solution)/shard_map/ppermute | solution.py:10
  19.9 3.0 %copy-start.24 = (bf16[128,384]{0,1:T(8,128)(2,1)}, bf16[128,384]{0,1:T(8,128)(2,1)S(1)}, u32[]{:S(2)}) copy-start(bf16[128,384]{0,1:T(8,128)(2,1)S(1)} %copy.299) | copy-start | bytes 294916
  20.3 2.6 %copy-start.26 = (bf16[128,384]{0,1:T(8,128)(2,1)}, bf16[128,384]{0,1:T(8,128)(2,1)S(1)}, u32[]{:S(2)}) copy-start(bf16[128,384]{0,1:T(8,128)(2,1)S(1)} %copy.321) | copy-start | bytes 294916
  24.1 13.7 %collective-permute-start.5 = (bf16[128,384]{1,0:T(8,128)(2,1)}, bf16[128,384]{1,0:T(8,128)(2,1)}, u32[]{:S(2)}, u32[]{:S(2)}) collective-permute-start(bf16[128,384]{1,0:T(8,128)(2,1)} %bitcast.146), channel_id=1, source_target_pairs={{0,4},{1,5},{2,6},{3,7},{4,0},{5,1},{6,2},{7,3},{8,12},{9,13},{10,... | collective-permute-start | bytes 294920 | tf_op jit(solution)/shard_map/ppermute | solution.py:10
  26.8 5.2 %copy-start.35 = (bf16[32,6,64]{2,1,0:T(8,128)(2,1)S(1)}, bf16[32,6,64]{2,1,0:T(8,128)(2,1)}, u32[]{:S(2)}) copy-start(bf16[32,6,64]{2,1,0:T(8,128)(2,1)} %convert_element_type.251) | copy-start | bytes 73732
  27.2 4.7 %collective-permute-start.2 = (bf16[128,384]{1,0:T(8,128)(2,1)S(1)}, bf16[128,384]{1,0:T(8,128)(2,1)S(1)}, u32[]{:S(2)}, u32[]{:S(2)}) collective-permute-start(bf16[128,384]{1,0:T(8,128)(2,1)S(1)} %fusion.35), channel_id=1, source_target_pairs={{0,4},{1,5},{2,6},{3,7},{4,0},{5,1},{6,2},{7,3},{8,12},{9,13},{10,... | collective-permute-start | bytes 294920 | tf_op jit(solution)/shard_map/ppermute | solution.py:10
  28.8 4.1 %copy-start.14 = (bf16[128,384]{0,1:T(8,128)(2,1)}, bf16[128,384]{0,1:T(8,128)(2,1)S(1)}, u32[]{:S(2)}) copy-start(bf16[128,384]{0,1:T(8,128)(2,1)S(1)} %copy.302) | copy-start | bytes 294916
  32.2 6.5 %copy-start.7 = (f32[6,32,128]{2,1,0:T(8,128)}, f32[6,32,128]{2,1,0:T(8,128)S(1)}, u32[]{:S(2)}) copy-start(f32[6,32,128]{2,1,0:T(8,128)S(1)} %get-tuple-element.37) | copy-start | bytes 294916
  35.1 4.2 %copy-start.38 = (f32[64,384]{1,0:T(8,128)S(1)}, f32[64,384]{1,0:T(8,128)}, u32[]{:S(2)}) copy-start(f32[64,384]{1,0:T(8,128)} %copy.328) | copy-start | bytes 294916
  43.0 2.3 %copy-start.5 = (bf16[1,256,384]{1,2,0:T(8,128)(2,1)S(1)}, bf16[1,256,384]{1,2,0:T(8,128)(2,1)}, u32[]{:S(2)}) copy-start(bf16[1,256,384]{1,2,0:T(8,128)(2,1)} %copy.316) | copy-start | bytes 589828
  43.0 2.3 %copy-start.10 = (f32[256,384]{0,1:T(8,128)S(1)}, f32[256,384]{0,1:T(8,128)}, u32[]{:S(2)}) copy-start(f32[256,384]{0,1:T(8,128)} %copy.317) | copy-start | bytes 1179652
  45.2 1.8 copy-start.41
  50.1 2.7 %copy-start.34 = (f32[256,6]{1,0:T(8,128)S(1)}, f32[256,6]{1,0:T(8,128)}, u32[]{:S(2)}) copy-start(f32[256,6]{1,0:T(8,128)} %copy.335) | copy-start | bytes 18436
  50.1 3.4 %copy-start.8 = (f32[6,32,128]{2,1,0:T(8,128)S(1)}, f32[6,32,128]{2,1,0:T(8,128)}, u32[]{:S(2)}) copy-start(f32[6,32,128]{2,1,0:T(8,128)} %copy-done.7) | copy-start | bytes 294916
  50.1 3.7 %copy-start.19 = (bf16[128,384]{0,1:T(8,128)(2,1)S(1)}, bf16[128,384]{0,1:T(8,128)(2,1)}, u32[]{:S(2)}) copy-start(bf16[128,384]{0,1:T(8,128)(2,1)} %copy-done.18) | copy-start | bytes 294916
  51.7 2.2 %copy-start.17 = (bf16[128,384]{0,1:T(8,128)(2,1)S(1)}, bf16[128,384]{0,1:T(8,128)(2,1)}, u32[]{:S(2)}) copy-start(bf16[128,384]{0,1:T(8,128)(2,1)} %copy-done.16) | copy-start | bytes 294916
  51.7 2.3 %copy-start.36 = (bf16[32,6,64]{2,1,0:T(8,128)(2,1)S(1)}, bf16[32,6,64]{2,1,0:T(8,128)(2,1)}, u32[]{:S(2)}) copy-start(bf16[32,6,64]{2,1,0:T(8,128)(2,1)} %convert_element_type.251) | copy-start | bytes 73732
  52.7 2.0 copy-start.27
  53.2 1.8 copy-start.23
  54.5 3.5 %copy-start.21 = (bf16[128,384]{0,1:T(8,128)(2,1)S(1)}, bf16[128,384]{0,1:T(8,128)(2,1)}, u32[]{:S(2)}) copy-start(bf16[128,384]{0,1:T(8,128)(2,1)} %copy-done.20) | copy-start | bytes 294916
  54.7 3.5 %copy-start.13 = (bf16[64,384]{0,1:T(8,128)(2,1)S(1)}, bf16[64,384]{0,1:T(8,128)(2,1)}, u32[]{:S(2)}) copy-start(bf16[64,384]{0,1:T(8,128)(2,1)} %copy-done.12) | copy-start | bytes 147460
  54.8 3.7 %copy-start.15 = (bf16[128,384]{0,1:T(8,128)(2,1)S(1)}, bf16[128,384]{0,1:T(8,128)(2,1)}, u32[]{:S(2)}) copy-start(bf16[128,384]{0,1:T(8,128)(2,1)} %copy-done.14) | copy-start | bytes 294916
  55.1 3.6 %copy-start.9 = (f32[6,64,256]{2,1,0:T(8,128)S(1)}, f32[6,64,256]{2,1,0:T(8,128)}, u32[]{:S(2)}) copy-start(f32[6,64,256]{2,1,0:T(8,128)} %fusion.16) | copy-start | bytes 1179652
  59.0 3.4 %copy-start.32 = (f32[6,64,128]{2,1,0:T(8,128)S(1)}, f32[6,64,128]{2,1,0:T(8,128)}, u32[]{:S(2)}) copy-start(f32[6,64,128]{2,1,0:T(8,128)} %fusion.44) | copy-start | bytes 589828
  61.3 2.2 %copy-start.31 = (f32[6,64,128]{2,1,0:T(8,128)S(1)}, f32[6,64,128]{2,1,0:T(8,128)}, u32[]{:S(2)}) copy-start(f32[6,64,128]{2,1,0:T(8,128)} %fusion.68) | copy-start | bytes 589828
  64.1 11.0 %copy-start.39 = (f32[128,384]{1,0:T(8,128)S(1)}, f32[128,384]{1,0:T(8,128)}, u32[]{:S(2)}) copy-start(f32[128,384]{1,0:T(8,128)} %copy.357) | copy-start | bytes 589828
  64.7 126.7 %collective-permute-start.8 = (f32[128,384]{1,0:T(8,128)S(1)}, f32[128,384]{1,0:T(8,128)}, u32[]{:S(2)}, u32[]{:S(2)}) collective-permute-start(f32[128,384]{1,0:T(8,128)S(1)} %copy.351), channel_id=1, source_target_pairs={{0,2},{1,3},{2,0},{3,1},{4,6},{5,7},{6,4},{7,5},{8,10},{9,11},{10,... | collective-permute-start | bytes 589832 | tf_op jit(solution)/shard_map/ppermute | solution.py:10
  67.0 133.2 %collective-permute-start.10 = (f32[128,384]{1,0:T(8,128)S(1)}, f32[128,384]{1,0:T(8,128)}, u32[]{:S(2)}, u32[]{:S(2)}) collective-permute-start(f32[128,384]{1,0:T(8,128)S(1)} %copy.353), channel_id=1, source_target_pairs={{0,1},{1,0},{2,3},{3,2},{4,5},{5,4},{6,7},{7,6},{8,9},{9,8},{10,11... | collective-permute-start | bytes 589832 | tf_op jit(solution)/shard_map/ppermute | solution.py:10
  67.0 134.7 %collective-permute-start.15 = (f32[128,384]{1,0:T(8,128)S(1)}, f32[128,384]{1,0:T(8,128)S(1)}, u32[]{:S(2)}, u32[]{:S(2)}) collective-permute-start(f32[128,384]{1,0:T(8,128)S(1)} %copy.361), channel_id=1, source_target_pairs={{0,1},{1,0},{2,3},{3,2},{4,5},{5,4},{6,7},{7,6},{8,9},{9,8},{10,11... | collective-permute-start | bytes 589832 | tf_op jit(solution)/shard_map/ppermute | solution.py:10
  67.5 7.6 %collective-permute-start.6 = (f32[128,384]{1,0:T(8,128)}, f32[128,384]{1,0:T(8,128)S(1)}, u32[]{:S(2)}, u32[]{:S(2)}) collective-permute-start(f32[128,384]{1,0:T(8,128)} %copy.349), channel_id=1, source_target_pairs={{0,4},{1,5},{2,6},{3,7},{4,0},{5,1},{6,2},{7,3},{8,12},{9,13},{10,... | collective-permute-start | bytes 589832 | tf_op jit(solution)/shard_map/ppermute | solution.py:10
  68.2 126.2 %collective-permute-start.13 = (f32[128,384]{1,0:T(8,128)S(1)}, f32[128,384]{1,0:T(8,128)}, u32[]{:S(2)}, u32[]{:S(2)}) collective-permute-start(f32[128,384]{1,0:T(8,128)S(1)} %copy.359), channel_id=1, source_target_pairs={{0,2},{1,3},{2,0},{3,1},{4,6},{5,7},{6,4},{7,5},{8,10},{9,11},{10,... | collective-permute-start | bytes 589832 | tf_op jit(solution)/shard_map/ppermute | solution.py:10
  75.1 6.6 %collective-permute-start.11 = (f32[128,384]{1,0:T(8,128)S(1)}, f32[128,384]{1,0:T(8,128)S(1)}, u32[]{:S(2)}, u32[]{:S(2)}) collective-permute-start(f32[128,384]{1,0:T(8,128)S(1)} %copy-done.39), channel_id=1, source_target_pairs={{0,4},{1,5},{2,6},{3,7},{4,0},{5,1},{6,2},{7,3},{8,12},{9,13},{10,... | collective-permute-start | bytes 589832 | tf_op jit(solution)/shard_map/ppermute | solution.py:10
  81.7 111.2 %collective-permute-start.7 = (f32[128,384]{1,0:T(8,128)S(1)}, f32[128,384]{1,0:T(8,128)S(1)}, u32[]{:S(2)}, u32[]{:S(2)}) collective-permute-start(f32[128,384]{1,0:T(8,128)S(1)} %select_n.151), channel_id=1, source_target_pairs={{0,2},{1,3},{2,0},{3,1},{4,6},{5,7},{6,4},{7,5},{8,10},{9,11},{10,... | collective-permute-start | bytes 589832 | tf_op jit(solution)/shard_map/ppermute | solution.py:10
  191.4 7.2 %collective-permute-start.12 = (f32[128,384]{1,0:T(8,128)S(1)}, f32[128,384]{1,0:T(8,128)}, u32[]{:S(2)}, u32[]{:S(2)}) collective-permute-start(f32[128,384]{1,0:T(8,128)S(1)} %select_n.159), channel_id=1, source_target_pairs={{0,2},{1,3},{2,0},{3,1},{4,6},{5,7},{6,4},{7,5},{8,10},{9,11},{10,... | collective-permute-start | bytes 589832 | tf_op jit(solution)/shard_map/ppermute | solution.py:10
  194.3 5.9 %collective-permute-start.9 = (f32[128,384]{1,0:T(8,128)S(1)}, f32[128,384]{1,0:T(8,128)S(1)}, u32[]{:S(2)}, u32[]{:S(2)}) collective-permute-start(f32[128,384]{1,0:T(8,128)S(1)} %select_n.155), channel_id=1, source_target_pairs={{0,1},{1,0},{2,3},{3,2},{4,5},{5,4},{6,7},{7,6},{8,9},{9,8},{10,11... | collective-permute-start | bytes 589832 | tf_op jit(solution)/shard_map/ppermute | solution.py:10
  200.1 1.5 collective-permute-start.14
  (12 other events, 14.4 us)
Sparse Core Ops, SparseCore 0:
  61.4 128.3 all-reduce.1
where the time goes:
time: 211 us; the launch traced here: 210 us
  waiting for transfers between devices  126 us (60%)
  local copies, waits for them, and re-layouts  32.4 us (15%)
  between operations  15.5 us (7%)
  other arithmetic  12.8 us (6%)
  matrix products  12.6 us (6%)
  starting transfers between devices  11.5 us (5%)
    psum x1, waiting for transfers between devices, shards(): summed = lax.psum(weight_term, ('dp', 'seqhi', 'seqlo'))  107 us
    ppermute x16, waiting for transfers between devices, swapped(): return lax.ppermute(value, axis, pairs)  18.2 us
    ppermute x16, starting transfers between devices, swapped(): return lax.ppermute(value, axis, pairs)  11.4 us
  transfers between devices with their start and end apart: 17, of which 6 were waited for; matrix products, arithmetic and copies ran while one was open for 14% of the time, Pallas kernels for 0%

commit v1 on v0

v1 whole, which is shorter than its diff:
```python
import functools
import math

import jax
import jax.numpy as jnp
from jax import lax
from jax.experimental import pallas as pl
from jax.experimental.pallas import tpu as pltpu
from jax.sharding import PartitionSpec as P

BF = jnp.bfloat16
F32 = jnp.float32
SEQ = ("seqhi", "seqlo")
LANES = 128
HALF = 64
LOG2E = math.log2(math.e)
NN = (((1,), (0,)), ((), ()))
NT = (((1,), (1,)), ((), ()))
TN = (((0,), (0,)), ((), ()))


def dot(left, right, dims=NN):
    return lax.dot_general(left, right, dims, preferred_element_type=F32)


def iota(shape, dim):
    return lax.broadcasted_iota(jnp.int32, shape, dim)


def order_matrix(rows, top, inverse=False):
    source = iota((rows, rows), 0 if inverse else 1)
    place = source >> top
    for bit in range(top):
        place = place + ((source >> bit) & 1) * (rows >> (bit + 1))
    return jnp.where(place == iota((rows, rows), 1 if inverse else 0), 1.0, 0.0).astype(BF)


def side_masks():
    lane = iota((1, LANES), 1)
    low = jnp.where(lane < HALF, 1.0, 0.0)
    return low.astype(BF), (1.0 - low).astype(BF)


def side_factor(scale_ref, pair):
    lane = iota((1, LANES), 1)
    return jnp.where(lane < HALF, scale_ref[2 * pair], scale_ref[2 * pair + 1]) * (HALF**-0.5)


def exponent(scale_ref, head):
    return scale_ref[head] * (HALF**-0.5 * LOG2E)


def stack(parts, axis):
    return parts[0] if len(parts) == 1 else jnp.concatenate(parts, axis=axis)


def doubled(value):
    return jnp.concatenate([value, value], axis=0)


def halves_sum(value):
    half = value.shape[0] // 2
    return value[:half] + value[half:]


def lane_pair(offset, pair):
    return slice(offset + LANES * pair, offset + LANES * (pair + 1))


def denom_slot(pair, side, amount, rows):
    lane = iota((1, LANES), 1)
    slot = lane - side * HALF
    hit = (slot == 16 * pair) | (slot == 16 * pair + 8)
    row = jnp.where(hit, float(amount), 0.0)
    return jnp.broadcast_to(row, (rows, LANES)).astype(BF)


def denom_lanes(denoms):
    lane = iota((1, LANES), 1)
    slot = (lane % HALF) // 8
    packed = jnp.zeros(denoms[0].shape, F32)
    for pair, value in enumerate(denoms):
        high = value.astype(BF).astype(F32)
        packed = jnp.where(slot == 2 * pair, high, packed)
        packed = jnp.where(slot == 2 * pair + 1, value - high, packed)
    return packed.astype(BF)


def pool_kernel(top, q_ref, k_ref, v_ref, *level_refs):
    rows, width = q_ref.shape
    order = order_matrix(rows, top)
    for which, ref in enumerate((q_ref, k_ref, v_ref)):
        current = dot(order, ref[...])
        columns = slice(which * width, (which + 1) * width)
        level_refs[0][:, columns] = current.astype(BF)
        for height in range(1, top + 1):
            total = halves_sum(current)
            rounded = (total if which == 2 else 0.5 * total).astype(BF)
            level_refs[height][:, columns] = rounded
            current = rounded.astype(F32)


def attend(scale_ref, pair, queries, keys, values, amount, low, high):
    weights = []
    for side, mask in enumerate((low, high)):
        logits = dot(queries * mask, keys, NT)
        weights.append(jnp.exp2(logits * exponent(scale_ref, 2 * pair + side)).astype(BF))
    count = jnp.full(values.shape, float(amount), BF)
    right = stack([stack([values * mask, count * mask], 1) for mask in (low, high)], 0)
    return dot(stack(weights, 1), right)


def base_kernel(top, scale_ref, x_ref, cot_ref, w_ref, numer_ref, denom_ref, cotp_ref, back_ref):
    rows, width = cot_ref.shape
    low, high = side_masks()
    for pair in range(width // LANES):
        q, k, v = (x_ref[:, lane_pair(width * which, pair)] for which in range(3))
        both = attend(scale_ref, pair, q, k, v, 1, low, high)
        numer_ref[:, lane_pair(0, pair)] = both[:, :LANES]
        denom_ref[:, lane_pair(0, pair)] = both[:, LANES:]
    cotan = dot(order_matrix(rows, top), cot_ref[...]).astype(BF)
    cotp_ref[...] = cotan
    back_ref[...] = dot(cotan, w_ref[...], NT).astype(BF)


def forward_kernel(top, counts, parts, scale_ref, place_ref, numer_ref, denom_ref, cotp_ref, back_ref, *refs):
    own, refs = refs[:top], refs[top:]
    siblings = []
    for count in counts:
        siblings.append(refs[:count])
        refs = refs[count:]
    grads, refs = refs[: top + 1], refs[top + 1 :]
    pieces, (weight_ref,) = refs[:parts], refs[parts:]
    width = numer_ref.shape[1]
    low, high = side_masks()
    lane = iota((LANES, LANES), 1)
    ones = jnp.where(lane // HALF == iota((LANES, LANES), 0) // HALF, 1.0, 0.0).astype(BF)
    adder = doubled(ones)
    grad_rows = []
    denom_rows = []
    attended = []
    for pair in range(width // LANES):
        total = None
        for height in range(top, 0, -1):
            keys, values = (
                stack([ref[:, lane_pair(width * which, pair)] for ref in siblings[height - 1]], 0)
                for which in (1, 2)
            )
            queries = own[height - 1][:, lane_pair(0, pair)]
            both = attend(scale_ref, pair, queries, keys, values, 2**height, low, high)
            total = both if total is None else both + doubled(total)
        total = doubled(total)
        numer = numer_ref[:, lane_pair(0, pair)] + total[:, :LANES]
        inverse = 1.0 / (denom_ref[:, lane_pair(0, pair)] + total[:, LANES:])
        ratio = numer * inverse
        attended.append(ratio.astype(BF))
        back = back_ref[:, lane_pair(0, pair)].astype(F32)
        product = back * ratio
        product_high = product.astype(BF)
        product_low = (product - product_high.astype(F32)).astype(BF)
        summed = dot(stack([product_high, product_low], 1), adder)
        grad_rows.append(back * inverse)
        denom_rows.append(-summed * inverse)
    weight_ref[...] = dot(stack(attended, 1), cotp_ref[...], TN)
    own_rows = width // parts
    for step in range(parts):
        start = lax.rem(place_ref[0] + step, parts) * own_rows
        piece = weight_ref[pl.ds(pl.multiple_of(start, 16), own_rows), :]
        pieces[step][...] = piece.astype(BF)
    for height in range(top + 1):
        if height:
            grad_rows = [halves_sum(value) for value in grad_rows]
            denom_rows = [halves_sum(value) for value in denom_rows]
        for pair, value in enumerate(grad_rows):
            grads[height][:, lane_pair(0, pair)] = value.astype(BF)
        grads[height][:, width:] = denom_lanes(denom_rows)


def slopes(scale_ref, pair, first, second, left, right, low, high):
    weights, slope = [], []
    for side, mask in enumerate((low, high)):
        logits = dot(first * mask, second, NT)
        weight = jnp.exp2(logits * exponent(scale_ref, 2 * pair + side))
        weights.append(weight.astype(BF))
        slope.append((weight * dot(left[side], right[side], NT)).astype(BF))
    return weights, slope


def masked_stack(value, low, high):
    return stack([value * low, value * high], 0)


def query_kernel(top, counts, scale_ref, x_ref, gh_ref, *refs):
    own, refs = refs[:top], refs[top:]
    own_grads, refs = refs[:top], refs[top:]
    siblings = []
    for count in counts:
        siblings.append(refs[:count])
        refs = refs[count:]
    out_ref, base_key_ref, base_value_ref = refs
    rows, width = out_ref.shape
    low, high = side_masks()
    results = []
    for pair in range(width // LANES):
        factor = side_factor(scale_ref, pair)
        total = None
        for height in range(top, -1, -1):
            if height:
                queries = own[height - 1][:, lane_pair(0, pair)]
                keys, values = (
                    stack([ref[:, lane_pair(width * which, pair)] for ref in siblings[height - 1]], 0)
                    for which in (1, 2)
                )
                grad_ref = own_grads[height - 1]
            else:
                queries, keys, values = (x_ref[:, lane_pair(width * which, pair)] for which in range(3))
                grad_ref = gh_ref
            grad = grad_ref[:, lane_pair(0, pair)]
            denom = grad_ref[:, width:]
            left = [stack([grad * mask, denom], 1) for mask in (low, high)]
            right = [
                stack([values, denom_slot(pair, side, 2**height, values.shape[0])], 1) for side in (0, 1)
            ]
            weights, slope = slopes(scale_ref, pair, queries, keys, left, right, low, high)
            piece = dot(stack(slope, 1), masked_stack(keys, low, high)) * factor
            total = piece if total is None else piece + 0.5 * doubled(total)
            if not height:
                key_piece = dot(stack(slope, 0), masked_stack(queries, low, high), TN)
                value_piece = dot(stack(weights, 0), masked_stack(grad, low, high), TN)
                base_key_ref[:, lane_pair(0, pair)] = key_piece * factor
                base_value_ref[:, lane_pair(0, pair)] = value_piece
        results.append(total.astype(BF))
    out_ref[...] = dot(order_matrix(rows, top, True), stack(results, 1)).astype(BF)


def key_kernel(top, counts, scale_ref, base_key_ref, base_value_ref, *refs):
    own, refs = refs[:top], refs[top:]
    siblings = []
    for count in counts:
        siblings.append(refs[:count])
        refs = refs[count:]
    sibling_grads = []
    for count in counts:
        sibling_grads.append(refs[:count])
        refs = refs[count:]
    key_out_ref, value_out_ref = refs
    rows, width = key_out_ref.shape
    low, high = side_masks()
    key_results, value_results = [], []
    for pair in range(width // LANES):
        factor = side_factor(scale_ref, pair)
        key_total = value_total = None
        for height in range(top, 0, -1):
            keys, values = (own[height - 1][:, lane_pair(width * which, pair)] for which in (1, 2))
            queries = stack([ref[:, lane_pair(0, pair)] for ref in siblings[height - 1]], 0)
            grad = stack([ref[:, lane_pair(0, pair)] for ref in sibling_grads[height - 1]], 0)
            denom = stack([ref[:, width:] for ref in sibling_grads[height - 1]], 0)
            left = [
                stack([values * mask, denom_slot(pair, side, 2**height, values.shape[0])], 1)
                for side, mask in enumerate((low, high))
            ]
            right = [stack([grad, denom], 1)] * 2
            weights, slope = slopes(scale_ref, pair, keys, queries, left, right, low, high)
            key_piece = dot(stack(slope, 1), masked_stack(queries, low, high)) * factor
            value_piece = dot(stack(weights, 1), masked_stack(grad, low, high))
            if key_total is not None:
                key_piece = key_piece + 0.5 * doubled(key_total)
                value_piece = value_piece + doubled(value_total)
            key_total, value_total = key_piece, value_piece
        key_total = base_key_ref[:, lane_pair(0, pair)] + 0.5 * doubled(key_total)
        value_total = base_value_ref[:, lane_pair(0, pair)] + doubled(value_total)
        key_results.append(key_total.astype(BF))
        value_results.append(value_total.astype(BF))
    back = order_matrix(rows, top, True)
    key_out_ref[...] = dot(back, stack(key_results, 1)).astype(BF)
    value_out_ref[...] = dot(back, stack(value_results, 1)).astype(BF)


VMEM = pl.BlockSpec(memory_space=pltpu.VMEM)
SMEM = pl.BlockSpec(memory_space=pltpu.SMEM)


def call(kernel, name, shapes, scalars, arrays, scratch=()):
    return pl.pallas_call(
        kernel,
        out_shape=[jax.ShapeDtypeStruct(shape, kind) for shape, kind in shapes],
        in_specs=[SMEM] * len(scalars) + [VMEM] * len(arrays),
        out_specs=[VMEM] * len(shapes),
        scratch_shapes=list(scratch),
        compiler_params=pltpu.CompilerParams(vmem_limit_bytes=48 * 2**20),
        name=name,
    )(*scalars, *arrays)


def traded(value, mask):
    return lax.ppermute(value, SEQ, [(source, source ^ mask) for source in range(lax.axis_size(SEQ))])


def from_siblings(levels, top):
    arrived = {}
    for offset in range(1, 2**top):
        height = offset.bit_length()
        if offset == 1:
            arrived[1] = traded(levels[1], 1)
        elif offset % 2 == 0:
            arrived[offset] = traded(levels[height], offset)
        else:
            arrived[offset] = traded(arrived[offset - 1], 1)
    grouped = []
    for height in range(1, top + 1):
        parts = [arrived[offset] for offset in range(2 ** (height - 1), 2**height)]
        if parts[0].shape[0] < 16:
            parts = [jnp.concatenate(parts, axis=0)]
        grouped.append(parts)
    return grouped


def flat(groups):
    return [part for group in groups for part in group]


def shards(queries, key_rows, value_rows, head_scale, out_weight, cotangent):
    rows, width = queries.shape[1:]
    top = lax.axis_size(SEQ).bit_length() - 1
    parts = lax.axis_size("dp")
    assert width == HALF * head_scale.shape[0] and width % LANES == 0 and width <= 4 * LANES
    whole = (rows, width)
    levels = call(
        functools.partial(pool_kernel, top),
        "pool",
        [((rows >> height, 3 * width), BF) for height in range(top + 1)],
        [],
        [queries[0], key_rows[0], value_rows[0]],
    )
    siblings = from_siblings(levels, top)
    counts = [len(group) for group in siblings]
    numer, denom, cotan, back = call(
        functools.partial(base_kernel, top),
        "base",
        [(whole, F32), (whole, F32), (whole, BF), (whole, BF)],
        [head_scale],
        [levels[0], cotangent[0], out_weight],
    )
    place = lax.axis_index("dp").astype(jnp.int32).reshape(1)
    outs = call(
        functools.partial(forward_kernel, top, counts, parts),
        "forward",
        [((rows >> height, width + LANES), BF) for height in range(top + 1)]
        + [((width // parts, width), BF)] * parts,
        [head_scale, place],
        [numer, denom, cotan, back, *levels[1:], *flat(siblings)],
        [pltpu.VMEM((width, width), F32)],
    )
    grads, pieces = outs[: top + 1], outs[top + 1 :]
    weight = pieces[0].astype(F32)
    for step in range(1, parts):
        weight = weight + lax.ppermute(
            pieces[step], "dp", [(source, (source + step) % parts) for source in range(parts)]
        ).astype(F32)
    weight = weight.astype(BF)
    sibling_grads = from_siblings(grads, top)
    query_grad, base_key, base_value = call(
        functools.partial(query_kernel, top, counts),
        "query",
        [(whole, BF), (whole, F32), (whole, F32)],
        [head_scale],
        [levels[0], grads[0], *levels[1:], *grads[1:], *flat(siblings)],
    )
    key_grad, value_grad = call(
        functools.partial(key_kernel, top, counts),
        "key",
        [(whole, BF), (whole, BF)],
        [head_scale],
        [base_key, base_value, *levels[1:], *flat(siblings), *flat(sibling_grads)],
    )
    bit = 1
    while bit < top:
        group = [weight]
        for mask in range(1, 2 ** min(2, top - bit)):
            group.append(traded(weight, mask << bit))
        last = bit + 2 >= top
        if last:
            group = group + [traded(value, 1) for value in group]
        weight = sum(value.astype(F32) for value in group)
        if not last:
            weight = weight.astype(BF)
        bit += 2
    if top < 2:
        weight = weight.astype(F32)
        if top == 1:
            weight = weight + traded(weight, 1)
    return query_grad[None], key_grad[None], value_grad[None], weight


def solution(mesh):
    spread = P("dp", SEQ, None)
    return jax.shard_map(
        shards,
        mesh=mesh,
        in_specs=(spread, spread, spread, P(), P(), spread),
        out_specs=(spread, spread, spread, P("dp", None)),
        check_vma=False,
    )
```

time: 211 us -> 46.5 us (0.22)
  waiting for transfers between devices: 126 us -> 8.61 us
  local copies, waits for them, and re-layouts: 32.4 us -> 3.43 us
  between operations: 15.5 us -> 0.74 us
  matrix products: 12.6 us -> 0 us
  Pallas kernels: 0 us -> 12.5 us
  other arithmetic: 12.8 us -> 0.79 us
  starting transfers between devices: 11.5 us -> 20.1 us
    psum x1 -> x0, waiting for transfers between devices: 107 us -> none  [shards(): summed = lax.psum(weight_term, ('dp', 'seqhi', 'seqlo'))]
    dot_general x26 -> x0, matrix products: 12.6 us -> none  [the longest x4 2.37 us: attend_back(): jnp.einsum('hrc,rhe->che', probabilities, grad_heads, preferred_element_t...]
    pallas_call x0 -> x5, Pallas kernels: none -> 12.5 us  [call(): pl.pallas_call(kernel, out_shape=[jax.ShapeDtypeStruct(shape, kind) for s...]
    ppermute x16 -> x24, waiting for transfers between devices: 18.2 us -> 8.61 us  [the longest x21 8.6 us: traded(): lax.ppermute(value, SEQ, [(source, source ^ mask) for source in range(lax...]
    ppermute x16 -> x24, starting transfers between devices: 11.4 us -> 20.1 us  [the longest x21 14.5 us: traded(): lax.ppermute(value, SEQ, [(source, source ^ mask) for source in range(lax...]
    reshape x27 -> x0, local copies, waits for them, and re-layouts: 7.93 us -> none  [the longest x12 3.99 us: spread_rows(): return widened.reshape((matrix.shape[0] * factor,) + matrix.shape[1:])]
    convert_element_type x18 -> x0, local copies, waits for them, and re-layouts: 7.82 us -> none  [the longest x6 2 us: pair_mean(): matrix.astype(jnp.float32).reshape(matrix.shape[0] // 2, 2, matrix.shape[1])]
    convert_element_type x19 -> x1, other arithmetic: 5.36 us -> 0.04 us  [shards(): weight = weight.astype(BF)]
  transfers between devices with their start and end apart: 17 -> 24, of which waited for: 6 -> 7; matrix products, arithmetic and copies ran while one was open for 14% -> 0% of each run, Pallas kernels for 0% -> 20%
where the time goes in v1:
time: 46.5 us; the launch traced here: 46.2 us
  starting transfers between devices  20.1 us (43%)
  Pallas kernels  12.5 us (27%)
  waiting for transfers between devices  8.61 us (19%)
  local copies, waits for them, and re-layouts  3.43 us (7%)
  other arithmetic  0.79 us (2%)
  between operations  0.74 us (2%)
    ppermute x21, starting transfers between devices, traded(): lax.ppermute(value, SEQ, [(source, source ^ mask) for source in range(lax...  14.5 us
    pallas_call x5, Pallas kernels, call(): pl.pallas_call(kernel, out_shape=[jax.ShapeDtypeStruct(shape, kind) for s...  12.5 us
    ppermute x21, waiting for transfers between devices, traded(): lax.ppermute(value, SEQ, [(source, source ^ mask) for source in range(lax...  8.6 us
    ppermute x3, starting transfers between devices, shards(): lax.ppermute(pieces[step], 'dp', [(source, (source + step) % parts) for s...  5.6 us
    unnamed x12, local copies, waits for them, and re-layouts  3.43 us
  transfers between devices with their start and end apart: 24, of which 7 were waited for; matrix products, arithmetic and copies ran while one was open for 0% of the time, Pallas kernels for 20%

profile of v1, /device:TPU:0, one launch (start us, length us, event | category | flops | bytes accessed | tf_op | source)
XLA Modules:
  0.0 46.2 jit_solution(10465265485208596534)
XLA Ops:
  0.6 0.9 %copy-done.1 = bf16[1,256,384]{2,1,0:T(8,128)(2,1)S(1)} copy-done((bf16[1,256,384]{2,1,0:T(8,128)(2,1)S(1)}, bf16[1,256,384]{2,1,0:T(8,128)(2,1)}, u32[]{:S(2)}) %copy-start.1) | copy-done | bytes 196632
  1.6 0.9 %copy-done.2 = bf16[1,256,384]{2,1,0:T(8,128)(2,1)S(1)} copy-done((bf16[1,256,384]{2,1,0:T(8,128)(2,1)S(1)}, bf16[1,256,384]{2,1,0:T(8,128)(2,1)}, u32[]{:S(2)}) %copy-start.2) | copy-done | bytes 196632
  2.5 0.9 %copy-done.3 = bf16[1,256,384]{2,1,0:T(8,128)(2,1)S(1)} copy-done((bf16[1,256,384]{2,1,0:T(8,128)(2,1)S(1)}, bf16[1,256,384]{2,1,0:T(8,128)(2,1)}, u32[]{:S(2)}) %copy-start.3) | copy-done | bytes 196632
  3.4 0.4 pool.1
  3.8 3.0 %collective-permute-start.1 = (bf16[64,1152]{1,0:T(8,128)(2,1)S(1)}, bf16[64,1152]{1,0:T(8,128)(2,1)S(1)}, u32[]{:S(2)}, u32[]{:S(2)}) collective-permute-start(bf16[64,1152]{1,0:T(8,128)(2,1)S(1)} %get-tuple-element.31.refs_1_), channel_id=1, source_target_pairs={{0,2},{1,3},{2,0},{3,1},{4,6},{5,7},{6,4},{7,5},{8,10},{9,11},{10,... | collective-permute-start | bytes 442376 | tf_op jit(solution)/shard_map/ppermute | solution.py:296
  6.8 0.0 collective-permute-start
  6.8 1.4 %collective-permute-start.5 = (bf16[32,1152]{1,0:T(8,128)(2,1)S(1)}, bf16[32,1152]{1,0:T(8,128)(2,1)S(1)}, u32[]{:S(2)}, u32[]{:S(2)}) collective-permute-start(bf16[32,1152]{1,0:T(8,128)(2,1)S(1)} %get-tuple-element.32.refs_2_), channel_id=1, source_target_pairs={{0,6},{1,7},{2,4},{3,5},{4,2},{5,3},{6,0},{7,1},{8,14},{9,15},{10,... | collective-permute-start | bytes 221192 | tf_op jit(solution)/shard_map/ppermute | solution.py:296
  8.3 0.2 collective-permute-start.3
  8.5 3.0 %collective-permute-done.1.refs_4_.refs_7_ = bf16[64,1152]{1,0:T(8,128)(2,1)S(1)} collective-permute-done((bf16[64,1152]{1,0:T(8,128)(2,1)S(1)}, bf16[64,1152]{1,0:T(8,128)(2,1)S(1)}, u32[]{:S(2)}, u32[]{:S(2)}) %collective-permute-start.1) | collective-permute-done | bytes 147488 | tf_op jit(solution)/shard_map/ppermute | solution.py:296
  11.5 1.3 %collective-permute-done.5.refs_8_.refs_11_ = bf16[32,1152]{1,0:T(8,128)(2,1)S(1)} collective-permute-done((bf16[32,1152]{1,0:T(8,128)(2,1)S(1)}, bf16[32,1152]{1,0:T(8,128)(2,1)S(1)}, u32[]{:S(2)}, u32[]{:S(2)}) %collective-permute-start.5) | collective-permute-done | bytes 73760 | tf_op jit(solution)/shard_map/ppermute | solution.py:296
  12.8 0.1 collective-permute-done.3.refs_6_.refs_9_
  12.9 0.4 collective-permute-start.4
  13.3 0.6 %copy-done.5 = f32[6]{0:T(128)S(1)} copy-done((f32[6]{0:T(128)S(1)}, f32[6]{0:T(128)}, u32[]{:S(2)}) %copy-start.5) | copy-done | bytes 48
  14.0 1.4 %base.1 = (f32[256,384]{1,0:T(8,128)S(1)}, f32[256,384]{1,0:T(8,128)S(1)}, bf16[256,384]{1,0:T(8,128)(2,1)S(1)}, bf16[256,384]{1,0:T(8,128)(2,1)S(1)}) custom-call(f32[6]{0:T(128)S(1)} %copy-done.5, bf16[256,1152]{1,0:T(8,128)(2,1)S(1)} %get-tuple-element.25.x_ref, bf16[256,384]{1,0:T(8,128)(2,1)S(1)} %bitcast.11, bf16[384,384]{1,0:T(8,128)(2,1)S(1)} %copy-done), custom_call_target="tpu_custom_call" | custom-call | tf_op jit(solution)/shard_map/base/pallas_call | solution.py:284
  15.4 0.0 collective-permute-done.6.refs_9_.refs_12_
  15.4 0.0 collective-permute-done.refs_3_.refs_6_
  15.4 2.7 %forward.1 = (bf16[256,512]{1,0:T(8,128)(2,1)S(1)}, bf16[128,512]{1,0:T(8,128)(2,1)S(1)}, bf16[64,512]{1,0:T(8,128)(2,1)S(1)}, bf16[32,512]{1,0:T(8,128)(2,1)S(1...) custom-call(f32[6]{0:T(128)S(1)} %copy-done.5, ...), custom_call_target="tpu_custom_call" | custom-call | tf_op jit(solution)/shard_map/forward/pallas_call | solution.py:284
  18.1 1.7 %collective-permute-start.14 = (bf16[96,384]{1,0:T(8,128)(2,1)S(1)}, bf16[96,384]{1,0:T(8,128)(2,1)S(1)}, u32[]{:S(2)}, u32[]{:S(2)}) collective-permute-start(bf16[96,384]{1,0:T(8,128)(2,1)S(1)} %get-tuple-element.43), channel_id=1, source_target_pairs={{0,8},{8,16},{16,24},{24,0},{1,9},{9,17},{17,25},{25,1},{2,10},{10... | collective-permute-start | bytes 221192 | tf_op jit(solution)/shard_map/ppermute | solution.py:357
  19.8 2.6 %collective-permute-start.15 = (bf16[96,384]{1,0:T(8,128)(2,1)S(1)}, bf16[96,384]{1,0:T(8,128)(2,1)S(1)}, u32[]{:S(2)}, u32[]{:S(2)}) collective-permute-start(bf16[96,384]{1,0:T(8,128)(2,1)S(1)} %get-tuple-element.44), channel_id=1, source_target_pairs={{0,16},{8,24},{16,0},{24,8},{1,17},{9,25},{17,1},{25,9},{2,18},{10... | collective-permute-start | bytes 221192 | tf_op jit(solution)/shard_map/ppermute | solution.py:357
  22.4 1.3 %collective-permute-start.16 = (bf16[96,384]{1,0:T(8,128)(2,1)S(1)}, bf16[96,384]{1,0:T(8,128)(2,1)S(1)}, u32[]{:S(2)}, u32[]{:S(2)}) collective-permute-start(bf16[96,384]{1,0:T(8,128)(2,1)S(1)} %get-tuple-element.45), channel_id=1, source_target_pairs={{0,24},{8,0},{16,8},{24,16},{1,25},{9,1},{17,9},{25,17},{2,26},{10... | collective-permute-start | bytes 221192 | tf_op jit(solution)/shard_map/ppermute | solution.py:357
  23.7 2.2 %collective-permute-start.12 = (bf16[32,512]{1,0:T(8,128)(2,1)S(1)}, bf16[32,512]{1,0:T(8,128)(2,1)S(1)}, u32[]{:S(2)}, u32[]{:S(2)}) collective-permute-start(bf16[32,512]{1,0:T(8,128)(2,1)S(1)} %get-tuple-element.36.refs_5_), channel_id=1, source_target_pairs={{0,6},{1,7},{2,4},{3,5},{4,2},{5,3},{6,0},{7,1},{8,14},{9,15},{10,... | collective-permute-start | bytes 98312 | tf_op jit(solution)/shard_map/ppermute | solution.py:296
  25.9 0.5 %collective-permute-start.10 = (bf16[32,512]{1,0:T(8,128)(2,1)S(1)}, bf16[32,512]{1,0:T(8,128)(2,1)S(1)}, u32[]{:S(2)}, u32[]{:S(2)}) collective-permute-start(bf16[32,512]{1,0:T(8,128)(2,1)S(1)} %get-tuple-element.36.refs_5_), channel_id=1, source_target_pairs={{0,4},{1,5},{2,6},{3,7},{4,0},{5,1},{6,2},{7,3},{8,12},{9,13},{10,... | collective-permute-start | bytes 98312 | tf_op jit(solution)/shard_map/ppermute | solution.py:296
  26.4 2.1 %collective-permute-done.12.refs_15_ = bf16[32,512]{1,0:T(8,128)(2,1)S(1)} collective-permute-done((bf16[32,512]{1,0:T(8,128)(2,1)S(1)}, bf16[32,512]{1,0:T(8,128)(2,1)S(1)}, u32[]{:S(2)}, u32[]{:S(2)}) %collective-permute-start.12) | collective-permute-done | bytes 32800 | tf_op jit(solution)/shard_map/ppermute | solution.py:296
  28.5 1.5 %collective-permute-start.8 = (bf16[64,512]{1,0:T(8,128)(2,1)S(1)}, bf16[64,512]{1,0:T(8,128)(2,1)S(1)}, u32[]{:S(2)}, u32[]{:S(2)}) collective-permute-start(bf16[64,512]{1,0:T(8,128)(2,1)S(1)} %get-tuple-element.35.refs_4_), channel_id=1, source_target_pairs={{0,2},{1,3},{2,0},{3,1},{4,6},{5,7},{6,4},{7,5},{8,10},{9,11},{10,... | collective-permute-start | bytes 196616 | tf_op jit(solution)/shard_map/ppermute | solution.py:296
  30.0 0.0 collective-permute-done.10.refs_13_
  30.0 0.0 collective-permute-start.13
  30.0 0.0 collective-permute-done.14
  30.0 0.5 %collective-permute-start.11 = (bf16[32,512]{1,0:T(8,128)(2,1)S(1)}, bf16[32,512]{1,0:T(8,128)(2,1)S(1)}, u32[]{:S(2)}, u32[]{:S(2)}) collective-permute-start(bf16[32,512]{1,0:T(8,128)(2,1)S(1)} %collective-permute-done.10.refs_13_), channel_id=1, source_target_pairs={{0,1},{1,0},{2,3},{3,2},{4,5},{5,4},{6,7},{7,6},{8,9},{9,8},{10,11... | collective-permute-start | bytes 98312 | tf_op jit(solution)/shard_map/ppermute | solution.py:296
  30.5 0.0 collective-permute-done.15
  30.5 0.0 collective-permute-done.16
  30.6 1.5 %collective-permute-start.19 = (bf16[96,384]{1,0:T(8,128)(2,1)S(1)}, bf16[96,384]{1,0:T(8,128)(2,1)S(1)}, u32[]{:S(2)}, u32[]{:S(2)}) collective-permute-start(bf16[96,384]{1,0:T(8,128)(2,1)S(1)} %add_convert_fusion), channel_id=1, source_target_pairs={{0,6},{1,7},{2,4},{3,5},{4,2},{5,3},{6,0},{7,1},{8,14},{9,15},{10,... | collective-permute-start | bytes 221192 | tf_op jit(solution)/shard_map/ppermute | solution.py:296
  32.1 0.6 %collective-permute-start.18 = (bf16[96,384]{1,0:T(8,128)(2,1)S(1)}, bf16[96,384]{1,0:T(8,128)(2,1)S(1)}, u32[]{:S(2)}, u32[]{:S(2)}) collective-permute-start(bf16[96,384]{1,0:T(8,128)(2,1)S(1)} %add_convert_fusion), channel_id=1, source_target_pairs={{0,4},{1,5},{2,6},{3,7},{4,0},{5,1},{6,2},{7,3},{8,12},{9,13},{10,... | collective-permute-start | bytes 221192 | tf_op jit(solution)/shard_map/ppermute | solution.py:296
  32.7 0.0 collective-permute-done.13.refs_16_
  32.7 1.5 %collective-permute-start.17 = (bf16[96,384]{1,0:T(8,128)(2,1)S(1)}, bf16[96,384]{1,0:T(8,128)(2,1)S(1)}, u32[]{:S(2)}, u32[]{:S(2)}) collective-permute-start(bf16[96,384]{1,0:T(8,128)(2,1)S(1)} %add_convert_fusion), channel_id=1, source_target_pairs={{0,2},{1,3},{2,0},{3,1},{4,6},{5,7},{6,4},{7,5},{8,10},{9,11},{10,... | collective-permute-start | bytes 221192 | tf_op jit(solution)/shard_map/ppermute | solution.py:296
  34.1 0.0 collective-permute-start.9
  34.1 0.0 collective-permute-done.11.refs_14_
  34.2 0.5 %collective-permute-start.7 = (bf16[128,512]{1,0:T(8,128)(2,1)S(1)}, bf16[128,512]{1,0:T(8,128)(2,1)S(1)}, u32[]{:S(2)}, u32[]{:S(2)}) collective-permute-start(bf16[128,512]{1,0:T(8,128)(2,1)S(1)} %get-tuple-element.34.refs_3_), channel_id=1, source_target_pairs={{0,1},{1,0},{2,3},{3,2},{4,5},{5,4},{6,7},{7,6},{8,9},{9,8},{10,11... | collective-permute-start | bytes 393224 | tf_op jit(solution)/shard_map/ppermute | solution.py:296
  34.7 0.7 %collective-permute-done.9.refs_12_ = bf16[64,512]{1,0:T(8,128)(2,1)S(1)} collective-permute-done((bf16[64,512]{1,0:T(8,128)(2,1)S(1)}, bf16[64,512]{1,0:T(8,128)(2,1)S(1)}, u32[]{:S(2)}, u32[]{:S(2)}) %collective-permute-start.9) | collective-permute-done | bytes 65568 | tf_op jit(solution)/shard_map/ppermute | solution.py:296
  35.4 0.2 collective-permute-start.20
  35.6 1.1 %collective-permute-done.19 = bf16[96,384]{1,0:T(8,128)(2,1)S(1)} collective-permute-done((bf16[96,384]{1,0:T(8,128)(2,1)S(1)}, bf16[96,384]{1,0:T(8,128)(2,1)S(1)}, u32[]{:S(2)}, u32[]{:S(2)}) %collective-permute-start.19) | collective-permute-done | bytes 73760 | tf_op jit(solution)/shard_map/ppermute | solution.py:296
  36.6 0.0 collective-permute-start.23
  36.6 0.0 collective-permute-done.18
  36.6 0.5 %collective-permute-start.22 = (bf16[96,384]{1,0:T(8,128)(2,1)S(1)}, bf16[96,384]{1,0:T(8,128)(2,1)S(1)}, u32[]{:S(2)}, u32[]{:S(2)}) collective-permute-start(bf16[96,384]{1,0:T(8,128)(2,1)S(1)} %collective-permute-done.18), channel_id=1, source_target_pairs={{0,1},{1,0},{2,3},{3,2},{4,5},{5,4},{6,7},{7,6},{8,9},{9,8},{10,11... | collective-permute-start | bytes 221192 | tf_op jit(solution)/shard_map/ppermute | solution.py:296
  37.1 0.2 collective-permute-done.17
  37.4 4.6 %query.1 = (bf16[256,384]{1,0:T(8,128)(2,1)}, f32[256,384]{1,0:T(8,128)S(1)}, f32[256,384]{1,0:T(8,128)S(1)}) custom-call(f32[6]{0:T(128)S(1)} %copy-done.5, bf16[256,1152]{1,0:T(8,128)(2,1)S(1)} %get-tuple-element.25.x_ref, bf16[256,512]{1,0:T(8,128)(2,1)S(1)} %get-tuple-element.33.gh_ref, bf16[128,1152]{1,0:T(8,128)(2,1)S(1)} %get-tuple-element.30.refs_0_, ...), custom_call_target="tpu_custom_call" | custom-call | tf_op jit(solution)/shard_map/query/pallas_call | solution.py:284
  42.0 0.0 collective-permute-done.7.refs_10_
  42.0 3.5 %key.1 = (bf16[256,384]{1,0:T(8,128)(2,1)}, bf16[256,384]{1,0:T(8,128)(2,1)}) custom-call(f32[6]{0:T(128)S(1)} %copy-done.5, f32[256,384]{1,0:T(8,128)S(1)} %get-tuple-element.38.base_key_ref, f32[256,384]{1,0:T(8,128)S(1)} %get-tuple-element.39.base_value_ref, bf16[128,1152]{1,0:T(8,128)(2,1)S(1)} %get-tuple-element.30.refs_0_, ...), custom_call_target="tpu_custom_call" | custom-call | tf_op jit(solution)/shard_map/key/pallas_call | solution.py:284
  45.5 0.7 %convert_add_fusion = f32[96,384]{1,0:T(8,128)} fusion(bf16[96,384]{1,0:T(8,128)(2,1)S(1)} %collective-permute-done.23, bf16[96,384]{1,0:T(8,128)(2,1)S(1)} %collective-permute-done.22, bf16[96,384]{1,0:T(8,128)(2,1)S(1)} %collective-permute-done.21, bf16[96,384]{1,0:T(8,128)(2,1)S(1)} %collective-permute-done.20, ...), kind=kLoop, calls=%fused_computation | loop fusion | flops 552960 | bytes 737280 | tf_op jit(solution)/shard_map/add | solution.py:384
  (19 shorter events, 0.1 us)
Async XLA Ops:
  0.6 0.9 %copy-start.1 = (bf16[1,256,384]{2,1,0:T(8,128)(2,1)S(1)}, bf16[1,256,384]{2,1,0:T(8,128)(2,1)}, u32[]{:S(2)}) copy-start(bf16[1,256,384]{2,1,0:T(8,128)(2,1)} %param.6) | copy-start | bytes 589828
  1.6 0.9 %copy-start.2 = (bf16[1,256,384]{2,1,0:T(8,128)(2,1)S(1)}, bf16[1,256,384]{2,1,0:T(8,128)(2,1)}, u32[]{:S(2)}) copy-start(bf16[1,256,384]{2,1,0:T(8,128)(2,1)} %param.7) | copy-start | bytes 589828
  2.5 0.9 %copy-start.3 = (bf16[1,256,384]{2,1,0:T(8,128)(2,1)S(1)}, bf16[1,256,384]{2,1,0:T(8,128)(2,1)}, u32[]{:S(2)}) copy-start(bf16[1,256,384]{2,1,0:T(8,128)(2,1)} %param.8) | copy-start | bytes 589828
  3.4 9.9 %copy-start = (bf16[384,384]{1,0:T(8,128)(2,1)S(1)}, bf16[384,384]{1,0:T(8,128)(2,1)}, u32[]{:S(2)}) copy-start(bf16[384,384]{1,0:T(8,128)(2,1)} %w_ref.1) | copy-start | bytes 884740
  3.4 9.9 %copy-start.4 = (bf16[1,256,384]{2,1,0:T(8,128)(2,1)S(1)}, bf16[1,256,384]{2,1,0:T(8,128)(2,1)}, u32[]{:S(2)}) copy-start(bf16[1,256,384]{2,1,0:T(8,128)(2,1)} %param.11) | copy-start | bytes 589828
  3.8 7.7 %collective-permute-start.1 = (bf16[64,1152]{1,0:T(8,128)(2,1)S(1)}, bf16[64,1152]{1,0:T(8,128)(2,1)S(1)}, u32[]{:S(2)}, u32[]{:S(2)}) collective-permute-start(bf16[64,1152]{1,0:T(8,128)(2,1)S(1)} %get-tuple-element.31.refs_1_), channel_id=1, source_target_pairs={{0,2},{1,3},{2,0},{3,1},{4,6},{5,7},{6,4},{7,5},{8,10},{9,11},{10,... | collective-permute-start | bytes 442376 | tf_op jit(solution)/shard_map/ppermute | solution.py:296
  6.8 8.6 %collective-permute-start = (bf16[128,1152]{1,0:T(8,128)(2,1)S(1)}, bf16[128,1152]{1,0:T(8,128)(2,1)S(1)}, u32[]{:S(2)}, u32[]{:S(2)}) collective-permute-start(bf16[128,1152]{1,0:T(8,128)(2,1)S(1)} %get-tuple-element.30.refs_0_), channel_id=1, source_target_pairs={{0,1},{1,0},{2,3},{3,2},{4,5},{5,4},{6,7},{7,6},{8,9},{9,8},{10,11... | collective-permute-start | bytes 884744 | tf_op jit(solution)/shard_map/ppermute | solution.py:296
  6.8 6.0 %collective-permute-start.5 = (bf16[32,1152]{1,0:T(8,128)(2,1)S(1)}, bf16[32,1152]{1,0:T(8,128)(2,1)S(1)}, u32[]{:S(2)}, u32[]{:S(2)}) collective-permute-start(bf16[32,1152]{1,0:T(8,128)(2,1)S(1)} %get-tuple-element.32.refs_2_), channel_id=1, source_target_pairs={{0,6},{1,7},{2,4},{3,5},{4,2},{5,3},{6,0},{7,1},{8,14},{9,15},{10,... | collective-permute-start | bytes 221192 | tf_op jit(solution)/shard_map/ppermute | solution.py:296
  8.3 4.6 %collective-permute-start.3 = (bf16[32,1152]{1,0:T(8,128)(2,1)S(1)}, bf16[32,1152]{1,0:T(8,128)(2,1)S(1)}, u32[]{:S(2)}, u32[]{:S(2)}) collective-permute-start(bf16[32,1152]{1,0:T(8,128)(2,1)S(1)} %get-tuple-element.32.refs_2_), channel_id=1, source_target_pairs={{0,4},{1,5},{2,6},{3,7},{4,0},{5,1},{6,2},{7,3},{8,12},{9,13},{10,... | collective-permute-start | bytes 221192 | tf_op jit(solution)/shard_map/ppermute | solution.py:296
  11.5 3.9 %collective-permute-start.2 = (bf16[64,1152]{1,0:T(8,128)(2,1)S(1)}, bf16[64,1152]{1,0:T(8,128)(2,1)S(1)}, u32[]{:S(2)}, u32[]{:S(2)}) collective-permute-start(bf16[64,1152]{1,0:T(8,128)(2,1)S(1)} %collective-permute-done.1.refs_4_.refs_7_), channel_id=1, source_target_pairs={{0,1},{1,0},{2,3},{3,2},{4,5},{5,4},{6,7},{7,6},{8,9},{9,8},{10,11... | collective-permute-start | bytes 442376 | tf_op jit(solution)/shard_map/ppermute | solution.py:296
  12.8 2.6 %collective-permute-start.6 = (bf16[32,1152]{1,0:T(8,128)(2,1)S(1)}, bf16[32,1152]{1,0:T(8,128)(2,1)S(1)}, u32[]{:S(2)}, u32[]{:S(2)}) collective-permute-start(bf16[32,1152]{1,0:T(8,128)(2,1)S(1)} %collective-permute-done.5.refs_8_.refs_11_), channel_id=1, source_target_pairs={{0,1},{1,0},{2,3},{3,2},{4,5},{5,4},{6,7},{7,6},{8,9},{9,8},{10,11... | collective-permute-start | bytes 221192 | tf_op jit(solution)/shard_map/ppermute | solution.py:296
  12.9 2.5 %collective-permute-start.4 = (bf16[32,1152]{1,0:T(8,128)(2,1)S(1)}, bf16[32,1152]{1,0:T(8,128)(2,1)S(1)}, u32[]{:S(2)}, u32[]{:S(2)}) collective-permute-start(bf16[32,1152]{1,0:T(8,128)(2,1)S(1)} %collective-permute-done.3.refs_6_.refs_9_), channel_id=1, source_target_pairs={{0,1},{1,0},{2,3},{3,2},{4,5},{5,4},{6,7},{7,6},{8,9},{9,8},{10,11... | collective-permute-start | bytes 221192 | tf_op jit(solution)/shard_map/ppermute | solution.py:296
  13.3 0.7 %copy-start.5 = (f32[6]{0:T(128)S(1)}, f32[6]{0:T(128)}, u32[]{:S(2)}) copy-start(f32[6]{0:T(128)} %scale_ref.7) | copy-start | bytes 76
  18.1 11.9 %collective-permute-start.14 = (bf16[96,384]{1,0:T(8,128)(2,1)S(1)}, bf16[96,384]{1,0:T(8,128)(2,1)S(1)}, u32[]{:S(2)}, u32[]{:S(2)}) collective-permute-start(bf16[96,384]{1,0:T(8,128)(2,1)S(1)} %get-tuple-element.43), channel_id=1, source_target_pairs={{0,8},{8,16},{16,24},{24,0},{1,9},{9,17},{17,25},{25,1},{2,10},{10... | collective-permute-start | bytes 221192 | tf_op jit(solution)/shard_map/ppermute | solution.py:357
  19.8 10.8 %collective-permute-start.15 = (bf16[96,384]{1,0:T(8,128)(2,1)S(1)}, bf16[96,384]{1,0:T(8,128)(2,1)S(1)}, u32[]{:S(2)}, u32[]{:S(2)}) collective-permute-start(bf16[96,384]{1,0:T(8,128)(2,1)S(1)} %get-tuple-element.44), channel_id=1, source_target_pairs={{0,16},{8,24},{16,0},{24,8},{1,17},{9,25},{17,1},{25,9},{2,18},{10... | collective-permute-start | bytes 221192 | tf_op jit(solution)/shard_map/ppermute | solution.py:357
  22.4 8.2 %collective-permute-start.16 = (bf16[96,384]{1,0:T(8,128)(2,1)S(1)}, bf16[96,384]{1,0:T(8,128)(2,1)S(1)}, u32[]{:S(2)}, u32[]{:S(2)}) collective-permute-start(bf16[96,384]{1,0:T(8,128)(2,1)S(1)} %get-tuple-element.45), channel_id=1, source_target_pairs={{0,24},{8,0},{16,8},{24,16},{1,25},{9,1},{17,9},{25,17},{2,26},{10... | collective-permute-start | bytes 221192 | tf_op jit(solution)/shard_map/ppermute | solution.py:357
  23.7 4.8 %collective-permute-start.12 = (bf16[32,512]{1,0:T(8,128)(2,1)S(1)}, bf16[32,512]{1,0:T(8,128)(2,1)S(1)}, u32[]{:S(2)}, u32[]{:S(2)}) collective-permute-start(bf16[32,512]{1,0:T(8,128)(2,1)S(1)} %get-tuple-element.36.refs_5_), channel_id=1, source_target_pairs={{0,6},{1,7},{2,4},{3,5},{4,2},{5,3},{6,0},{7,1},{8,14},{9,15},{10,... | collective-permute-start | bytes 98312 | tf_op jit(solution)/shard_map/ppermute | solution.py:296
  25.9 4.1 %collective-permute-start.10 = (bf16[32,512]{1,0:T(8,128)(2,1)S(1)}, bf16[32,512]{1,0:T(8,128)(2,1)S(1)}, u32[]{:S(2)}, u32[]{:S(2)}) collective-permute-start(bf16[32,512]{1,0:T(8,128)(2,1)S(1)} %get-tuple-element.36.refs_5_), channel_id=1, source_target_pairs={{0,4},{1,5},{2,6},{3,7},{4,0},{5,1},{6,2},{7,3},{8,12},{9,13},{10,... | collective-permute-start | bytes 98312 | tf_op jit(solution)/shard_map/ppermute | solution.py:296
  28.5 5.6 %collective-permute-start.8 = (bf16[64,512]{1,0:T(8,128)(2,1)S(1)}, bf16[64,512]{1,0:T(8,128)(2,1)S(1)}, u32[]{:S(2)}, u32[]{:S(2)}) collective-permute-start(bf16[64,512]{1,0:T(8,128)(2,1)S(1)} %get-tuple-element.35.refs_4_), channel_id=1, source_target_pairs={{0,2},{1,3},{2,0},{3,1},{4,6},{5,7},{6,4},{7,5},{8,10},{9,11},{10,... | collective-permute-start | bytes 196616 | tf_op jit(solution)/shard_map/ppermute | solution.py:296
  30.0 2.7 %collective-permute-start.13 = (bf16[32,512]{1,0:T(8,128)(2,1)S(1)}, bf16[32,512]{1,0:T(8,128)(2,1)S(1)}, u32[]{:S(2)}, u32[]{:S(2)}) collective-permute-start(bf16[32,512]{1,0:T(8,128)(2,1)S(1)} %collective-permute-done.12.refs_15_), channel_id=1, source_target_pairs={{0,1},{1,0},{2,3},{3,2},{4,5},{5,4},{6,7},{7,6},{8,9},{9,8},{10,11... | collective-permute-start | bytes 98312 | tf_op jit(solution)/shard_map/ppermute | solution.py:296
  30.0 4.1 %collective-permute-start.11 = (bf16[32,512]{1,0:T(8,128)(2,1)S(1)}, bf16[32,512]{1,0:T(8,128)(2,1)S(1)}, u32[]{:S(2)}, u32[]{:S(2)}) collective-permute-start(bf16[32,512]{1,0:T(8,128)(2,1)S(1)} %collective-permute-done.10.refs_13_), channel_id=1, source_target_pairs={{0,1},{1,0},{2,3},{3,2},{4,5},{5,4},{6,7},{7,6},{8,9},{9,8},{10,11... | collective-permute-start | bytes 98312 | tf_op jit(solution)/shard_map/ppermute | solution.py:296
  30.6 6.0 %collective-permute-start.19 = (bf16[96,384]{1,0:T(8,128)(2,1)S(1)}, bf16[96,384]{1,0:T(8,128)(2,1)S(1)}, u32[]{:S(2)}, u32[]{:S(2)}) collective-permute-start(bf16[96,384]{1,0:T(8,128)(2,1)S(1)} %add_convert_fusion), channel_id=1, source_target_pairs={{0,6},{1,7},{2,4},{3,5},{4,2},{5,3},{6,0},{7,1},{8,14},{9,15},{10,... | collective-permute-start | bytes 221192 | tf_op jit(solution)/shard_map/ppermute | solution.py:296
  32.1 4.5 %collective-permute-start.18 = (bf16[96,384]{1,0:T(8,128)(2,1)S(1)}, bf16[96,384]{1,0:T(8,128)(2,1)S(1)}, u32[]{:S(2)}, u32[]{:S(2)}) collective-permute-start(bf16[96,384]{1,0:T(8,128)(2,1)S(1)} %add_convert_fusion), channel_id=1, source_target_pairs={{0,4},{1,5},{2,6},{3,7},{4,0},{5,1},{6,2},{7,3},{8,12},{9,13},{10,... | collective-permute-start | bytes 221192 | tf_op jit(solution)/shard_map/ppermute | solution.py:296
  32.7 4.7 %collective-permute-start.17 = (bf16[96,384]{1,0:T(8,128)(2,1)S(1)}, bf16[96,384]{1,0:T(8,128)(2,1)S(1)}, u32[]{:S(2)}, u32[]{:S(2)}) collective-permute-start(bf16[96,384]{1,0:T(8,128)(2,1)S(1)} %add_convert_fusion), channel_id=1, source_target_pairs={{0,2},{1,3},{2,0},{3,1},{4,6},{5,7},{6,4},{7,5},{8,10},{9,11},{10,... | collective-permute-start | bytes 221192 | tf_op jit(solution)/shard_map/ppermute | solution.py:296
  34.1 1.3 %collective-permute-start.9 = (bf16[64,512]{1,0:T(8,128)(2,1)S(1)}, bf16[64,512]{1,0:T(8,128)(2,1)S(1)}, u32[]{:S(2)}, u32[]{:S(2)}) collective-permute-start(bf16[64,512]{1,0:T(8,128)(2,1)S(1)} %collective-permute-done.8.refs_11_), channel_id=1, source_target_pairs={{0,1},{1,0},{2,3},{3,2},{4,5},{5,4},{6,7},{7,6},{8,9},{9,8},{10,11... | collective-permute-start | bytes 196616 | tf_op jit(solution)/shard_map/ppermute | solution.py:296
  34.2 7.8 %collective-permute-start.7 = (bf16[128,512]{1,0:T(8,128)(2,1)S(1)}, bf16[128,512]{1,0:T(8,128)(2,1)S(1)}, u32[]{:S(2)}, u32[]{:S(2)}) collective-permute-start(bf16[128,512]{1,0:T(8,128)(2,1)S(1)} %get-tuple-element.34.refs_3_), channel_id=1, source_target_pairs={{0,1},{1,0},{2,3},{3,2},{4,5},{5,4},{6,7},{7,6},{8,9},{9,8},{10,11... | collective-permute-start | bytes 393224 | tf_op jit(solution)/shard_map/ppermute | solution.py:296
  35.4 10.1 %collective-permute-start.20 = (bf16[96,384]{1,0:T(8,128)(2,1)S(1)}, bf16[96,384]{1,0:T(8,128)(2,1)S(1)}, u32[]{:S(2)}, u32[]{:S(2)}) collective-permute-start(bf16[96,384]{1,0:T(8,128)(2,1)S(1)} %add_convert_fusion), channel_id=1, source_target_pairs={{0,1},{1,0},{2,3},{3,2},{4,5},{5,4},{6,7},{7,6},{8,9},{9,8},{10,11... | collective-permute-start | bytes 221192 | tf_op jit(solution)/shard_map/ppermute | solution.py:296
  36.6 8.8 %collective-permute-start.23 = (bf16[96,384]{1,0:T(8,128)(2,1)S(1)}, bf16[96,384]{1,0:T(8,128)(2,1)S(1)}, u32[]{:S(2)}, u32[]{:S(2)}) collective-permute-start(bf16[96,384]{1,0:T(8,128)(2,1)S(1)} %collective-permute-done.19), channel_id=1, source_target_pairs={{0,1},{1,0},{2,3},{3,2},{4,5},{5,4},{6,7},{7,6},{8,9},{9,8},{10,11... | collective-permute-start | bytes 221192 | tf_op jit(solution)/shard_map/ppermute | solution.py:296
  36.6 8.8 %collective-permute-start.22 = (bf16[96,384]{1,0:T(8,128)(2,1)S(1)}, bf16[96,384]{1,0:T(8,128)(2,1)S(1)}, u32[]{:S(2)}, u32[]{:S(2)}) collective-permute-start(bf16[96,384]{1,0:T(8,128)(2,1)S(1)} %collective-permute-done.18), channel_id=1, source_target_pairs={{0,1},{1,0},{2,3},{3,2},{4,5},{5,4},{6,7},{7,6},{8,9},{9,8},{10,11... | collective-permute-start | bytes 221192 | tf_op jit(solution)/shard_map/ppermute | solution.py:296
  37.4 8.1 %collective-permute-start.21 = (bf16[96,384]{1,0:T(8,128)(2,1)S(1)}, bf16[96,384]{1,0:T(8,128)(2,1)S(1)}, u32[]{:S(2)}, u32[]{:S(2)}) collective-permute-start(bf16[96,384]{1,0:T(8,128)(2,1)S(1)} %collective-permute-done.17), channel_id=1, source_target_pairs={{0,1},{1,0},{2,3},{3,2},{4,5},{5,4},{6,7},{7,6},{8,9},{9,8},{10,11... | collective-permute-start | bytes 221192 | tf_op jit(solution)/shard_map/ppermute | solution.py:296

commit v2 on v1

v2 whole, which is shorter than its diff:
```python
import functools
import math

import jax
import jax.numpy as jnp
from jax import lax
from jax.experimental import pallas as pl
from jax.experimental.pallas import tpu as pltpu
from jax.sharding import PartitionSpec as P

BF = jnp.bfloat16
F32 = jnp.float32
SEQ = ("seqhi", "seqlo")
LANES = 128
HALF = 64
LOG2E = math.log2(math.e)
NN = (((1,), (0,)), ((), ()))
NT = (((1,), (1,)), ((), ()))
TN = (((0,), (0,)), ((), ()))


def dot(left, right, dims=NN):
    return lax.dot_general(left, right, dims, preferred_element_type=F32)


def iota(shape, dim):
    return lax.broadcasted_iota(jnp.int32, shape, dim)


def order_matrix(rows, top, inverse=False):
    source = iota((rows, rows), 0 if inverse else 1)
    place = source >> top
    for bit in range(top):
        place = place + ((source >> bit) & 1) * (rows >> (bit + 1))
    return jnp.where(place == iota((rows, rows), 1 if inverse else 0), 1.0, 0.0).astype(BF)


def side_masks():
    lane = iota((1, LANES), 1)
    low = jnp.where(lane < HALF, 1.0, 0.0)
    return low.astype(BF), (1.0 - low).astype(BF)


def factor_rows(heads):
    return -(-(heads + heads // 2) // 8) * 8


def fill_factors(scale_ref, factor_ref):
    heads = scale_ref.shape[0]
    lane = iota((1, LANES), 1)
    for head in range(heads):
        factor_ref[head : head + 1, :] = jnp.full((1, LANES), scale_ref[head] * (HALF**-0.5 * LOG2E), F32)
    for pair in range(heads // 2):
        both = jnp.where(lane < HALF, scale_ref[2 * pair], scale_ref[2 * pair + 1]) * (HALF**-0.5)
        factor_ref[heads + pair : heads + pair + 1, :] = both


def exponent(factor_ref, head, columns):
    return stack([factor_ref[head : head + 1, :]] * (columns // LANES), 1)


def side_factor(factor_ref, heads, pair):
    return factor_ref[heads + pair : heads + pair + 1, :]


def stack(parts, axis):
    return parts[0] if len(parts) == 1 else jnp.concatenate(parts, axis=axis)


def doubled(value):
    return jnp.concatenate([value, value], axis=0)


def halves_sum(value):
    half = value.shape[0] // 2
    return value[:half] + value[half:]


def lane_pair(offset, pair):
    return slice(offset + LANES * pair, offset + LANES * (pair + 1))


def denom_slot(pair, side, amount, rows):
    lane = iota((1, LANES), 1)
    slot = lane - side * HALF
    hit = (slot == 16 * pair) | (slot == 16 * pair + 8)
    row = jnp.where(hit, float(amount), 0.0)
    return jnp.broadcast_to(row, (rows, LANES)).astype(BF)


def denom_lanes(denoms):
    lane = iota((1, LANES), 1)
    slot = (lane % HALF) // 8
    packed = jnp.zeros(denoms[0].shape, F32)
    for pair, value in enumerate(denoms):
        high = value.astype(BF).astype(F32)
        packed = jnp.where(slot == 2 * pair, high, packed)
        packed = jnp.where(slot == 2 * pair + 1, value - high, packed)
    return packed.astype(BF)


class View:
    def __init__(self, array, start=0, rows=None):
        self.array = array
        self.start = start
        self.rows = array.shape[0] - start if rows is None else rows


VMEM = pl.BlockSpec(memory_space=pltpu.VMEM)
SMEM = pl.BlockSpec(memory_space=pltpu.SMEM)
HBM = pl.BlockSpec(memory_space=pltpu.HBM)


def call(kernel, name, shapes, arrays, views=(), scalars=(), flops=0, scratch=(), specs=None):
    unique, where = [], []
    for group in views:
        places = []
        for view in group:
            spot = next((at for at, array in enumerate(unique) if array is view.array), None)
            if spot is None:
                spot = len(unique)
                unique.append(view.array)
            places.append((spot, view.start, view.rows))
        where.append(places)

    def body(*refs):
        scalar_refs, refs = refs[: len(scalars)], refs[len(scalars) :]
        array_refs, refs = refs[: len(arrays)], refs[len(arrays) :]
        view_refs, refs = refs[: len(unique)], refs[len(unique) :]

        def load(group, columns):
            return stack(
                [view_refs[spot][start : start + rows, columns] for spot, start, rows in where[group]], 0
            )

        kernel(load, *scalar_refs, *array_refs, *refs)

    moved = sum(math.prod(shape) * jnp.dtype(kind).itemsize for shape, kind in shapes)
    return pl.pallas_call(
        body,
        out_shape=[jax.ShapeDtypeStruct(shape, kind) for shape, kind in shapes],
        in_specs=[SMEM] * len(scalars) + (specs or [VMEM] * len(arrays)) + [VMEM] * len(unique),
        out_specs=[VMEM] * len(shapes),
        scratch_shapes=list(scratch),
        compiler_params=pltpu.CompilerParams(vmem_limit_bytes=48 * 2**20),
        cost_estimate=pl.CostEstimate(flops=flops, transcendentals=0, bytes_accessed=moved),
        name=name,
    )(*scalars, *arrays, *unique)


def pool_kernel(top, places, load, q_hbm, k_hbm, v_hbm, scale_hbm, factor_ref, *refs):
    level_refs, (q_ref, k_ref, v_ref, scale_ref, sems) = refs[:-5], refs[-5:]
    copies = [
        pltpu.make_async_copy(source, target, sems.at[index])
        for index, (source, target) in enumerate(
            ((q_hbm, q_ref), (k_hbm, k_ref), (v_hbm, v_ref), (scale_hbm, scale_ref))
        )
    ]
    for copy in copies:
        copy.start()
    rows, width = q_ref.shape
    order = order_matrix(rows, top)
    for which, ref in enumerate((q_ref, k_ref, v_ref)):
        copies[which].wait()
        current = dot(order, ref[...])
        columns = slice(which * width, (which + 1) * width)
        level_refs[0][:, columns] = current.astype(BF)
        for height in range(1, top + 1):
            total = halves_sum(current)
            rounded = (total if which == 2 else 0.5 * total).astype(BF)
            target, start = places[height - 1]
            level_refs[target][start : start + rounded.shape[0], columns] = rounded
            current = rounded.astype(F32)
    copies[3].wait()
    fill_factors(scale_ref, factor_ref)


def attend(factor_ref, pair, queries, keys, values, amount, low, high):
    weights = []
    for side, mask in enumerate((low, high)):
        logits = dot(queries * mask, keys, NT)
        weights.append(jnp.exp2(logits * exponent(factor_ref, 2 * pair + side, keys.shape[0])).astype(BF))
    count = jnp.full(values.shape, float(amount), BF)
    right = stack([stack([values * mask, count * mask], 1) for mask in (low, high)], 0)
    return dot(stack(weights, 1), right)


def base_kernel(top, load, factor_ref, x_ref, cot_ref, w_ref, numer_ref, denom_ref, cotp_ref, back_ref):
    rows, width = cot_ref.shape
    low, high = side_masks()
    for pair in range(width // LANES):
        q, k, v = (x_ref[:, lane_pair(width * which, pair)] for which in range(3))
        both = attend(factor_ref, pair, q, k, v, 1, low, high)
        numer_ref[:, lane_pair(0, pair)] = both[:, :LANES]
        denom_ref[:, lane_pair(0, pair)] = both[:, LANES:]
    cotan = dot(order_matrix(rows, top), cot_ref[...]).astype(BF)
    cotp_ref[...] = cotan
    back_ref[...] = dot(cotan, w_ref[...], NT).astype(BF)


def packed_rows(own_rows, width):
    return own_rows * width // (width + LANES)


def pack(piece):
    own_rows, width = piece.shape
    rows = packed_rows(own_rows, width)
    tail = stack([piece[rows:, lane_pair(0, block)] for block in range(width // LANES)], 0)
    return stack([piece[:rows], tail], 1)


def unpack_into(packed, out_ref):
    own_rows, width = out_ref.shape
    rows = packed.shape[0]
    out_ref[:rows, :] = packed[:, :width]
    extra = own_rows - rows
    for block in range(width // LANES):
        out_ref[rows:, lane_pair(0, block)] = packed[block * extra : (block + 1) * extra, width:]


def forward_kernel(
    top, parts, packed, grad_places, piece_places,
    load, place_ref, factor_ref, numer_ref, denom_ref, cotp_ref, back_ref, *refs
):
    out_refs, weight_ref = refs[:-1], refs[-1]
    rows, width = numer_ref.shape
    low, high = side_masks()
    lane = iota((LANES, LANES), 1)
    ones = jnp.where(lane // HALF == iota((LANES, LANES), 0) // HALF, 1.0, 0.0).astype(BF)
    adder = doubled(ones)
    grad_rows = []
    denom_rows = []
    attended = []
    for pair in range(width // LANES):
        total = None
        for height in range(top, 0, -1):
            keys, values = (load(top + height - 1, lane_pair(width * which, pair)) for which in (1, 2))
            queries = load(height - 1, lane_pair(0, pair))
            both = attend(factor_ref, pair, queries, keys, values, 2**height, low, high)
            total = both if total is None else both + doubled(total)
        total = doubled(total)
        numer = numer_ref[:, lane_pair(0, pair)] + total[:, :LANES]
        inverse = 1.0 / (denom_ref[:, lane_pair(0, pair)] + total[:, LANES:])
        ratio = numer * inverse
        attended.append(ratio.astype(BF))
        back = back_ref[:, lane_pair(0, pair)].astype(F32)
        product = back * ratio
        product_high = product.astype(BF)
        product_low = (product - product_high.astype(F32)).astype(BF)
        summed = dot(stack([product_high, product_low], 1), adder)
        grad_rows.append(back * inverse)
        denom_rows.append(-summed * inverse)
    weight_ref[...] = dot(stack(attended, 1), cotp_ref[...], TN)
    own_rows = width // parts
    for step, (target, start) in enumerate(piece_places):
        first = pl.multiple_of(place_ref[step] * own_rows, math.gcd(own_rows, 8))
        piece = weight_ref[pl.ds(first, own_rows), :]
        if packed:
            piece = pack(piece)
        out_refs[target][start : start + piece.shape[0], :] = piece.astype(BF)
    for height, (target, start) in enumerate(grad_places):
        if height:
            grad_rows = [halves_sum(value) for value in grad_rows]
            denom_rows = [halves_sum(value) for value in denom_rows]
        span = slice(start, start + (rows >> height))
        for pair, value in enumerate(grad_rows):
            out_refs[target][span, lane_pair(0, pair)] = value.astype(BF)
        out_refs[target][span, width:] = denom_lanes(denom_rows)


def slopes(factor_ref, pair, first, second, left, right, low, high):
    weights, slope = [], []
    for side, mask in enumerate((low, high)):
        logits = dot(first * mask, second, NT)
        weight = jnp.exp2(logits * exponent(factor_ref, 2 * pair + side, second.shape[0]))
        weights.append(weight.astype(BF))
        slope.append((weight * dot(left[side], right[side], NT)).astype(BF))
    return weights, slope


def masked_stack(value, low, high):
    return stack([value * low, value * high], 0)


def slope_sides(grad, denom, values, pair, height, low, high):
    slots = [denom_slot(pair, side, 2**height, values.shape[0]) for side in (0, 1)]
    queries = [stack([grad * mask, denom], 1) for mask in (low, high)]
    return queries, [stack([values, slot], 1) for slot in slots]


def near_kernel(load, factor_ref, x_ref, gh_ref, query_ref, key_ref, value_ref):
    rows, width = query_ref.shape
    heads = width // HALF
    low, high = side_masks()
    for pair in range(width // LANES):
        factor = side_factor(factor_ref, heads, pair)
        queries, keys, values = (x_ref[:, lane_pair(width * which, pair)] for which in range(3))
        grad = gh_ref[:, lane_pair(0, pair)]
        left, right = slope_sides(grad, gh_ref[:, width:], values, pair, 0, low, high)
        weights, slope = slopes(factor_ref, pair, queries, keys, left, right, low, high)
        query_ref[:, lane_pair(0, pair)] = dot(stack(slope, 1), masked_stack(keys, low, high)) * factor
        key_ref[:, lane_pair(0, pair)] = dot(stack(slope, 0), masked_stack(queries, low, high), TN) * factor
        value_ref[:, lane_pair(0, pair)] = dot(stack(weights, 0), masked_stack(grad, low, high), TN)


def far_kernel(top, load, factor_ref, base_ref, out_ref):
    rows, width = out_ref.shape
    heads = width // HALF
    low, high = side_masks()
    results = []
    for pair in range(width // LANES):
        factor = side_factor(factor_ref, heads, pair)
        total = None
        for height in range(top, 0, -1):
            queries = load(height - 1, lane_pair(0, pair))
            grad = load(top + height - 1, lane_pair(0, pair))
            denom = load(top + height - 1, slice(width, width + LANES))
            keys, values = (load(2 * top + height - 1, lane_pair(width * which, pair)) for which in (1, 2))
            left, right = slope_sides(grad, denom, values, pair, height, low, high)
            _, slope = slopes(factor_ref, pair, queries, keys, left, right, low, high)
            piece = dot(stack(slope, 1), masked_stack(keys, low, high)) * factor
            total = piece if total is None else piece + 0.5 * doubled(total)
        total = base_ref[:, lane_pair(0, pair)] + 0.5 * doubled(total)
        results.append(total.astype(BF))
    out_ref[...] = dot(order_matrix(rows, top, True), stack(results, 1)).astype(BF)


def key_kernel(top, load, factor_ref, base_key_ref, base_value_ref, key_out_ref, value_out_ref):
    rows, width = key_out_ref.shape
    heads = width // HALF
    low, high = side_masks()
    key_results, value_results = [], []
    for pair in range(width // LANES):
        factor = side_factor(factor_ref, heads, pair)
        key_total = value_total = None
        for height in range(top, 0, -1):
            keys, values = (load(height - 1, lane_pair(width * which, pair)) for which in (1, 2))
            queries = load(top + height - 1, lane_pair(0, pair))
            grad = load(2 * top + height - 1, lane_pair(0, pair))
            denom = load(2 * top + height - 1, slice(width, width + LANES))
            left = [
                stack([values * mask, denom_slot(pair, side, 2**height, values.shape[0])], 1)
                for side, mask in enumerate((low, high))
            ]
            right = [stack([grad, denom], 1)] * 2
            weights, slope = slopes(factor_ref, pair, keys, queries, left, right, low, high)
            key_piece = dot(stack(slope, 1), masked_stack(queries, low, high)) * factor
            value_piece = dot(stack(weights, 1), masked_stack(grad, low, high))
            if key_total is not None:
                key_piece = key_piece + 0.5 * doubled(key_total)
                value_piece = value_piece + doubled(value_total)
            key_total, value_total = key_piece, value_piece
        key_total = base_key_ref[:, lane_pair(0, pair)] + 0.5 * doubled(key_total)
        value_total = base_value_ref[:, lane_pair(0, pair)] + doubled(value_total)
        key_results.append(key_total.astype(BF))
        value_results.append(value_total.astype(BF))
    back = order_matrix(rows, top, True)
    key_out_ref[...] = dot(back, stack(key_results, 1)).astype(BF)
    value_out_ref[...] = dot(back, stack(value_results, 1)).astype(BF)


def pair_payload_kernel(rows, load, *refs):
    out_ref = refs[-1]
    every = slice(None)
    out_ref[:rows, :] = load(0, every)
    out_ref[rows : 2 * rows, :] = load(1, every)
    if out_ref.shape[0] > 2 * rows:
        out_ref[2 * rows :, :] = total_of(load, (2, 3)).astype(BF)


def total_of(load, groups):
    total = None
    for group in groups:
        value = load(group, slice(None)).astype(F32)
        total = value if total is None else total + value
    return total


def sum_kernel(count, load, out_ref):
    out_ref[...] = total_of(load, range(count)).astype(out_ref.dtype)


def unpack_sum_kernel(count, load, out_ref):
    unpack_into(total_of(load, range(count)), out_ref)


def traded(value, mask):
    return lax.ppermute(value, SEQ, [(source, source ^ mask) for source in range(lax.axis_size(SEQ))])


def split_traded(value):
    return lax.ppermute(
        value, SEQ, [(source, source ^ (4 + 2 * (source % 2))) for source in range(lax.axis_size(SEQ))]
    )


def from_siblings(levels, top):
    arrived = {}
    for offset in range(1, 2**top):
        height = offset.bit_length()
        if offset == 1:
            arrived[1] = traded(levels[1], 1)
        elif offset % 2 == 0:
            arrived[offset] = traded(levels[height], offset)
        else:
            arrived[offset] = traded(arrived[offset - 1], 1)
    grouped = []
    for height in range(1, top + 1):
        parts = [arrived[offset] for offset in range(2 ** (height - 1), 2**height)]
        if parts[0].shape[0] < 16:
            parts = [jnp.concatenate(parts, axis=0)]
        grouped.append([View(part) for part in parts])
    return grouped


def shards(queries, key_rows, value_rows, head_scale, out_weight, cotangent):
    rows, width = queries.shape[1:]
    heads = head_scale.shape[0]
    top = lax.axis_size(SEQ).bit_length() - 1
    parts = lax.axis_size("dp")
    assert width == HALF * heads and width % LANES == 0 and width <= 4 * LANES
    riding = top == 3 and parts == 4 and rows == 256
    whole = (rows, width)
    wide = width + LANES
    sizes = [rows >> height for height in range(top + 1)]
    if riding:
        places = [(1, 0), (2, 0), (1, sizes[1])]
        pooled = [rows, sizes[1] + sizes[3], sizes[2]]
    else:
        places = [(height, 0) for height in range(1, top + 1)]
        pooled = sizes
    factors, base_rows, *levels = call(
        functools.partial(pool_kernel, top, places),
        "pool",
        [((factor_rows(heads), LANES), F32)] + [((count, 3 * width), BF) for count in pooled],
        [queries[0], key_rows[0], value_rows[0], head_scale],
        specs=[HBM] * 4,
        scratch=[pltpu.VMEM(whole, BF)] * 3 + [pltpu.SMEM((heads,), F32), pltpu.SemaphoreType.DMA((4,))],
    )
    levels = [base_rows, *levels]
    numer, denom, cotan, back = call(
        functools.partial(base_kernel, top),
        "base",
        [(whole, F32), (whole, F32), (whole, BF), (whole, BF)],
        [factors, base_rows, cotangent[0], out_weight],
        flops=4 * rows * rows * width * 4,
    )
    own = [[View(levels[target], start, sizes[height + 1])] for height, (target, start) in enumerate(places)]
    if riding:
        within = traded(levels[1], 1)
        across = traded(levels[2], 2)
        (third,) = call(
            functools.partial(pair_payload_kernel, sizes[3]),
            "third_rows",
            [((2 * sizes[3], 3 * width), BF)],
            [],
            views=[own[2], [View(within, sizes[1], sizes[3])]],
        )
        split = split_traded(third)
        across, numer = lax.optimization_barrier((across, numer))
        across_too = traded(across, 1)
        split_too = traded(split, 1)
        siblings = [
            [View(within, 0, sizes[1])],
            [View(across), View(across_too)],
            [View(split), View(split_too)],
        ]
    else:
        siblings = from_siblings(levels, top)
    own_rows = width // parts
    if riding:
        spot = lax.axis_index(SEQ).astype(jnp.int32)
        chip, core = spot // 2, spot % 2
        place = jnp.stack([chip, chip ^ 1, chip ^ (3 - core), chip ^ (2 + core)])
        packed = packed_rows(own_rows, width)
        grad_places = [(0, 0), (1, sizes[3]), (2, 0), (1, 0)]
        near_rows = sizes[1] + sizes[3]
        piece_places = [(1, near_rows), (2, sizes[2]), (1, near_rows + packed), (3, 0)]
        shapes = [(rows, wide), (near_rows + 2 * packed, wide), (sizes[2] + packed, wide), (packed, wide)]
    else:
        place = (lax.axis_index("dp").astype(jnp.int32) + jnp.arange(parts, dtype=jnp.int32)) % parts
        grad_places = [(height, 0) for height in range(top + 1)]
        piece_places = [(top + 1 + step, 0) for step in range(parts)]
        shapes = [(size, wide) for size in sizes] + [(own_rows, width)] * parts
    outs = call(
        functools.partial(forward_kernel, top, parts, riding, grad_places, piece_places),
        "forward",
        [(shape, BF) for shape in shapes],
        [factors, numer, denom, cotan, back],
        views=own + siblings,
        scalars=[place],
        scratch=[pltpu.VMEM((width, width), F32)],
    )
    near_query, near_key, near_value = call(
        near_kernel,
        "near",
        [(whole, F32)] * 3,
        [factors, base_rows, outs[0]],
        flops=8 * rows * rows * width * 4,
    )
    own_grads = [[View(outs[target], start, sizes[height])] for height, (target, start) in enumerate(grad_places)]
    def far_call():
        return call(
            functools.partial(far_kernel, top),
            "far",
            [(whole, BF)],
            [factors, near_query],
            views=own + own_grads[1:] + siblings,
            flops=8 * rows * rows * width,
        )[0]

    def key_call():
        return call(
            functools.partial(key_kernel, top),
            "key",
            [(whole, BF), (whole, BF)],
            [factors, near_key, near_value],
            views=own + siblings + sibling_grads,
            flops=8 * rows * rows * width * 2,
        )

    if riding:
        near, far, mine = outs[1:4]
        near_in = traded(near, 1)
        far_in = traded(far, 2)
        (third,) = call(
            functools.partial(pair_payload_kernel, sizes[3]),
            "third_grads",
            [((2 * sizes[3] + packed, wide), BF)],
            [],
            views=[
                own_grads[3],
                [View(near_in, 0, sizes[3])],
                [View(mine)],
                [View(near_in, near_rows + packed, packed)],
            ],
        )
        third_in = split_traded(third)
        far_in, near_query = lax.optimization_barrier((far_in, near_query))
        far_too = traded(far_in, 1)
        third_too = traded(third_in, 1)
        sibling_grads = [
            [View(near_in, sizes[3], sizes[1])],
            [View(far_in, 0, sizes[2]), View(far_too, 0, sizes[2])],
            [View(third_in, 0, 2 * sizes[3]), View(third_too, 0, 2 * sizes[3])],
        ]
        (weight,) = call(
            functools.partial(sum_kernel, 6),
            "weight_seq",
            [((packed, wide), BF)],
            [],
            views=[[View(value, value.shape[0] - packed)] for value in (far_in, far_too, third_in, third_too)]
            + [[View(value, near_rows, packed)] for value in (near, near_in)],
        )
        moves = [[], []]
        for z in range(4):
            for k in range(4):
                for c in range(2):
                    for turn in range(2):
                        target = (k * 4 + (z - 2 * turn - c) % 4) * 2 + c
                        moves[turn].append(((z * 4 + k) * 2 + c, target))
        first, second = (lax.ppermute(weight, ("dp", *SEQ), pairs) for pairs in moves)
        key_grad, value_grad = key_call()
        first, key_grad = lax.optimization_barrier((first, key_grad))
        (half,) = call(
            functools.partial(sum_kernel, 2),
            "weight_core",
            [((packed, wide), BF)],
            [],
            views=[[View(first)], [View(second)]],
        )
        other = traded(half, 1)
        query_grad = far_call()
        other, query_grad = lax.optimization_barrier((other, query_grad))
        (weight,) = call(
            functools.partial(unpack_sum_kernel, 2),
            "weight_out",
            [((own_rows, width), F32)],
            [],
            views=[[View(half)], [View(other)]],
        )
    else:
        grads, pieces = outs[: top + 1], outs[top + 1 :]
        weight = pieces[0].astype(F32)
        for step in range(1, parts):
            weight = weight + lax.ppermute(
                pieces[step], "dp", [(source, (source + step) % parts) for source in range(parts)]
            ).astype(F32)
        sibling_grads = from_siblings(grads, top)
        bit = 1
        while bit < top:
            weight = weight.astype(BF)
            group = [weight] + [traded(weight, mask << bit) for mask in range(1, 2 ** min(2, top - bit))]
            weight = sum(value.astype(F32) for value in group)
            bit += 2
        weight = weight.astype(BF)
        weight = weight.astype(F32) + traded(weight, 1).astype(F32)
        query_grad = far_call()
        key_grad, value_grad = key_call()
    return query_grad[None], key_grad[None], value_grad[None], weight


def solution(mesh):
    spread = P("dp", SEQ, None)
    return jax.shard_map(
        shards,
        mesh=mesh,
        in_specs=(spread, spread, spread, P(), P(), spread),
        out_specs=(spread, spread, spread, P("dp", None)),
        check_vma=False,
    )
```

time: 46.5 us -> 47.5 us (1.022)
  the two profiles are of different devices: /device:TPU:0 before, /device:TPU:25 now
where the time goes in v2:
time: 47.5 us; the launch traced here: 47.3 us
  starting transfers between devices  19.2 us (40%)
  Pallas kernels  13 us (27%)
  waiting for transfers between devices  10.9 us (23%)
  local copies, waits for them, and re-layouts  3.43 us (7%)
  between operations  0.71 us (1%)
    pallas_call x11, Pallas kernels, call(): pl.pallas_call(body, out_shape=[jax.ShapeDtypeStruct(shape, kind) for sha...  13 us
    ppermute x9, starting transfers between devices, traded(): lax.ppermute(value, SEQ, [(source, source ^ mask) for source in range(lax...  11.4 us
    ppermute x9, waiting for transfers between devices, traded(): lax.ppermute(value, SEQ, [(source, source ^ mask) for source in range(lax...  5.57 us
    ppermute x2, waiting for transfers between devices, shards(): lax.ppermute(weight, ('dp', *SEQ), pairs)  5.21 us
    ppermute x2, starting transfers between devices, split_traded(): lax.ppermute(value, SEQ, [(source, source ^ 4 + 2 * (source % 2)) for sou...  4.21 us
    ppermute x2, starting transfers between devices, shards(): lax.ppermute(weight, ('dp', *SEQ), pairs)  3.55 us
    unnamed x12, local copies, waits for them, and re-layouts  3.43 us
  transfers between devices with their start and end apart: 13, of which 8 were waited for; matrix products, arithmetic and copies ran while one was open for 0% of the time, Pallas kernels for 17%

profile of v2, /device:TPU:25, one launch (start us, length us, event | category | flops | bytes accessed | tf_op | source)
XLA Modules:
  0.0 47.3 jit_solution(14702291749489735843)
XLA Ops:
  0.6 0.0 copy-start.3
  0.6 0.6 %copy-done.3 = f32[6]{0:T(128)S(1)} copy-done((f32[6]{0:T(128)S(1)}, f32[6]{0:T(128)}, u32[]{:S(2)}) %copy-start.3) | copy-done | bytes 48
  1.3 0.0 copy-start
  1.3 0.9 %copy-done = bf16[1,256,384]{2,1,0:T(8,128)(2,1)S(1)} copy-done((bf16[1,256,384]{2,1,0:T(8,128)(2,1)S(1)}, bf16[1,256,384]{2,1,0:T(8,128)(2,1)}, u32[]{:S(2)}) %copy-start) | copy-done | bytes 196632
  2.2 0.0 copy-start.1
  2.2 0.9 %copy-done.1 = bf16[1,256,384]{2,1,0:T(8,128)(2,1)S(1)} copy-done((bf16[1,256,384]{2,1,0:T(8,128)(2,1)S(1)}, bf16[1,256,384]{2,1,0:T(8,128)(2,1)}, u32[]{:S(2)}) %copy-start.1) | copy-done | bytes 196632
  3.1 0.0 copy-start.2
  3.1 0.9 %copy-done.2 = bf16[1,256,384]{2,1,0:T(8,128)(2,1)S(1)} copy-done((bf16[1,256,384]{2,1,0:T(8,128)(2,1)S(1)}, bf16[1,256,384]{2,1,0:T(8,128)(2,1)}, u32[]{:S(2)}) %copy-start.2) | copy-done | bytes 196632
  4.1 1.5 %pool.1 = (f32[16,128]{1,0:T(8,128)S(1)}, bf16[256,1152]{1,0:T(8,128)(2,1)S(1)}, bf16[160,1152]{1,0:T(8,128)(2,1)S(1)}, bf16[64,1152]{1,0:T(8,128)(2,1)S(1)}) custom-call(bf16[256,384]{1,0:T(8,128)(2,1)S(1)} %bitcast.11, bf16[256,384]{1,0:T(8,128)(2,1)S(1)} %bitcast.12, bf16[256,384]{1,0:T(8,128)(2,1)S(1)} %bitcast.13, f32[6]{0:T(128)S(1)} %copy-done.3), custom_call_target="tpu_custom_call" | custom-call | bytes 1114112 | tf_op jit(solution)/shard_map/pool/pallas_call | solution.py:139
  5.6 0.7 %collective-permute-start.1 = (bf16[160,1152]{1,0:T(8,128)(2,1)S(1)}, bf16[160,1152]{1,0:T(8,128)(2,1)S(1)}, u32[]{:S(2)}, u32[]{:S(2)}) collective-permute-start(bf16[160,1152]{1,0:T(8,128)(2,1)S(1)} %get-tuple-element.37.refs_0_.refs_6_.refs_3_.refs_2_), channel_id=1, source_target_pairs={{0,1},{1,0},{2,3},{3,2},{4,5},{5,4},{6,7},{7,6},{8,9},{9,8},{10,11... | collective-permute-start | bytes 1105928 | tf_op jit(solution)/shard_map/ppermute | solution.py:388
  6.4 0.0 copy-start.4
  6.4 0.0 copy-start.5
  6.4 1.3 %collective-permute-start = (bf16[64,1152]{1,0:T(8,128)(2,1)S(1)}, bf16[64,1152]{1,0:T(8,128)(2,1)S(1)}, u32[]{:S(2)}, u32[]{:S(2)}) collective-permute-start(bf16[64,1152]{1,0:T(8,128)(2,1)S(1)} %get-tuple-element.30.refs_7_.refs_4_.refs_3_), channel_id=1, source_target_pairs={{0,2},{1,3},{2,0},{3,1},{4,6},{5,7},{6,4},{7,5},{8,10},{9,11},{10,... | collective-permute-start | bytes 442376 | tf_op jit(solution)/shard_map/ppermute | solution.py:388
  7.6 0.0 collective-permute-done.1.refs_1_.refs_8_.refs_5_.refs_6_
  7.7 2.2 %collective-permute-start.3 = (bf16[64,1152]{1,0:T(8,128)(2,1)S(1)}, bf16[64,1152]{1,0:T(8,128)(2,1)S(1)}, u32[]{:S(2)}, u32[]{:S(2)}) collective-permute-start(bf16[64,1152]{1,0:T(8,128)(2,1)S(1)} %third_rows.1), channel_id=1, source_target_pairs={{0,4},{1,7},{2,6},{3,5},{4,0},{5,3},{6,2},{7,1},{8,12},{9,15},{10,... | collective-permute-start | bytes 442376 | tf_op jit(solution)/shard_map/ppermute | solution.py:392
  9.9 0.0 copy-done.4
  9.9 0.0 copy-done.5
  9.9 0.8 %base.1 = (f32[256,384]{1,0:T(8,128)S(1)}, f32[256,384]{1,0:T(8,128)S(1)}, bf16[256,384]{1,0:T(8,128)(2,1)S(1)}, bf16[256,384]{1,0:T(8,128)(2,1)S(1)}) custom-call(f32[16,128]{1,0:T(8,128)S(1)} %get-tuple-element.29.refs_0_.refs_1_, bf16[256,1152]{1,0:T(8,128)(2,1)S(1)} %get-tuple-element.31.refs_1_, bf16[256,384]{1,0:T(8,128)(2,1)S(1)} %bitcast.14, ...), custom_call_target="tpu_custom_call" | custom-call | flops 402653184 | bytes 1179648 | tf_op jit(solution)/shard_map/base/pallas_call | solution.py:139
  10.8 2.3 %collective-permute-done.refs_9_.refs_6_.refs_7_ = bf16[64,1152]{1,0:T(8,128)(2,1)S(1)} collective-permute-done((bf16[64,1152]{1,0:T(8,128)(2,1)S(1)}, bf16[64,1152]{1,0:T(8,128)(2,1)S(1)}, u32[]{:S(2)}, u32[]{:S(2)}) %collective-permute-start) | collective-permute-done | bytes 147488 | tf_op jit(solution)/shard_map/ppermute | solution.py:388
  13.1 1.2 %collective-permute-start.2 = (bf16[64,1152]{1,0:T(8,128)(2,1)S(1)}, bf16[64,1152]{1,0:T(8,128)(2,1)S(1)}, u32[]{:S(2)}, u32[]{:S(2)}) collective-permute-start(bf16[64,1152]{1,0:T(8,128)(2,1)S(1)} %collective-permute-done.refs_9_.refs_6_.refs_7_), channel_id=1, source_target_pairs={{0,1},{1,0},{2,3},{3,2},{4,5},{5,4},{6,7},{7,6},{8,9},{9,8},{10,11... | collective-permute-start | bytes 442376 | tf_op jit(solution)/shard_map/ppermute | solution.py:388
  14.2 0.0 collective-permute-done.3.refs_11_.refs_8_.refs_9_
  14.2 0.5 %collective-permute-start.4 = (bf16[64,1152]{1,0:T(8,128)(2,1)S(1)}, bf16[64,1152]{1,0:T(8,128)(2,1)S(1)}, u32[]{:S(2)}, u32[]{:S(2)}) collective-permute-start(bf16[64,1152]{1,0:T(8,128)(2,1)S(1)} %collective-permute-done.3.refs_11_.refs_8_.refs_9_), channel_id=1, source_target_pairs={{0,1},{1,0},{2,3},{3,2},{4,5},{5,4},{6,7},{7,6},{8,9},{9,8},{10,11... | collective-permute-start | bytes 442376 | tf_op jit(solution)/shard_map/ppermute | solution.py:388
  14.7 0.1 pad_add_fusion.refs_0_
  14.8 0.4 collective-permute-done.2.refs_10_.refs_7_.refs_8_
  15.2 0.5 %collective-permute-done.4.refs_12_.refs_9_.refs_10_ = bf16[64,1152]{1,0:T(8,128)(2,1)S(1)} collective-permute-done((bf16[64,1152]{1,0:T(8,128)(2,1)S(1)}, bf16[64,1152]{1,0:T(8,128)(2,1)S(1)}, u32[]{:S(2)}, u32[]{:S(2)}) %collective-permute-start.4) | collective-permute-done | bytes 147488 | tf_op jit(solution)/shard_map/ppermute | solution.py:388
  15.7 2.6 %forward.1 = (bf16[256,512]{1,0:T(8,128)(2,1)S(1)}, bf16[304,512]{1,0:T(8,128)(2,1)S(1)}, bf16[136,512]{1,0:T(8,128)(2,1)S(1)}, bf16[72,512]{1,0:T(8,128)(2,1)S(1)}) custom-call(s32[4]{0:T(128)S(1)} %pad_add_fusion.refs_0_, f32[16,128]{1,0:T(8,128)S(1)} %get-tuple-element.29.refs_0_.refs_1_, f32[256,384]{1,0:T(8,128)S(1)} %get-tuple-element.33.refs_2_, ...), custom_call_target="tpu_custom_call" | custom-call | bytes 786432 | tf_op jit(solution)/shard_map/forward/pallas_call | solution.py:139
  18.4 0.4 collective-permute-start.7
  18.8 0.8 %collective-permute-start.5 = (bf16[136,512]{1,0:T(8,128)(2,1)S(1)}, bf16[136,512]{1,0:T(8,128)(2,1)S(1)}, u32[]{:S(2)}, u32[]{:S(2)}) collective-permute-start(bf16[136,512]{1,0:T(8,128)(2,1)S(1)} %get-tuple-element.39.refs_5_), channel_id=1, source_target_pairs={{0,2},{1,3},{2,0},{3,1},{4,6},{5,7},{6,4},{7,5},{8,10},{9,11},{10,... | collective-permute-start | bytes 417800 | tf_op jit(solution)/shard_map/ppermute | solution.py:388
  19.6 0.5 collective-permute-done.7.refs_1_.refs_5_.refs_10_
  20.1 2.0 %collective-permute-start.8 = (bf16[136,512]{1,0:T(8,128)(2,1)S(1)}, bf16[136,512]{1,0:T(8,128)(2,1)S(1)}, u32[]{:S(2)}, u32[]{:S(2)}) collective-permute-start(bf16[136,512]{1,0:T(8,128)(2,1)S(1)} %third_grads.1), channel_id=1, source_target_pairs={{0,4},{1,7},{2,6},{3,5},{4,0},{5,3},{6,2},{7,1},{8,12},{9,15},{10,... | collective-permute-start | bytes 417800 | tf_op jit(solution)/shard_map/ppermute | solution.py:392
  22.1 1.5 %near.1 = (f32[256,384]{1,0:T(8,128)S(1)}, f32[256,384]{1,0:T(8,128)S(1)}, f32[256,384]{1,0:T(8,128)S(1)}) custom-call(f32[16,128]{1,0:T(8,128)S(1)} %get-tuple-element.29.refs_0_.refs_1_, bf16[256,1152]{1,0:T(8,128)(2,1)S(1)} %get-tuple-element.31.refs_1_, bf16[256,512]{1,0:T(8,128)(2,1)S(1)} %get-tuple-element.40.refs_2_), custom_call_target="tpu_custom_call" | custom-call | flops 805306368 | bytes 1179648 | tf_op jit(solution)/shard_map/near/pallas_call | solution.py:139
  23.6 0.8 %collective-permute-done.5.refs_0_.refs_11_ = bf16[136,512]{1,0:T(8,128)(2,1)S(1)} collective-permute-done((bf16[136,512]{1,0:T(8,128)(2,1)S(1)}, bf16[136,512]{1,0:T(8,128)(2,1)S(1)}, u32[]{:S(2)}, u32[]{:S(2)}) %collective-permute-start.5) | collective-permute-done | bytes 139296 | tf_op jit(solution)/shard_map/ppermute | solution.py:388
  24.4 1.5 %collective-permute-start.6 = (bf16[136,512]{1,0:T(8,128)(2,1)S(1)}, bf16[136,512]{1,0:T(8,128)(2,1)S(1)}, u32[]{:S(2)}, u32[]{:S(2)}) collective-permute-start(bf16[136,512]{1,0:T(8,128)(2,1)S(1)} %collective-permute-done.5.refs_0_.refs_11_), channel_id=1, source_target_pairs={{0,1},{1,0},{2,3},{3,2},{4,5},{5,4},{6,7},{7,6},{8,9},{9,8},{10,11... | collective-permute-start | bytes 417800 | tf_op jit(solution)/shard_map/ppermute | solution.py:388
  26.0 0.1 collective-permute-done.8.refs_2_.refs_13_
  26.1 0.8 %collective-permute-start.9 = (bf16[136,512]{1,0:T(8,128)(2,1)S(1)}, bf16[136,512]{1,0:T(8,128)(2,1)S(1)}, u32[]{:S(2)}, u32[]{:S(2)}) collective-permute-start(bf16[136,512]{1,0:T(8,128)(2,1)S(1)} %collective-permute-done.8.refs_2_.refs_13_), channel_id=1, source_target_pairs={{0,1},{1,0},{2,3},{3,2},{4,5},{5,4},{6,7},{7,6},{8,9},{9,8},{10,11... | collective-permute-start | bytes 417800 | tf_op jit(solution)/shard_map/ppermute | solution.py:388
  26.9 0.0 collective-permute-done.6.refs_1_.refs_12_
  27.0 1.0 %collective-permute-done.9.refs_3_.refs_14_ = bf16[136,512]{1,0:T(8,128)(2,1)S(1)} collective-permute-done((bf16[136,512]{1,0:T(8,128)(2,1)S(1)}, bf16[136,512]{1,0:T(8,128)(2,1)S(1)}, u32[]{:S(2)}, u32[]{:S(2)}) %collective-permute-start.9) | collective-permute-done | bytes 139296 | tf_op jit(solution)/shard_map/ppermute | solution.py:388
  27.9 0.1 weight_seq.1
  28.0 2.8 %collective-permute-start.10 = (bf16[72,512]{1,0:T(8,128)(2,1)S(1)}, bf16[72,512]{1,0:T(8,128)(2,1)S(1)}, u32[]{:S(2)}, u32[]{:S(2)}) collective-permute-start(bf16[72,512]{1,0:T(8,128)(2,1)S(1)} %weight_seq.1), channel_id=1, source_target_pairs={{0,0},{1,7},{2,8},{3,15},{4,16},{5,23},{6,24},{7,31},{8,2},{9,1},{... | collective-permute-start | bytes 221192 | tf_op jit(solution)/shard_map/ppermute | solution.py:562
  30.8 0.8 %collective-permute-start.11 = (bf16[72,512]{1,0:T(8,128)(2,1)S(1)}, bf16[72,512]{1,0:T(8,128)(2,1)S(1)}, u32[]{:S(2)}, u32[]{:S(2)}) collective-permute-start(bf16[72,512]{1,0:T(8,128)(2,1)S(1)} %weight_seq.1), channel_id=1, source_target_pairs={{0,4},{1,3},{2,12},{3,11},{4,20},{5,19},{6,28},{7,27},{8,6},{9,5},... | collective-permute-start | bytes 221192 | tf_op jit(solution)/shard_map/ppermute | solution.py:562
  31.6 3.0 %key.1 = (bf16[256,384]{1,0:T(8,128)(2,1)}, bf16[256,384]{1,0:T(8,128)(2,1)}) custom-call(f32[16,128]{1,0:T(8,128)S(1)} %get-tuple-element.29.refs_0_.refs_1_, f32[256,384]{1,0:T(8,128)S(1)} %get-tuple-element.45.refs_1_, f32[256,384]{1,0:T(8,128)S(1)} %get-tuple-element.46.refs_2_, bf16[160,1152]{1,0:T(8,128)(2,1)S(1)} %get-tuple-element.37.refs_0_.refs_6_.refs_3_.refs_2_, ...), custom_call_target="tpu_custom_call" | custom-call | flops 402653184 | bytes 393216 | tf_op jit(solution)/shard_map/key/pallas_call | solution.py:139
  34.5 5.2 %collective-permute-done.10.refs_0_ = bf16[72,512]{1,0:T(8,128)(2,1)S(1)} collective-permute-done((bf16[72,512]{1,0:T(8,128)(2,1)S(1)}, bf16[72,512]{1,0:T(8,128)(2,1)S(1)}, u32[]{:S(2)}, u32[]{:S(2)}) %collective-permute-start.10) | collective-permute-done | bytes 73760 | tf_op jit(solution)/shard_map/ppermute | solution.py:562
  39.7 0.0 collective-permute-done.11.refs_1_
  39.7 4.2 %collective-permute-start.12 = (bf16[72,512]{1,0:T(8,128)(2,1)S(1)}, bf16[72,512]{1,0:T(8,128)(2,1)S(1)}, u32[]{:S(2)}, u32[]{:S(2)}) collective-permute-start(bf16[72,512]{1,0:T(8,128)(2,1)S(1)} %weight_core.1.refs_0_), channel_id=1, source_target_pairs={{0,1},{1,0},{2,3},{3,2},{4,5},{5,4},{6,7},{7,6},{8,9},{9,8},{10,11... | collective-permute-start | bytes 221192 | tf_op jit(solution)/shard_map/ppermute | solution.py:388
  44.0 2.7 %far.1 = bf16[256,384]{1,0:T(8,128)(2,1)} custom-call(f32[16,128]{1,0:T(8,128)S(1)} %get-tuple-element.29.refs_0_.refs_1_, f32[256,384]{1,0:T(8,128)S(1)} %get-tuple-element.49.refs_1_, bf16[160,1152]{1,0:T(8,128)(2,1)S(1)} %get-tuple-element.37.refs_0_.refs_6_.refs_3_.refs_2_, bf16[64,1152]{1,0:T(8,128)(2,1)S(1)} %get-tuple-element.30.refs_7_.refs_4_.refs_3_, ...), custom_call_target="tpu_custom_call" | custom-call | flops 201326592 | bytes 196608 | tf_op jit(solution)/shard_map/far/pallas_call | solution.py:139
  46.7 0.0 collective-permute-done.12.refs_1_
  46.7 0.7 %weight_out.1 = f32[96,384]{1,0:T(8,128)} custom-call(bf16[72,512]{1,0:T(8,128)(2,1)S(1)} %weight_core.1.refs_0_, bf16[72,512]{1,0:T(8,128)(2,1)S(1)} %collective-permute-done.12.refs_1_), custom_call_target="tpu_custom_call" | custom-call | bytes 147456 | tf_op jit(solution)/shard_map/weight_out/pallas_call | solution.py:139
  (3 shorter events, 0.1 us)
Async XLA Ops:
  0.6 0.7 %copy-start.3 = (f32[6]{0:T(128)S(1)}, f32[6]{0:T(128)}, u32[]{:S(2)}) copy-start(f32[6]{0:T(128)} %refs_3_.2) | copy-start | bytes 76
  1.3 0.9 %copy-start = (bf16[1,256,384]{2,1,0:T(8,128)(2,1)S(1)}, bf16[1,256,384]{2,1,0:T(8,128)(2,1)}, u32[]{:S(2)}) copy-start(bf16[1,256,384]{2,1,0:T(8,128)(2,1)} %param.6) | copy-start | bytes 589828
  2.2 0.9 %copy-start.1 = (bf16[1,256,384]{2,1,0:T(8,128)(2,1)S(1)}, bf16[1,256,384]{2,1,0:T(8,128)(2,1)}, u32[]{:S(2)}) copy-start(bf16[1,256,384]{2,1,0:T(8,128)(2,1)} %param.7) | copy-start | bytes 589828
  3.1 0.9 %copy-start.2 = (bf16[1,256,384]{2,1,0:T(8,128)(2,1)S(1)}, bf16[1,256,384]{2,1,0:T(8,128)(2,1)}, u32[]{:S(2)}) copy-start(bf16[1,256,384]{2,1,0:T(8,128)(2,1)} %param.8) | copy-start | bytes 589828
  5.6 2.1 %collective-permute-start.1 = (bf16[160,1152]{1,0:T(8,128)(2,1)S(1)}, bf16[160,1152]{1,0:T(8,128)(2,1)S(1)}, u32[]{:S(2)}, u32[]{:S(2)}) collective-permute-start(bf16[160,1152]{1,0:T(8,128)(2,1)S(1)} %get-tuple-element.37.refs_0_.refs_6_.refs_3_.refs_2_), channel_id=1, source_target_pairs={{0,1},{1,0},{2,3},{3,2},{4,5},{5,4},{6,7},{7,6},{8,9},{9,8},{10,11... | collective-permute-start | bytes 1105928 | tf_op jit(solution)/shard_map/ppermute | solution.py:388
  6.4 3.6 %copy-start.4 = (bf16[384,384]{1,0:T(8,128)(2,1)S(1)}, bf16[384,384]{1,0:T(8,128)(2,1)}, u32[]{:S(2)}) copy-start(bf16[384,384]{1,0:T(8,128)(2,1)} %refs_3_.3) | copy-start | bytes 884740
  6.4 3.6 %copy-start.5 = (bf16[1,256,384]{2,1,0:T(8,128)(2,1)S(1)}, bf16[1,256,384]{2,1,0:T(8,128)(2,1)}, u32[]{:S(2)}) copy-start(bf16[1,256,384]{2,1,0:T(8,128)(2,1)} %param.11) | copy-start | bytes 589828
  6.4 6.7 %collective-permute-start = (bf16[64,1152]{1,0:T(8,128)(2,1)S(1)}, bf16[64,1152]{1,0:T(8,128)(2,1)S(1)}, u32[]{:S(2)}, u32[]{:S(2)}) collective-permute-start(bf16[64,1152]{1,0:T(8,128)(2,1)S(1)} %get-tuple-element.30.refs_7_.refs_4_.refs_3_), channel_id=1, source_target_pairs={{0,2},{1,3},{2,0},{3,1},{4,6},{5,7},{6,4},{7,5},{8,10},{9,11},{10,... | collective-permute-start | bytes 442376 | tf_op jit(solution)/shard_map/ppermute | solution.py:388
  7.7 6.5 %collective-permute-start.3 = (bf16[64,1152]{1,0:T(8,128)(2,1)S(1)}, bf16[64,1152]{1,0:T(8,128)(2,1)S(1)}, u32[]{:S(2)}, u32[]{:S(2)}) collective-permute-start(bf16[64,1152]{1,0:T(8,128)(2,1)S(1)} %third_rows.1), channel_id=1, source_target_pairs={{0,4},{1,7},{2,6},{3,5},{4,0},{5,3},{6,2},{7,1},{8,12},{9,15},{10,... | collective-permute-start | bytes 442376 | tf_op jit(solution)/shard_map/ppermute | solution.py:392
  13.1 2.2 %collective-permute-start.2 = (bf16[64,1152]{1,0:T(8,128)(2,1)S(1)}, bf16[64,1152]{1,0:T(8,128)(2,1)S(1)}, u32[]{:S(2)}, u32[]{:S(2)}) collective-permute-start(bf16[64,1152]{1,0:T(8,128)(2,1)S(1)} %collective-permute-done.refs_9_.refs_6_.refs_7_), channel_id=1, source_target_pairs={{0,1},{1,0},{2,3},{3,2},{4,5},{5,4},{6,7},{7,6},{8,9},{9,8},{10,11... | collective-permute-start | bytes 442376 | tf_op jit(solution)/shard_map/ppermute | solution.py:388
  14.2 1.5 %collective-permute-start.4 = (bf16[64,1152]{1,0:T(8,128)(2,1)S(1)}, bf16[64,1152]{1,0:T(8,128)(2,1)S(1)}, u32[]{:S(2)}, u32[]{:S(2)}) collective-permute-start(bf16[64,1152]{1,0:T(8,128)(2,1)S(1)} %collective-permute-done.3.refs_11_.refs_8_.refs_9_), channel_id=1, source_target_pairs={{0,1},{1,0},{2,3},{3,2},{4,5},{5,4},{6,7},{7,6},{8,9},{9,8},{10,11... | collective-permute-start | bytes 442376 | tf_op jit(solution)/shard_map/ppermute | solution.py:388
  18.4 1.7 %collective-permute-start.7 = (bf16[304,512]{1,0:T(8,128)(2,1)S(1)}, bf16[304,512]{1,0:T(8,128)(2,1)S(1)}, u32[]{:S(2)}, u32[]{:S(2)}) collective-permute-start(bf16[304,512]{1,0:T(8,128)(2,1)S(1)} %get-tuple-element.43.refs_0_.refs_4_), channel_id=1, source_target_pairs={{0,1},{1,0},{2,3},{3,2},{4,5},{5,4},{6,7},{7,6},{8,9},{9,8},{10,11... | collective-permute-start | bytes 933896 | tf_op jit(solution)/shard_map/ppermute | solution.py:388
  18.8 5.6 %collective-permute-start.5 = (bf16[136,512]{1,0:T(8,128)(2,1)S(1)}, bf16[136,512]{1,0:T(8,128)(2,1)S(1)}, u32[]{:S(2)}, u32[]{:S(2)}) collective-permute-start(bf16[136,512]{1,0:T(8,128)(2,1)S(1)} %get-tuple-element.39.refs_5_), channel_id=1, source_target_pairs={{0,2},{1,3},{2,0},{3,1},{4,6},{5,7},{6,4},{7,5},{8,10},{9,11},{10,... | collective-permute-start | bytes 417800 | tf_op jit(solution)/shard_map/ppermute | solution.py:388
  20.1 6.0 %collective-permute-start.8 = (bf16[136,512]{1,0:T(8,128)(2,1)S(1)}, bf16[136,512]{1,0:T(8,128)(2,1)S(1)}, u32[]{:S(2)}, u32[]{:S(2)}) collective-permute-start(bf16[136,512]{1,0:T(8,128)(2,1)S(1)} %third_grads.1), channel_id=1, source_target_pairs={{0,4},{1,7},{2,6},{3,5},{4,0},{5,3},{6,2},{7,1},{8,12},{9,15},{10,... | collective-permute-start | bytes 417800 | tf_op jit(solution)/shard_map/ppermute | solution.py:392
  24.4 2.5 %collective-permute-start.6 = (bf16[136,512]{1,0:T(8,128)(2,1)S(1)}, bf16[136,512]{1,0:T(8,128)(2,1)S(1)}, u32[]{:S(2)}, u32[]{:S(2)}) collective-permute-start(bf16[136,512]{1,0:T(8,128)(2,1)S(1)} %collective-permute-done.5.refs_0_.refs_11_), channel_id=1, source_target_pairs={{0,1},{1,0},{2,3},{3,2},{4,5},{5,4},{6,7},{7,6},{8,9},{9,8},{10,11... | collective-permute-start | bytes 417800 | tf_op jit(solution)/shard_map/ppermute | solution.py:388
  26.1 1.8 %collective-permute-start.9 = (bf16[136,512]{1,0:T(8,128)(2,1)S(1)}, bf16[136,512]{1,0:T(8,128)(2,1)S(1)}, u32[]{:S(2)}, u32[]{:S(2)}) collective-permute-start(bf16[136,512]{1,0:T(8,128)(2,1)S(1)} %collective-permute-done.8.refs_2_.refs_13_), channel_id=1, source_target_pairs={{0,1},{1,0},{2,3},{3,2},{4,5},{5,4},{6,7},{7,6},{8,9},{9,8},{10,11... | collective-permute-start | bytes 417800 | tf_op jit(solution)/shard_map/ppermute | solution.py:388
  28.0 11.7 %collective-permute-start.10 = (bf16[72,512]{1,0:T(8,128)(2,1)S(1)}, bf16[72,512]{1,0:T(8,128)(2,1)S(1)}, u32[]{:S(2)}, u32[]{:S(2)}) collective-permute-start(bf16[72,512]{1,0:T(8,128)(2,1)S(1)} %weight_seq.1), channel_id=1, source_target_pairs={{0,0},{1,7},{2,8},{3,15},{4,16},{5,23},{6,24},{7,31},{8,2},{9,1},{... | collective-permute-start | bytes 221192 | tf_op jit(solution)/shard_map/ppermute | solution.py:562
  30.8 8.9 %collective-permute-start.11 = (bf16[72,512]{1,0:T(8,128)(2,1)S(1)}, bf16[72,512]{1,0:T(8,128)(2,1)S(1)}, u32[]{:S(2)}, u32[]{:S(2)}) collective-permute-start(bf16[72,512]{1,0:T(8,128)(2,1)S(1)} %weight_seq.1), channel_id=1, source_target_pairs={{0,4},{1,3},{2,12},{3,11},{4,20},{5,19},{6,28},{7,27},{8,6},{9,5},... | collective-permute-start | bytes 221192 | tf_op jit(solution)/shard_map/ppermute | solution.py:562
  39.7 6.9 %collective-permute-start.12 = (bf16[72,512]{1,0:T(8,128)(2,1)S(1)}, bf16[72,512]{1,0:T(8,128)(2,1)S(1)}, u32[]{:S(2)}, u32[]{:S(2)}) collective-permute-start(bf16[72,512]{1,0:T(8,128)(2,1)S(1)} %weight_core.1.refs_0_), channel_id=1, source_target_pairs={{0,1},{1,0},{2,3},{3,2},{4,5},{5,4},{6,7},{7,6},{8,9},{9,8},{10,11... | collective-permute-start | bytes 221192 | tf_op jit(solution)/shard_map/ppermute | solution.py:388

commit v3 on v2

v3 whole, which is shorter than its diff:
```python
import functools
import math

import jax
import jax.numpy as jnp
from jax import lax
from jax.experimental import pallas as pl
from jax.experimental.pallas import tpu as pltpu
from jax.sharding import PartitionSpec as P

BF = jnp.bfloat16
F32 = jnp.float32
SEQ = ("seqhi", "seqlo")
LANES = 128
HALF = 64
LOG2E = math.log2(math.e)
NN = (((1,), (0,)), ((), ()))
NT = (((1,), (1,)), ((), ()))
TN = (((0,), (0,)), ((), ()))


def dot(left, right, dims=NN):
    return lax.dot_general(left, right, dims, preferred_element_type=F32)


def iota(shape, dim):
    return lax.broadcasted_iota(jnp.int32, shape, dim)


def order_matrix(rows, top, inverse=False):
    source = iota((rows, rows), 0 if inverse else 1)
    place = source >> top
    for bit in range(top):
        place = place + ((source >> bit) & 1) * (rows >> (bit + 1))
    return jnp.where(place == iota((rows, rows), 1 if inverse else 0), 1.0, 0.0).astype(BF)


def side_masks():
    lane = iota((1, LANES), 1)
    low = jnp.where(lane < HALF, 1.0, 0.0)
    return low.astype(BF), (1.0 - low).astype(BF)


def factor_rows(heads):
    return -(-(heads + heads // 2) // 8) * 8


def fill_factors(scale_ref, factor_ref):
    heads = scale_ref.shape[0]
    lane = iota((1, LANES), 1)
    for head in range(heads):
        factor_ref[head : head + 1, :] = jnp.full((1, LANES), scale_ref[head] * (HALF**-0.5 * LOG2E), F32)
    for pair in range(heads // 2):
        both = jnp.where(lane < HALF, scale_ref[2 * pair], scale_ref[2 * pair + 1]) * (HALF**-0.5)
        factor_ref[heads + pair : heads + pair + 1, :] = both


def exponent(factor_ref, head, columns):
    return stack([factor_ref[head : head + 1, :]] * (columns // LANES), 1)


def side_factor(factor_ref, heads, pair):
    return factor_ref[heads + pair : heads + pair + 1, :]


def stack(parts, axis):
    return parts[0] if len(parts) == 1 else jnp.concatenate(parts, axis=axis)


def doubled(value):
    return jnp.concatenate([value, value], axis=0)


def halves_sum(value):
    half = value.shape[0] // 2
    return value[:half] + value[half:]


def lane_pair(offset, pair):
    return slice(offset + LANES * pair, offset + LANES * (pair + 1))


def slot_masks(pair):
    lane = iota((1, LANES), 1)
    masks = []
    for side in (0, 1):
        slot = lane - side * HALF
        hit = (slot == 16 * pair) | (slot == 16 * pair + 8)
        masks.append(jnp.where(hit, 1.0, 0.0).astype(BF))
    return masks


def denom_lanes(denoms):
    lane = iota((1, LANES), 1)
    slot = (lane % HALF) // 8
    packed = jnp.zeros(denoms[0].shape, F32)
    for pair, value in enumerate(denoms):
        high = value.astype(BF).astype(F32)
        packed = jnp.where(slot == 2 * pair, high, packed)
        packed = jnp.where(slot == 2 * pair + 1, value - high, packed)
    return packed.astype(BF)


class View:
    def __init__(self, array, start=0, rows=None):
        self.array = array
        self.start = start
        self.rows = array.shape[0] - start if rows is None else rows


VMEM = pl.BlockSpec(memory_space=pltpu.VMEM)
SMEM = pl.BlockSpec(memory_space=pltpu.SMEM)
HBM = pl.BlockSpec(memory_space=pltpu.HBM)


def call(kernel, name, shapes, arrays, views=(), scalars=(), flops=0, scratch=(), specs=None):
    unique, where = [], []
    for group in views:
        places = []
        for view in group:
            spot = next((at for at, array in enumerate(unique) if array is view.array), None)
            if spot is None:
                spot = len(unique)
                unique.append(view.array)
            places.append((spot, view.start, view.rows))
        where.append(places)

    def body(*refs):
        scalar_refs, refs = refs[: len(scalars)], refs[len(scalars) :]
        array_refs, refs = refs[: len(arrays)], refs[len(arrays) :]
        view_refs, refs = refs[: len(unique)], refs[len(unique) :]

        def load(group, columns):
            return stack(
                [view_refs[spot][start : start + rows, columns] for spot, start, rows in where[group]], 0
            )

        kernel(load, *scalar_refs, *array_refs, *refs)

    moved = sum(math.prod(shape) * jnp.dtype(kind).itemsize for shape, kind in shapes)
    return pl.pallas_call(
        body,
        out_shape=[jax.ShapeDtypeStruct(shape, kind) for shape, kind in shapes],
        in_specs=[SMEM] * len(scalars) + (specs or [VMEM] * len(arrays)) + [VMEM] * len(unique),
        out_specs=[VMEM] * len(shapes),
        scratch_shapes=list(scratch),
        compiler_params=pltpu.CompilerParams(vmem_limit_bytes=16 * 2**20),
        cost_estimate=pl.CostEstimate(flops=flops, transcendentals=0, bytes_accessed=moved),
        name=name,
    )(*scalars, *arrays, *unique)


def pool_kernel(top, places, load, q_hbm, k_hbm, v_hbm, scale_hbm, factor_ref, *refs):
    out_refs, (q_ref, k_ref, v_ref, scale_ref, sems) = refs[:-5], refs[-5:]
    level_refs, query_refs = out_refs[:-top], out_refs[-top:]
    copies = [
        pltpu.make_async_copy(source, target, sems.at[index])
        for index, (source, target) in enumerate(
            ((q_hbm, q_ref), (k_hbm, k_ref), (v_hbm, v_ref), (scale_hbm, scale_ref))
        )
    ]
    for which in (1, 2, 0, 3):
        copies[which].start()
    rows, width = q_ref.shape
    order = order_matrix(rows, top)
    for which, ref in ((1, k_ref), (2, v_ref), (0, q_ref)):
        copies[which].wait()
        current = dot(order, ref[...])
        level_refs[0][:, which * width : (which + 1) * width] = current.astype(BF)
        for height in range(1, top + 1):
            total = halves_sum(current)
            rounded = (total if which == 2 else 0.5 * total).astype(BF)
            if which:
                target, start = places[height - 1]
                columns = slice((which - 1) * width, which * width)
                level_refs[target][start : start + rounded.shape[0], columns] = rounded
            else:
                query_refs[height - 1][...] = rounded
            current = rounded.astype(F32)
    copies[3].wait()
    fill_factors(scale_ref, factor_ref)


def masked_stack(value, masks):
    return stack([value * mask for mask in masks], 0)


def both_weights(factor_ref, pair, first, second, masks):
    rows = first.shape[0]
    logits = dot(masked_stack(first, masks), second, NT)
    columns = second.shape[0]
    return [
        jnp.exp2(logits[side * rows : (side + 1) * rows] * exponent(factor_ref, 2 * pair + side, columns))
        for side in (0, 1)
    ]


def attend(factor_ref, pair, queries, keys, values, amount, masks):
    weights = both_weights(factor_ref, pair, queries, keys, masks)
    joined = stack([weight.astype(BF) for weight in weights], 1)
    count = jnp.full(values.shape, float(amount), BF)
    right = stack([stack([values * mask, count * mask], 1) for mask in masks], 0)
    return joined, dot(joined, right)


def base_kernel(top, load, factor_ref, x_ref, cot_ref, w_ref, numer_ref, denom_ref, weights_ref, cotp_ref, back_ref):
    rows, width = cot_ref.shape
    masks = side_masks()
    for pair in range(width // LANES):
        q, k, v = (x_ref[:, lane_pair(width * which, pair)] for which in range(3))
        joined, both = attend(factor_ref, pair, q, k, v, 1, masks)
        numer_ref[:, lane_pair(0, pair)] = both[:, :LANES]
        denom_ref[:, lane_pair(0, pair)] = both[:, LANES:]
        weights_ref[:, 2 * rows * pair : 2 * rows * (pair + 1)] = joined
    cotan = dot(order_matrix(rows, top), cot_ref[...]).astype(BF)
    cotp_ref[...] = cotan
    back_ref[...] = dot(cotan, w_ref[...], NT).astype(BF)


def forward_kernel(
    top, parts, grad_places, pieces,
    load, place_ref, factor_ref, numer_ref, denom_ref, cotp_ref, back_ref, *refs
):
    weights_refs, out_refs, weight_ref = refs[:top], refs[top:-1], refs[-1]
    rows, width = numer_ref.shape
    masks = side_masks()
    lane = iota((LANES, LANES), 1)
    ones = jnp.where(lane // HALF == iota((LANES, LANES), 0) // HALF, 1.0, 0.0).astype(BF)
    adder = doubled(ones)
    grad_rows = []
    denom_rows = []
    attended = []
    for pair in range(width // LANES):
        total = None
        for height in range(top, 0, -1):
            queries = load(height - 1, lane_pair(0, pair))
            keys, values = (load(top + height - 1, lane_pair(start, pair)) for start in (0, width))
            joined, both = attend(factor_ref, pair, queries, keys, values, 2**height, masks)
            columns = joined.shape[1]
            weights_refs[height - 1][:, columns * pair : columns * (pair + 1)] = joined
            total = both if total is None else both + doubled(total)
        total = doubled(total)
        numer = numer_ref[:, lane_pair(0, pair)] + total[:, :LANES]
        inverse = 1.0 / (denom_ref[:, lane_pair(0, pair)] + total[:, LANES:])
        ratio = numer * inverse
        attended.append(ratio.astype(BF))
        back = back_ref[:, lane_pair(0, pair)].astype(F32)
        product = back * ratio
        product_high = product.astype(BF)
        product_low = (product - product_high.astype(F32)).astype(BF)
        summed = dot(stack([product_high, product_low], 1), adder)
        grad_rows.append(back * inverse)
        denom_rows.append(-summed * inverse)
    weight_ref[...] = dot(stack(attended, 1), cotp_ref[...], TN)
    own_rows = width // parts
    for entry, offset, count, target, start in pieces:
        shift = offset if isinstance(offset, int) else offset(place_ref)
        first = pl.multiple_of(place_ref[entry] * own_rows + shift, math.gcd(own_rows, count))
        out_refs[target][start : start + count, :] = weight_ref[pl.ds(first, count), :].astype(BF)
    for height, (target, start) in enumerate(grad_places):
        if height:
            grad_rows = [halves_sum(value) for value in grad_rows]
            denom_rows = [halves_sum(value) for value in denom_rows]
        span = slice(start, start + (rows >> height))
        for pair, value in enumerate(grad_rows):
            out_refs[target][span, lane_pair(0, pair)] = value.astype(BF)
        out_refs[target][span, width : width + LANES] = denom_lanes(denom_rows)
        if height:
            out_refs[target][span, width + LANES :] = load(height - 1, slice(None))


def query_slopes(joined, grad, denom, values, pair, height, masks):
    rows, columns = grad.shape[0], values.shape[0]
    left = stack([stack([grad * mask, denom * slot], 1) for mask, slot in zip(masks, slot_masks(pair))], 0)
    right = stack([values, jnp.full((columns, LANES), float(2**height), BF)], 1)
    product = dot(left, right, NT)
    return [
        (joined[:, side * columns : (side + 1) * columns].astype(F32) * product[side * rows : (side + 1) * rows])
        .astype(BF)
        for side in (0, 1)
    ]


def near_kernel(load, factor_ref, x_ref, gh_ref, weights_ref, query_ref, key_ref, value_ref):
    rows, width = query_ref.shape
    heads = width // HALF
    masks = side_masks()
    for pair in range(width // LANES):
        factor = side_factor(factor_ref, heads, pair)
        queries, keys, values = (x_ref[:, lane_pair(width * which, pair)] for which in range(3))
        grad = gh_ref[:, lane_pair(0, pair)]
        joined = weights_ref[:, 2 * rows * pair : 2 * rows * (pair + 1)]
        slope = query_slopes(joined, grad, gh_ref[:, width:], values, pair, 0, masks)
        query_ref[:, lane_pair(0, pair)] = dot(stack(slope, 1), masked_stack(keys, masks)) * factor
        key_ref[:, lane_pair(0, pair)] = dot(stack(slope, 0), masked_stack(queries, masks), TN) * factor
        weights = stack([joined[:, :rows], joined[:, rows:]], 0)
        value_ref[:, lane_pair(0, pair)] = dot(weights, masked_stack(grad, masks), TN)


def far_kernel(top, load, factor_ref, base_ref, *refs):
    weights_refs, out_ref = refs[:top], refs[top]
    rows, width = out_ref.shape
    heads = width // HALF
    masks = side_masks()
    results = []
    for pair in range(width // LANES):
        factor = side_factor(factor_ref, heads, pair)
        total = None
        for height in range(top, 0, -1):
            grad = load(height - 1, lane_pair(0, pair))
            denom = load(height - 1, slice(width, width + LANES))
            keys, values = (load(top + height - 1, lane_pair(start, pair)) for start in (0, width))
            columns = 2 * keys.shape[0]
            joined = weights_refs[height - 1][:, columns * pair : columns * (pair + 1)]
            slope = query_slopes(joined, grad, denom, values, pair, height, masks)
            piece = dot(stack(slope, 1), masked_stack(keys, masks)) * factor
            total = piece if total is None else piece + 0.5 * doubled(total)
        total = base_ref[:, lane_pair(0, pair)] + 0.5 * doubled(total)
        results.append(total.astype(BF))
    out_ref[...] = dot(order_matrix(rows, top, True), stack(results, 1)).astype(BF)


def key_kernel(top, load, factor_ref, base_key_ref, base_value_ref, key_out_ref, value_out_ref):
    rows, width = key_out_ref.shape
    heads = width // HALF
    masks = side_masks()
    key_results, value_results = [], []
    for pair in range(width // LANES):
        factor = side_factor(factor_ref, heads, pair)
        key_total = value_total = None
        for height in range(top, 0, -1):
            keys, values = (load(height - 1, lane_pair(start, pair)) for start in (0, width))
            grad = load(top + height - 1, lane_pair(0, pair))
            denom = load(top + height - 1, slice(width, width + LANES))
            queries = load(top + height - 1, lane_pair(width + LANES, pair))
            count = keys.shape[0]
            weights = both_weights(factor_ref, pair, keys, queries, masks)
            left = stack(
                [
                    stack([values * mask, jnp.broadcast_to(slot * float(2**height), (count, LANES))], 1)
                    for mask, slot in zip(masks, slot_masks(pair))
                ],
                0,
            )
            product = dot(left, stack([grad, denom], 1), NT)
            slope = [
                (weight * product[side * count : (side + 1) * count]).astype(BF)
                for side, weight in enumerate(weights)
            ]
            key_piece = dot(stack(slope, 1), masked_stack(queries, masks)) * factor
            value_piece = dot(stack([weight.astype(BF) for weight in weights], 1), masked_stack(grad, masks))
            if key_total is not None:
                key_piece = key_piece + 0.5 * doubled(key_total)
                value_piece = value_piece + doubled(value_total)
            key_total, value_total = key_piece, value_piece
        key_total = base_key_ref[:, lane_pair(0, pair)] + 0.5 * doubled(key_total)
        value_total = base_value_ref[:, lane_pair(0, pair)] + doubled(value_total)
        key_results.append(key_total.astype(BF))
        value_results.append(value_total.astype(BF))
    back = order_matrix(rows, top, True)
    key_out_ref[...] = dot(back, stack(key_results, 1)).astype(BF)
    value_out_ref[...] = dot(back, stack(value_results, 1)).astype(BF)


def place_kernel(spots, load, *refs):
    for target, start, groups in spots:
        total = None
        for group in groups:
            value = load(group, slice(None))
            if len(groups) > 1 or refs[target].dtype == F32:
                value = value.astype(F32)
            total = value if total is None else total + value
        refs[target][start : start + total.shape[0], :] = total.astype(refs[target].dtype)


def placed(name, shapes, spots):
    views, listed = [], []
    for target, start, parts in spots:
        listed.append((target, start, range(len(views), len(views) + len(parts))))
        views += [[part] for part in parts]
    return call(functools.partial(place_kernel, listed), name, shapes, [], views=views)


def total_kernel(load, core_ref, own_ref, partner_ref, *refs):
    half = own_ref.shape[0] // 3
    base_ref = refs[0] if refs[0].shape[0] == 2 * half and len(refs) == 3 and refs[1].dtype == F32 else None
    out_refs = refs[:-1] if base_ref is None else refs[1:-1]
    sum_ref = refs[-1]
    total = own_ref[: 2 * half, :].astype(F32) + partner_ref[: 2 * half, :].astype(F32)
    if base_ref is not None:
        total = total + base_ref[...].astype(F32)
    sum_ref[...] = total
    for ref, core in ((own_ref, core_ref[0]), (partner_ref, 1 - core_ref[0])):
        span = pl.ds(pl.multiple_of(core * half, half), half)
        sum_ref[span, :] = sum_ref[span, :] + ref[2 * half :, :].astype(F32)
    out_refs[0][...] = sum_ref[...].astype(out_refs[0].dtype)
    if len(out_refs) > 1:
        span = pl.ds(pl.multiple_of(core_ref[0] * half, half), half)
        out_refs[1][...] = sum_ref[span, :].astype(BF)


def chip_total(name, core, arrays, half, kind):
    width = arrays[0].shape[1]
    shapes = [((2 * half, width), kind)] + [((half, width), BF)] * (kind == BF)
    return call(
        total_kernel, name, shapes, arrays, scalars=[core.reshape(1)], scratch=[pltpu.VMEM((2 * half, width), F32)]
    )


def traded(value, mask):
    return lax.ppermute(value, SEQ, [(source, source ^ mask) for source in range(lax.axis_size(SEQ))])


def split_traded(value, first, second):
    return lax.ppermute(
        value,
        SEQ,
        [(source, source ^ (2 * (second if source % 2 else first))) for source in range(lax.axis_size(SEQ))],
    )


def layer_traded(value, first, second):
    axes = ("dp", *SEQ)
    count = lax.axis_size(SEQ)
    pairs = []
    for source in range(lax.axis_size(axes)):
        layer, spot = divmod(source, count)
        pairs.append((source, (layer ^ (second if spot % 2 else first)) * count + spot))
    return lax.ppermute(value, axes, pairs)


def from_siblings(levels, top):
    arrived = {}
    for offset in range(1, 2**top):
        height = offset.bit_length()
        if offset == 1:
            arrived[1] = traded(levels[0], 1)
        elif offset % 2 == 0:
            arrived[offset] = traded(levels[height - 1], offset)
        else:
            arrived[offset] = traded(arrived[offset - 1], 1)
    grouped = []
    for height in range(1, top + 1):
        parts = [arrived[offset] for offset in range(2 ** (height - 1), 2**height)]
        if parts[0].shape[0] < 16:
            parts = [jnp.concatenate(parts, axis=0)]
        grouped.append([View(part) for part in parts])
    return grouped


def shards(queries, key_rows, value_rows, head_scale, out_weight, cotangent):
    rows, width = queries.shape[1:]
    heads = head_scale.shape[0]
    top = lax.axis_size(SEQ).bit_length() - 1
    parts = lax.axis_size("dp")
    assert width == HALF * heads and width % LANES == 0 and width <= 4 * LANES
    paired = top == 3 and parts == 4 and rows == 256
    whole = (rows, width)
    wide = width + LANES
    sizes = [rows >> height for height in range(top + 1)]
    if paired:
        places = [(1, 0), (2, 0), (1, sizes[1])]
        pooled = [sizes[1] + sizes[3], sizes[2]]
    else:
        places = [(height, 0) for height in range(1, top + 1)]
        pooled = sizes[1:]
    factors, base_rows, *outs = call(
        functools.partial(pool_kernel, top, places),
        "pool",
        [((factor_rows(heads), LANES), F32), ((rows, 3 * width), BF)]
        + [((count, 2 * width), BF) for count in pooled]
        + [((size, width), BF) for size in sizes[1:]],
        [pltpu.with_memory_space_constraint(value, pltpu.HBM) for value in (queries[0], key_rows[0], value_rows[0], head_scale)],
        specs=[HBM] * 4,
        scratch=[pltpu.VMEM(whole, BF)] * 3 + [pltpu.SMEM((heads,), F32), pltpu.SemaphoreType.DMA((4,))],
    )
    levels, level_queries = outs[:-top], [[View(value)] for value in outs[-top:]]
    own = [[View(levels[target - 1], start, sizes[height + 1])] for height, (target, start) in enumerate(places)]
    numer, denom, base_weights, cotan, back = call(
        functools.partial(base_kernel, top),
        "base",
        [(whole, F32), (whole, F32), ((rows, heads * rows), BF), (whole, BF), (whole, BF)],
        [factors, base_rows, cotangent[0], out_weight],
        flops=4 * rows * rows * width * 4,
    )
    if paired:
        within = traded(levels[0], 1)
        across = traded(levels[1], 2)
        (third,) = placed(
            "third_rows",
            [((2 * sizes[3], 2 * width), BF)],
            [(0, 0, [own[2][0]]), (0, sizes[3], [View(within, sizes[1], sizes[3])])],
        )
        split = split_traded(third, 2, 3)
        across, numer = lax.optimization_barrier((across, numer))
        across_too = traded(across, 1)
        split_too = traded(split, 1)
        siblings = [
            [View(within, 0, sizes[1])],
            [View(across), View(across_too)],
            [View(split), View(split_too)],
        ]
    else:
        siblings = from_siblings(levels, top)
    own_rows = width // parts
    half = own_rows // 2
    layer = lax.axis_index("dp").astype(jnp.int32)
    if paired:
        core = lax.axis_index(SEQ).astype(jnp.int32) % 2
        place = jnp.stack([layer, layer ^ (1 + 2 * core), layer ^ (3 - 2 * core), layer ^ 2, core * half])
        grad_places = [(0, 0), (1, 0), (2, 0), (1, sizes[1])]
        shapes = [(rows, wide), (sizes[1] + sizes[3], wide + width), (sizes[2], wide + width)]
        pieces = [
            (0, 0, own_rows, 3, 0),
            (1, 0, own_rows, 4, 0),
            (3, lambda ref: ref[4], half, 4, own_rows),
            (2, 0, own_rows, 5, 0),
            (3, lambda ref: half - ref[4], half, 5, own_rows),
        ]
        shapes += [(own_rows, width), (own_rows + half, width), (own_rows + half, width)]
    else:
        place = (layer + jnp.arange(parts, dtype=jnp.int32)) % parts
        grad_places = [(height, 0) for height in range(top + 1)]
        pieces = [(step, 0, own_rows, top + 1 + step, 0) for step in range(parts)]
        shapes = [(rows, wide)] + [(size, wide + width) for size in sizes[1:]] + [(own_rows, width)] * parts
    outs = call(
        functools.partial(forward_kernel, top, parts, grad_places, pieces),
        "forward",
        [((size, heads * rows // 2), BF) for size in sizes[1:]] + [(shape, BF) for shape in shapes],
        [factors, numer, denom, cotan, back],
        views=level_queries + siblings,
        scalars=[place],
        scratch=[pltpu.VMEM((width, width), F32)],
    )
    level_weights, outs = outs[:top], outs[top:]
    own_grads = [
        [View(outs[target], start, sizes[height])] for height, (target, start) in enumerate(grad_places) if height
    ]
    near_query, near_key, near_value = call(
        near_kernel,
        "near",
        [(whole, F32)] * 3,
        [factors, base_rows, outs[0], base_weights],
        flops=8 * rows * rows * width * 4,
    )
    (query_grad,) = call(
        functools.partial(far_kernel, top),
        "far",
        [(whole, BF)],
        [factors, near_query, *level_weights],
        views=own_grads + siblings,
        flops=8 * rows * rows * width,
    )

    def key_call(sibling_grads):
        return call(
            functools.partial(key_kernel, top),
            "key",
            [(whole, BF), (whole, BF)],
            [factors, near_key, near_value],
            views=own + sibling_grads,
            flops=8 * rows * rows * width * 2,
        )

    if paired:
        near, far, mine, send, theirs = outs[1:6]
        theirs_in = traded(theirs, 1)
        near_in = traded(near, 1)
        far_in = traded(far, 2)
        send_one, send_half = placed(
            "layer_rows",
            [((own_rows, width), BF), ((half, width), BF)],
            [
                (0, 0, [View(send, 0, own_rows), View(theirs_in, 0, own_rows)]),
                (1, 0, [View(send, own_rows), View(theirs_in, own_rows)]),
            ],
        )
        layer_one = layer_traded(send_one, 1, 3)
        layer_half = layer_traded(send_half, 2, 2)
        (third,) = placed(
            "third_grads",
            [((2 * sizes[3], wide + width), BF)],
            [(0, 0, [own_grads[2][0]]), (0, sizes[3], [View(near_in, sizes[1])])],
        )
        third_in = split_traded(third, 2, 3)
        far_in, near_query = lax.optimization_barrier((far_in, near_query))
        far_too = traded(far_in, 1)
        layer_one, query_grad = lax.optimization_barrier((layer_one, query_grad))
        third_too = traded(third_in, 1)
        sibling_grads = [
            [View(near_in, 0, sizes[1])],
            [View(far_in), View(far_too)],
            [View(third_in), View(third_too)],
        ]
        (joint,) = placed(
            "layer_sum",
            [((own_rows + half, width), BF)],
            [(0, 0, [View(mine), View(layer_one)]), (0, own_rows, [View(layer_half)])],
        )
        joint_in = traded(joint, 1)
        weight, weight_half = chip_total("layer_total", core, [joint, joint_in], half, BF)
        plane_one = split_traded(weight, 1, 2)
        plane_half = traded(weight_half, 6)
        key_grad, value_grad = key_call(sibling_grads)
        plane_one, key_grad = lax.optimization_barrier((plane_one, key_grad))
        (joint,) = placed(
            "plane_rows",
            [((own_rows + half, width), BF)],
            [(0, 0, [View(plane_one)]), (0, own_rows, [View(plane_half)])],
        )
        joint_in = traded(joint, 1)
        (weight,) = chip_total("weight_out", core, [joint, joint_in, weight], half, F32)
    else:
        pieces = outs[top + 1 :]
        weight = pieces[0].astype(F32)
        for step in range(1, parts):
            weight = weight + lax.ppermute(
                pieces[step], "dp", [(source, (source + step) % parts) for source in range(parts)]
            ).astype(F32)
        sibling_grads = from_siblings(outs[1 : top + 1], top)
        bit = 1
        while bit < top:
            weight = weight.astype(BF)
            group = [weight] + [traded(weight, mask << bit) for mask in range(1, 2 ** min(2, top - bit))]
            weight = sum(value.astype(F32) for value in group)
            bit += 2
        weight = weight.astype(BF)
        weight = weight.astype(F32) + traded(weight, 1).astype(F32)
        key_grad, value_grad = key_call(sibling_grads)
    return query_grad[None], key_grad[None], value_grad[None], weight


def solution(mesh):
    spread = P("dp", SEQ, None)
    return jax.shard_map(
        shards,
        mesh=mesh,
        in_specs=(spread, spread, spread, P(), P(), spread),
        out_specs=(spread, spread, spread, P("dp", None)),
        check_vma=False,
    )
```

time: 47.5 us -> 35.3 us (0.74)
  the two profiles are of different devices: /device:TPU:25 before, /device:TPU:0 now
where the time goes in v3:
time: 35.3 us; the launch traced here: 35.1 us
  starting transfers between devices  15.4 us (44%)
  Pallas kernels  11.8 us (33%)
  waiting for transfers between devices  6.22 us (18%)
  local copies, waits for them, and re-layouts  0.97 us (3%)
  between operations  0.75 us (2%)
    pallas_call x13, Pallas kernels, call(): pl.pallas_call(body, out_shape=[jax.ShapeDtypeStruct(shape, kind) for sha...  11.8 us
    ppermute x12, starting transfers between devices, traded(): lax.ppermute(value, SEQ, [(source, source ^ mask) for source in range(lax...  7.07 us
    ppermute x12, waiting for transfers between devices, traded(): lax.ppermute(value, SEQ, [(source, source ^ mask) for source in range(lax...  4.5 us
    ppermute x2, starting transfers between devices, layer_traded(): return lax.ppermute(value, axes, pairs)  4.24 us
    ppermute x3, starting transfers between devices, split_traded(): lax.ppermute(value, SEQ, [(source, source ^ 2 * (second if source % 2 els...  4.08 us
    ppermute x3, waiting for transfers between devices, split_traded(): lax.ppermute(value, SEQ, [(source, source ^ 2 * (second if source % 2 els...  1.71 us
    unnamed x8, local copies, waits for them, and re-layouts  0.89 us
  transfers between devices with their start and end apart: 17, of which 6 were waited for; matrix products, arithmetic and copies ran while one was open for 0% of the time, Pallas kernels for 21%

profile of v3, /device:TPU:0, one launch (start us, length us, event | category | flops | bytes accessed | tf_op | source)
XLA Modules:
  0.0 35.1 jit_solution(2433949643795326425)
XLA Ops:
  0.6 1.7 %pool.1 = (f32[16,128]{1,0:T(8,128)S(1)}, bf16[256,1152]{1,0:T(8,128)(2,1)S(1)}, bf16[160,768]{1,0:T(8,128)(2,1)S(1)}, bf16[64,768]{1,0:T(8,128)(2,1)S(1)}, bf16...) custom-call(bf16[256,384]{1,0:T(8,128)(2,1)} %bitcast.14, ...), custom_call_target="tpu_custom_call" | custom-call | bytes 1114112 | tf_op jit(solution)/shard_map/pool/pallas_call | solution.py:141
  2.3 0.5 %collective-permute-start.1 = (bf16[160,768]{1,0:T(8,128)(2,1)S(1)}, bf16[160,768]{1,0:T(8,128)(2,1)S(1)}, u32[]{:S(2)}, u32[]{:S(2)}) collective-permute-start(bf16[160,768]{1,0:T(8,128)(2,1)S(1)} %get-tuple-element.52.refs_0_.refs_3_), channel_id=1, source_target_pairs={{0,1},{1,0},{2,3},{3,2},{4,5},{5,4},{6,7},{7,6},{8,9},{9,8},{10,11... | collective-permute-start | bytes 737288 | tf_op jit(solution)/shard_map/ppermute | solution.py:411
  2.9 2.6 %collective-permute-start = (bf16[64,768]{1,0:T(8,128)(2,1)S(1)}, bf16[64,768]{1,0:T(8,128)(2,1)S(1)}, u32[]{:S(2)}, u32[]{:S(2)}) collective-permute-start(bf16[64,768]{1,0:T(8,128)(2,1)S(1)} %get-tuple-element.42.refs_4_), channel_id=1, source_target_pairs={{0,2},{1,3},{2,0},{3,1},{4,6},{5,7},{6,4},{7,5},{8,10},{9,11},{10,... | collective-permute-start | bytes 294920 | tf_op jit(solution)/shard_map/ppermute | solution.py:411
  5.5 0.0 collective-permute-done.1.refs_1_.refs_9_.refs_7_
  5.5 1.6 %collective-permute-start.3 = (bf16[64,768]{1,0:T(8,128)(2,1)S(1)}, bf16[64,768]{1,0:T(8,128)(2,1)S(1)}, u32[]{:S(2)}, u32[]{:S(2)}) collective-permute-start(bf16[64,768]{1,0:T(8,128)(2,1)S(1)} %third_rows.1), channel_id=1, source_target_pairs={{0,4},{1,7},{2,6},{3,5},{4,0},{5,3},{6,2},{7,1},{8,12},{9,15},{10,... | collective-permute-start | bytes 294920 | tf_op jit(solution)/shard_map/ppermute | solution.py:415
  7.0 0.0 copy-done
  7.1 0.0 copy-done.1
  7.1 0.9 %base.1 = (f32[256,384]{1,0:T(8,128)S(1)}, f32[256,384]{1,0:T(8,128)S(1)}, bf16[256,1536]{1,0:T(8,128)(2,1)S(1)}, bf16[256,384]{1,0:T(8,128)(2,1)S(1)}, bf16[256,384]{1,0:T(8,128)(2,1)S(1)}) custom-call(f32[16,128]{1,0:T(8,128)S(1)} %get-tuple-element.41.refs_0_.refs_1_, bf16[256,1152]{1,0:T(8,128)(2,1)S(1)} %get-tuple-element.43.refs_1_, ...), custom_call_target="tpu_custom_call" | custom-call | flops 402653184 | bytes 1966080 | tf_op jit(solution)/shard_map/base/pallas_call | solution.py:141
  7.9 0.0 copy-start.2
  7.9 0.9 %copy-done.2 = bf16[256,1536]{1,0:T(8,128)(2,1)} copy-done((bf16[256,1536]{1,0:T(8,128)(2,1)}, bf16[256,1536]{1,0:T(8,128)(2,1)S(1)}, u32[]{:S(2)}) %copy-start.2) | copy-done | bytes 786456
  8.8 0.0 collective-permute-done.refs_10_.refs_8_
  8.8 0.6 %collective-permute-start.2 = (bf16[64,768]{1,0:T(8,128)(2,1)S(1)}, bf16[64,768]{1,0:T(8,128)(2,1)S(1)}, u32[]{:S(2)}, u32[]{:S(2)}) collective-permute-start(bf16[64,768]{1,0:T(8,128)(2,1)S(1)} %collective-permute-done.refs_10_.refs_8_), channel_id=1, source_target_pairs={{0,1},{1,0},{2,3},{3,2},{4,5},{5,4},{6,7},{7,6},{8,9},{9,8},{10,11... | collective-permute-start | bytes 294920 | tf_op jit(solution)/shard_map/ppermute | solution.py:411
  9.5 1.7 %collective-permute-done.3.refs_12_.refs_10_ = bf16[64,768]{1,0:T(8,128)(2,1)S(1)} collective-permute-done((bf16[64,768]{1,0:T(8,128)(2,1)S(1)}, bf16[64,768]{1,0:T(8,128)(2,1)S(1)}, u32[]{:S(2)}, u32[]{:S(2)}) %collective-permute-start.3) | collective-permute-done | bytes 98336 | tf_op jit(solution)/shard_map/ppermute | solution.py:415
  11.2 0.0 collective-permute-start.4
  11.2 0.1 stack.23.refs_0_
  11.3 0.0 collective-permute-done.2.refs_11_.refs_9_
  11.3 1.2 %collective-permute-done.4.refs_13_.refs_11_ = bf16[64,768]{1,0:T(8,128)(2,1)S(1)} collective-permute-done((bf16[64,768]{1,0:T(8,128)(2,1)S(1)}, bf16[64,768]{1,0:T(8,128)(2,1)S(1)}, u32[]{:S(2)}, u32[]{:S(2)}) %collective-permute-start.4) | collective-permute-done | bytes 98336 | tf_op jit(solution)/shard_map/ppermute | solution.py:411
  12.5 2.0 %forward.1 = (bf16[128,768]{1,0:T(8,128)(2,1)S(1)}, bf16[64,768]{1,0:T(8,128)(2,1)S(1)}, bf16[32,768]{1,0:T(8,128)(2,1)S(1)}, bf16[256,512]{1,0:T(8,128)(2,1)S(1...) custom-call(s32[5]{0:T(128)S(1)} %stack.23.refs_0_, ...), custom_call_target="tpu_custom_call" | custom-call | bytes 1302528 | tf_op jit(solution)/shard_map/forward/pallas_call | solution.py:141
  14.5 0.0 copy-start.3
  14.6 0.2 collective-permute-start.10
  14.8 0.4 %collective-permute-start.5 = (bf16[144,384]{1,0:T(8,128)(2,1)S(1)}, bf16[144,384]{1,0:T(8,128)(2,1)S(1)}, u32[]{:S(2)}, u32[]{:S(2)}) collective-permute-start(bf16[144,384]{1,0:T(8,128)(2,1)S(1)} %get-tuple-element.55), channel_id=1, source_target_pairs={{0,1},{1,0},{2,3},{3,2},{4,5},{5,4},{6,7},{7,6},{8,9},{9,8},{10,11... | collective-permute-start | bytes 331784 | tf_op jit(solution)/shard_map/ppermute | solution.py:411
  15.1 0.9 %collective-permute-start.11 = (bf16[64,896]{1,0:T(8,128)(2,1)S(1)}, bf16[64,896]{1,0:T(8,128)(2,1)S(1)}, u32[]{:S(2)}, u32[]{:S(2)}) collective-permute-start(bf16[64,896]{1,0:T(8,128)(2,1)S(1)} %get-tuple-element.64.refs_6_), channel_id=1, source_target_pairs={{0,2},{1,3},{2,0},{3,1},{4,6},{5,7},{6,4},{7,5},{8,10},{9,11},{10,... | collective-permute-start | bytes 344072 | tf_op jit(solution)/shard_map/ppermute | solution.py:411
  16.0 0.3 collective-permute-done.5.refs_1_
  16.4 2.7 %collective-permute-start.7 = (bf16[48,384]{1,0:T(8,128)(2,1)S(1)}, bf16[48,384]{1,0:T(8,128)(2,1)S(1)}, u32[]{:S(2)}, u32[]{:S(2)}) collective-permute-start(bf16[48,384]{1,0:T(8,128)(2,1)S(1)} %get-tuple-element.68), channel_id=1, source_target_pairs={{0,16},{1,17},{2,18},{3,19},{4,20},{5,21},{6,22},{7,23},{8,24},{9,... | collective-permute-start | bytes 110600 | tf_op jit(solution)/shard_map/ppermute | solution.py:429
  19.0 1.6 %collective-permute-start.6 = (bf16[96,384]{1,0:T(8,128)(2,1)S(1)}, bf16[96,384]{1,0:T(8,128)(2,1)S(1)}, u32[]{:S(2)}, u32[]{:S(2)}) collective-permute-start(bf16[96,384]{1,0:T(8,128)(2,1)S(1)} %get-tuple-element.56), channel_id=1, source_target_pairs={{0,8},{1,25},{2,10},{3,27},{4,12},{5,29},{6,14},{7,31},{8,0},{9,17... | collective-permute-start | bytes 221192 | tf_op jit(solution)/shard_map/ppermute | solution.py:429
  20.6 0.0 collective-permute-done.10.refs_1_.refs_5_
  20.6 1.6 %collective-permute-start.13 = (bf16[64,896]{1,0:T(8,128)(2,1)S(1)}, bf16[64,896]{1,0:T(8,128)(2,1)S(1)}, u32[]{:S(2)}, u32[]{:S(2)}) collective-permute-start(bf16[64,896]{1,0:T(8,128)(2,1)S(1)} %third_grads.1), channel_id=1, source_target_pairs={{0,4},{1,7},{2,6},{3,5},{4,0},{5,3},{6,2},{7,1},{8,12},{9,15},{10,... | collective-permute-start | bytes 344072 | tf_op jit(solution)/shard_map/ppermute | solution.py:415
  22.2 0.0 copy-done.3
  22.2 1.4 %near.1 = (f32[256,384]{1,0:T(8,128)S(1)}, f32[256,384]{1,0:T(8,128)S(1)}, f32[256,384]{1,0:T(8,128)S(1)}) custom-call(f32[16,128]{1,0:T(8,128)S(1)} %get-tuple-element.41.refs_0_.refs_1_, bf16[256,1152]{1,0:T(8,128)(2,1)S(1)} %get-tuple-element.43.refs_1_, bf16[256,512]{1,0:T(8,128)(2,1)S(1)} %get-tuple-element.57.refs_2_, bf16[256,1536]{1,0:T(8,128)(2,1)S(1)} %copy-done.3), custom_call_target="tpu_custom_call" | custom-call | flops 805306368 | bytes 1179648 | tf_op jit(solution)/shard_map/near/pallas_call | solution.py:141
  23.6 2.1 %far.1 = bf16[256,384]{1,0:T(8,128)(2,1)} custom-call(f32[16,128]{1,0:T(8,128)S(1)} %get-tuple-element.41.refs_0_.refs_1_, f32[256,384]{1,0:T(8,128)S(1)} %get-tuple-element.59.refs_1_, bf16[128,768]{1,0:T(8,128)(2,1)S(1)} %get-tuple-element.60.refs_2_, bf16[64,768]{1,0:T(8,128)(2,1)S(1)} %get-tuple-element.61.refs_3_, ...), custom_call_target="tpu_custom_call" | custom-call | flops 201326592 | bytes 196608 | tf_op jit(solution)/shard_map/far/pallas_call | solution.py:141
  25.7 0.0 collective-permute-done.6.refs_1_
  25.7 0.0 collective-permute-done.7.refs_2_
  25.8 0.1 collective-permute-start.8
  25.8 0.0 collective-permute-done.11.refs_6_
  25.9 0.5 %collective-permute-start.12 = (bf16[64,896]{1,0:T(8,128)(2,1)S(1)}, bf16[64,896]{1,0:T(8,128)(2,1)S(1)}, u32[]{:S(2)}, u32[]{:S(2)}) collective-permute-start(bf16[64,896]{1,0:T(8,128)(2,1)S(1)} %collective-permute-done.11.refs_6_), channel_id=1, source_target_pairs={{0,1},{1,0},{2,3},{3,2},{4,5},{5,4},{6,7},{7,6},{8,9},{9,8},{10,11... | collective-permute-start | bytes 344072 | tf_op jit(solution)/shard_map/ppermute | solution.py:411
  26.3 0.0 collective-permute-done.13.refs_8_
  26.4 0.1 collective-permute-start.14
  26.4 0.7 %collective-permute-done.8.refs_2_ = bf16[144,384]{1,0:T(8,128)(2,1)S(1)} collective-permute-done((bf16[144,384]{1,0:T(8,128)(2,1)S(1)}, bf16[144,384]{1,0:T(8,128)(2,1)S(1)}, u32[]{:S(2)}, u32[]{:S(2)}) %collective-permute-start.8) | collective-permute-done | bytes 110624 | tf_op jit(solution)/shard_map/ppermute | solution.py:411
  27.2 1.0 %collective-permute-start.9 = (bf16[96,384]{1,0:T(8,128)(2,1)S(1)}, bf16[96,384]{1,0:T(8,128)(2,1)S(1)}, u32[]{:S(2)}, u32[]{:S(2)}) collective-permute-start(bf16[96,384]{1,0:T(8,128)(2,1)S(1)} %get-tuple-element.69.refs_3_), channel_id=1, source_target_pairs={{0,2},{1,5},{2,0},{3,7},{4,6},{5,1},{6,4},{7,3},{8,10},{9,13},{10,... | collective-permute-start | bytes 221192 | tf_op jit(solution)/shard_map/ppermute | solution.py:415
  28.2 1.1 %collective-permute-start.15 = (bf16[48,384]{1,0:T(8,128)(2,1)S(1)}, bf16[48,384]{1,0:T(8,128)(2,1)S(1)}, u32[]{:S(2)}, u32[]{:S(2)}) collective-permute-start(bf16[48,384]{1,0:T(8,128)(2,1)S(1)} %get-tuple-element.77), channel_id=1, source_target_pairs={{0,6},{1,7},{2,4},{3,5},{4,2},{5,3},{6,0},{7,1},{8,14},{9,15},{10,... | collective-permute-start | bytes 110600 | tf_op jit(solution)/shard_map/ppermute | solution.py:411
  29.3 0.0 collective-permute-done.12.refs_7_
  29.3 0.0 collective-permute-done.14.refs_9_
  29.3 2.8 %key.1 = (bf16[256,384]{1,0:T(8,128)(2,1)}, bf16[256,384]{1,0:T(8,128)(2,1)}) custom-call(f32[16,128]{1,0:T(8,128)S(1)} %get-tuple-element.41.refs_0_.refs_1_, f32[256,384]{1,0:T(8,128)S(1)} %get-tuple-element.70.refs_1_, f32[256,384]{1,0:T(8,128)S(1)} %get-tuple-element.71.refs_2_, bf16[160,768]{1,0:T(8,128)(2,1)S(1)} %get-tuple-element.52.refs_0_.refs_3_, ...), custom_call_target="tpu_custom_call" | custom-call | flops 402653184 | bytes 393216 | tf_op jit(solution)/shard_map/key/pallas_call | solution.py:141
  32.1 0.0 collective-permute-done.9.refs_0_
  32.1 0.9 %collective-permute-done.15.refs_1_ = bf16[48,384]{1,0:T(8,128)(2,1)S(1)} collective-permute-done((bf16[48,384]{1,0:T(8,128)(2,1)S(1)}, bf16[48,384]{1,0:T(8,128)(2,1)S(1)}, u32[]{:S(2)}, u32[]{:S(2)}) %collective-permute-start.15) | collective-permute-done | bytes 36896 | tf_op jit(solution)/shard_map/ppermute | solution.py:411
  33.0 0.1 collective-permute-start.16
  33.1 1.3 %collective-permute-done.16.refs_2_ = bf16[144,384]{1,0:T(8,128)(2,1)S(1)} collective-permute-done((bf16[144,384]{1,0:T(8,128)(2,1)S(1)}, bf16[144,384]{1,0:T(8,128)(2,1)S(1)}, u32[]{:S(2)}, u32[]{:S(2)}) %collective-permute-start.16) | collective-permute-done | bytes 110624 | tf_op jit(solution)/shard_map/ppermute | solution.py:411
  34.4 0.7 %weight_out.1 = f32[96,384]{1,0:T(8,128)} custom-call(s32[1]{0:T(128)} %bitcast.10.refs_0_, bf16[144,384]{1,0:T(8,128)(2,1)S(1)} %plane_rows.1.refs_1_, bf16[144,384]{1,0:T(8,128)(2,1)S(1)} %collective-permute-done.16.refs_2_, bf16[96,384]{1,0:T(8,128)(2,1)S(1)} %get-tuple-element.69.refs_3_), custom_call_target="tpu_custom_call" | custom-call | bytes 147456 | tf_op jit(solution)/shard_map/weight_out/pallas_call | solution.py:141
  (8 shorter events, 0.1 us)
Async XLA Ops:
  2.3 3.1 %collective-permute-start.1 = (bf16[160,768]{1,0:T(8,128)(2,1)S(1)}, bf16[160,768]{1,0:T(8,128)(2,1)S(1)}, u32[]{:S(2)}, u32[]{:S(2)}) collective-permute-start(bf16[160,768]{1,0:T(8,128)(2,1)S(1)} %get-tuple-element.52.refs_0_.refs_3_), channel_id=1, source_target_pairs={{0,1},{1,0},{2,3},{3,2},{4,5},{5,4},{6,7},{7,6},{8,9},{9,8},{10,11... | collective-permute-start | bytes 737288 | tf_op jit(solution)/shard_map/ppermute | solution.py:411
  2.9 4.2 %copy-start = (bf16[384,384]{1,0:T(8,128)(2,1)S(1)}, bf16[384,384]{1,0:T(8,128)(2,1)}, u32[]{:S(2)}) copy-start(bf16[384,384]{1,0:T(8,128)(2,1)} %refs_3_.3) | copy-start | bytes 884740
  2.9 4.2 %copy-start.1 = (bf16[1,256,384]{2,1,0:T(8,128)(2,1)S(1)}, bf16[1,256,384]{2,1,0:T(8,128)(2,1)}, u32[]{:S(2)}) copy-start(bf16[1,256,384]{2,1,0:T(8,128)(2,1)} %param.11) | copy-start | bytes 589828
  2.9 6.0 %collective-permute-start = (bf16[64,768]{1,0:T(8,128)(2,1)S(1)}, bf16[64,768]{1,0:T(8,128)(2,1)S(1)}, u32[]{:S(2)}, u32[]{:S(2)}) collective-permute-start(bf16[64,768]{1,0:T(8,128)(2,1)S(1)} %get-tuple-element.42.refs_4_), channel_id=1, source_target_pairs={{0,2},{1,3},{2,0},{3,1},{4,6},{5,7},{6,4},{7,5},{8,10},{9,11},{10,... | collective-permute-start | bytes 294920 | tf_op jit(solution)/shard_map/ppermute | solution.py:411
  5.5 5.7 %collective-permute-start.3 = (bf16[64,768]{1,0:T(8,128)(2,1)S(1)}, bf16[64,768]{1,0:T(8,128)(2,1)S(1)}, u32[]{:S(2)}, u32[]{:S(2)}) collective-permute-start(bf16[64,768]{1,0:T(8,128)(2,1)S(1)} %third_rows.1), channel_id=1, source_target_pairs={{0,4},{1,7},{2,6},{3,5},{4,0},{5,3},{6,2},{7,1},{8,12},{9,15},{10,... | collective-permute-start | bytes 294920 | tf_op jit(solution)/shard_map/ppermute | solution.py:415
  7.9 0.9 %copy-start.2 = (bf16[256,1536]{1,0:T(8,128)(2,1)}, bf16[256,1536]{1,0:T(8,128)(2,1)S(1)}, u32[]{:S(2)}) copy-start(bf16[256,1536]{1,0:T(8,128)(2,1)S(1)} %get-tuple-element.58.refs_3_) | copy-start | bytes 2359300
  8.8 2.4 %collective-permute-start.2 = (bf16[64,768]{1,0:T(8,128)(2,1)S(1)}, bf16[64,768]{1,0:T(8,128)(2,1)S(1)}, u32[]{:S(2)}, u32[]{:S(2)}) collective-permute-start(bf16[64,768]{1,0:T(8,128)(2,1)S(1)} %collective-permute-done.refs_10_.refs_8_), channel_id=1, source_target_pairs={{0,1},{1,0},{2,3},{3,2},{4,5},{5,4},{6,7},{7,6},{8,9},{9,8},{10,11... | collective-permute-start | bytes 294920 | tf_op jit(solution)/shard_map/ppermute | solution.py:411
  11.2 1.3 %collective-permute-start.4 = (bf16[64,768]{1,0:T(8,128)(2,1)S(1)}, bf16[64,768]{1,0:T(8,128)(2,1)S(1)}, u32[]{:S(2)}, u32[]{:S(2)}) collective-permute-start(bf16[64,768]{1,0:T(8,128)(2,1)S(1)} %collective-permute-done.3.refs_12_.refs_10_), channel_id=1, source_target_pairs={{0,1},{1,0},{2,3},{3,2},{4,5},{5,4},{6,7},{7,6},{8,9},{9,8},{10,11... | collective-permute-start | bytes 294920 | tf_op jit(solution)/shard_map/ppermute | solution.py:411
  14.5 7.7 %copy-start.3 = (bf16[256,1536]{1,0:T(8,128)(2,1)S(1)}, bf16[256,1536]{1,0:T(8,128)(2,1)}, u32[]{:S(2)}) copy-start(bf16[256,1536]{1,0:T(8,128)(2,1)} %copy-done.2) | copy-start | bytes 2359300
  14.6 6.1 %collective-permute-start.10 = (bf16[160,896]{1,0:T(8,128)(2,1)S(1)}, bf16[160,896]{1,0:T(8,128)(2,1)S(1)}, u32[]{:S(2)}, u32[]{:S(2)}) collective-permute-start(bf16[160,896]{1,0:T(8,128)(2,1)S(1)} %get-tuple-element.63.refs_5_.refs_0_), channel_id=1, source_target_pairs={{0,1},{1,0},{2,3},{3,2},{4,5},{5,4},{6,7},{7,6},{8,9},{9,8},{10,11... | collective-permute-start | bytes 860168 | tf_op jit(solution)/shard_map/ppermute | solution.py:411
  14.8 1.6 %collective-permute-start.5 = (bf16[144,384]{1,0:T(8,128)(2,1)S(1)}, bf16[144,384]{1,0:T(8,128)(2,1)S(1)}, u32[]{:S(2)}, u32[]{:S(2)}) collective-permute-start(bf16[144,384]{1,0:T(8,128)(2,1)S(1)} %get-tuple-element.55), channel_id=1, source_target_pairs={{0,1},{1,0},{2,3},{3,2},{4,5},{5,4},{6,7},{7,6},{8,9},{9,8},{10,11... | collective-permute-start | bytes 331784 | tf_op jit(solution)/shard_map/ppermute | solution.py:411
  15.1 10.7 %collective-permute-start.11 = (bf16[64,896]{1,0:T(8,128)(2,1)S(1)}, bf16[64,896]{1,0:T(8,128)(2,1)S(1)}, u32[]{:S(2)}, u32[]{:S(2)}) collective-permute-start(bf16[64,896]{1,0:T(8,128)(2,1)S(1)} %get-tuple-element.64.refs_6_), channel_id=1, source_target_pairs={{0,2},{1,3},{2,0},{3,1},{4,6},{5,7},{6,4},{7,5},{8,10},{9,11},{10,... | collective-permute-start | bytes 344072 | tf_op jit(solution)/shard_map/ppermute | solution.py:411
  16.4 9.4 %collective-permute-start.7 = (bf16[48,384]{1,0:T(8,128)(2,1)S(1)}, bf16[48,384]{1,0:T(8,128)(2,1)S(1)}, u32[]{:S(2)}, u32[]{:S(2)}) collective-permute-start(bf16[48,384]{1,0:T(8,128)(2,1)S(1)} %get-tuple-element.68), channel_id=1, source_target_pairs={{0,16},{1,17},{2,18},{3,19},{4,20},{5,21},{6,22},{7,23},{8,24},{9,... | collective-permute-start | bytes 110600 | tf_op jit(solution)/shard_map/ppermute | solution.py:429
  19.0 6.7 %collective-permute-start.6 = (bf16[96,384]{1,0:T(8,128)(2,1)S(1)}, bf16[96,384]{1,0:T(8,128)(2,1)S(1)}, u32[]{:S(2)}, u32[]{:S(2)}) collective-permute-start(bf16[96,384]{1,0:T(8,128)(2,1)S(1)} %get-tuple-element.56), channel_id=1, source_target_pairs={{0,8},{1,25},{2,10},{3,27},{4,12},{5,29},{6,14},{7,31},{8,0},{9,17... | collective-permute-start | bytes 221192 | tf_op jit(solution)/shard_map/ppermute | solution.py:429
  20.6 5.7 %collective-permute-start.13 = (bf16[64,896]{1,0:T(8,128)(2,1)S(1)}, bf16[64,896]{1,0:T(8,128)(2,1)S(1)}, u32[]{:S(2)}, u32[]{:S(2)}) collective-permute-start(bf16[64,896]{1,0:T(8,128)(2,1)S(1)} %third_grads.1), channel_id=1, source_target_pairs={{0,4},{1,7},{2,6},{3,5},{4,0},{5,3},{6,2},{7,1},{8,12},{9,15},{10,... | collective-permute-start | bytes 344072 | tf_op jit(solution)/shard_map/ppermute | solution.py:415
  25.8 1.4 %collective-permute-start.8 = (bf16[144,384]{1,0:T(8,128)(2,1)S(1)}, bf16[144,384]{1,0:T(8,128)(2,1)S(1)}, u32[]{:S(2)}, u32[]{:S(2)}) collective-permute-start(bf16[144,384]{1,0:T(8,128)(2,1)S(1)} %layer_sum.1.refs_1_), channel_id=1, source_target_pairs={{0,1},{1,0},{2,3},{3,2},{4,5},{5,4},{6,7},{7,6},{8,9},{9,8},{10,11... | collective-permute-start | bytes 331784 | tf_op jit(solution)/shard_map/ppermute | solution.py:411
  25.9 3.4 %collective-permute-start.12 = (bf16[64,896]{1,0:T(8,128)(2,1)S(1)}, bf16[64,896]{1,0:T(8,128)(2,1)S(1)}, u32[]{:S(2)}, u32[]{:S(2)}) collective-permute-start(bf16[64,896]{1,0:T(8,128)(2,1)S(1)} %collective-permute-done.11.refs_6_), channel_id=1, source_target_pairs={{0,1},{1,0},{2,3},{3,2},{4,5},{5,4},{6,7},{7,6},{8,9},{9,8},{10,11... | collective-permute-start | bytes 344072 | tf_op jit(solution)/shard_map/ppermute | solution.py:411
  26.4 2.9 %collective-permute-start.14 = (bf16[64,896]{1,0:T(8,128)(2,1)S(1)}, bf16[64,896]{1,0:T(8,128)(2,1)S(1)}, u32[]{:S(2)}, u32[]{:S(2)}) collective-permute-start(bf16[64,896]{1,0:T(8,128)(2,1)S(1)} %collective-permute-done.13.refs_8_), channel_id=1, source_target_pairs={{0,1},{1,0},{2,3},{3,2},{4,5},{5,4},{6,7},{7,6},{8,9},{9,8},{10,11... | collective-permute-start | bytes 344072 | tf_op jit(solution)/shard_map/ppermute | solution.py:411
  27.2 4.9 %collective-permute-start.9 = (bf16[96,384]{1,0:T(8,128)(2,1)S(1)}, bf16[96,384]{1,0:T(8,128)(2,1)S(1)}, u32[]{:S(2)}, u32[]{:S(2)}) collective-permute-start(bf16[96,384]{1,0:T(8,128)(2,1)S(1)} %get-tuple-element.69.refs_3_), channel_id=1, source_target_pairs={{0,2},{1,5},{2,0},{3,7},{4,6},{5,1},{6,4},{7,3},{8,10},{9,13},{10,... | collective-permute-start | bytes 221192 | tf_op jit(solution)/shard_map/ppermute | solution.py:415
  28.2 4.9 %collective-permute-start.15 = (bf16[48,384]{1,0:T(8,128)(2,1)S(1)}, bf16[48,384]{1,0:T(8,128)(2,1)S(1)}, u32[]{:S(2)}, u32[]{:S(2)}) collective-permute-start(bf16[48,384]{1,0:T(8,128)(2,1)S(1)} %get-tuple-element.77), channel_id=1, source_target_pairs={{0,6},{1,7},{2,4},{3,5},{4,2},{5,3},{6,0},{7,1},{8,14},{9,15},{10,... | collective-permute-start | bytes 110600 | tf_op jit(solution)/shard_map/ppermute | solution.py:411
  33.0 1.4 %collective-permute-start.16 = (bf16[144,384]{1,0:T(8,128)(2,1)S(1)}, bf16[144,384]{1,0:T(8,128)(2,1)S(1)}, u32[]{:S(2)}, u32[]{:S(2)}) collective-permute-start(bf16[144,384]{1,0:T(8,128)(2,1)S(1)} %plane_rows.1.refs_1_), channel_id=1, source_target_pairs={{0,1},{1,0},{2,3},{3,2},{4,5},{5,4},{6,7},{7,6},{8,9},{9,8},{10,11... | collective-permute-start | bytes 331784 | tf_op jit(solution)/shard_map/ppermute | solution.py:411

commit v4 on v3

--- a/solution.py
+++ b/solution.py
@@ -113,7 +113,7 @@
 HBM = pl.BlockSpec(memory_space=pltpu.HBM)
 
 
-def call(kernel, name, shapes, arrays, views=(), scalars=(), flops=0, scratch=(), specs=None):
+def call(kernel, name, shapes, arrays, views=(), scalars=(), flops=0, scratch=(), specs=None, out_specs=None):
     unique, where = [], []
     for group in views:
         places = []
@@ -142,7 +142,7 @@
         body,
         out_shape=[jax.ShapeDtypeStruct(shape, kind) for shape, kind in shapes],
         in_specs=[SMEM] * len(scalars) + (specs or [VMEM] * len(arrays)) + [VMEM] * len(unique),
-        out_specs=[VMEM] * len(shapes),
+        out_specs=out_specs or [VMEM] * len(shapes),
         scratch_shapes=list(scratch),
         compiler_params=pltpu.CompilerParams(vmem_limit_bytes=16 * 2**20),
         cost_estimate=pl.CostEstimate(flops=flops, transcendentals=0, bytes_accessed=moved),
@@ -218,17 +218,14 @@
 
 
 def forward_kernel(
-    top, parts, grad_places, pieces,
-    load, place_ref, factor_ref, numer_ref, denom_ref, cotp_ref, back_ref, *refs
+    top, parts, pieces, load, place_ref, factor_ref, numer_ref, denom_ref, cotp_ref, back_ref, _, *refs
 ):
-    weights_refs, out_refs, weight_ref = refs[:top], refs[top:-1], refs[-1]
+    weights_refs, (grad_ref, slope_ref), out_refs, weight_ref = refs[:top], refs[top : top + 2], refs[top + 2 : -1], refs[-1]
     rows, width = numer_ref.shape
     masks = side_masks()
     lane = iota((LANES, LANES), 1)
     ones = jnp.where(lane // HALF == iota((LANES, LANES), 0) // HALF, 1.0, 0.0).astype(BF)
     adder = doubled(ones)
-    grad_rows = []
-    denom_rows = []
     attended = []
     for pair in range(width // LANES):
         total = None
@@ -249,14 +246,20 @@
         product_high = product.astype(BF)
         product_low = (product - product_high.astype(F32)).astype(BF)
         summed = dot(stack([product_high, product_low], 1), adder)
-        grad_rows.append(back * inverse)
-        denom_rows.append(-summed * inverse)
+        grad_ref[:, lane_pair(0, pair)] = back * inverse
+        slope_ref[:, lane_pair(0, pair)] = -summed * inverse
     weight_ref[...] = dot(stack(attended, 1), cotp_ref[...], TN)
     own_rows = width // parts
     for entry, offset, count, target, start in pieces:
         shift = offset if isinstance(offset, int) else offset(place_ref)
         first = pl.multiple_of(place_ref[entry] * own_rows + shift, math.gcd(own_rows, count))
         out_refs[target][start : start + count, :] = weight_ref[pl.ds(first, count), :].astype(BF)
+
+
+def grads_kernel(grad_places, load, grad_ref, slope_ref, *out_refs):
+    rows, width = grad_ref.shape
+    grad_rows = [grad_ref[:, lane_pair(0, pair)] for pair in range(width // LANES)]
+    denom_rows = [slope_ref[:, lane_pair(0, pair)] for pair in range(width // LANES)]
     for height, (target, start) in enumerate(grad_places):
         if height:
             grad_rows = [halves_sum(value) for value in grad_rows]
@@ -373,6 +376,28 @@
         refs[target][start : start + total.shape[0], :] = total.astype(refs[target].dtype)
 
 
+def flush_kernel(load, *refs):
+    count = (len(refs) - 1) // 2
+    copies = [
+        pltpu.make_async_copy(refs[at], refs[count + at], refs[-1].at[at]) for at in range(count)
+    ]
+    for copy in copies:
+        copy.start()
+    for copy in copies:
+        copy.wait()
+
+
+def flush(*arrays):
+    return call(
+        flush_kernel,
+        "flush",
+        [(array.shape, array.dtype) for array in arrays],
+        arrays,
+        out_specs=[HBM] * len(arrays),
+        scratch=[pltpu.SemaphoreType.DMA((len(arrays),))],
+    )
+
+
 def placed(name, shapes, spots):
     views, listed = [], []
     for target, start, parts in spots:
@@ -509,33 +534,47 @@
         core = lax.axis_index(SEQ).astype(jnp.int32) % 2
         place = jnp.stack([layer, layer ^ (1 + 2 * core), layer ^ (3 - 2 * core), layer ^ 2, core * half])
         grad_places = [(0, 0), (1, 0), (2, 0), (1, sizes[1])]
-        shapes = [(rows, wide), (sizes[1] + sizes[3], wide + width), (sizes[2], wide + width)]
+        grad_shapes = [(rows, wide), (sizes[1] + sizes[3], wide + width), (sizes[2], wide + width)]
         pieces = [
-            (0, 0, own_rows, 3, 0),
-            (1, 0, own_rows, 4, 0),
-            (3, lambda ref: ref[4], half, 4, own_rows),
-            (2, 0, own_rows, 5, 0),
-            (3, lambda ref: half - ref[4], half, 5, own_rows),
+            (0, 0, own_rows, 0, 0),
+            (1, 0, own_rows, 1, 0),
+            (3, lambda ref: ref[4], half, 1, own_rows),
+            (2, 0, own_rows, 2, 0),
+            (3, lambda ref: half - ref[4], half, 2, own_rows),
         ]
-        shapes += [(own_rows, width), (own_rows + half, width), (own_rows + half, width)]
+        shapes = [(own_rows, width), (own_rows + half, width), (own_rows + half, width)]
     else:
         place = (layer + jnp.arange(parts, dtype=jnp.int32)) % parts
         grad_places = [(height, 0) for height in range(top + 1)]
-        pieces = [(step, 0, own_rows, top + 1 + step, 0) for step in range(parts)]
-        shapes = [(rows, wide)] + [(size, wide + width) for size in sizes[1:]] + [(own_rows, width)] * parts
+        pieces = [(step, 0, own_rows, step, 0) for step in range(parts)]
+        grad_shapes = [(rows, wide)] + [(size, wide + width) for size in sizes[1:]]
+        shapes = [(own_rows, width)] * parts
     outs = call(
-        functools.partial(forward_kernel, top, parts, grad_places, pieces),
+        functools.partial(forward_kernel, top, parts, pieces),
         "forward",
-        [((size, heads * rows // 2), BF) for size in sizes[1:]] + [(shape, BF) for shape in shapes],
-        [factors, numer, denom, cotan, back],
+        [((size, heads * rows // 2), BF) for size in sizes[1:]]
+        + [(whole, F32), (whole, F32)]
+        + [(shape, BF) for shape in shapes],
+        [factors, numer, denom, cotan, back, base_weights],
         views=level_queries + siblings,
         scalars=[place],
         scratch=[pltpu.VMEM((width, width), F32)],
     )
-    level_weights, outs = outs[:top], outs[top:]
-    own_grads = [
-        [View(outs[target], start, sizes[height])] for height, (target, start) in enumerate(grad_places) if height
-    ]
+    level_weights, (grad_rows, denom_rows), pieces = outs[:top], outs[top : top + 2], outs[top + 2 :]
+    outs = call(
+        functools.partial(grads_kernel, grad_places),
+        "grads",
+        [(shape, BF) for shape in grad_shapes],
+        [grad_rows, denom_rows],
+        views=level_queries,
+        flops=4 * rows * rows * width * 4,
+    )
+
+    def own_grads(arrays):
+        return [
+            [View(arrays[target], start, sizes[height])] for height, (target, start) in enumerate(grad_places) if height
+        ]
+
     near_query, near_key, near_value = call(
         near_kernel,
         "near",
@@ -548,7 +587,7 @@
         "far",
         [(whole, BF)],
         [factors, near_query, *level_weights],
-        views=own_grads + siblings,
+        views=own_grads(outs) + siblings,
         flops=8 * rows * rows * width,
     )
 
@@ -563,10 +602,9 @@
         )
 
     if paired:
-        near, far, mine, send, theirs = outs[1:6]
+        near, far = outs[1:3]
+        mine, send, theirs = pieces
         theirs_in = traded(theirs, 1)
-        near_in = traded(near, 1)
-        far_in = traded(far, 2)
         send_one, send_half = placed(
             "layer_rows",
             [((own_rows, width), BF), ((half, width), BF)],
@@ -575,12 +613,15 @@
                 (1, 0, [View(send, own_rows), View(theirs_in, own_rows)]),
             ],
         )
+        near, far, send_one = lax.optimization_barrier((near, far, send_one))
+        near_in = traded(near, 1)
+        far_in = traded(far, 2)
         layer_one = layer_traded(send_one, 1, 3)
         layer_half = layer_traded(send_half, 2, 2)
         (third,) = placed(
             "third_grads",
             [((2 * sizes[3], wide + width), BF)],
-            [(0, 0, [own_grads[2][0]]), (0, sizes[3], [View(near_in, sizes[1])])],
+            [(0, 0, [View(near, sizes[1])]), (0, sizes[3], [View(near_in, sizes[1])])],
         )
         third_in = split_traded(third, 2, 3)
         far_in, near_query = lax.optimization_barrier((far_in, near_query))
@@ -609,9 +650,10 @@
             [(0, 0, [View(plane_one)]), (0, own_rows, [View(plane_half)])],
         )
         joint_in = traded(joint, 1)
+        query_grad, key_grad, value_grad = flush(query_grad, key_grad, value_grad)
+        joint_in, key_grad = lax.optimization_barrier((joint_in, key_grad))
         (weight,) = chip_total("weight_out", core, [joint, joint_in, weight], half, F32)
     else:
-        pieces = outs[top + 1 :]
         weight = pieces[0].astype(F32)
         for step in range(1, parts):
             weight = weight + lax.ppermute(

time: 35.3 us -> 35.5 us (level)
  waiting for transfers between devices: 6.22 us -> 7.77 us
  local copies, waits for them, and re-layouts: 0.97 us -> 0.1 us
    ppermute x12, waiting for transfers between devices: 4.5 us -> 5.42 us  [traded(): lax.ppermute(value, SEQ, [(source, source ^ mask) for source in range(lax...]
    unnamed x8, local copies, waits for them, and re-layouts: 0.89 us -> 0.02 us
    ppermute x3, waiting for transfers between devices: 1.71 us -> 2.35 us  [split_traded(): lax.ppermute(value, SEQ, [(source, source ^ 2 * (second if source % 2 els...]
    pallas_call x13 -> x15, Pallas kernels: 11.8 us -> 11.5 us  [call(): pl.pallas_call(body, out_shape=[jax.ShapeDtypeStruct(shape, kind) for sha...]
  transfers between devices with their start and end apart: 17 -> 17, of which waited for: 6 -> 8; matrix products, arithmetic and copies ran while one was open for 0% -> 0% of each run, Pallas kernels for 21% -> 20%
where the time goes in v4:
time: 35.5 us; the launch traced here: 35.3 us
  starting transfers between devices  15.2 us (43%)
  Pallas kernels  11.5 us (32%)
  waiting for transfers between devices  7.77 us (22%)
  between operations  0.79 us (2%)
    pallas_call x15, Pallas kernels, call(): pl.pallas_call(body, out_shape=[jax.ShapeDtypeStruct(shape, kind) for sha...  11.5 us
    ppermute x12, starting transfers between devices, traded(): lax.ppermute(value, SEQ, [(source, source ^ mask) for source in range(lax...  6.91 us
    ppermute x12, waiting for transfers between devices, traded(): lax.ppermute(value, SEQ, [(source, source ^ mask) for source in range(lax...  5.42 us
    ppermute x2, starting transfers between devices, layer_traded(): return lax.ppermute(value, axes, pairs)  4.19 us
    ppermute x3, starting transfers between devices, split_traded(): lax.ppermute(value, SEQ, [(source, source ^ 2 * (second if source % 2 els...  4.12 us
    ppermute x3, waiting for transfers between devices, split_traded(): lax.ppermute(value, SEQ, [(source, source ^ 2 * (second if source % 2 els...  2.35 us
  transfers between devices with their start and end apart: 17, of which 8 were waited for; matrix products, arithmetic and copies ran while one was open for 0% of the time, Pallas kernels for 20%

profile of v4, /device:TPU:0, one launch (start us, length us, event | category | flops | bytes accessed | tf_op | source)
XLA Modules:
  0.0 35.3 jit_solution(8179962901507221839)
XLA Ops:
  0.6 1.7 %pool.1 = (f32[16,128]{1,0:T(8,128)S(1)}, bf16[256,1152]{1,0:T(8,128)(2,1)S(1)}, bf16[160,768]{1,0:T(8,128)(2,1)S(1)}, bf16[64,768]{1,0:T(8,128)(2,1)S(1)}, bf16...) custom-call(bf16[256,384]{1,0:T(8,128)(2,1)} %bitcast.14, ...), custom_call_target="tpu_custom_call" | custom-call | bytes 1114112 | tf_op jit(solution)/shard_map/pool/pallas_call | solution.py:141
  2.3 0.0 copy-start
  2.3 0.5 %collective-permute-start.1 = (bf16[160,768]{1,0:T(8,128)(2,1)S(1)}, bf16[160,768]{1,0:T(8,128)(2,1)S(1)}, u32[]{:S(2)}, u32[]{:S(2)}) collective-permute-start(bf16[160,768]{1,0:T(8,128)(2,1)S(1)} %get-tuple-element.63.refs_0_.refs_3_), channel_id=1, source_target_pairs={{0,1},{1,0},{2,3},{3,2},{4,5},{5,4},{6,7},{7,6},{8,9},{9,8},{10,11... | collective-permute-start | bytes 737288 | tf_op jit(solution)/shard_map/ppermute | solution.py:436
  2.9 2.6 %collective-permute-start = (bf16[64,768]{1,0:T(8,128)(2,1)S(1)}, bf16[64,768]{1,0:T(8,128)(2,1)S(1)}, u32[]{:S(2)}, u32[]{:S(2)}) collective-permute-start(bf16[64,768]{1,0:T(8,128)(2,1)S(1)} %get-tuple-element.52.refs_4_), channel_id=1, source_target_pairs={{0,2},{1,3},{2,0},{3,1},{4,6},{5,7},{6,4},{7,5},{8,10},{9,11},{10,... | collective-permute-start | bytes 294920 | tf_op jit(solution)/shard_map/ppermute | solution.py:436
  5.5 0.0 collective-permute-done.1.refs_1_.refs_10_.refs_7_
  5.5 1.6 %collective-permute-start.3 = (bf16[64,768]{1,0:T(8,128)(2,1)S(1)}, bf16[64,768]{1,0:T(8,128)(2,1)S(1)}, u32[]{:S(2)}, u32[]{:S(2)}) collective-permute-start(bf16[64,768]{1,0:T(8,128)(2,1)S(1)} %third_rows.1), channel_id=1, source_target_pairs={{0,4},{1,7},{2,6},{3,5},{4,0},{5,3},{6,2},{7,1},{8,12},{9,15},{10,... | collective-permute-start | bytes 294920 | tf_op jit(solution)/shard_map/ppermute | solution.py:440
  7.1 0.0 copy-done.2
  7.1 0.0 copy-done.3
  7.1 0.9 %base.1 = (f32[256,384]{1,0:T(8,128)S(1)}, f32[256,384]{1,0:T(8,128)S(1)}, bf16[256,1536]{1,0:T(8,128)(2,1)S(1)}, bf16[256,384]{1,0:T(8,128)(2,1)S(1)}, bf16[256,384]{1,0:T(8,128)(2,1)S(1)}) custom-call(f32[16,128]{1,0:T(8,128)S(1)} %get-tuple-element.51.refs_0_.refs_1_, bf16[256,1152]{1,0:T(8,128)(2,1)S(1)} %get-tuple-element.53.refs_1_, ...), custom_call_target="tpu_custom_call" | custom-call | flops 402653184 | bytes 1966080 | tf_op jit(solution)/shard_map/base/pallas_call | solution.py:141
  7.9 0.0 copy-done
  8.0 0.9 %collective-permute-done.refs_11_.refs_8_ = bf16[64,768]{1,0:T(8,128)(2,1)S(1)} collective-permute-done((bf16[64,768]{1,0:T(8,128)(2,1)S(1)}, bf16[64,768]{1,0:T(8,128)(2,1)S(1)}, u32[]{:S(2)}, u32[]{:S(2)}) %collective-permute-start) | collective-permute-done | bytes 98336 | tf_op jit(solution)/shard_map/ppermute | solution.py:436
  8.9 0.0 collective-permute-start.2
  8.9 2.3 %collective-permute-done.3.refs_13_.refs_10_ = bf16[64,768]{1,0:T(8,128)(2,1)S(1)} collective-permute-done((bf16[64,768]{1,0:T(8,128)(2,1)S(1)}, bf16[64,768]{1,0:T(8,128)(2,1)S(1)}, u32[]{:S(2)}, u32[]{:S(2)}) %collective-permute-start.3) | collective-permute-done | bytes 98336 | tf_op jit(solution)/shard_map/ppermute | solution.py:440
  11.2 0.0 collective-permute-start.4
  11.2 0.1 stack.23.refs_0_
  11.3 0.0 collective-permute-done.2.refs_12_.refs_9_
  11.3 1.2 %collective-permute-done.4.refs_14_.refs_11_ = bf16[64,768]{1,0:T(8,128)(2,1)S(1)} collective-permute-done((bf16[64,768]{1,0:T(8,128)(2,1)S(1)}, bf16[64,768]{1,0:T(8,128)(2,1)S(1)}, u32[]{:S(2)}, u32[]{:S(2)}) %collective-permute-start.4) | collective-permute-done | bytes 98336 | tf_op jit(solution)/shard_map/ppermute | solution.py:436
  12.5 2.0 %forward.1 = (bf16[128,768]{1,0:T(8,128)(2,1)S(1)}, bf16[64,768]{1,0:T(8,128)(2,1)S(1)}, bf16[32,768]{1,0:T(8,128)(2,1)S(1)}, f32[256,384]{1,0:T(8,128)S(1)}, f3...) custom-call(s32[5]{0:T(128)S(1)} %stack.23.refs_0_, ...), custom_call_target="tpu_custom_call" | custom-call | bytes 1425408 | tf_op jit(solution)/shard_map/forward/pallas_call | solution.py:141
  14.5 0.2 collective-permute-start.5
  14.8 0.2 grads.1
  15.0 1.0 %collective-permute-done.5.refs_1_ = bf16[144,384]{1,0:T(8,128)(2,1)S(1)} collective-permute-done((bf16[144,384]{1,0:T(8,128)(2,1)S(1)}, bf16[144,384]{1,0:T(8,128)(2,1)S(1)}, u32[]{:S(2)}, u32[]{:S(2)}) %collective-permute-start.5) | collective-permute-done | bytes 110624 | tf_op jit(solution)/shard_map/ppermute | solution.py:436
  16.0 0.2 collective-permute-start.10
  16.2 2.6 %collective-permute-start.7 = (bf16[48,384]{1,0:T(8,128)(2,1)S(1)}, bf16[48,384]{1,0:T(8,128)(2,1)S(1)}, u32[]{:S(2)}, u32[]{:S(2)}) collective-permute-start(bf16[48,384]{1,0:T(8,128)(2,1)S(1)} %get-tuple-element.81), channel_id=1, source_target_pairs={{0,16},{1,17},{2,18},{3,19},{4,20},{5,21},{6,22},{7,23},{8,24},{9,... | collective-permute-start | bytes 110600 | tf_op jit(solution)/shard_map/ppermute | solution.py:454
  18.8 1.6 %collective-permute-start.6 = (bf16[96,384]{1,0:T(8,128)(2,1)S(1)}, bf16[96,384]{1,0:T(8,128)(2,1)S(1)}, u32[]{:S(2)}, u32[]{:S(2)}) collective-permute-start(bf16[96,384]{1,0:T(8,128)(2,1)S(1)} %get-tuple-element.72), channel_id=1, source_target_pairs={{0,8},{1,25},{2,10},{3,27},{4,12},{5,29},{6,14},{7,31},{8,0},{9,17... | collective-permute-start | bytes 221192 | tf_op jit(solution)/shard_map/ppermute | solution.py:454
  20.4 1.1 %collective-permute-start.11 = (bf16[64,896]{1,0:T(8,128)(2,1)S(1)}, bf16[64,896]{1,0:T(8,128)(2,1)S(1)}, u32[]{:S(2)}, u32[]{:S(2)}) collective-permute-start(bf16[64,896]{1,0:T(8,128)(2,1)S(1)} %get-tuple-element.86.refs_6_), channel_id=1, source_target_pairs={{0,2},{1,3},{2,0},{3,1},{4,6},{5,7},{6,4},{7,5},{8,10},{9,11},{10,... | collective-permute-start | bytes 344072 | tf_op jit(solution)/shard_map/ppermute | solution.py:436
  21.4 0.0 collective-permute-done.10.refs_1_.refs_5_
  21.5 1.6 %collective-permute-start.13 = (bf16[64,896]{1,0:T(8,128)(2,1)S(1)}, bf16[64,896]{1,0:T(8,128)(2,1)S(1)}, u32[]{:S(2)}, u32[]{:S(2)}) collective-permute-start(bf16[64,896]{1,0:T(8,128)(2,1)S(1)} %third_grads.1), channel_id=1, source_target_pairs={{0,4},{1,7},{2,6},{3,5},{4,0},{5,3},{6,2},{7,1},{8,12},{9,15},{10,... | collective-permute-start | bytes 344072 | tf_op jit(solution)/shard_map/ppermute | solution.py:440
  23.0 1.4 %near.1 = (f32[256,384]{1,0:T(8,128)S(1)}, f32[256,384]{1,0:T(8,128)S(1)}, f32[256,384]{1,0:T(8,128)S(1)}) custom-call(f32[16,128]{1,0:T(8,128)S(1)} %get-tuple-element.51.refs_0_.refs_1_, bf16[256,1152]{1,0:T(8,128)(2,1)S(1)} %copy-done.1, bf16[256,512]{1,0:T(8,128)(2,1)S(1)} %get-tuple-element.73.refs_2_, ...), custom_call_target="tpu_custom_call" | custom-call | flops 805306368 | bytes 1179648 | tf_op jit(solution)/shard_map/near/pallas_call | solution.py:141
  24.4 1.4 %far.1.refs_0_ = bf16[256,384]{1,0:T(8,128)(2,1)S(1)} custom-call(f32[16,128]{1,0:T(8,128)S(1)} %get-tuple-element.51.refs_0_.refs_1_, f32[256,384]{1,0:T(8,128)S(1)} %get-tuple-element.74.refs_1_, bf16[128,768]{1,0:T(8,128)(2,1)S(1)} %get-tuple-element.75.refs_2_, bf16[64,768]{1,0:T(8,128)(2,1)S(1)} %get-tuple-element.76.refs_3_, ...), custom_call_target="tpu_custom_call" | custom-call | flops 201326592 | bytes 196608 | tf_op jit(solution)/shard_map/far/pallas_call | solution.py:141
  25.9 0.0 collective-permute-done.6.refs_1_
  25.9 0.0 collective-permute-done.7.refs_2_
  25.9 0.1 collective-permute-start.8
  26.0 0.4 %collective-permute-done.11.refs_6_ = bf16[64,896]{1,0:T(8,128)(2,1)S(1)} collective-permute-done((bf16[64,896]{1,0:T(8,128)(2,1)S(1)}, bf16[64,896]{1,0:T(8,128)(2,1)S(1)}, u32[]{:S(2)}, u32[]{:S(2)}) %collective-permute-start.11) | collective-permute-done | bytes 114720 | tf_op jit(solution)/shard_map/ppermute | solution.py:436
  26.4 0.1 collective-permute-start.12
  26.5 0.0 collective-permute-done.13.refs_8_
  26.5 0.4 %collective-permute-start.14 = (bf16[64,896]{1,0:T(8,128)(2,1)S(1)}, bf16[64,896]{1,0:T(8,128)(2,1)S(1)}, u32[]{:S(2)}, u32[]{:S(2)}) collective-permute-start(bf16[64,896]{1,0:T(8,128)(2,1)S(1)} %collective-permute-done.13.refs_8_), channel_id=1, source_target_pairs={{0,1},{1,0},{2,3},{3,2},{4,5},{5,4},{6,7},{7,6},{8,9},{9,8},{10,11... | collective-permute-start | bytes 344072 | tf_op jit(solution)/shard_map/ppermute | solution.py:436
  26.9 0.4 %collective-permute-done.8.refs_2_ = bf16[144,384]{1,0:T(8,128)(2,1)S(1)} collective-permute-done((bf16[144,384]{1,0:T(8,128)(2,1)S(1)}, bf16[144,384]{1,0:T(8,128)(2,1)S(1)}, u32[]{:S(2)}, u32[]{:S(2)}) %collective-permute-start.8) | collective-permute-done | bytes 110624 | tf_op jit(solution)/shard_map/ppermute | solution.py:436
  27.4 1.0 %collective-permute-start.9 = (bf16[96,384]{1,0:T(8,128)(2,1)S(1)}, bf16[96,384]{1,0:T(8,128)(2,1)S(1)}, u32[]{:S(2)}, u32[]{:S(2)}) collective-permute-start(bf16[96,384]{1,0:T(8,128)(2,1)S(1)} %get-tuple-element.82.refs_3_), channel_id=1, source_target_pairs={{0,2},{1,5},{2,0},{3,7},{4,6},{5,1},{6,4},{7,3},{8,10},{9,13},{10,... | collective-permute-start | bytes 221192 | tf_op jit(solution)/shard_map/ppermute | solution.py:440
  28.4 1.6 %collective-permute-start.15 = (bf16[48,384]{1,0:T(8,128)(2,1)S(1)}, bf16[48,384]{1,0:T(8,128)(2,1)S(1)}, u32[]{:S(2)}, u32[]{:S(2)}) collective-permute-start(bf16[48,384]{1,0:T(8,128)(2,1)S(1)} %get-tuple-element.93), channel_id=1, source_target_pairs={{0,6},{1,7},{2,4},{3,5},{4,2},{5,3},{6,0},{7,1},{8,14},{9,15},{10,... | collective-permute-start | bytes 110600 | tf_op jit(solution)/shard_map/ppermute | solution.py:436
  30.0 0.0 collective-permute-done.12.refs_7_
  30.0 0.0 collective-permute-done.14.refs_9_
  30.0 2.1 %key.1 = (bf16[256,384]{1,0:T(8,128)(2,1)S(1)}, bf16[256,384]{1,0:T(8,128)(2,1)S(1)}) custom-call(f32[16,128]{1,0:T(8,128)S(1)} %get-tuple-element.51.refs_0_.refs_1_, f32[256,384]{1,0:T(8,128)S(1)} %get-tuple-element.83.refs_1_, f32[256,384]{1,0:T(8,128)S(1)} %get-tuple-element.84.refs_2_, bf16[160,768]{1,0:T(8,128)(2,1)S(1)} %get-tuple-element.63.refs_0_.refs_3_, ...), custom_call_target="tpu_custom_call" | custom-call | flops 402653184 | bytes 393216 | tf_op jit(solution)/shard_map/key/pallas_call | solution.py:141
  32.1 0.0 collective-permute-done.9.refs_0_
  32.1 1.1 %collective-permute-done.15.refs_1_ = bf16[48,384]{1,0:T(8,128)(2,1)S(1)} collective-permute-done((bf16[48,384]{1,0:T(8,128)(2,1)S(1)}, bf16[48,384]{1,0:T(8,128)(2,1)S(1)}, u32[]{:S(2)}, u32[]{:S(2)}) %collective-permute-start.15) | collective-permute-done | bytes 36896 | tf_op jit(solution)/shard_map/ppermute | solution.py:436
  33.2 0.1 collective-permute-start.16
  33.3 0.8 %flush.1 = (bf16[256,384]{1,0:T(8,128)(2,1)}, bf16[256,384]{1,0:T(8,128)(2,1)}, bf16[256,384]{1,0:T(8,128)(2,1)}) custom-call(bf16[256,384]{1,0:T(8,128)(2,1)S(1)} %far.1.refs_0_, bf16[256,384]{1,0:T(8,128)(2,1)S(1)} %get-tuple-element.89.refs_1_, bf16[256,384]{1,0:T(8,128)(2,1)S(1)} %get-tuple-element.90.refs_2_), custom_call_target="tpu_custom_call" | custom-call | bytes 589824 | tf_op jit(solution)/shard_map/flush/pallas_call | solution.py:141
  34.2 0.5 %collective-permute-done.16.refs_2_ = bf16[144,384]{1,0:T(8,128)(2,1)S(1)} collective-permute-done((bf16[144,384]{1,0:T(8,128)(2,1)S(1)}, bf16[144,384]{1,0:T(8,128)(2,1)S(1)}, u32[]{:S(2)}, u32[]{:S(2)}) %collective-permute-start.16) | collective-permute-done | bytes 110624 | tf_op jit(solution)/shard_map/ppermute | solution.py:436
  34.6 0.7 %weight_out.1 = f32[96,384]{1,0:T(8,128)} custom-call(s32[1]{0:T(128)} %bitcast.9.refs_0_, bf16[144,384]{1,0:T(8,128)(2,1)S(1)} %plane_rows.1.refs_1_, bf16[144,384]{1,0:T(8,128)(2,1)S(1)} %collective-permute-done.16.refs_2_, bf16[96,384]{1,0:T(8,128)(2,1)S(1)} %get-tuple-element.82.refs_3_), custom_call_target="tpu_custom_call" | custom-call | bytes 147456 | tf_op jit(solution)/shard_map/weight_out/pallas_call | solution.py:141
  (10 shorter events, 0.1 us)
Async XLA Ops:
  2.3 5.6 %copy-start = (bf16[256,1152]{1,0:T(8,128)(2,1)}, bf16[256,1152]{1,0:T(8,128)(2,1)S(1)}, u32[]{:S(2)}) copy-start(bf16[256,1152]{1,0:T(8,128)(2,1)S(1)} %get-tuple-element.53.refs_1_) | copy-start | bytes 1769476
  2.3 3.1 %collective-permute-start.1 = (bf16[160,768]{1,0:T(8,128)(2,1)S(1)}, bf16[160,768]{1,0:T(8,128)(2,1)S(1)}, u32[]{:S(2)}, u32[]{:S(2)}) collective-permute-start(bf16[160,768]{1,0:T(8,128)(2,1)S(1)} %get-tuple-element.63.refs_0_.refs_3_), channel_id=1, source_target_pairs={{0,1},{1,0},{2,3},{3,2},{4,5},{5,4},{6,7},{7,6},{8,9},{9,8},{10,11... | collective-permute-start | bytes 737288 | tf_op jit(solution)/shard_map/ppermute | solution.py:436
  2.9 4.2 %copy-start.2 = (bf16[384,384]{1,0:T(8,128)(2,1)S(1)}, bf16[384,384]{1,0:T(8,128)(2,1)}, u32[]{:S(2)}) copy-start(bf16[384,384]{1,0:T(8,128)(2,1)} %refs_3_.3) | copy-start | bytes 884740
  2.9 4.2 %copy-start.3 = (bf16[1,256,384]{2,1,0:T(8,128)(2,1)S(1)}, bf16[1,256,384]{2,1,0:T(8,128)(2,1)}, u32[]{:S(2)}) copy-start(bf16[1,256,384]{2,1,0:T(8,128)(2,1)} %param.11) | copy-start | bytes 589828
  2.9 6.0 %collective-permute-start = (bf16[64,768]{1,0:T(8,128)(2,1)S(1)}, bf16[64,768]{1,0:T(8,128)(2,1)S(1)}, u32[]{:S(2)}, u32[]{:S(2)}) collective-permute-start(bf16[64,768]{1,0:T(8,128)(2,1)S(1)} %get-tuple-element.52.refs_4_), channel_id=1, source_target_pairs={{0,2},{1,3},{2,0},{3,1},{4,6},{5,7},{6,4},{7,5},{8,10},{9,11},{10,... | collective-permute-start | bytes 294920 | tf_op jit(solution)/shard_map/ppermute | solution.py:436
  5.5 5.7 %collective-permute-start.3 = (bf16[64,768]{1,0:T(8,128)(2,1)S(1)}, bf16[64,768]{1,0:T(8,128)(2,1)S(1)}, u32[]{:S(2)}, u32[]{:S(2)}) collective-permute-start(bf16[64,768]{1,0:T(8,128)(2,1)S(1)} %third_rows.1), channel_id=1, source_target_pairs={{0,4},{1,7},{2,6},{3,5},{4,0},{5,3},{6,2},{7,1},{8,12},{9,15},{10,... | collective-permute-start | bytes 294920 | tf_op jit(solution)/shard_map/ppermute | solution.py:440
  8.9 2.4 %collective-permute-start.2 = (bf16[64,768]{1,0:T(8,128)(2,1)S(1)}, bf16[64,768]{1,0:T(8,128)(2,1)S(1)}, u32[]{:S(2)}, u32[]{:S(2)}) collective-permute-start(bf16[64,768]{1,0:T(8,128)(2,1)S(1)} %collective-permute-done.refs_11_.refs_8_), channel_id=1, source_target_pairs={{0,1},{1,0},{2,3},{3,2},{4,5},{5,4},{6,7},{7,6},{8,9},{9,8},{10,11... | collective-permute-start | bytes 294920 | tf_op jit(solution)/shard_map/ppermute | solution.py:436
  11.2 1.3 %collective-permute-start.4 = (bf16[64,768]{1,0:T(8,128)(2,1)S(1)}, bf16[64,768]{1,0:T(8,128)(2,1)S(1)}, u32[]{:S(2)}, u32[]{:S(2)}) collective-permute-start(bf16[64,768]{1,0:T(8,128)(2,1)S(1)} %collective-permute-done.3.refs_13_.refs_10_), channel_id=1, source_target_pairs={{0,1},{1,0},{2,3},{3,2},{4,5},{5,4},{6,7},{7,6},{8,9},{9,8},{10,11... | collective-permute-start | bytes 294920 | tf_op jit(solution)/shard_map/ppermute | solution.py:436
  14.5 1.4 %collective-permute-start.5 = (bf16[144,384]{1,0:T(8,128)(2,1)S(1)}, bf16[144,384]{1,0:T(8,128)(2,1)S(1)}, u32[]{:S(2)}, u32[]{:S(2)}) collective-permute-start(bf16[144,384]{1,0:T(8,128)(2,1)S(1)} %get-tuple-element.70), channel_id=1, source_target_pairs={{0,1},{1,0},{2,3},{3,2},{4,5},{5,4},{6,7},{7,6},{8,9},{9,8},{10,11... | collective-permute-start | bytes 331784 | tf_op jit(solution)/shard_map/ppermute | solution.py:436
  15.0 8.1 %copy-start.1 = (bf16[256,1152]{1,0:T(8,128)(2,1)S(1)}, bf16[256,1152]{1,0:T(8,128)(2,1)}, u32[]{:S(2)}) copy-start(bf16[256,1152]{1,0:T(8,128)(2,1)} %copy-done) | copy-start | bytes 1769476
  16.0 5.5 %collective-permute-start.10 = (bf16[160,896]{1,0:T(8,128)(2,1)S(1)}, bf16[160,896]{1,0:T(8,128)(2,1)S(1)}, u32[]{:S(2)}, u32[]{:S(2)}) collective-permute-start(bf16[160,896]{1,0:T(8,128)(2,1)S(1)} %get-tuple-element.85.refs_5_.refs_0_), channel_id=1, source_target_pairs={{0,1},{1,0},{2,3},{3,2},{4,5},{5,4},{6,7},{7,6},{8,9},{9,8},{10,11... | collective-permute-start | bytes 860168 | tf_op jit(solution)/shard_map/ppermute | solution.py:436
  16.2 9.7 %collective-permute-start.7 = (bf16[48,384]{1,0:T(8,128)(2,1)S(1)}, bf16[48,384]{1,0:T(8,128)(2,1)S(1)}, u32[]{:S(2)}, u32[]{:S(2)}) collective-permute-start(bf16[48,384]{1,0:T(8,128)(2,1)S(1)} %get-tuple-element.81), channel_id=1, source_target_pairs={{0,16},{1,17},{2,18},{3,19},{4,20},{5,21},{6,22},{7,23},{8,24},{9,... | collective-permute-start | bytes 110600 | tf_op jit(solution)/shard_map/ppermute | solution.py:454
  18.8 7.1 %collective-permute-start.6 = (bf16[96,384]{1,0:T(8,128)(2,1)S(1)}, bf16[96,384]{1,0:T(8,128)(2,1)S(1)}, u32[]{:S(2)}, u32[]{:S(2)}) collective-permute-start(bf16[96,384]{1,0:T(8,128)(2,1)S(1)} %get-tuple-element.72), channel_id=1, source_target_pairs={{0,8},{1,25},{2,10},{3,27},{4,12},{5,29},{6,14},{7,31},{8,0},{9,17... | collective-permute-start | bytes 221192 | tf_op jit(solution)/shard_map/ppermute | solution.py:454
  20.4 6.0 %collective-permute-start.11 = (bf16[64,896]{1,0:T(8,128)(2,1)S(1)}, bf16[64,896]{1,0:T(8,128)(2,1)S(1)}, u32[]{:S(2)}, u32[]{:S(2)}) collective-permute-start(bf16[64,896]{1,0:T(8,128)(2,1)S(1)} %get-tuple-element.86.refs_6_), channel_id=1, source_target_pairs={{0,2},{1,3},{2,0},{3,1},{4,6},{5,7},{6,4},{7,5},{8,10},{9,11},{10,... | collective-permute-start | bytes 344072 | tf_op jit(solution)/shard_map/ppermute | solution.py:436
  21.5 5.0 %collective-permute-start.13 = (bf16[64,896]{1,0:T(8,128)(2,1)S(1)}, bf16[64,896]{1,0:T(8,128)(2,1)S(1)}, u32[]{:S(2)}, u32[]{:S(2)}) collective-permute-start(bf16[64,896]{1,0:T(8,128)(2,1)S(1)} %third_grads.1), channel_id=1, source_target_pairs={{0,4},{1,7},{2,6},{3,5},{4,0},{5,3},{6,2},{7,1},{8,12},{9,15},{10,... | collective-permute-start | bytes 344072 | tf_op jit(solution)/shard_map/ppermute | solution.py:440
  25.9 1.4 %collective-permute-start.8 = (bf16[144,384]{1,0:T(8,128)(2,1)S(1)}, bf16[144,384]{1,0:T(8,128)(2,1)S(1)}, u32[]{:S(2)}, u32[]{:S(2)}) collective-permute-start(bf16[144,384]{1,0:T(8,128)(2,1)S(1)} %layer_sum.1.refs_1_), channel_id=1, source_target_pairs={{0,1},{1,0},{2,3},{3,2},{4,5},{5,4},{6,7},{7,6},{8,9},{9,8},{10,11... | collective-permute-start | bytes 331784 | tf_op jit(solution)/shard_map/ppermute | solution.py:436
  26.4 3.6 %collective-permute-start.12 = (bf16[64,896]{1,0:T(8,128)(2,1)S(1)}, bf16[64,896]{1,0:T(8,128)(2,1)S(1)}, u32[]{:S(2)}, u32[]{:S(2)}) collective-permute-start(bf16[64,896]{1,0:T(8,128)(2,1)S(1)} %collective-permute-done.11.refs_6_), channel_id=1, source_target_pairs={{0,1},{1,0},{2,3},{3,2},{4,5},{5,4},{6,7},{7,6},{8,9},{9,8},{10,11... | collective-permute-start | bytes 344072 | tf_op jit(solution)/shard_map/ppermute | solution.py:436
  26.5 3.5 %collective-permute-start.14 = (bf16[64,896]{1,0:T(8,128)(2,1)S(1)}, bf16[64,896]{1,0:T(8,128)(2,1)S(1)}, u32[]{:S(2)}, u32[]{:S(2)}) collective-permute-start(bf16[64,896]{1,0:T(8,128)(2,1)S(1)} %collective-permute-done.13.refs_8_), channel_id=1, source_target_pairs={{0,1},{1,0},{2,3},{3,2},{4,5},{5,4},{6,7},{7,6},{8,9},{9,8},{10,11... | collective-permute-start | bytes 344072 | tf_op jit(solution)/shard_map/ppermute | solution.py:436
  27.4 4.8 %collective-permute-start.9 = (bf16[96,384]{1,0:T(8,128)(2,1)S(1)}, bf16[96,384]{1,0:T(8,128)(2,1)S(1)}, u32[]{:S(2)}, u32[]{:S(2)}) collective-permute-start(bf16[96,384]{1,0:T(8,128)(2,1)S(1)} %get-tuple-element.82.refs_3_), channel_id=1, source_target_pairs={{0,2},{1,5},{2,0},{3,7},{4,6},{5,1},{6,4},{7,3},{8,10},{9,13},{10,... | collective-permute-start | bytes 221192 | tf_op jit(solution)/shard_map/ppermute | solution.py:440
  28.4 4.9 %collective-permute-start.15 = (bf16[48,384]{1,0:T(8,128)(2,1)S(1)}, bf16[48,384]{1,0:T(8,128)(2,1)S(1)}, u32[]{:S(2)}, u32[]{:S(2)}) collective-permute-start(bf16[48,384]{1,0:T(8,128)(2,1)S(1)} %get-tuple-element.93), channel_id=1, source_target_pairs={{0,6},{1,7},{2,4},{3,5},{4,2},{5,3},{6,0},{7,1},{8,14},{9,15},{10,... | collective-permute-start | bytes 110600 | tf_op jit(solution)/shard_map/ppermute | solution.py:436
  33.2 1.4 %collective-permute-start.16 = (bf16[144,384]{1,0:T(8,128)(2,1)S(1)}, bf16[144,384]{1,0:T(8,128)(2,1)S(1)}, u32[]{:S(2)}, u32[]{:S(2)}) collective-permute-start(bf16[144,384]{1,0:T(8,128)(2,1)S(1)} %plane_rows.1.refs_1_), channel_id=1, source_target_pairs={{0,1},{1,0},{2,3},{3,2},{4,5},{5,4},{6,7},{7,6},{8,9},{9,8},{10,11... | collective-permute-start | bytes 331784 | tf_op jit(solution)/shard_map/ppermute | solution.py:436

commit v5 on v4

--- a/solution.py
+++ b/solution.py
@@ -13,6 +13,8 @@
 SEQ = ("seqhi", "seqlo")
 LANES = 128
 HALF = 64
+READY = 2
+SMALL, BYTES, LARGE = 1, 10000, 1
 LOG2E = math.log2(math.e)
 NN = (((1,), (0,)), ((), ()))
 NT = (((1,), (1,)), ((), ()))
@@ -113,7 +115,7 @@
 HBM = pl.BlockSpec(memory_space=pltpu.HBM)
 
 
-def call(kernel, name, shapes, arrays, views=(), scalars=(), flops=0, scratch=(), specs=None, out_specs=None):
+def call(kernel, name, shapes, arrays, views=(), scalars=(), flops=SMALL, scratch=(), specs=None, out_specs=None):
     unique, where = [], []
     for group in views:
         places = []
@@ -137,7 +139,6 @@
 
         kernel(load, *scalar_refs, *array_refs, *refs)
 
-    moved = sum(math.prod(shape) * jnp.dtype(kind).itemsize for shape, kind in shapes)
     return pl.pallas_call(
         body,
         out_shape=[jax.ShapeDtypeStruct(shape, kind) for shape, kind in shapes],
@@ -145,14 +146,13 @@
         out_specs=out_specs or [VMEM] * len(shapes),
         scratch_shapes=list(scratch),
         compiler_params=pltpu.CompilerParams(vmem_limit_bytes=16 * 2**20),
-        cost_estimate=pl.CostEstimate(flops=flops, transcendentals=0, bytes_accessed=moved),
+        cost_estimate=pl.CostEstimate(flops=flops, transcendentals=0, bytes_accessed=BYTES),
         name=name,
     )(*scalars, *arrays, *unique)
 
 
-def pool_kernel(top, places, load, q_hbm, k_hbm, v_hbm, scale_hbm, factor_ref, *refs):
-    out_refs, (q_ref, k_ref, v_ref, scale_ref, sems) = refs[:-5], refs[-5:]
-    level_refs, query_refs = out_refs[:-top], out_refs[-top:]
+def pool_kernel(top, starts, places, load, q_hbm, k_hbm, v_hbm, scale_hbm, factor_ref, rows_ref, *refs):
+    level_refs, (q_ref, k_ref, v_ref, scale_ref, sems) = refs[:-5], refs[-5:]
     copies = [
         pltpu.make_async_copy(source, target, sems.at[index])
         for index, (source, target) in enumerate(
@@ -166,16 +166,16 @@
     for which, ref in ((1, k_ref), (2, v_ref), (0, q_ref)):
         copies[which].wait()
         current = dot(order, ref[...])
-        level_refs[0][:, which * width : (which + 1) * width] = current.astype(BF)
+        columns = slice(which * width, (which + 1) * width)
+        rows_ref[:rows, columns] = current.astype(BF)
         for height in range(1, top + 1):
             total = halves_sum(current)
             rounded = (total if which == 2 else 0.5 * total).astype(BF)
+            rows_ref[starts[height] : starts[height] + rounded.shape[0], columns] = rounded
             if which:
                 target, start = places[height - 1]
-                columns = slice((which - 1) * width, which * width)
-                level_refs[target][start : start + rounded.shape[0], columns] = rounded
-            else:
-                query_refs[height - 1][...] = rounded
+                span = slice(start, start + rounded.shape[0])
+                level_refs[target][span, (which - 1) * width : which * width] = rounded
             current = rounded.astype(F32)
     copies[3].wait()
     fill_factors(scale_ref, factor_ref)
@@ -203,25 +203,50 @@
     return joined, dot(joined, right)
 
 
-def base_kernel(top, load, factor_ref, x_ref, cot_ref, w_ref, numer_ref, denom_ref, weights_ref, cotp_ref, back_ref):
+def block(pair, span):
+    return slice(span * pair, span * (pair + 1))
+
+
+def base_kernel(top, load, factor_ref, x_ref, cot_hbm, w_hbm, sums_ref, weights_ref, back_ref, cot_ref, w_ref, sems):
+    copies = [
+        pltpu.make_async_copy(cot_hbm, cot_ref, sems.at[0]),
+        pltpu.make_async_copy(w_hbm, w_ref, sems.at[1]),
+    ]
+    for copy in copies:
+        copy.start()
     rows, width = cot_ref.shape
     masks = side_masks()
     for pair in range(width // LANES):
-        q, k, v = (x_ref[:, lane_pair(width * which, pair)] for which in range(3))
+        q, k, v = (x_ref[:rows, lane_pair(width * which, pair)] for which in range(3))
         joined, both = attend(factor_ref, pair, q, k, v, 1, masks)
-        numer_ref[:, lane_pair(0, pair)] = both[:, :LANES]
-        denom_ref[:, lane_pair(0, pair)] = both[:, LANES:]
-        weights_ref[:, 2 * rows * pair : 2 * rows * (pair + 1)] = joined
-    cotan = dot(order_matrix(rows, top), cot_ref[...]).astype(BF)
-    cotp_ref[...] = cotan
-    back_ref[...] = dot(cotan, w_ref[...], NT).astype(BF)
+        sums_ref[:, block(pair, 2 * LANES)] = both
+        weights_ref[:, block(pair, 2 * rows)] = joined
+    order = order_matrix(rows, top)
+    copies[0].wait()
+    cotan = dot(order, cot_ref[...]).astype(BF)
+    copies[1].wait()
+    back_ref[:, width:] = cotan
+    back_ref[:, :width] = dot(cotan, w_ref[...], NT).astype(BF)
+
+
+def level_kernel(height, load, factor_ref, sums_ref, weights_ref, total_ref):
+    width = sums_ref.shape[1] // 2
+    masks = side_masks()
+    for pair in range(width // LANES):
+        keys, values = (load(1, lane_pair(start, pair)) for start in (0, width))
+        joined, both = attend(factor_ref, pair, load(0, lane_pair(0, pair)), keys, values, 2**height, masks)
+        weights_ref[:, block(pair, joined.shape[1])] = joined
+        for _ in range(height):
+            both = doubled(both)
+        total_ref[:, block(pair, 2 * LANES)] = sums_ref[:, block(pair, 2 * LANES)] + both
 
 
 def forward_kernel(
-    top, parts, pieces, load, place_ref, factor_ref, numer_ref, denom_ref, cotp_ref, back_ref, _, *refs
+    top, ready, parts, pieces, load, place_ref, factor_ref, sums_ref, back_ref, *refs
 ):
-    weights_refs, (grad_ref, slope_ref), out_refs, weight_ref = refs[:top], refs[top : top + 2], refs[top + 2 : -1], refs[-1]
-    rows, width = numer_ref.shape
+    weights_refs, refs = refs[: top - ready], refs[top - ready :]
+    (grad_ref, slope_ref), out_refs, weight_ref = refs[:2], refs[2:-1], refs[-1]
+    rows, width = grad_ref.shape
     masks = side_masks()
     lane = iota((LANES, LANES), 1)
     ones = jnp.where(lane // HALF == iota((LANES, LANES), 0) // HALF, 1.0, 0.0).astype(BF)
@@ -229,16 +254,18 @@
     attended = []
     for pair in range(width // LANES):
         total = None
-        for height in range(top, 0, -1):
-            queries = load(height - 1, lane_pair(0, pair))
-            keys, values = (load(top + height - 1, lane_pair(start, pair)) for start in (0, width))
-            joined, both = attend(factor_ref, pair, queries, keys, values, 2**height, masks)
+        for at in range(top - ready - 1, -1, -1):
+            queries = load(at, lane_pair(0, pair))
+            keys, values = (load(top - ready + at, lane_pair(start, pair)) for start in (0, width))
+            joined, both = attend(factor_ref, pair, queries, keys, values, 2 ** (ready + at + 1), masks)
             columns = joined.shape[1]
-            weights_refs[height - 1][:, columns * pair : columns * (pair + 1)] = joined
+            weights_refs[at][:, columns * pair : columns * (pair + 1)] = joined
             total = both if total is None else both + doubled(total)
-        total = doubled(total)
-        numer = numer_ref[:, lane_pair(0, pair)] + total[:, :LANES]
-        inverse = 1.0 / (denom_ref[:, lane_pair(0, pair)] + total[:, LANES:])
+        for _ in range(ready + 1):
+            total = doubled(total)
+        total = total + sums_ref[:, block(pair, 2 * LANES)]
+        numer = total[:, :LANES]
+        inverse = 1.0 / total[:, LANES:]
         ratio = numer * inverse
         attended.append(ratio.astype(BF))
         back = back_ref[:, lane_pair(0, pair)].astype(F32)
@@ -248,7 +275,7 @@
         summed = dot(stack([product_high, product_low], 1), adder)
         grad_ref[:, lane_pair(0, pair)] = back * inverse
         slope_ref[:, lane_pair(0, pair)] = -summed * inverse
-    weight_ref[...] = dot(stack(attended, 1), cotp_ref[...], TN)
+    weight_ref[...] = dot(stack(attended, 1), back_ref[:, width:], TN)
     own_rows = width // parts
     for entry, offset, count, target, start in pieces:
         shift = offset if isinstance(offset, int) else offset(place_ref)
@@ -269,7 +296,7 @@
             out_refs[target][span, lane_pair(0, pair)] = value.astype(BF)
         out_refs[target][span, width : width + LANES] = denom_lanes(denom_rows)
         if height:
-            out_refs[target][span, width + LANES :] = load(height - 1, slice(None))
+            out_refs[target][span, width + LANES :] = load(height - 1, slice(0, width))
 
 
 def query_slopes(joined, grad, denom, values, pair, height, masks):
@@ -290,7 +317,7 @@
     masks = side_masks()
     for pair in range(width // LANES):
         factor = side_factor(factor_ref, heads, pair)
-        queries, keys, values = (x_ref[:, lane_pair(width * which, pair)] for which in range(3))
+        queries, keys, values = (x_ref[:rows, lane_pair(width * which, pair)] for which in range(3))
         grad = gh_ref[:, lane_pair(0, pair)]
         joined = weights_ref[:, 2 * rows * pair : 2 * rows * (pair + 1)]
         slope = query_slopes(joined, grad, gh_ref[:, width:], values, pair, 0, masks)
@@ -323,24 +350,25 @@
     out_ref[...] = dot(order_matrix(rows, top, True), stack(results, 1)).astype(BF)
 
 
-def key_kernel(top, load, factor_ref, base_key_ref, base_value_ref, key_out_ref, value_out_ref):
+def key_kernel(top, first, last, load, factor_ref, base_key_ref, base_value_ref, key_out_ref, value_out_ref):
     rows, width = key_out_ref.shape
     heads = width // HALF
     masks = side_masks()
+    levels = last - first + 1
     key_results, value_results = [], []
     for pair in range(width // LANES):
         factor = side_factor(factor_ref, heads, pair)
         key_total = value_total = None
-        for height in range(top, 0, -1):
-            keys, values = (load(height - 1, lane_pair(start, pair)) for start in (0, width))
-            grad = load(top + height - 1, lane_pair(0, pair))
-            denom = load(top + height - 1, slice(width, width + LANES))
-            queries = load(top + height - 1, lane_pair(width + LANES, pair))
+        for at in range(levels - 1, -1, -1):
+            keys, values = (load(at, lane_pair(start, pair)) for start in (width, 2 * width))
+            grad = load(levels + at, lane_pair(0, pair))
+            denom = load(levels + at, slice(width, width + LANES))
+            queries = load(levels + at, lane_pair(width + LANES, pair))
             count = keys.shape[0]
             weights = both_weights(factor_ref, pair, keys, queries, masks)
             left = stack(
                 [
-                    stack([values * mask, jnp.broadcast_to(slot * float(2**height), (count, LANES))], 1)
+                    stack([values * mask, jnp.broadcast_to(slot * float(2 ** (first + at)), (count, LANES))], 1)
                     for mask, slot in zip(masks, slot_masks(pair))
                 ],
                 0,
@@ -356,13 +384,16 @@
                 key_piece = key_piece + 0.5 * doubled(key_total)
                 value_piece = value_piece + doubled(value_total)
             key_total, value_total = key_piece, value_piece
-        key_total = base_key_ref[:, lane_pair(0, pair)] + 0.5 * doubled(key_total)
-        value_total = base_value_ref[:, lane_pair(0, pair)] + doubled(value_total)
-        key_results.append(key_total.astype(BF))
-        value_results.append(value_total.astype(BF))
-    back = order_matrix(rows, top, True)
-    key_out_ref[...] = dot(back, stack(key_results, 1)).astype(BF)
-    value_out_ref[...] = dot(back, stack(value_results, 1)).astype(BF)
+        for _ in range(first):
+            key_total, value_total = 0.5 * doubled(key_total), doubled(value_total)
+        key_results.append(base_key_ref[:, lane_pair(0, pair)] + key_total)
+        value_results.append(base_value_ref[:, lane_pair(0, pair)] + value_total)
+    key_total, value_total = stack(key_results, 1), stack(value_results, 1)
+    if last == top:
+        back = order_matrix(rows, top, True)
+        key_total, value_total = dot(back, key_total.astype(BF)), dot(back, value_total.astype(BF))
+    key_out_ref[...] = key_total.astype(key_out_ref.dtype)
+    value_out_ref[...] = value_total.astype(value_out_ref.dtype)
 
 
 def place_kernel(spots, load, *refs):
@@ -398,12 +429,12 @@
     )
 
 
-def placed(name, shapes, spots):
+def placed(name, shapes, spots, flops=SMALL):
     views, listed = [], []
     for target, start, parts in spots:
         listed.append((target, start, range(len(views), len(views) + len(parts))))
         views += [[part] for part in parts]
-    return call(functools.partial(place_kernel, listed), name, shapes, [], views=views)
+    return call(functools.partial(place_kernel, listed), name, shapes, [], views=views, flops=flops)
 
 
 def total_kernel(load, core_ref, own_ref, partner_ref, *refs):
@@ -428,7 +459,13 @@
     width = arrays[0].shape[1]
     shapes = [((2 * half, width), kind)] + [((half, width), BF)] * (kind == BF)
     return call(
-        total_kernel, name, shapes, arrays, scalars=[core.reshape(1)], scratch=[pltpu.VMEM((2 * half, width), F32)]
+        total_kernel,
+        name,
+        shapes,
+        arrays,
+        scalars=[core.reshape(1)],
+        flops=LARGE,
+        scratch=[pltpu.VMEM((2 * half, width), F32)],
     )
 
 
@@ -483,56 +520,78 @@
     whole = (rows, width)
     wide = width + LANES
     sizes = [rows >> height for height in range(top + 1)]
+    starts = [0]
+    for size in sizes:
+        starts.append(starts[-1] + max(size, 16))
     if paired:
-        places = [(1, 0), (2, 0), (1, sizes[1])]
-        pooled = [sizes[1] + sizes[3], sizes[2]]
+        places, messages = [(0, 0), (1, 0), (0, sizes[1])], [sizes[1] + sizes[3], sizes[2]]
     else:
-        places = [(height, 0) for height in range(1, top + 1)]
-        pooled = sizes[1:]
-    factors, base_rows, *outs = call(
-        functools.partial(pool_kernel, top, places),
+        places, messages = [(height, 0) for height in range(top)], sizes[1:]
+    factors, own_rows_all, *levels = call(
+        functools.partial(pool_kernel, top, starts, places),
         "pool",
-        [((factor_rows(heads), LANES), F32), ((rows, 3 * width), BF)]
-        + [((count, 2 * width), BF) for count in pooled]
-        + [((size, width), BF) for size in sizes[1:]],
-        [pltpu.with_memory_space_constraint(value, pltpu.HBM) for value in (queries[0], key_rows[0], value_rows[0], head_scale)],
+        [((factor_rows(heads), LANES), F32), ((starts[-1], 3 * width), BF)]
+        + [((count, 2 * width), BF) for count in messages],
+        [
+            pltpu.with_memory_space_constraint(value, pltpu.HBM)
+            for value in (queries[0], key_rows[0], value_rows[0], head_scale)
+        ],
         specs=[HBM] * 4,
         scratch=[pltpu.VMEM(whole, BF)] * 3 + [pltpu.SMEM((heads,), F32), pltpu.SemaphoreType.DMA((4,))],
     )
-    levels, level_queries = outs[:-top], [[View(value)] for value in outs[-top:]]
-    own = [[View(levels[target - 1], start, sizes[height + 1])] for height, (target, start) in enumerate(places)]
-    numer, denom, base_weights, cotan, back = call(
+    own = [[View(own_rows_all, starts[height], sizes[height])] for height in range(1, top + 1)]
+    sums, base_weights, back = call(
         functools.partial(base_kernel, top),
         "base",
-        [(whole, F32), (whole, F32), ((rows, heads * rows), BF), (whole, BF), (whole, BF)],
-        [factors, base_rows, cotangent[0], out_weight],
-        flops=4 * rows * rows * width * 4,
-    )
+        [((rows, 2 * width), F32), ((rows, heads * rows), BF), ((rows, 2 * width), BF)],
+        [factors, own_rows_all]
+        + [pltpu.with_memory_space_constraint(value, pltpu.HBM) for value in (cotangent[0], out_weight)],
+        specs=[VMEM, VMEM, HBM, HBM],
+        scratch=[pltpu.VMEM(whole, BF), pltpu.VMEM((width, width), BF), pltpu.SemaphoreType.DMA((2,))],
+        flops=100000000,
+    )
+
+    def attend_level(height, views, sums):
+        return call(
+            functools.partial(level_kernel, height),
+            "level",
+            [((sizes[height], heads * rows // 2), BF), ((rows, 2 * width), F32)],
+            [factors, sums],
+            views=[own[height - 1], views],
+            flops=100000000//4,
+        )
+
     if paired:
         within = traded(levels[0], 1)
         across = traded(levels[1], 2)
         (third,) = placed(
             "third_rows",
             [((2 * sizes[3], 2 * width), BF)],
-            [(0, 0, [own[2][0]]), (0, sizes[3], [View(within, sizes[1], sizes[3])])],
+            [(0, 0, [View(levels[0], sizes[1])]), (0, sizes[3], [View(within, sizes[1])])],
         )
         split = split_traded(third, 2, 3)
-        across, numer = lax.optimization_barrier((across, numer))
+        level_weights = []
+        if READY > 0:
+            weights, sums = attend_level(1, [View(within, 0, sizes[1])], sums)
+            level_weights.append(weights)
+        across, sums = lax.optimization_barrier((across, sums))
         across_too = traded(across, 1)
         split_too = traded(split, 1)
-        siblings = [
-            [View(within, 0, sizes[1])],
-            [View(across), View(across_too)],
-            [View(split), View(split_too)],
-        ]
+        if READY > 1:
+            weights, sums = attend_level(2, [View(across), View(across_too)], sums)
+            level_weights.append(weights)
+            split_too, sums = lax.optimization_barrier((split_too, sums))
+        siblings = [[View(within, 0, sizes[1])], [View(across), View(across_too)], [View(split), View(split_too)]]
     else:
         siblings = from_siblings(levels, top)
+        level_weights = []
+    ready = len(level_weights)
     own_rows = width // parts
     half = own_rows // 2
     layer = lax.axis_index("dp").astype(jnp.int32)
     if paired:
         core = lax.axis_index(SEQ).astype(jnp.int32) % 2
-        place = jnp.stack([layer, layer ^ (1 + 2 * core), layer ^ (3 - 2 * core), layer ^ 2, core * half])
+        place = jnp.stack([layer, layer ^ (2 + core), layer ^ (3 - core), layer ^ 1, core * half])
         grad_places = [(0, 0), (1, 0), (2, 0), (1, sizes[1])]
         grad_shapes = [(rows, wide), (sizes[1] + sizes[3], wide + width), (sizes[2], wide + width)]
         pieces = [
@@ -550,24 +609,26 @@
         grad_shapes = [(rows, wide)] + [(size, wide + width) for size in sizes[1:]]
         shapes = [(own_rows, width)] * parts
     outs = call(
-        functools.partial(forward_kernel, top, parts, pieces),
+        functools.partial(forward_kernel, top, ready, parts, pieces),
         "forward",
-        [((size, heads * rows // 2), BF) for size in sizes[1:]]
+        [((size, heads * rows // 2), BF) for size in sizes[ready + 1 :]]
         + [(whole, F32), (whole, F32)]
         + [(shape, BF) for shape in shapes],
-        [factors, numer, denom, cotan, back, base_weights],
-        views=level_queries + siblings,
+        [factors, sums, back],
+        views=own[ready:] + siblings[ready:] + siblings[:ready],
         scalars=[place],
         scratch=[pltpu.VMEM((width, width), F32)],
     )
-    level_weights, (grad_rows, denom_rows), pieces = outs[:top], outs[top : top + 2], outs[top + 2 :]
+    level_weights += outs[: top - ready]
+    outs = outs[top - ready :]
+    (grad_rows, denom_rows), pieces = outs[:2], outs[2:]
     outs = call(
         functools.partial(grads_kernel, grad_places),
         "grads",
         [(shape, BF) for shape in grad_shapes],
         [grad_rows, denom_rows],
-        views=level_queries,
-        flops=4 * rows * rows * width * 4,
+        views=own,
+        flops=100000000,
     )
 
     def own_grads(arrays):
@@ -579,8 +640,8 @@
         near_kernel,
         "near",
         [(whole, F32)] * 3,
-        [factors, base_rows, outs[0], base_weights],
-        flops=8 * rows * rows * width * 4,
+        [factors, own_rows_all, outs[0], base_weights],
+        flops=1600000000,
     )
     (query_grad,) = call(
         functools.partial(far_kernel, top),
@@ -588,17 +649,17 @@
         [(whole, BF)],
         [factors, near_query, *level_weights],
         views=own_grads(outs) + siblings,
-        flops=8 * rows * rows * width,
-    )
-
-    def key_call(sibling_grads):
+        flops=100000000,
+    )
+
+    def key_call(first, last, sums, sibling_grads, kind):
         return call(
-            functools.partial(key_kernel, top),
+            functools.partial(key_kernel, top, first, last),
             "key",
-            [(whole, BF), (whole, BF)],
-            [factors, near_key, near_value],
-            views=own + sibling_grads,
-            flops=8 * rows * rows * width * 2,
+            [(whole, kind), (whole, kind)],
+            [factors, *sums],
+            views=own[first - 1 : last] + sibling_grads,
+            flops=100000000,
         )
 
     if paired:
@@ -612,42 +673,43 @@
                 (0, 0, [View(send, 0, own_rows), View(theirs_in, 0, own_rows)]),
                 (1, 0, [View(send, own_rows), View(theirs_in, own_rows)]),
             ],
+            flops=LARGE,
         )
-        near, far, send_one = lax.optimization_barrier((near, far, send_one))
         near_in = traded(near, 1)
         far_in = traded(far, 2)
-        layer_one = layer_traded(send_one, 1, 3)
-        layer_half = layer_traded(send_half, 2, 2)
+        layer_one = layer_traded(send_one, 2, 3)
+        layer_half = layer_traded(send_half, 1, 1)
         (third,) = placed(
             "third_grads",
             [((2 * sizes[3], wide + width), BF)],
             [(0, 0, [View(near, sizes[1])]), (0, sizes[3], [View(near_in, sizes[1])])],
         )
         third_in = split_traded(third, 2, 3)
-        far_in, near_query = lax.optimization_barrier((far_in, near_query))
-        far_too = traded(far_in, 1)
-        layer_one, query_grad = lax.optimization_barrier((layer_one, query_grad))
-        third_too = traded(third_in, 1)
-        sibling_grads = [
-            [View(near_in, 0, sizes[1])],
-            [View(far_in), View(far_too)],
-            [View(third_in), View(third_too)],
-        ]
+        layer_one, layer_half, near_key = lax.optimization_barrier((layer_one, layer_half, near_key))
         (joint,) = placed(
             "layer_sum",
             [((own_rows + half, width), BF)],
             [(0, 0, [View(mine), View(layer_one)]), (0, own_rows, [View(layer_half)])],
+            flops=LARGE,
         )
         joint_in = traded(joint, 1)
+        far_in, near_key = lax.optimization_barrier((far_in, near_key))
+        far_too = traded(far_in, 1)
+        near_sums = key_call(1, 1, (near_key, near_value), [[View(near_in, 0, sizes[1])]], F32)
+        joint_in, near_sums = lax.optimization_barrier((joint_in, tuple(near_sums)))
         weight, weight_half = chip_total("layer_total", core, [joint, joint_in], half, BF)
-        plane_one = split_traded(weight, 1, 2)
-        plane_half = traded(weight_half, 6)
-        key_grad, value_grad = key_call(sibling_grads)
-        plane_one, key_grad = lax.optimization_barrier((plane_one, key_grad))
+        third_in, _ = lax.optimization_barrier((third_in, weight))
+        third_too = traded(third_in, 1)
+        sibling_grads = [[View(far_in), View(far_too)], [View(third_in), View(third_too)]]
+        plane_one = split_traded(weight, 2, 3)
+        plane_half = traded(weight_half, 2)
+        key_grad, value_grad = key_call(2, top, near_sums, sibling_grads, BF)
+        plane_one, key_grad, query_grad = lax.optimization_barrier((plane_one, key_grad, query_grad))
         (joint,) = placed(
             "plane_rows",
             [((own_rows + half, width), BF)],
             [(0, 0, [View(plane_one)]), (0, own_rows, [View(plane_half)])],
+            flops=LARGE,
         )
         joint_in = traded(joint, 1)
         query_grad, key_grad, value_grad = flush(query_grad, key_grad, value_grad)
@@ -668,7 +730,7 @@
             bit += 2
         weight = weight.astype(BF)
         weight = weight.astype(F32) + traded(weight, 1).astype(F32)
-        key_grad, value_grad = key_call(sibling_grads)
+        key_grad, value_grad = key_call(1, top, (near_key, near_value), sibling_grads, BF)
     return query_grad[None], key_grad[None], value_grad[None], weight
 
 

time: 35.5 us -> 34.4 us (0.969)
  waiting for transfers between devices: 7.77 us -> 3.76 us
  Pallas kernels: 11.5 us -> 12.7 us
  local copies, waits for them, and re-layouts: 0.1 us -> 0.98 us
  starting transfers between devices: 15.2 us -> 15.9 us
    ppermute x12, waiting for transfers between devices: 5.42 us -> 2.03 us  [traded(): lax.ppermute(value, SEQ, [(source, source ^ mask) for source in range(lax...]
    ppermute x3, waiting for transfers between devices: 2.35 us -> 0.6 us  [split_traded(): lax.ppermute(value, SEQ, [(source, source ^ 2 * (second if source % 2 els...]
    pallas_call x15 -> x18, Pallas kernels: 11.5 us -> 12.7 us  [call(): pl.pallas_call(body, out_shape=[jax.ShapeDtypeStruct(shape, kind) for sha...]
    ppermute x2, waiting for transfers between devices: 0.01 us -> 1.13 us  [layer_traded(): return lax.ppermute(value, axes, pairs)]
    unnamed x8 -> x4, local copies, waits for them, and re-layouts: 0.02 us -> 0.9 us
    ppermute x3, starting transfers between devices: 4.12 us -> 4.6 us  [split_traded(): lax.ppermute(value, SEQ, [(source, source ^ 2 * (second if source % 2 els...]
  transfers between devices with their start and end apart: 17 -> 17, of which waited for: 8 -> 7; matrix products, arithmetic and copies ran while one was open for 0% -> 0% of each run, Pallas kernels for 20% -> 25%
where the time goes in v5:
time: 34.4 us; the launch traced here: 34.2 us
  starting transfers between devices  15.9 us (46%)
  Pallas kernels  12.7 us (37%)
  waiting for transfers between devices  3.76 us (11%)
  local copies, waits for them, and re-layouts  0.98 us (3%)
  between operations  0.84 us (2%)
    pallas_call x18, Pallas kernels, call(): pl.pallas_call(body, out_shape=[jax.ShapeDtypeStruct(shape, kind) for sha...  12.7 us
    ppermute x12, starting transfers between devices, traded(): lax.ppermute(value, SEQ, [(source, source ^ mask) for source in range(lax...  7.1 us
    ppermute x3, starting transfers between devices, split_traded(): lax.ppermute(value, SEQ, [(source, source ^ 2 * (second if source % 2 els...  4.6 us
    ppermute x2, starting transfers between devices, layer_traded(): return lax.ppermute(value, axes, pairs)  4.23 us
    ppermute x12, waiting for transfers between devices, traded(): lax.ppermute(value, SEQ, [(source, source ^ mask) for source in range(lax...  2.03 us
    ppermute x2, waiting for transfers between devices, layer_traded(): return lax.ppermute(value, axes, pairs)  1.13 us
    unnamed x4, local copies, waits for them, and re-layouts  0.9 us
  transfers between devices with their start and end apart: 17, of which 7 were waited for; matrix products, arithmetic and copies ran while one was open for 0% of the time, Pallas kernels for 25%

profile of v5, /device:TPU:0, one launch (start us, length us, event | category | flops | bytes accessed | tf_op | source)
XLA Modules:
  0.0 34.2 jit_solution(15183660669416321096)
XLA Ops:
  0.6 1.7 %pool.1 = (f32[16,128]{1,0:T(8,128)S(1)}, bf16[480,1152]{1,0:T(8,128)(2,1)S(1)}, bf16[160,768]{1,0:T(8,128)(2,1)S(1)}, bf16[64,768]{1,0:T(8,128)(2,1)S(1)}) custom-call(bf16[256,384]{1,0:T(8,128)(2,1)} %bitcast.14, bf16[256,384]{1,0:T(8,128)(2,1)} %bitcast.15, bf16[256,384]{1,0:T(8,128)(2,1)} %bitcast.16, f32[6]{0:T(128)} %refs_3_.2), custom_call_target="tpu_custom_call" | custom-call | flops 1 | bytes 10000 | tf_op jit(solution)/shard_map/pool/pallas_call | solution.py:142
  2.3 0.5 %collective-permute-start = (bf16[160,768]{1,0:T(8,128)(2,1)S(1)}, bf16[160,768]{1,0:T(8,128)(2,1)S(1)}, u32[]{:S(2)}, u32[]{:S(2)}) collective-permute-start(bf16[160,768]{1,0:T(8,128)(2,1)S(1)} %get-tuple-element.57.refs_0_), channel_id=1, source_target_pairs={{0,1},{1,0},{2,3},{3,2},{4,5},{5,4},{6,7},{7,6},{8,9},{9,8},{10,11... | collective-permute-start | bytes 737288 | tf_op jit(solution)/shard_map/ppermute | solution.py:473
  2.9 2.6 %collective-permute-start.3 = (bf16[64,768]{1,0:T(8,128)(2,1)S(1)}, bf16[64,768]{1,0:T(8,128)(2,1)S(1)}, u32[]{:S(2)}, u32[]{:S(2)}) collective-permute-start(bf16[64,768]{1,0:T(8,128)(2,1)S(1)} %get-tuple-element.58), channel_id=1, source_target_pairs={{0,2},{1,3},{2,0},{3,1},{4,6},{5,7},{6,4},{7,5},{8,10},{9,11},{10,... | collective-permute-start | bytes 294920 | tf_op jit(solution)/shard_map/ppermute | solution.py:473
  5.5 0.0 collective-permute-done.refs_1_.refs_3_.refs_7_
  5.5 1.6 %collective-permute-start.1 = (bf16[64,768]{1,0:T(8,128)(2,1)S(1)}, bf16[64,768]{1,0:T(8,128)(2,1)S(1)}, u32[]{:S(2)}, u32[]{:S(2)}) collective-permute-start(bf16[64,768]{1,0:T(8,128)(2,1)S(1)} %third_rows.1), channel_id=1, source_target_pairs={{0,4},{1,7},{2,6},{3,5},{4,0},{5,3},{6,2},{7,1},{8,12},{9,15},{10,... | collective-permute-start | bytes 294920 | tf_op jit(solution)/shard_map/ppermute | solution.py:477
  7.0 1.5 %base.1 = (f32[256,768]{1,0:T(8,128)S(1)}, bf16[256,1536]{1,0:T(8,128)(2,1)S(1)}, bf16[256,768]{1,0:T(8,128)(2,1)S(1)}) custom-call(f32[16,128]{1,0:T(8,128)S(1)} %get-tuple-element.56.refs_0_.refs_1_, bf16[480,1152]{1,0:T(8,128)(2,1)S(1)} %get-tuple-element.59.refs_1_.refs_2_.refs_4_.refs_3_, bf16[256,384]{1,0:T(8,128)(2,1)} %bitcast.13, ...), custom_call_target="tpu_custom_call" | custom-call | flops 100000000 | bytes 10000 | tf_op jit(solution)/shard_map/base/pallas_call | solution.py:142
  8.5 0.9 %copy-done = bf16[256,1536]{1,0:T(8,128)(2,1)} copy-done((bf16[256,1536]{1,0:T(8,128)(2,1)}, bf16[256,1536]{1,0:T(8,128)(2,1)S(1)}, u32[]{:S(2)}) %copy-start) | copy-done | bytes 786456
  9.4 0.4 %level.2 = (bf16[128,768]{1,0:T(8,128)(2,1)S(1)}, f32[256,768]{1,0:T(8,128)S(1)}) custom-call(f32[16,128]{1,0:T(8,128)S(1)} %get-tuple-element.56.refs_0_.refs_1_, f32[256,768]{1,0:T(8,128)S(1)} %get-tuple-element.60.refs_1_, bf16[480,1152]{1,0:T(8,128)(2,1)S(1)} %get-tuple-element.59.refs_1_.refs_2_.refs_4_.refs_3_, ...), custom_call_target="tpu_custom_call" | custom-call | flops 25000000 | bytes 10000 | tf_op jit(solution)/shard_map/level/pallas_call | solution.py:142
  9.8 0.0 collective-permute-done.3.refs_3_.refs_8_
  9.8 0.7 %collective-permute-start.4 = (bf16[64,768]{1,0:T(8,128)(2,1)S(1)}, bf16[64,768]{1,0:T(8,128)(2,1)S(1)}, u32[]{:S(2)}, u32[]{:S(2)}) collective-permute-start(bf16[64,768]{1,0:T(8,128)(2,1)S(1)} %collective-permute-done.3.refs_3_.refs_8_), channel_id=1, source_target_pairs={{0,1},{1,0},{2,3},{3,2},{4,5},{5,4},{6,7},{7,6},{8,9},{9,8},{10,11... | collective-permute-start | bytes 294920 | tf_op jit(solution)/shard_map/ppermute | solution.py:473
  10.6 0.6 %collective-permute-done.1.refs_5_.refs_10_ = bf16[64,768]{1,0:T(8,128)(2,1)S(1)} collective-permute-done((bf16[64,768]{1,0:T(8,128)(2,1)S(1)}, bf16[64,768]{1,0:T(8,128)(2,1)S(1)}, u32[]{:S(2)}, u32[]{:S(2)}) %collective-permute-start.1) | collective-permute-done | bytes 98336 | tf_op jit(solution)/shard_map/ppermute | solution.py:477
  11.2 0.0 collective-permute-start.2
  11.2 0.1 stack.23.refs_0_
  11.3 0.3 collective-permute-done.4.refs_4_.refs_9_
  11.5 0.4 %level.3 = (bf16[64,768]{1,0:T(8,128)(2,1)S(1)}, f32[256,768]{1,0:T(8,128)S(1)}) custom-call(f32[16,128]{1,0:T(8,128)S(1)} %get-tuple-element.56.refs_0_.refs_1_, f32[256,768]{1,0:T(8,128)S(1)} %get-tuple-element.62.refs_1_, bf16[480,1152]{1,0:T(8,128)(2,1)S(1)} %get-tuple-element.59.refs_1_.refs_2_.refs_4_.refs_3_, ...), custom_call_target="tpu_custom_call" | custom-call | flops 25000000 | bytes 10000 | tf_op jit(solution)/shard_map/level/pallas_call | solution.py:142
  11.9 0.6 %collective-permute-done.2.refs_6_.refs_11_ = bf16[64,768]{1,0:T(8,128)(2,1)S(1)} collective-permute-done((bf16[64,768]{1,0:T(8,128)(2,1)S(1)}, bf16[64,768]{1,0:T(8,128)(2,1)S(1)}, u32[]{:S(2)}, u32[]{:S(2)}) %collective-permute-start.2) | collective-permute-done | bytes 98336 | tf_op jit(solution)/shard_map/ppermute | solution.py:473
  12.5 1.7 %forward.1 = (bf16[32,768]{1,0:T(8,128)(2,1)S(1)}, f32[256,384]{1,0:T(8,128)S(1)}, f32[256,384]{1,0:T(8,128)S(1)}, bf16[96,384]{1,0:T(8,128)(2,1)S(1)}, bf16[144...) custom-call(s32[5]{0:T(128)S(1)} %stack.23.refs_0_, f32[16,128]{1,0:T(8,128)S(1)} %get-tuple-element.56.refs_0_.refs_1_, ...), custom_call_target="tpu_custom_call" | custom-call | flops 1 | bytes 10000 | tf_op jit(solution)/shard_map/forward/pallas_call | solution.py:142
  14.2 0.2 grads.1
  14.4 0.2 collective-permute-start.10
  14.6 0.4 %collective-permute-start.5 = (bf16[144,384]{1,0:T(8,128)(2,1)S(1)}, bf16[144,384]{1,0:T(8,128)(2,1)S(1)}, u32[]{:S(2)}, u32[]{:S(2)}) collective-permute-start(bf16[144,384]{1,0:T(8,128)(2,1)S(1)} %get-tuple-element.70), channel_id=1, source_target_pairs={{0,1},{1,0},{2,3},{3,2},{4,5},{5,4},{6,7},{7,6},{8,9},{9,8},{10,11... | collective-permute-start | bytes 331784 | tf_op jit(solution)/shard_map/ppermute | solution.py:473
  14.9 0.9 %collective-permute-start.9 = (bf16[64,896]{1,0:T(8,128)(2,1)S(1)}, bf16[64,896]{1,0:T(8,128)(2,1)S(1)}, u32[]{:S(2)}, u32[]{:S(2)}) collective-permute-start(bf16[64,896]{1,0:T(8,128)(2,1)S(1)} %get-tuple-element.80.refs_6_), channel_id=1, source_target_pairs={{0,2},{1,3},{2,0},{3,1},{4,6},{5,7},{6,4},{7,5},{8,10},{9,11},{10,... | collective-permute-start | bytes 344072 | tf_op jit(solution)/shard_map/ppermute | solution.py:473
  15.9 0.3 collective-permute-done.5.refs_1_
  16.2 1.6 %collective-permute-start.7 = (bf16[48,384]{1,0:T(8,128)(2,1)S(1)}, bf16[48,384]{1,0:T(8,128)(2,1)S(1)}, u32[]{:S(2)}, u32[]{:S(2)}) collective-permute-start(bf16[48,384]{1,0:T(8,128)(2,1)S(1)} %get-tuple-element.72), channel_id=1, source_target_pairs={{0,8},{1,9},{2,10},{3,11},{4,12},{5,13},{6,14},{7,15},{8,0},{9,1},... | collective-permute-start | bytes 110600 | tf_op jit(solution)/shard_map/ppermute | solution.py:491
  17.8 2.6 %collective-permute-start.6 = (bf16[96,384]{1,0:T(8,128)(2,1)S(1)}, bf16[96,384]{1,0:T(8,128)(2,1)S(1)}, u32[]{:S(2)}, u32[]{:S(2)}) collective-permute-start(bf16[96,384]{1,0:T(8,128)(2,1)S(1)} %get-tuple-element.71), channel_id=1, source_target_pairs={{0,16},{1,25},{2,18},{3,27},{4,20},{5,29},{6,22},{7,31},{8,24},{9,... | collective-permute-start | bytes 221192 | tf_op jit(solution)/shard_map/ppermute | solution.py:491
  20.4 0.0 collective-permute-done.10.refs_4_.refs_1_
  20.5 1.6 %collective-permute-start.13 = (bf16[64,896]{1,0:T(8,128)(2,1)S(1)}, bf16[64,896]{1,0:T(8,128)(2,1)S(1)}, u32[]{:S(2)}, u32[]{:S(2)}) collective-permute-start(bf16[64,896]{1,0:T(8,128)(2,1)S(1)} %third_grads.1), channel_id=1, source_target_pairs={{0,4},{1,7},{2,6},{3,5},{4,0},{5,3},{6,2},{7,1},{8,12},{9,15},{10,... | collective-permute-start | bytes 344072 | tf_op jit(solution)/shard_map/ppermute | solution.py:477
  22.0 1.4 %near.1 = (f32[256,384]{1,0:T(8,128)S(1)}, f32[256,384]{1,0:T(8,128)S(1)}, f32[256,384]{1,0:T(8,128)S(1)}) custom-call(f32[16,128]{1,0:T(8,128)S(1)} %get-tuple-element.56.refs_0_.refs_1_, bf16[480,1152]{1,0:T(8,128)(2,1)S(1)} %get-tuple-element.59.refs_1_.refs_2_.refs_4_.refs_3_, bf16[256,512]{1,0:T(8,128)(2,1)S(1)} %get-tuple-element.75.refs_2_, ...), custom_call_target="tpu_custom_call" | custom-call | flops 1600000000 | bytes 10000 | tf_op jit(solution)/shard_map/near/pallas_call | solution.py:142
  23.4 0.0 collective-permute-done.7.refs_2_
  23.4 1.1 %collective-permute-done.6.refs_1_ = bf16[96,384]{1,0:T(8,128)(2,1)S(1)} collective-permute-done((bf16[96,384]{1,0:T(8,128)(2,1)S(1)}, bf16[96,384]{1,0:T(8,128)(2,1)S(1)}, u32[]{:S(2)}, u32[]{:S(2)}) %collective-permute-start.6) | collective-permute-done | bytes 73760 | tf_op jit(solution)/shard_map/ppermute | solution.py:491
  24.6 0.1 collective-permute-start.8
  24.7 0.0 collective-permute-done.9.refs_4_
  24.7 0.5 %collective-permute-start.12 = (bf16[64,896]{1,0:T(8,128)(2,1)S(1)}, bf16[64,896]{1,0:T(8,128)(2,1)S(1)}, u32[]{:S(2)}, u32[]{:S(2)}) collective-permute-start(bf16[64,896]{1,0:T(8,128)(2,1)S(1)} %collective-permute-done.9.refs_4_), channel_id=1, source_target_pairs={{0,1},{1,0},{2,3},{3,2},{4,5},{5,4},{6,7},{7,6},{8,9},{9,8},{10,11... | collective-permute-start | bytes 344072 | tf_op jit(solution)/shard_map/ppermute | solution.py:473
  25.2 0.9 %key.2 = (f32[256,384]{1,0:T(8,128)S(1)}, f32[256,384]{1,0:T(8,128)S(1)}) custom-call(f32[16,128]{1,0:T(8,128)S(1)} %get-tuple-element.56.refs_0_.refs_1_, f32[256,384]{1,0:T(8,128)S(1)} %get-tuple-element.82.refs_1_, f32[256,384]{1,0:T(8,128)S(1)} %get-tuple-element.83.refs_2_, bf16[480,1152]{1,0:T(8,128)(2,1)S(1)} %get-tuple-element.59.refs_1_.refs_2_.refs_4_.refs_3_, ...), custom_call_target="tpu_custom_call" | custom-call | flops 100000000 | bytes 10000 | tf_op jit(solution)/shard_map/key/pallas_call | solution.py:142
  26.0 0.0 collective-permute-done.8.refs_2_
  26.1 0.1 layer_total.1
  26.1 0.0 collective-permute-done.13.refs_6_
  26.1 0.1 collective-permute-start.14
  26.3 1.5 %collective-permute-start.11 = (bf16[96,384]{1,0:T(8,128)(2,1)S(1)}, bf16[96,384]{1,0:T(8,128)(2,1)S(1)}, u32[]{:S(2)}, u32[]{:S(2)}) collective-permute-start(bf16[96,384]{1,0:T(8,128)(2,1)S(1)} %get-tuple-element.88.refs_3_), channel_id=1, source_target_pairs={{0,4},{1,7},{2,6},{3,5},{4,0},{5,3},{6,2},{7,1},{8,12},{9,15},{10,... | collective-permute-start | bytes 221192 | tf_op jit(solution)/shard_map/ppermute | solution.py:477
  27.8 1.0 %collective-permute-start.15 = (bf16[48,384]{1,0:T(8,128)(2,1)S(1)}, bf16[48,384]{1,0:T(8,128)(2,1)S(1)}, u32[]{:S(2)}, u32[]{:S(2)}) collective-permute-start(bf16[48,384]{1,0:T(8,128)(2,1)S(1)} %get-tuple-element.103), channel_id=1, source_target_pairs={{0,2},{1,3},{2,0},{3,1},{4,6},{5,7},{6,4},{7,5},{8,10},{9,11},{10,... | collective-permute-start | bytes 110600 | tf_op jit(solution)/shard_map/ppermute | solution.py:473
  28.7 1.4 %far.1.refs_0_ = bf16[256,384]{1,0:T(8,128)(2,1)S(1)} custom-call(f32[16,128]{1,0:T(8,128)S(1)} %get-tuple-element.56.refs_0_.refs_1_, f32[256,384]{1,0:T(8,128)S(1)} %get-tuple-element.94.refs_1_, bf16[128,768]{1,0:T(8,128)(2,1)S(1)} %get-tuple-element.95.refs_2_, bf16[64,768]{1,0:T(8,128)(2,1)S(1)} %get-tuple-element.96.refs_3_, ...), custom_call_target="tpu_custom_call" | custom-call | flops 100000000 | bytes 10000 | tf_op jit(solution)/shard_map/far/pallas_call | solution.py:142
  30.2 0.0 collective-permute-done.12.refs_5_
  30.2 1.5 %key.3 = (bf16[256,384]{1,0:T(8,128)(2,1)S(1)}, bf16[256,384]{1,0:T(8,128)(2,1)S(1)}) custom-call(f32[16,128]{1,0:T(8,128)S(1)} %get-tuple-element.56.refs_0_.refs_1_, f32[256,384]{1,0:T(8,128)S(1)} %get-tuple-element.89.refs_1_, f32[256,384]{1,0:T(8,128)S(1)} %get-tuple-element.90.refs_2_, ...), custom_call_target="tpu_custom_call" | custom-call | flops 100000000 | bytes 10000 | tf_op jit(solution)/shard_map/key/pallas_call | solution.py:142
  31.7 0.0 collective-permute-done.11.refs_0_
  31.7 0.4 %collective-permute-done.15.refs_1_ = bf16[48,384]{1,0:T(8,128)(2,1)S(1)} collective-permute-done((bf16[48,384]{1,0:T(8,128)(2,1)S(1)}, bf16[48,384]{1,0:T(8,128)(2,1)S(1)}, u32[]{:S(2)}, u32[]{:S(2)}) %collective-permute-start.15) | collective-permute-done | bytes 36896 | tf_op jit(solution)/shard_map/ppermute | solution.py:473
  32.1 0.1 collective-permute-start.16
  32.2 0.8 %flush.1 = (bf16[256,384]{1,0:T(8,128)(2,1)}, bf16[256,384]{1,0:T(8,128)(2,1)}, bf16[256,384]{1,0:T(8,128)(2,1)}) custom-call(bf16[256,384]{1,0:T(8,128)(2,1)S(1)} %far.1.refs_0_, bf16[256,384]{1,0:T(8,128)(2,1)S(1)} %get-tuple-element.99.refs_1_, bf16[256,384]{1,0:T(8,128)(2,1)S(1)} %get-tuple-element.100.refs_2_), custom_call_target="tpu_custom_call" | custom-call | flops 1 | bytes 10000 | tf_op jit(solution)/shard_map/flush/pallas_call | solution.py:142
  33.0 0.5 %collective-permute-done.16.refs_2_ = bf16[144,384]{1,0:T(8,128)(2,1)S(1)} collective-permute-done((bf16[144,384]{1,0:T(8,128)(2,1)S(1)}, bf16[144,384]{1,0:T(8,128)(2,1)S(1)}, u32[]{:S(2)}, u32[]{:S(2)}) %collective-permute-start.16) | collective-permute-done | bytes 110624 | tf_op jit(solution)/shard_map/ppermute | solution.py:473
  33.5 0.7 %weight_out.1 = f32[96,384]{1,0:T(8,128)} custom-call(s32[1]{0:T(128)} %bitcast.refs_0_, bf16[144,384]{1,0:T(8,128)(2,1)S(1)} %plane_rows.1.refs_1_, bf16[144,384]{1,0:T(8,128)(2,1)S(1)} %collective-permute-done.16.refs_2_, bf16[96,384]{1,0:T(8,128)(2,1)S(1)} %get-tuple-element.88.refs_3_), custom_call_target="tpu_custom_call" | custom-call | flops 1 | bytes 10000 | tf_op jit(solution)/shard_map/weight_out/pallas_call | solution.py:142
  (9 shorter events, 0.1 us)
Async XLA Ops:
  2.3 3.1 %collective-permute-start = (bf16[160,768]{1,0:T(8,128)(2,1)S(1)}, bf16[160,768]{1,0:T(8,128)(2,1)S(1)}, u32[]{:S(2)}, u32[]{:S(2)}) collective-permute-start(bf16[160,768]{1,0:T(8,128)(2,1)S(1)} %get-tuple-element.57.refs_0_), channel_id=1, source_target_pairs={{0,1},{1,0},{2,3},{3,2},{4,5},{5,4},{6,7},{7,6},{8,9},{9,8},{10,11... | collective-permute-start | bytes 737288 | tf_op jit(solution)/shard_map/ppermute | solution.py:473
  2.9 7.0 %collective-permute-start.3 = (bf16[64,768]{1,0:T(8,128)(2,1)S(1)}, bf16[64,768]{1,0:T(8,128)(2,1)S(1)}, u32[]{:S(2)}, u32[]{:S(2)}) collective-permute-start(bf16[64,768]{1,0:T(8,128)(2,1)S(1)} %get-tuple-element.58), channel_id=1, source_target_pairs={{0,2},{1,3},{2,0},{3,1},{4,6},{5,7},{6,4},{7,5},{8,10},{9,11},{10,... | collective-permute-start | bytes 294920 | tf_op jit(solution)/shard_map/ppermute | solution.py:473
  5.5 5.7 %collective-permute-start.1 = (bf16[64,768]{1,0:T(8,128)(2,1)S(1)}, bf16[64,768]{1,0:T(8,128)(2,1)S(1)}, u32[]{:S(2)}, u32[]{:S(2)}) collective-permute-start(bf16[64,768]{1,0:T(8,128)(2,1)S(1)} %third_rows.1), channel_id=1, source_target_pairs={{0,4},{1,7},{2,6},{3,5},{4,0},{5,3},{6,2},{7,1},{8,12},{9,15},{10,... | collective-permute-start | bytes 294920 | tf_op jit(solution)/shard_map/ppermute | solution.py:477
  8.5 0.9 %copy-start = (bf16[256,1536]{1,0:T(8,128)(2,1)}, bf16[256,1536]{1,0:T(8,128)(2,1)S(1)}, u32[]{:S(2)}) copy-start(bf16[256,1536]{1,0:T(8,128)(2,1)S(1)} %get-tuple-element.76.refs_3_) | copy-start | bytes 2359300
  9.8 1.7 %collective-permute-start.4 = (bf16[64,768]{1,0:T(8,128)(2,1)S(1)}, bf16[64,768]{1,0:T(8,128)(2,1)S(1)}, u32[]{:S(2)}, u32[]{:S(2)}) collective-permute-start(bf16[64,768]{1,0:T(8,128)(2,1)S(1)} %collective-permute-done.3.refs_3_.refs_8_), channel_id=1, source_target_pairs={{0,1},{1,0},{2,3},{3,2},{4,5},{5,4},{6,7},{7,6},{8,9},{9,8},{10,11... | collective-permute-start | bytes 294920 | tf_op jit(solution)/shard_map/ppermute | solution.py:473
  11.2 1.3 %collective-permute-start.2 = (bf16[64,768]{1,0:T(8,128)(2,1)S(1)}, bf16[64,768]{1,0:T(8,128)(2,1)S(1)}, u32[]{:S(2)}, u32[]{:S(2)}) collective-permute-start(bf16[64,768]{1,0:T(8,128)(2,1)S(1)} %collective-permute-done.1.refs_5_.refs_10_), channel_id=1, source_target_pairs={{0,1},{1,0},{2,3},{3,2},{4,5},{5,4},{6,7},{7,6},{8,9},{9,8},{10,11... | collective-permute-start | bytes 294920 | tf_op jit(solution)/shard_map/ppermute | solution.py:473
  14.2 7.9 %copy-start.1 = (bf16[256,1536]{1,0:T(8,128)(2,1)S(1)}, bf16[256,1536]{1,0:T(8,128)(2,1)}, u32[]{:S(2)}) copy-start(bf16[256,1536]{1,0:T(8,128)(2,1)} %copy-done) | copy-start | bytes 2359300
  14.4 6.1 %collective-permute-start.10 = (bf16[160,896]{1,0:T(8,128)(2,1)S(1)}, bf16[160,896]{1,0:T(8,128)(2,1)S(1)}, u32[]{:S(2)}, u32[]{:S(2)}) collective-permute-start(bf16[160,896]{1,0:T(8,128)(2,1)S(1)} %get-tuple-element.84.refs_0_.refs_5_), channel_id=1, source_target_pairs={{0,1},{1,0},{2,3},{3,2},{4,5},{5,4},{6,7},{7,6},{8,9},{9,8},{10,11... | collective-permute-start | bytes 860168 | tf_op jit(solution)/shard_map/ppermute | solution.py:473
  14.6 1.6 %collective-permute-start.5 = (bf16[144,384]{1,0:T(8,128)(2,1)S(1)}, bf16[144,384]{1,0:T(8,128)(2,1)S(1)}, u32[]{:S(2)}, u32[]{:S(2)}) collective-permute-start(bf16[144,384]{1,0:T(8,128)(2,1)S(1)} %get-tuple-element.70), channel_id=1, source_target_pairs={{0,1},{1,0},{2,3},{3,2},{4,5},{5,4},{6,7},{7,6},{8,9},{9,8},{10,11... | collective-permute-start | bytes 331784 | tf_op jit(solution)/shard_map/ppermute | solution.py:473
  14.9 9.7 %collective-permute-start.9 = (bf16[64,896]{1,0:T(8,128)(2,1)S(1)}, bf16[64,896]{1,0:T(8,128)(2,1)S(1)}, u32[]{:S(2)}, u32[]{:S(2)}) collective-permute-start(bf16[64,896]{1,0:T(8,128)(2,1)S(1)} %get-tuple-element.80.refs_6_), channel_id=1, source_target_pairs={{0,2},{1,3},{2,0},{3,1},{4,6},{5,7},{6,4},{7,5},{8,10},{9,11},{10,... | collective-permute-start | bytes 344072 | tf_op jit(solution)/shard_map/ppermute | solution.py:473
  16.2 7.2 %collective-permute-start.7 = (bf16[48,384]{1,0:T(8,128)(2,1)S(1)}, bf16[48,384]{1,0:T(8,128)(2,1)S(1)}, u32[]{:S(2)}, u32[]{:S(2)}) collective-permute-start(bf16[48,384]{1,0:T(8,128)(2,1)S(1)} %get-tuple-element.72), channel_id=1, source_target_pairs={{0,8},{1,9},{2,10},{3,11},{4,12},{5,13},{6,14},{7,15},{8,0},{9,1},... | collective-permute-start | bytes 110600 | tf_op jit(solution)/shard_map/ppermute | solution.py:491
  17.8 6.7 %collective-permute-start.6 = (bf16[96,384]{1,0:T(8,128)(2,1)S(1)}, bf16[96,384]{1,0:T(8,128)(2,1)S(1)}, u32[]{:S(2)}, u32[]{:S(2)}) collective-permute-start(bf16[96,384]{1,0:T(8,128)(2,1)S(1)} %get-tuple-element.71), channel_id=1, source_target_pairs={{0,16},{1,25},{2,18},{3,27},{4,20},{5,29},{6,22},{7,31},{8,24},{9,... | collective-permute-start | bytes 221192 | tf_op jit(solution)/shard_map/ppermute | solution.py:491
  20.5 5.7 %collective-permute-start.13 = (bf16[64,896]{1,0:T(8,128)(2,1)S(1)}, bf16[64,896]{1,0:T(8,128)(2,1)S(1)}, u32[]{:S(2)}, u32[]{:S(2)}) collective-permute-start(bf16[64,896]{1,0:T(8,128)(2,1)S(1)} %third_grads.1), channel_id=1, source_target_pairs={{0,4},{1,7},{2,6},{3,5},{4,0},{5,3},{6,2},{7,1},{8,12},{9,15},{10,... | collective-permute-start | bytes 344072 | tf_op jit(solution)/shard_map/ppermute | solution.py:477
  24.6 1.4 %collective-permute-start.8 = (bf16[144,384]{1,0:T(8,128)(2,1)S(1)}, bf16[144,384]{1,0:T(8,128)(2,1)S(1)}, u32[]{:S(2)}, u32[]{:S(2)}) collective-permute-start(bf16[144,384]{1,0:T(8,128)(2,1)S(1)} %layer_sum.1.refs_1_), channel_id=1, source_target_pairs={{0,1},{1,0},{2,3},{3,2},{4,5},{5,4},{6,7},{7,6},{8,9},{9,8},{10,11... | collective-permute-start | bytes 331784 | tf_op jit(solution)/shard_map/ppermute | solution.py:473
  24.7 5.5 %collective-permute-start.12 = (bf16[64,896]{1,0:T(8,128)(2,1)S(1)}, bf16[64,896]{1,0:T(8,128)(2,1)S(1)}, u32[]{:S(2)}, u32[]{:S(2)}) collective-permute-start(bf16[64,896]{1,0:T(8,128)(2,1)S(1)} %collective-permute-done.9.refs_4_), channel_id=1, source_target_pairs={{0,1},{1,0},{2,3},{3,2},{4,5},{5,4},{6,7},{7,6},{8,9},{9,8},{10,11... | collective-permute-start | bytes 344072 | tf_op jit(solution)/shard_map/ppermute | solution.py:473
  26.1 4.0 %collective-permute-start.14 = (bf16[64,896]{1,0:T(8,128)(2,1)S(1)}, bf16[64,896]{1,0:T(8,128)(2,1)S(1)}, u32[]{:S(2)}, u32[]{:S(2)}) collective-permute-start(bf16[64,896]{1,0:T(8,128)(2,1)S(1)} %collective-permute-done.13.refs_6_), channel_id=1, source_target_pairs={{0,1},{1,0},{2,3},{3,2},{4,5},{5,4},{6,7},{7,6},{8,9},{9,8},{10,11... | collective-permute-start | bytes 344072 | tf_op jit(solution)/shard_map/ppermute | solution.py:473
  26.3 5.4 %collective-permute-start.11 = (bf16[96,384]{1,0:T(8,128)(2,1)S(1)}, bf16[96,384]{1,0:T(8,128)(2,1)S(1)}, u32[]{:S(2)}, u32[]{:S(2)}) collective-permute-start(bf16[96,384]{1,0:T(8,128)(2,1)S(1)} %get-tuple-element.88.refs_3_), channel_id=1, source_target_pairs={{0,4},{1,7},{2,6},{3,5},{4,0},{5,3},{6,2},{7,1},{8,12},{9,15},{10,... | collective-permute-start | bytes 221192 | tf_op jit(solution)/shard_map/ppermute | solution.py:477
  27.8 4.3 %collective-permute-start.15 = (bf16[48,384]{1,0:T(8,128)(2,1)S(1)}, bf16[48,384]{1,0:T(8,128)(2,1)S(1)}, u32[]{:S(2)}, u32[]{:S(2)}) collective-permute-start(bf16[48,384]{1,0:T(8,128)(2,1)S(1)} %get-tuple-element.103), channel_id=1, source_target_pairs={{0,2},{1,3},{2,0},{3,1},{4,6},{5,7},{6,4},{7,5},{8,10},{9,11},{10,... | collective-permute-start | bytes 110600 | tf_op jit(solution)/shard_map/ppermute | solution.py:473
  32.1 1.4 %collective-permute-start.16 = (bf16[144,384]{1,0:T(8,128)(2,1)S(1)}, bf16[144,384]{1,0:T(8,128)(2,1)S(1)}, u32[]{:S(2)}, u32[]{:S(2)}) collective-permute-start(bf16[144,384]{1,0:T(8,128)(2,1)S(1)} %plane_rows.1.refs_1_), channel_id=1, source_target_pairs={{0,1},{1,0},{2,3},{3,2},{4,5},{5,4},{6,7},{7,6},{8,9},{9,8},{10,11... | collective-permute-start | bytes 331784 | tf_op jit(solution)/shard_map/ppermute | solution.py:473

commit v6 on v5

--- a/solution.py
+++ b/solution.py
@@ -195,12 +195,17 @@
     ]
 
 
-def attend(factor_ref, pair, queries, keys, values, amount, masks):
-    weights = both_weights(factor_ref, pair, queries, keys, masks)
-    joined = stack([weight.astype(BF) for weight in weights], 1)
-    count = jnp.full(values.shape, float(amount), BF)
-    right = stack([stack([values * mask, count * mask], 1) for mask in masks], 0)
-    return joined, dot(joined, right)
+def attend(factor_ref, items, masks):
+    weights = [
+        stack([weight.astype(BF) for weight in both_weights(factor_ref, pair, queries, keys, masks)], 1)
+        for pair, queries, keys, _, _ in items
+    ]
+    results = []
+    for joined, (_, _, _, values, amount) in zip(weights, items):
+        count = jnp.full(values.shape, float(amount), BF)
+        right = stack([stack([values * mask, count * mask], 1) for mask in masks], 0)
+        results.append((joined, dot(joined, right)))
+    return results
 
 
 def block(pair, span):
@@ -216,9 +221,11 @@
         copy.start()
     rows, width = cot_ref.shape
     masks = side_masks()
-    for pair in range(width // LANES):
-        q, k, v = (x_ref[:rows, lane_pair(width * which, pair)] for which in range(3))
-        joined, both = attend(factor_ref, pair, q, k, v, 1, masks)
+    items = [
+        (pair, *(x_ref[:rows, lane_pair(width * which, pair)] for which in range(3)), 1)
+        for pair in range(width // LANES)
+    ]
+    for pair, (joined, both) in enumerate(attend(factor_ref, items, masks)):
         sums_ref[:, block(pair, 2 * LANES)] = both
         weights_ref[:, block(pair, 2 * rows)] = joined
     order = order_matrix(rows, top)
@@ -232,9 +239,11 @@
 def level_kernel(height, load, factor_ref, sums_ref, weights_ref, total_ref):
     width = sums_ref.shape[1] // 2
     masks = side_masks()
-    for pair in range(width // LANES):
-        keys, values = (load(1, lane_pair(start, pair)) for start in (0, width))
-        joined, both = attend(factor_ref, pair, load(0, lane_pair(0, pair)), keys, values, 2**height, masks)
+    items = [
+        (pair, load(0, lane_pair(0, pair)), *(load(1, lane_pair(start, pair)) for start in (0, width)), 2**height)
+        for pair in range(width // LANES)
+    ]
+    for pair, (joined, both) in enumerate(attend(factor_ref, items, masks)):
         weights_ref[:, block(pair, joined.shape[1])] = joined
         for _ in range(height):
             both = doubled(both)
@@ -251,31 +260,35 @@
     lane = iota((LANES, LANES), 1)
     ones = jnp.where(lane // HALF == iota((LANES, LANES), 0) // HALF, 1.0, 0.0).astype(BF)
     adder = doubled(ones)
-    attended = []
-    for pair in range(width // LANES):
-        total = None
-        for at in range(top - ready - 1, -1, -1):
-            queries = load(at, lane_pair(0, pair))
-            keys, values = (load(top - ready + at, lane_pair(start, pair)) for start in (0, width))
-            joined, both = attend(factor_ref, pair, queries, keys, values, 2 ** (ready + at + 1), masks)
-            columns = joined.shape[1]
-            weights_refs[at][:, columns * pair : columns * (pair + 1)] = joined
-            total = both if total is None else both + doubled(total)
+    pairs = range(width // LANES)
+    spots = [(pair, at) for pair in pairs for at in range(top - ready - 1, -1, -1)]
+    items = []
+    for pair, at in spots:
+        keys, values = (load(top - ready + at, lane_pair(start, pair)) for start in (0, width))
+        items.append((pair, load(at, lane_pair(0, pair)), keys, values, 2 ** (ready + at + 1)))
+    sums = {}
+    for (pair, at), (joined, both) in zip(spots, attend(factor_ref, items, masks)):
+        weights_refs[at][:, block(pair, joined.shape[1])] = joined
+        sums[pair, at] = both
+    attended, inverses, products = [], [], []
+    for pair in pairs:
+        total = sums[pair, top - ready - 1]
+        for at in range(top - ready - 2, -1, -1):
+            total = sums[pair, at] + doubled(total)
         for _ in range(ready + 1):
             total = doubled(total)
         total = total + sums_ref[:, block(pair, 2 * LANES)]
-        numer = total[:, :LANES]
         inverse = 1.0 / total[:, LANES:]
-        ratio = numer * inverse
+        ratio = total[:, :LANES] * inverse
         attended.append(ratio.astype(BF))
-        back = back_ref[:, lane_pair(0, pair)].astype(F32)
-        product = back * ratio
-        product_high = product.astype(BF)
-        product_low = (product - product_high.astype(F32)).astype(BF)
-        summed = dot(stack([product_high, product_low], 1), adder)
-        grad_ref[:, lane_pair(0, pair)] = back * inverse
-        slope_ref[:, lane_pair(0, pair)] = -summed * inverse
+        inverses.append(inverse)
+        products.append(back_ref[:, lane_pair(0, pair)].astype(F32) * ratio)
     weight_ref[...] = dot(stack(attended, 1), back_ref[:, width:], TN)
+    for pair in pairs:
+        high = products[pair].astype(BF)
+        low = (products[pair] - high.astype(F32)).astype(BF)
+        grad_ref[:, lane_pair(0, pair)] = back_ref[:, lane_pair(0, pair)].astype(F32) * inverses[pair]
+        slope_ref[:, lane_pair(0, pair)] = -dot(stack([high, low], 1), adder) * inverses[pair]
     own_rows = width // parts
     for entry, offset, count, target, start in pieces:
         shift = offset if isinstance(offset, int) else offset(place_ref)
@@ -315,16 +328,26 @@
     rows, width = query_ref.shape
     heads = width // HALF
     masks = side_masks()
-    for pair in range(width // LANES):
+    pairs = range(width // LANES)
+    slopes = []
+    for pair in pairs:
+        values = x_ref[:rows, lane_pair(2 * width, pair)]
+        joined = weights_ref[:, block(pair, 2 * rows)]
+        grad = gh_ref[:, lane_pair(0, pair)]
+        slopes.append(query_slopes(joined, grad, gh_ref[:, width:], values, pair, 0, masks))
+    for pair in pairs:
         factor = side_factor(factor_ref, heads, pair)
-        queries, keys, values = (x_ref[:rows, lane_pair(width * which, pair)] for which in range(3))
+        keys = x_ref[:rows, lane_pair(width, pair)]
+        query_ref[:, lane_pair(0, pair)] = dot(stack(slopes[pair], 1), masked_stack(keys, masks)) * factor
+    for pair in pairs:
+        joined = weights_ref[:, block(pair, 2 * rows)]
+        weights = stack([joined[:, :rows], joined[:, rows:]], 0)
         grad = gh_ref[:, lane_pair(0, pair)]
-        joined = weights_ref[:, 2 * rows * pair : 2 * rows * (pair + 1)]
-        slope = query_slopes(joined, grad, gh_ref[:, width:], values, pair, 0, masks)
-        query_ref[:, lane_pair(0, pair)] = dot(stack(slope, 1), masked_stack(keys, masks)) * factor
-        key_ref[:, lane_pair(0, pair)] = dot(stack(slope, 0), masked_stack(queries, masks), TN) * factor
-        weights = stack([joined[:, :rows], joined[:, rows:]], 0)
         value_ref[:, lane_pair(0, pair)] = dot(weights, masked_stack(grad, masks), TN)
+    for pair in pairs:
+        factor = side_factor(factor_ref, heads, pair)
+        queries = x_ref[:rows, lane_pair(0, pair)]
+        key_ref[:, lane_pair(0, pair)] = dot(stack(slopes[pair], 0), masked_stack(queries, masks), TN) * factor
 
 
 def far_kernel(top, load, factor_ref, base_ref, *refs):
@@ -332,19 +355,25 @@
     rows, width = out_ref.shape
     heads = width // HALF
     masks = side_masks()
-    results = []
-    for pair in range(width // LANES):
-        factor = side_factor(factor_ref, heads, pair)
-        total = None
+    pairs = range(width // LANES)
+    slopes = {}
+    for pair in pairs:
         for height in range(top, 0, -1):
             grad = load(height - 1, lane_pair(0, pair))
             denom = load(height - 1, slice(width, width + LANES))
-            keys, values = (load(top + height - 1, lane_pair(start, pair)) for start in (0, width))
-            columns = 2 * keys.shape[0]
-            joined = weights_refs[height - 1][:, columns * pair : columns * (pair + 1)]
-            slope = query_slopes(joined, grad, denom, values, pair, height, masks)
-            piece = dot(stack(slope, 1), masked_stack(keys, masks)) * factor
-            total = piece if total is None else piece + 0.5 * doubled(total)
+            values = load(top + height - 1, lane_pair(width, pair))
+            joined = weights_refs[height - 1][:, block(pair, 2 * values.shape[0])]
+            slopes[pair, height] = query_slopes(joined, grad, denom, values, pair, height, masks)
+    pieces = {}
+    for pair, height in slopes:
+        keys = load(top + height - 1, lane_pair(0, pair))
+        pieces[pair, height] = dot(stack(slopes[pair, height], 1), masked_stack(keys, masks))
+    results = []
+    for pair in pairs:
+        total = pieces[pair, top]
+        for height in range(top - 1, 0, -1):
+            total = pieces[pair, height] + 0.5 * doubled(total)
+        total = total * side_factor(factor_ref, heads, pair)
         total = base_ref[:, lane_pair(0, pair)] + 0.5 * doubled(total)
         results.append(total.astype(BF))
     out_ref[...] = dot(order_matrix(rows, top, True), stack(results, 1)).astype(BF)
@@ -355,35 +384,43 @@
     heads = width // HALF
     masks = side_masks()
     levels = last - first + 1
+    pairs = range(width // LANES)
+    spots = [(pair, at) for pair in pairs for at in range(levels - 1, -1, -1)]
+    weights, slopes, key_pieces, value_pieces = {}, {}, {}, {}
+    for pair, at in spots:
+        keys = load(at, lane_pair(width, pair))
+        queries = load(levels + at, lane_pair(width + LANES, pair))
+        weights[pair, at] = both_weights(factor_ref, pair, keys, queries, masks)
+    for pair, at in spots:
+        values = load(at, lane_pair(2 * width, pair))
+        grad = load(levels + at, lane_pair(0, pair))
+        denom = load(levels + at, slice(width, width + LANES))
+        count = values.shape[0]
+        left = stack(
+            [
+                stack([values * mask, jnp.broadcast_to(slot * float(2 ** (first + at)), (count, LANES))], 1)
+                for mask, slot in zip(masks, slot_masks(pair))
+            ],
+            0,
+        )
+        product = dot(left, stack([grad, denom], 1), NT)
+        slopes[pair, at] = [
+            (weight * product[side * count : (side + 1) * count]).astype(BF)
+            for side, weight in enumerate(weights[pair, at])
+        ]
+    for pair, at in spots:
+        grad = load(levels + at, lane_pair(0, pair))
+        rounded = stack([weight.astype(BF) for weight in weights[pair, at]], 1)
+        value_pieces[pair, at] = dot(rounded, masked_stack(grad, masks))
+        queries = load(levels + at, lane_pair(width + LANES, pair))
+        key_pieces[pair, at] = dot(stack(slopes[pair, at], 1), masked_stack(queries, masks))
     key_results, value_results = [], []
-    for pair in range(width // LANES):
-        factor = side_factor(factor_ref, heads, pair)
-        key_total = value_total = None
-        for at in range(levels - 1, -1, -1):
-            keys, values = (load(at, lane_pair(start, pair)) for start in (width, 2 * width))
-            grad = load(levels + at, lane_pair(0, pair))
-            denom = load(levels + at, slice(width, width + LANES))
-            queries = load(levels + at, lane_pair(width + LANES, pair))
-            count = keys.shape[0]
-            weights = both_weights(factor_ref, pair, keys, queries, masks)
-            left = stack(
-                [
-                    stack([values * mask, jnp.broadcast_to(slot * float(2 ** (first + at)), (count, LANES))], 1)
-                    for mask, slot in zip(masks, slot_masks(pair))
-                ],
-                0,
-            )
-            product = dot(left, stack([grad, denom], 1), NT)
-            slope = [
-                (weight * product[side * count : (side + 1) * count]).astype(BF)
-                for side, weight in enumerate(weights)
-            ]
-            key_piece = dot(stack(slope, 1), masked_stack(queries, masks)) * factor
-            value_piece = dot(stack([weight.astype(BF) for weight in weights], 1), masked_stack(grad, masks))
-            if key_total is not None:
-                key_piece = key_piece + 0.5 * doubled(key_total)
-                value_piece = value_piece + doubled(value_total)
-            key_total, value_total = key_piece, value_piece
+    for pair in pairs:
+        key_total, value_total = key_pieces[pair, levels - 1], value_pieces[pair, levels - 1]
+        for at in range(levels - 2, -1, -1):
+            key_total = key_pieces[pair, at] + 0.5 * doubled(key_total)
+            value_total = value_pieces[pair, at] + doubled(value_total)
+        key_total = key_total * side_factor(factor_ref, heads, pair)
         for _ in range(first):
             key_total, value_total = 0.5 * doubled(key_total), doubled(value_total)
         key_results.append(base_key_ref[:, lane_pair(0, pair)] + key_total)

time: 34.4 us -> 33.9 us (0.985)
  Pallas kernels: 12.7 us -> 10.2 us
  waiting for transfers between devices: 3.76 us -> 5.71 us
    pallas_call x18, Pallas kernels: 12.7 us -> 10.2 us  [call(): pl.pallas_call(body, out_shape=[jax.ShapeDtypeStruct(shape, kind) for sha...]
    ppermute x3, waiting for transfers between devices: 0.6 us -> 1.49 us  [split_traded(): lax.ppermute(value, SEQ, [(source, source ^ 2 * (second if source % 2 els...]
    ppermute x12, waiting for transfers between devices: 2.03 us -> 2.73 us  [traded(): lax.ppermute(value, SEQ, [(source, source ^ mask) for source in range(lax...]
    ppermute x2, waiting for transfers between devices: 1.13 us -> 1.49 us  [layer_traded(): return lax.ppermute(value, axes, pairs)]
  transfers between devices with their start and end apart: 17 -> 17, of which waited for: 7 -> 9; matrix products, arithmetic and copies ran while one was open for 0% -> 0% of each run, Pallas kernels for 25% -> 19%
where the time goes in v6:
time: 33.9 us; the launch traced here: 33.8 us
  starting transfers between devices  16 us (47%)
  Pallas kernels  10.2 us (30%)
  waiting for transfers between devices  5.71 us (17%)
  local copies, waits for them, and re-layouts  0.98 us (3%)
  between operations  0.82 us (2%)
    pallas_call x18, Pallas kernels, call(): pl.pallas_call(body, out_shape=[jax.ShapeDtypeStruct(shape, kind) for sha...  10.2 us
    ppermute x12, starting transfers between devices, traded(): lax.ppermute(value, SEQ, [(source, source ^ mask) for source in range(lax...  7.19 us
    ppermute x3, starting transfers between devices, split_traded(): lax.ppermute(value, SEQ, [(source, source ^ 2 * (second if source % 2 els...  4.6 us
    ppermute x2, starting transfers between devices, layer_traded(): return lax.ppermute(value, axes, pairs)  4.23 us
    ppermute x12, waiting for transfers between devices, traded(): lax.ppermute(value, SEQ, [(source, source ^ mask) for source in range(lax...  2.73 us
    ppermute x3, waiting for transfers between devices, split_traded(): lax.ppermute(value, SEQ, [(source, source ^ 2 * (second if source % 2 els...  1.49 us
    ppermute x2, waiting for transfers between devices, layer_traded(): return lax.ppermute(value, axes, pairs)  1.49 us
    unnamed x4, local copies, waits for them, and re-layouts  0.9 us
  transfers between devices with their start and end apart: 17, of which 9 were waited for; matrix products, arithmetic and copies ran while one was open for 0% of the time, Pallas kernels for 19%

profile of v6, /device:TPU:0, one launch (start us, length us, event | category | flops | bytes accessed | tf_op | source)
XLA Modules:
  0.0 33.8 jit_solution(17850521769635677358)
XLA Ops:
  0.6 1.7 %pool.1 = (f32[16,128]{1,0:T(8,128)S(1)}, bf16[480,1152]{1,0:T(8,128)(2,1)S(1)}, bf16[160,768]{1,0:T(8,128)(2,1)S(1)}, bf16[64,768]{1,0:T(8,128)(2,1)S(1)}) custom-call(bf16[256,384]{1,0:T(8,128)(2,1)} %bitcast.14, bf16[256,384]{1,0:T(8,128)(2,1)} %bitcast.15, bf16[256,384]{1,0:T(8,128)(2,1)} %bitcast.16, f32[6]{0:T(128)} %refs_3_.2), custom_call_target="tpu_custom_call" | custom-call | flops 1 | bytes 10000 | tf_op jit(solution)/shard_map/pool/pallas_call | solution.py:142
  2.3 0.5 %collective-permute-start = (bf16[160,768]{1,0:T(8,128)(2,1)S(1)}, bf16[160,768]{1,0:T(8,128)(2,1)S(1)}, u32[]{:S(2)}, u32[]{:S(2)}) collective-permute-start(bf16[160,768]{1,0:T(8,128)(2,1)S(1)} %get-tuple-element.57.refs_0_), channel_id=1, source_target_pairs={{0,1},{1,0},{2,3},{3,2},{4,5},{5,4},{6,7},{7,6},{8,9},{9,8},{10,11... | collective-permute-start | bytes 737288 | tf_op jit(solution)/shard_map/ppermute | solution.py:510
  2.9 2.6 %collective-permute-start.3 = (bf16[64,768]{1,0:T(8,128)(2,1)S(1)}, bf16[64,768]{1,0:T(8,128)(2,1)S(1)}, u32[]{:S(2)}, u32[]{:S(2)}) collective-permute-start(bf16[64,768]{1,0:T(8,128)(2,1)S(1)} %get-tuple-element.58), channel_id=1, source_target_pairs={{0,2},{1,3},{2,0},{3,1},{4,6},{5,7},{6,4},{7,5},{8,10},{9,11},{10,... | collective-permute-start | bytes 294920 | tf_op jit(solution)/shard_map/ppermute | solution.py:510
  5.5 0.0 collective-permute-done.refs_1_.refs_3_.refs_7_
  5.5 1.6 %collective-permute-start.1 = (bf16[64,768]{1,0:T(8,128)(2,1)S(1)}, bf16[64,768]{1,0:T(8,128)(2,1)S(1)}, u32[]{:S(2)}, u32[]{:S(2)}) collective-permute-start(bf16[64,768]{1,0:T(8,128)(2,1)S(1)} %third_rows.1), channel_id=1, source_target_pairs={{0,4},{1,7},{2,6},{3,5},{4,0},{5,3},{6,2},{7,1},{8,12},{9,15},{10,... | collective-permute-start | bytes 294920 | tf_op jit(solution)/shard_map/ppermute | solution.py:514
  7.0 1.5 %base.1 = (f32[256,768]{1,0:T(8,128)S(1)}, bf16[256,1536]{1,0:T(8,128)(2,1)S(1)}, bf16[256,768]{1,0:T(8,128)(2,1)S(1)}) custom-call(f32[16,128]{1,0:T(8,128)S(1)} %get-tuple-element.56.refs_0_.refs_1_, bf16[480,1152]{1,0:T(8,128)(2,1)S(1)} %get-tuple-element.59.refs_1_.refs_2_.refs_4_.refs_3_, bf16[256,384]{1,0:T(8,128)(2,1)} %bitcast.13, ...), custom_call_target="tpu_custom_call" | custom-call | flops 100000000 | bytes 10000 | tf_op jit(solution)/shard_map/base/pallas_call | solution.py:142
  8.5 0.9 %copy-done = bf16[256,1536]{1,0:T(8,128)(2,1)} copy-done((bf16[256,1536]{1,0:T(8,128)(2,1)}, bf16[256,1536]{1,0:T(8,128)(2,1)S(1)}, u32[]{:S(2)}) %copy-start) | copy-done | bytes 786456
  9.4 0.4 %level.2 = (bf16[128,768]{1,0:T(8,128)(2,1)S(1)}, f32[256,768]{1,0:T(8,128)S(1)}) custom-call(f32[16,128]{1,0:T(8,128)S(1)} %get-tuple-element.56.refs_0_.refs_1_, f32[256,768]{1,0:T(8,128)S(1)} %get-tuple-element.60.refs_1_, bf16[480,1152]{1,0:T(8,128)(2,1)S(1)} %get-tuple-element.59.refs_1_.refs_2_.refs_4_.refs_3_, ...), custom_call_target="tpu_custom_call" | custom-call | flops 25000000 | bytes 10000 | tf_op jit(solution)/shard_map/level/pallas_call | solution.py:142
  9.8 0.0 collective-permute-done.3.refs_3_.refs_8_
  9.9 0.7 %collective-permute-start.4 = (bf16[64,768]{1,0:T(8,128)(2,1)S(1)}, bf16[64,768]{1,0:T(8,128)(2,1)S(1)}, u32[]{:S(2)}, u32[]{:S(2)}) collective-permute-start(bf16[64,768]{1,0:T(8,128)(2,1)S(1)} %collective-permute-done.3.refs_3_.refs_8_), channel_id=1, source_target_pairs={{0,1},{1,0},{2,3},{3,2},{4,5},{5,4},{6,7},{7,6},{8,9},{9,8},{10,11... | collective-permute-start | bytes 294920 | tf_op jit(solution)/shard_map/ppermute | solution.py:510
  10.6 0.6 %collective-permute-done.1.refs_5_.refs_10_ = bf16[64,768]{1,0:T(8,128)(2,1)S(1)} collective-permute-done((bf16[64,768]{1,0:T(8,128)(2,1)S(1)}, bf16[64,768]{1,0:T(8,128)(2,1)S(1)}, u32[]{:S(2)}, u32[]{:S(2)}) %collective-permute-start.1) | collective-permute-done | bytes 98336 | tf_op jit(solution)/shard_map/ppermute | solution.py:514
  11.2 0.0 collective-permute-start.2
  11.2 0.1 stack.23.refs_0_
  11.3 0.3 collective-permute-done.4.refs_4_.refs_9_
  11.5 0.4 %level.3 = (bf16[64,768]{1,0:T(8,128)(2,1)S(1)}, f32[256,768]{1,0:T(8,128)S(1)}) custom-call(f32[16,128]{1,0:T(8,128)S(1)} %get-tuple-element.56.refs_0_.refs_1_, f32[256,768]{1,0:T(8,128)S(1)} %get-tuple-element.62.refs_1_, bf16[480,1152]{1,0:T(8,128)(2,1)S(1)} %get-tuple-element.59.refs_1_.refs_2_.refs_4_.refs_3_, ...), custom_call_target="tpu_custom_call" | custom-call | flops 25000000 | bytes 10000 | tf_op jit(solution)/shard_map/level/pallas_call | solution.py:142
  11.9 0.6 %collective-permute-done.2.refs_6_.refs_11_ = bf16[64,768]{1,0:T(8,128)(2,1)S(1)} collective-permute-done((bf16[64,768]{1,0:T(8,128)(2,1)S(1)}, bf16[64,768]{1,0:T(8,128)(2,1)S(1)}, u32[]{:S(2)}, u32[]{:S(2)}) %collective-permute-start.2) | collective-permute-done | bytes 98336 | tf_op jit(solution)/shard_map/ppermute | solution.py:510
  12.5 1.3 %forward.1 = (bf16[32,768]{1,0:T(8,128)(2,1)S(1)}, f32[256,384]{1,0:T(8,128)S(1)}, f32[256,384]{1,0:T(8,128)S(1)}, bf16[96,384]{1,0:T(8,128)(2,1)S(1)}, bf16[144...) custom-call(s32[5]{0:T(128)S(1)} %stack.23.refs_0_, f32[16,128]{1,0:T(8,128)S(1)} %get-tuple-element.56.refs_0_.refs_1_, ...), custom_call_target="tpu_custom_call" | custom-call | flops 1 | bytes 10000 | tf_op jit(solution)/shard_map/forward/pallas_call | solution.py:142
  13.8 0.2 grads.1
  14.0 0.2 collective-permute-start.10
  14.2 0.4 %collective-permute-start.5 = (bf16[144,384]{1,0:T(8,128)(2,1)S(1)}, bf16[144,384]{1,0:T(8,128)(2,1)S(1)}, u32[]{:S(2)}, u32[]{:S(2)}) collective-permute-start(bf16[144,384]{1,0:T(8,128)(2,1)S(1)} %get-tuple-element.70), channel_id=1, source_target_pairs={{0,1},{1,0},{2,3},{3,2},{4,5},{5,4},{6,7},{7,6},{8,9},{9,8},{10,11... | collective-permute-start | bytes 331784 | tf_op jit(solution)/shard_map/ppermute | solution.py:510
  14.6 0.9 %collective-permute-start.9 = (bf16[64,896]{1,0:T(8,128)(2,1)S(1)}, bf16[64,896]{1,0:T(8,128)(2,1)S(1)}, u32[]{:S(2)}, u32[]{:S(2)}) collective-permute-start(bf16[64,896]{1,0:T(8,128)(2,1)S(1)} %get-tuple-element.80.refs_6_), channel_id=1, source_target_pairs={{0,2},{1,3},{2,0},{3,1},{4,6},{5,7},{6,4},{7,5},{8,10},{9,11},{10,... | collective-permute-start | bytes 344072 | tf_op jit(solution)/shard_map/ppermute | solution.py:510
  15.5 0.3 collective-permute-done.5.refs_1_
  15.8 1.6 %collective-permute-start.7 = (bf16[48,384]{1,0:T(8,128)(2,1)S(1)}, bf16[48,384]{1,0:T(8,128)(2,1)S(1)}, u32[]{:S(2)}, u32[]{:S(2)}) collective-permute-start(bf16[48,384]{1,0:T(8,128)(2,1)S(1)} %get-tuple-element.72), channel_id=1, source_target_pairs={{0,8},{1,9},{2,10},{3,11},{4,12},{5,13},{6,14},{7,15},{8,0},{9,1},... | collective-permute-start | bytes 110600 | tf_op jit(solution)/shard_map/ppermute | solution.py:528
  17.5 2.6 %collective-permute-start.6 = (bf16[96,384]{1,0:T(8,128)(2,1)S(1)}, bf16[96,384]{1,0:T(8,128)(2,1)S(1)}, u32[]{:S(2)}, u32[]{:S(2)}) collective-permute-start(bf16[96,384]{1,0:T(8,128)(2,1)S(1)} %get-tuple-element.71), channel_id=1, source_target_pairs={{0,16},{1,25},{2,18},{3,27},{4,20},{5,29},{6,22},{7,31},{8,24},{9,... | collective-permute-start | bytes 221192 | tf_op jit(solution)/shard_map/ppermute | solution.py:528
  20.1 0.0 collective-permute-done.10.refs_4_.refs_1_
  20.1 1.6 %collective-permute-start.13 = (bf16[64,896]{1,0:T(8,128)(2,1)S(1)}, bf16[64,896]{1,0:T(8,128)(2,1)S(1)}, u32[]{:S(2)}, u32[]{:S(2)}) collective-permute-start(bf16[64,896]{1,0:T(8,128)(2,1)S(1)} %third_grads.1), channel_id=1, source_target_pairs={{0,4},{1,7},{2,6},{3,5},{4,0},{5,3},{6,2},{7,1},{8,12},{9,15},{10,... | collective-permute-start | bytes 344072 | tf_op jit(solution)/shard_map/ppermute | solution.py:514
  21.7 1.1 %near.1 = (f32[256,384]{1,0:T(8,128)S(1)}, f32[256,384]{1,0:T(8,128)S(1)}, f32[256,384]{1,0:T(8,128)S(1)}) custom-call(f32[16,128]{1,0:T(8,128)S(1)} %get-tuple-element.56.refs_0_.refs_1_, bf16[480,1152]{1,0:T(8,128)(2,1)S(1)} %get-tuple-element.59.refs_1_.refs_2_.refs_4_.refs_3_, bf16[256,512]{1,0:T(8,128)(2,1)S(1)} %get-tuple-element.75.refs_2_, ...), custom_call_target="tpu_custom_call" | custom-call | flops 1600000000 | bytes 10000 | tf_op jit(solution)/shard_map/near/pallas_call | solution.py:142
  22.7 0.0 collective-permute-done.7.refs_2_
  22.7 1.5 %collective-permute-done.6.refs_1_ = bf16[96,384]{1,0:T(8,128)(2,1)S(1)} collective-permute-done((bf16[96,384]{1,0:T(8,128)(2,1)S(1)}, bf16[96,384]{1,0:T(8,128)(2,1)S(1)}, u32[]{:S(2)}, u32[]{:S(2)}) %collective-permute-start.6) | collective-permute-done | bytes 73760 | tf_op jit(solution)/shard_map/ppermute | solution.py:528
  24.2 0.1 collective-permute-start.8
  24.3 0.0 collective-permute-done.9.refs_4_
  24.3 0.5 %collective-permute-start.12 = (bf16[64,896]{1,0:T(8,128)(2,1)S(1)}, bf16[64,896]{1,0:T(8,128)(2,1)S(1)}, u32[]{:S(2)}, u32[]{:S(2)}) collective-permute-start(bf16[64,896]{1,0:T(8,128)(2,1)S(1)} %collective-permute-done.9.refs_4_), channel_id=1, source_target_pairs={{0,1},{1,0},{2,3},{3,2},{4,5},{5,4},{6,7},{7,6},{8,9},{9,8},{10,11... | collective-permute-start | bytes 344072 | tf_op jit(solution)/shard_map/ppermute | solution.py:510
  24.8 0.5 %key.2 = (f32[256,384]{1,0:T(8,128)S(1)}, f32[256,384]{1,0:T(8,128)S(1)}) custom-call(f32[16,128]{1,0:T(8,128)S(1)} %get-tuple-element.56.refs_0_.refs_1_, f32[256,384]{1,0:T(8,128)S(1)} %get-tuple-element.82.refs_1_, f32[256,384]{1,0:T(8,128)S(1)} %get-tuple-element.83.refs_2_, bf16[480,1152]{1,0:T(8,128)(2,1)S(1)} %get-tuple-element.59.refs_1_.refs_2_.refs_4_.refs_3_, ...), custom_call_target="tpu_custom_call" | custom-call | flops 100000000 | bytes 10000 | tf_op jit(solution)/shard_map/key/pallas_call | solution.py:142
  25.3 0.3 collective-permute-done.8.refs_2_
  25.7 0.0 collective-permute-done.13.refs_6_
  25.7 0.2 collective-permute-start.14
  25.9 1.5 %collective-permute-start.11 = (bf16[96,384]{1,0:T(8,128)(2,1)S(1)}, bf16[96,384]{1,0:T(8,128)(2,1)S(1)}, u32[]{:S(2)}, u32[]{:S(2)}) collective-permute-start(bf16[96,384]{1,0:T(8,128)(2,1)S(1)} %get-tuple-element.88.refs_3_), channel_id=1, source_target_pairs={{0,4},{1,7},{2,6},{3,5},{4,0},{5,3},{6,2},{7,1},{8,12},{9,15},{10,... | collective-permute-start | bytes 221192 | tf_op jit(solution)/shard_map/ppermute | solution.py:514
  27.4 1.0 %collective-permute-start.15 = (bf16[48,384]{1,0:T(8,128)(2,1)S(1)}, bf16[48,384]{1,0:T(8,128)(2,1)S(1)}, u32[]{:S(2)}, u32[]{:S(2)}) collective-permute-start(bf16[48,384]{1,0:T(8,128)(2,1)S(1)} %get-tuple-element.103), channel_id=1, source_target_pairs={{0,2},{1,3},{2,0},{3,1},{4,6},{5,7},{6,4},{7,5},{8,10},{9,11},{10,... | collective-permute-start | bytes 110600 | tf_op jit(solution)/shard_map/ppermute | solution.py:510
  28.4 0.7 %far.1.refs_0_ = bf16[256,384]{1,0:T(8,128)(2,1)S(1)} custom-call(f32[16,128]{1,0:T(8,128)S(1)} %get-tuple-element.56.refs_0_.refs_1_, f32[256,384]{1,0:T(8,128)S(1)} %get-tuple-element.94.refs_1_, bf16[128,768]{1,0:T(8,128)(2,1)S(1)} %get-tuple-element.95.refs_2_, bf16[64,768]{1,0:T(8,128)(2,1)S(1)} %get-tuple-element.96.refs_3_, ...), custom_call_target="tpu_custom_call" | custom-call | flops 100000000 | bytes 10000 | tf_op jit(solution)/shard_map/far/pallas_call | solution.py:142
  29.1 0.0 collective-permute-done.12.refs_5_
  29.1 0.0 collective-permute-done.14.refs_7_
  29.2 0.8 %key.3 = (bf16[256,384]{1,0:T(8,128)(2,1)S(1)}, bf16[256,384]{1,0:T(8,128)(2,1)S(1)}) custom-call(f32[16,128]{1,0:T(8,128)S(1)} %get-tuple-element.56.refs_0_.refs_1_, f32[256,384]{1,0:T(8,128)S(1)} %get-tuple-element.89.refs_1_, f32[256,384]{1,0:T(8,128)S(1)} %get-tuple-element.90.refs_2_, ...), custom_call_target="tpu_custom_call" | custom-call | flops 100000000 | bytes 10000 | tf_op jit(solution)/shard_map/key/pallas_call | solution.py:142
  30.0 0.9 %collective-permute-done.11.refs_0_ = bf16[96,384]{1,0:T(8,128)(2,1)S(1)} collective-permute-done((bf16[96,384]{1,0:T(8,128)(2,1)S(1)}, bf16[96,384]{1,0:T(8,128)(2,1)S(1)}, u32[]{:S(2)}, u32[]{:S(2)}) %collective-permute-start.11) | collective-permute-done | bytes 73760 | tf_op jit(solution)/shard_map/ppermute | solution.py:514
  30.9 0.8 %collective-permute-done.15.refs_1_ = bf16[48,384]{1,0:T(8,128)(2,1)S(1)} collective-permute-done((bf16[48,384]{1,0:T(8,128)(2,1)S(1)}, bf16[48,384]{1,0:T(8,128)(2,1)S(1)}, u32[]{:S(2)}, u32[]{:S(2)}) %collective-permute-start.15) | collective-permute-done | bytes 36896 | tf_op jit(solution)/shard_map/ppermute | solution.py:510
  31.7 0.1 collective-permute-start.16
  31.7 0.8 %flush.1 = (bf16[256,384]{1,0:T(8,128)(2,1)}, bf16[256,384]{1,0:T(8,128)(2,1)}, bf16[256,384]{1,0:T(8,128)(2,1)}) custom-call(bf16[256,384]{1,0:T(8,128)(2,1)S(1)} %far.1.refs_0_, bf16[256,384]{1,0:T(8,128)(2,1)S(1)} %get-tuple-element.99.refs_1_, bf16[256,384]{1,0:T(8,128)(2,1)S(1)} %get-tuple-element.100.refs_2_), custom_call_target="tpu_custom_call" | custom-call | flops 1 | bytes 10000 | tf_op jit(solution)/shard_map/flush/pallas_call | solution.py:142
  32.6 0.5 %collective-permute-done.16.refs_2_ = bf16[144,384]{1,0:T(8,128)(2,1)S(1)} collective-permute-done((bf16[144,384]{1,0:T(8,128)(2,1)S(1)}, bf16[144,384]{1,0:T(8,128)(2,1)S(1)}, u32[]{:S(2)}, u32[]{:S(2)}) %collective-permute-start.16) | collective-permute-done | bytes 110624 | tf_op jit(solution)/shard_map/ppermute | solution.py:510
  33.0 0.7 %weight_out.1 = f32[96,384]{1,0:T(8,128)} custom-call(s32[1]{0:T(128)} %bitcast.refs_0_, bf16[144,384]{1,0:T(8,128)(2,1)S(1)} %plane_rows.1.refs_1_, bf16[144,384]{1,0:T(8,128)(2,1)S(1)} %collective-permute-done.16.refs_2_, bf16[96,384]{1,0:T(8,128)(2,1)S(1)} %get-tuple-element.88.refs_3_), custom_call_target="tpu_custom_call" | custom-call | flops 1 | bytes 10000 | tf_op jit(solution)/shard_map/weight_out/pallas_call | solution.py:142
  (9 shorter events, 0.1 us)
Async XLA Ops:
  2.3 3.1 %collective-permute-start = (bf16[160,768]{1,0:T(8,128)(2,1)S(1)}, bf16[160,768]{1,0:T(8,128)(2,1)S(1)}, u32[]{:S(2)}, u32[]{:S(2)}) collective-permute-start(bf16[160,768]{1,0:T(8,128)(2,1)S(1)} %get-tuple-element.57.refs_0_), channel_id=1, source_target_pairs={{0,1},{1,0},{2,3},{3,2},{4,5},{5,4},{6,7},{7,6},{8,9},{9,8},{10,11... | collective-permute-start | bytes 737288 | tf_op jit(solution)/shard_map/ppermute | solution.py:510
  2.9 7.0 %collective-permute-start.3 = (bf16[64,768]{1,0:T(8,128)(2,1)S(1)}, bf16[64,768]{1,0:T(8,128)(2,1)S(1)}, u32[]{:S(2)}, u32[]{:S(2)}) collective-permute-start(bf16[64,768]{1,0:T(8,128)(2,1)S(1)} %get-tuple-element.58), channel_id=1, source_target_pairs={{0,2},{1,3},{2,0},{3,1},{4,6},{5,7},{6,4},{7,5},{8,10},{9,11},{10,... | collective-permute-start | bytes 294920 | tf_op jit(solution)/shard_map/ppermute | solution.py:510
  5.5 5.7 %collective-permute-start.1 = (bf16[64,768]{1,0:T(8,128)(2,1)S(1)}, bf16[64,768]{1,0:T(8,128)(2,1)S(1)}, u32[]{:S(2)}, u32[]{:S(2)}) collective-permute-start(bf16[64,768]{1,0:T(8,128)(2,1)S(1)} %third_rows.1), channel_id=1, source_target_pairs={{0,4},{1,7},{2,6},{3,5},{4,0},{5,3},{6,2},{7,1},{8,12},{9,15},{10,... | collective-permute-start | bytes 294920 | tf_op jit(solution)/shard_map/ppermute | solution.py:514
  8.5 0.9 %copy-start = (bf16[256,1536]{1,0:T(8,128)(2,1)}, bf16[256,1536]{1,0:T(8,128)(2,1)S(1)}, u32[]{:S(2)}) copy-start(bf16[256,1536]{1,0:T(8,128)(2,1)S(1)} %get-tuple-element.76.refs_3_) | copy-start | bytes 2359300
  9.9 1.7 %collective-permute-start.4 = (bf16[64,768]{1,0:T(8,128)(2,1)S(1)}, bf16[64,768]{1,0:T(8,128)(2,1)S(1)}, u32[]{:S(2)}, u32[]{:S(2)}) collective-permute-start(bf16[64,768]{1,0:T(8,128)(2,1)S(1)} %collective-permute-done.3.refs_3_.refs_8_), channel_id=1, source_target_pairs={{0,1},{1,0},{2,3},{3,2},{4,5},{5,4},{6,7},{7,6},{8,9},{9,8},{10,11... | collective-permute-start | bytes 294920 | tf_op jit(solution)/shard_map/ppermute | solution.py:510
  11.2 1.3 %collective-permute-start.2 = (bf16[64,768]{1,0:T(8,128)(2,1)S(1)}, bf16[64,768]{1,0:T(8,128)(2,1)S(1)}, u32[]{:S(2)}, u32[]{:S(2)}) collective-permute-start(bf16[64,768]{1,0:T(8,128)(2,1)S(1)} %collective-permute-done.1.refs_5_.refs_10_), channel_id=1, source_target_pairs={{0,1},{1,0},{2,3},{3,2},{4,5},{5,4},{6,7},{7,6},{8,9},{9,8},{10,11... | collective-permute-start | bytes 294920 | tf_op jit(solution)/shard_map/ppermute | solution.py:510
  13.8 7.9 %copy-start.1 = (bf16[256,1536]{1,0:T(8,128)(2,1)S(1)}, bf16[256,1536]{1,0:T(8,128)(2,1)}, u32[]{:S(2)}) copy-start(bf16[256,1536]{1,0:T(8,128)(2,1)} %copy-done) | copy-start | bytes 2359300
  14.0 6.1 %collective-permute-start.10 = (bf16[160,896]{1,0:T(8,128)(2,1)S(1)}, bf16[160,896]{1,0:T(8,128)(2,1)S(1)}, u32[]{:S(2)}, u32[]{:S(2)}) collective-permute-start(bf16[160,896]{1,0:T(8,128)(2,1)S(1)} %get-tuple-element.84.refs_0_.refs_5_), channel_id=1, source_target_pairs={{0,1},{1,0},{2,3},{3,2},{4,5},{5,4},{6,7},{7,6},{8,9},{9,8},{10,11... | collective-permute-start | bytes 860168 | tf_op jit(solution)/shard_map/ppermute | solution.py:510
  14.2 1.6 %collective-permute-start.5 = (bf16[144,384]{1,0:T(8,128)(2,1)S(1)}, bf16[144,384]{1,0:T(8,128)(2,1)S(1)}, u32[]{:S(2)}, u32[]{:S(2)}) collective-permute-start(bf16[144,384]{1,0:T(8,128)(2,1)S(1)} %get-tuple-element.70), channel_id=1, source_target_pairs={{0,1},{1,0},{2,3},{3,2},{4,5},{5,4},{6,7},{7,6},{8,9},{9,8},{10,11... | collective-permute-start | bytes 331784 | tf_op jit(solution)/shard_map/ppermute | solution.py:510
  14.6 9.7 %collective-permute-start.9 = (bf16[64,896]{1,0:T(8,128)(2,1)S(1)}, bf16[64,896]{1,0:T(8,128)(2,1)S(1)}, u32[]{:S(2)}, u32[]{:S(2)}) collective-permute-start(bf16[64,896]{1,0:T(8,128)(2,1)S(1)} %get-tuple-element.80.refs_6_), channel_id=1, source_target_pairs={{0,2},{1,3},{2,0},{3,1},{4,6},{5,7},{6,4},{7,5},{8,10},{9,11},{10,... | collective-permute-start | bytes 344072 | tf_op jit(solution)/shard_map/ppermute | solution.py:510
  15.8 6.9 %collective-permute-start.7 = (bf16[48,384]{1,0:T(8,128)(2,1)S(1)}, bf16[48,384]{1,0:T(8,128)(2,1)S(1)}, u32[]{:S(2)}, u32[]{:S(2)}) collective-permute-start(bf16[48,384]{1,0:T(8,128)(2,1)S(1)} %get-tuple-element.72), channel_id=1, source_target_pairs={{0,8},{1,9},{2,10},{3,11},{4,12},{5,13},{6,14},{7,15},{8,0},{9,1},... | collective-permute-start | bytes 110600 | tf_op jit(solution)/shard_map/ppermute | solution.py:528
  17.5 6.7 %collective-permute-start.6 = (bf16[96,384]{1,0:T(8,128)(2,1)S(1)}, bf16[96,384]{1,0:T(8,128)(2,1)S(1)}, u32[]{:S(2)}, u32[]{:S(2)}) collective-permute-start(bf16[96,384]{1,0:T(8,128)(2,1)S(1)} %get-tuple-element.71), channel_id=1, source_target_pairs={{0,16},{1,25},{2,18},{3,27},{4,20},{5,29},{6,22},{7,31},{8,24},{9,... | collective-permute-start | bytes 221192 | tf_op jit(solution)/shard_map/ppermute | solution.py:528
  20.1 5.6 %collective-permute-start.13 = (bf16[64,896]{1,0:T(8,128)(2,1)S(1)}, bf16[64,896]{1,0:T(8,128)(2,1)S(1)}, u32[]{:S(2)}, u32[]{:S(2)}) collective-permute-start(bf16[64,896]{1,0:T(8,128)(2,1)S(1)} %third_grads.1), channel_id=1, source_target_pairs={{0,4},{1,7},{2,6},{3,5},{4,0},{5,3},{6,2},{7,1},{8,12},{9,15},{10,... | collective-permute-start | bytes 344072 | tf_op jit(solution)/shard_map/ppermute | solution.py:514
  24.2 1.4 %collective-permute-start.8 = (bf16[144,384]{1,0:T(8,128)(2,1)S(1)}, bf16[144,384]{1,0:T(8,128)(2,1)S(1)}, u32[]{:S(2)}, u32[]{:S(2)}) collective-permute-start(bf16[144,384]{1,0:T(8,128)(2,1)S(1)} %layer_sum.1.refs_1_), channel_id=1, source_target_pairs={{0,1},{1,0},{2,3},{3,2},{4,5},{5,4},{6,7},{7,6},{8,9},{9,8},{10,11... | collective-permute-start | bytes 331784 | tf_op jit(solution)/shard_map/ppermute | solution.py:510
  24.3 4.8 %collective-permute-start.12 = (bf16[64,896]{1,0:T(8,128)(2,1)S(1)}, bf16[64,896]{1,0:T(8,128)(2,1)S(1)}, u32[]{:S(2)}, u32[]{:S(2)}) collective-permute-start(bf16[64,896]{1,0:T(8,128)(2,1)S(1)} %collective-permute-done.9.refs_4_), channel_id=1, source_target_pairs={{0,1},{1,0},{2,3},{3,2},{4,5},{5,4},{6,7},{7,6},{8,9},{9,8},{10,11... | collective-permute-start | bytes 344072 | tf_op jit(solution)/shard_map/ppermute | solution.py:510
  25.7 3.4 %collective-permute-start.14 = (bf16[64,896]{1,0:T(8,128)(2,1)S(1)}, bf16[64,896]{1,0:T(8,128)(2,1)S(1)}, u32[]{:S(2)}, u32[]{:S(2)}) collective-permute-start(bf16[64,896]{1,0:T(8,128)(2,1)S(1)} %collective-permute-done.13.refs_6_), channel_id=1, source_target_pairs={{0,1},{1,0},{2,3},{3,2},{4,5},{5,4},{6,7},{7,6},{8,9},{9,8},{10,11... | collective-permute-start | bytes 344072 | tf_op jit(solution)/shard_map/ppermute | solution.py:510
  25.9 4.9 %collective-permute-start.11 = (bf16[96,384]{1,0:T(8,128)(2,1)S(1)}, bf16[96,384]{1,0:T(8,128)(2,1)S(1)}, u32[]{:S(2)}, u32[]{:S(2)}) collective-permute-start(bf16[96,384]{1,0:T(8,128)(2,1)S(1)} %get-tuple-element.88.refs_3_), channel_id=1, source_target_pairs={{0,4},{1,7},{2,6},{3,5},{4,0},{5,3},{6,2},{7,1},{8,12},{9,15},{10,... | collective-permute-start | bytes 221192 | tf_op jit(solution)/shard_map/ppermute | solution.py:514
  27.4 4.2 %collective-permute-start.15 = (bf16[48,384]{1,0:T(8,128)(2,1)S(1)}, bf16[48,384]{1,0:T(8,128)(2,1)S(1)}, u32[]{:S(2)}, u32[]{:S(2)}) collective-permute-start(bf16[48,384]{1,0:T(8,128)(2,1)S(1)} %get-tuple-element.103), channel_id=1, source_target_pairs={{0,2},{1,3},{2,0},{3,1},{4,6},{5,7},{6,4},{7,5},{8,10},{9,11},{10,... | collective-permute-start | bytes 110600 | tf_op jit(solution)/shard_map/ppermute | solution.py:510
  31.7 1.4 %collective-permute-start.16 = (bf16[144,384]{1,0:T(8,128)(2,1)S(1)}, bf16[144,384]{1,0:T(8,128)(2,1)S(1)}, u32[]{:S(2)}, u32[]{:S(2)}) collective-permute-start(bf16[144,384]{1,0:T(8,128)(2,1)S(1)} %plane_rows.1.refs_1_), channel_id=1, source_target_pairs={{0,1},{1,0},{2,3},{3,2},{4,5},{5,4},{6,7},{7,6},{8,9},{9,8},{10,11... | collective-permute-start | bytes 331784 | tf_op jit(solution)/shard_map/ppermute | solution.py:510

commit v7 on v6

--- a/solution.py
+++ b/solution.py
@@ -628,7 +628,7 @@
     layer = lax.axis_index("dp").astype(jnp.int32)
     if paired:
         core = lax.axis_index(SEQ).astype(jnp.int32) % 2
-        place = jnp.stack([layer, layer ^ (2 + core), layer ^ (3 - core), layer ^ 1, core * half])
+        place = jnp.stack([layer, layer ^ (1 + 2 * core), layer ^ (3 - 2 * core), layer ^ 2, core * half])
         grad_places = [(0, 0), (1, 0), (2, 0), (1, sizes[1])]
         grad_shapes = [(rows, wide), (sizes[1] + sizes[3], wide + width), (sizes[2], wide + width)]
         pieces = [
@@ -714,8 +714,8 @@
         )
         near_in = traded(near, 1)
         far_in = traded(far, 2)
-        layer_one = layer_traded(send_one, 2, 3)
-        layer_half = layer_traded(send_half, 1, 1)
+        layer_one = layer_traded(send_one, 1, 3)
+        layer_half = layer_traded(send_half, 2, 2)
         (third,) = placed(
             "third_grads",
             [((2 * sizes[3], wide + width), BF)],

time: 33.9 us -> 33.3 us (0.982)
  waiting for transfers between devices: 5.71 us -> 5.25 us
    ppermute x2, waiting for transfers between devices: 1.49 us -> 0.13 us  [layer_traded(): return lax.ppermute(value, axes, pairs)]
    ppermute x3, waiting for transfers between devices: 1.49 us -> 2.22 us  [split_traded(): lax.ppermute(value, SEQ, [(source, source ^ 2 * (second if source % 2 els...]
  transfers between devices with their start and end apart: 17 -> 17, of which waited for: 9 -> 10; matrix products, arithmetic and copies ran while one was open for 0% -> 0% of each run, Pallas kernels for 19% -> 19%
where the time goes in v7:
time: 33.3 us; the launch traced here: 33.2 us
  starting transfers between devices  15.9 us (48%)
  Pallas kernels  10.2 us (31%)
  waiting for transfers between devices  5.25 us (16%)
  local copies, waits for them, and re-layouts  0.98 us (3%)
  between operations  0.79 us (2%)
    pallas_call x18, Pallas kernels, call(): pl.pallas_call(body, out_shape=[jax.ShapeDtypeStruct(shape, kind) for sha...  10.2 us
    ppermute x12, starting transfers between devices, traded(): lax.ppermute(value, SEQ, [(source, source ^ mask) for source in range(lax...  7.09 us
    ppermute x3, starting transfers between devices, split_traded(): lax.ppermute(value, SEQ, [(source, source ^ 2 * (second if source % 2 els...  4.6 us
    ppermute x2, starting transfers between devices, layer_traded(): return lax.ppermute(value, axes, pairs)  4.23 us
    ppermute x12, waiting for transfers between devices, traded(): lax.ppermute(value, SEQ, [(source, source ^ mask) for source in range(lax...  2.89 us
    ppermute x3, waiting for transfers between devices, split_traded(): lax.ppermute(value, SEQ, [(source, source ^ 2 * (second if source % 2 els...  2.22 us
    unnamed x4, local copies, waits for them, and re-layouts  0.9 us
  transfers between devices with their start and end apart: 17, of which 10 were waited for; matrix products, arithmetic and copies ran while one was open for 0% of the time, Pallas kernels for 19%

profile of v7, /device:TPU:0, one launch (start us, length us, event | category | flops | bytes accessed | tf_op | source)
XLA Modules:
  0.0 33.2 jit_solution(1686579580174675518)
XLA Ops:
  0.6 1.7 %pool.1 = (f32[16,128]{1,0:T(8,128)S(1)}, bf16[480,1152]{1,0:T(8,128)(2,1)S(1)}, bf16[160,768]{1,0:T(8,128)(2,1)S(1)}, bf16[64,768]{1,0:T(8,128)(2,1)S(1)}) custom-call(bf16[256,384]{1,0:T(8,128)(2,1)} %bitcast.14, bf16[256,384]{1,0:T(8,128)(2,1)} %bitcast.15, bf16[256,384]{1,0:T(8,128)(2,1)} %bitcast.16, f32[6]{0:T(128)} %refs_3_.2), custom_call_target="tpu_custom_call" | custom-call | flops 1 | bytes 10000 | tf_op jit(solution)/shard_map/pool/pallas_call | solution.py:142
  2.3 0.5 %collective-permute-start = (bf16[160,768]{1,0:T(8,128)(2,1)S(1)}, bf16[160,768]{1,0:T(8,128)(2,1)S(1)}, u32[]{:S(2)}, u32[]{:S(2)}) collective-permute-start(bf16[160,768]{1,0:T(8,128)(2,1)S(1)} %get-tuple-element.57.refs_0_), channel_id=1, source_target_pairs={{0,1},{1,0},{2,3},{3,2},{4,5},{5,4},{6,7},{7,6},{8,9},{9,8},{10,11... | collective-permute-start | bytes 737288 | tf_op jit(solution)/shard_map/ppermute | solution.py:510
  2.9 2.6 %collective-permute-start.3 = (bf16[64,768]{1,0:T(8,128)(2,1)S(1)}, bf16[64,768]{1,0:T(8,128)(2,1)S(1)}, u32[]{:S(2)}, u32[]{:S(2)}) collective-permute-start(bf16[64,768]{1,0:T(8,128)(2,1)S(1)} %get-tuple-element.58), channel_id=1, source_target_pairs={{0,2},{1,3},{2,0},{3,1},{4,6},{5,7},{6,4},{7,5},{8,10},{9,11},{10,... | collective-permute-start | bytes 294920 | tf_op jit(solution)/shard_map/ppermute | solution.py:510
  5.5 0.0 collective-permute-done.refs_1_.refs_3_.refs_7_
  5.5 1.6 %collective-permute-start.1 = (bf16[64,768]{1,0:T(8,128)(2,1)S(1)}, bf16[64,768]{1,0:T(8,128)(2,1)S(1)}, u32[]{:S(2)}, u32[]{:S(2)}) collective-permute-start(bf16[64,768]{1,0:T(8,128)(2,1)S(1)} %third_rows.1), channel_id=1, source_target_pairs={{0,4},{1,7},{2,6},{3,5},{4,0},{5,3},{6,2},{7,1},{8,12},{9,15},{10,... | collective-permute-start | bytes 294920 | tf_op jit(solution)/shard_map/ppermute | solution.py:514
  7.0 1.5 %base.1 = (f32[256,768]{1,0:T(8,128)S(1)}, bf16[256,1536]{1,0:T(8,128)(2,1)S(1)}, bf16[256,768]{1,0:T(8,128)(2,1)S(1)}) custom-call(f32[16,128]{1,0:T(8,128)S(1)} %get-tuple-element.56.refs_0_.refs_1_, bf16[480,1152]{1,0:T(8,128)(2,1)S(1)} %get-tuple-element.59.refs_1_.refs_2_.refs_4_.refs_3_, bf16[256,384]{1,0:T(8,128)(2,1)} %bitcast.13, ...), custom_call_target="tpu_custom_call" | custom-call | flops 100000000 | bytes 10000 | tf_op jit(solution)/shard_map/base/pallas_call | solution.py:142
  8.5 0.9 %copy-done = bf16[256,1536]{1,0:T(8,128)(2,1)} copy-done((bf16[256,1536]{1,0:T(8,128)(2,1)}, bf16[256,1536]{1,0:T(8,128)(2,1)S(1)}, u32[]{:S(2)}) %copy-start) | copy-done | bytes 786456
  9.4 0.4 %level.2 = (bf16[128,768]{1,0:T(8,128)(2,1)S(1)}, f32[256,768]{1,0:T(8,128)S(1)}) custom-call(f32[16,128]{1,0:T(8,128)S(1)} %get-tuple-element.56.refs_0_.refs_1_, f32[256,768]{1,0:T(8,128)S(1)} %get-tuple-element.60.refs_1_, bf16[480,1152]{1,0:T(8,128)(2,1)S(1)} %get-tuple-element.59.refs_1_.refs_2_.refs_4_.refs_3_, ...), custom_call_target="tpu_custom_call" | custom-call | flops 25000000 | bytes 10000 | tf_op jit(solution)/shard_map/level/pallas_call | solution.py:142
  9.8 0.0 collective-permute-done.3.refs_3_.refs_8_
  9.9 0.7 %collective-permute-start.4 = (bf16[64,768]{1,0:T(8,128)(2,1)S(1)}, bf16[64,768]{1,0:T(8,128)(2,1)S(1)}, u32[]{:S(2)}, u32[]{:S(2)}) collective-permute-start(bf16[64,768]{1,0:T(8,128)(2,1)S(1)} %collective-permute-done.3.refs_3_.refs_8_), channel_id=1, source_target_pairs={{0,1},{1,0},{2,3},{3,2},{4,5},{5,4},{6,7},{7,6},{8,9},{9,8},{10,11... | collective-permute-start | bytes 294920 | tf_op jit(solution)/shard_map/ppermute | solution.py:510
  10.6 0.6 %collective-permute-done.1.refs_5_.refs_10_ = bf16[64,768]{1,0:T(8,128)(2,1)S(1)} collective-permute-done((bf16[64,768]{1,0:T(8,128)(2,1)S(1)}, bf16[64,768]{1,0:T(8,128)(2,1)S(1)}, u32[]{:S(2)}, u32[]{:S(2)}) %collective-permute-start.1) | collective-permute-done | bytes 98336 | tf_op jit(solution)/shard_map/ppermute | solution.py:514
  11.2 0.0 collective-permute-start.2
  11.2 0.1 stack.23.refs_0_
  11.3 0.3 collective-permute-done.4.refs_4_.refs_9_
  11.5 0.4 %level.3 = (bf16[64,768]{1,0:T(8,128)(2,1)S(1)}, f32[256,768]{1,0:T(8,128)S(1)}) custom-call(f32[16,128]{1,0:T(8,128)S(1)} %get-tuple-element.56.refs_0_.refs_1_, f32[256,768]{1,0:T(8,128)S(1)} %get-tuple-element.62.refs_1_, bf16[480,1152]{1,0:T(8,128)(2,1)S(1)} %get-tuple-element.59.refs_1_.refs_2_.refs_4_.refs_3_, ...), custom_call_target="tpu_custom_call" | custom-call | flops 25000000 | bytes 10000 | tf_op jit(solution)/shard_map/level/pallas_call | solution.py:142
  11.9 0.6 %collective-permute-done.2.refs_6_.refs_11_ = bf16[64,768]{1,0:T(8,128)(2,1)S(1)} collective-permute-done((bf16[64,768]{1,0:T(8,128)(2,1)S(1)}, bf16[64,768]{1,0:T(8,128)(2,1)S(1)}, u32[]{:S(2)}, u32[]{:S(2)}) %collective-permute-start.2) | collective-permute-done | bytes 98336 | tf_op jit(solution)/shard_map/ppermute | solution.py:510
  12.5 1.3 %forward.1 = (bf16[32,768]{1,0:T(8,128)(2,1)S(1)}, f32[256,384]{1,0:T(8,128)S(1)}, f32[256,384]{1,0:T(8,128)S(1)}, bf16[96,384]{1,0:T(8,128)(2,1)S(1)}, bf16[144...) custom-call(s32[5]{0:T(128)S(1)} %stack.23.refs_0_, f32[16,128]{1,0:T(8,128)S(1)} %get-tuple-element.56.refs_0_.refs_1_, ...), custom_call_target="tpu_custom_call" | custom-call | flops 1 | bytes 10000 | tf_op jit(solution)/shard_map/forward/pallas_call | solution.py:142
  13.8 0.2 grads.1
  14.0 0.2 collective-permute-start.10
  14.2 0.4 %collective-permute-start.5 = (bf16[144,384]{1,0:T(8,128)(2,1)S(1)}, bf16[144,384]{1,0:T(8,128)(2,1)S(1)}, u32[]{:S(2)}, u32[]{:S(2)}) collective-permute-start(bf16[144,384]{1,0:T(8,128)(2,1)S(1)} %get-tuple-element.70), channel_id=1, source_target_pairs={{0,1},{1,0},{2,3},{3,2},{4,5},{5,4},{6,7},{7,6},{8,9},{9,8},{10,11... | collective-permute-start | bytes 331784 | tf_op jit(solution)/shard_map/ppermute | solution.py:510
  14.6 0.9 %collective-permute-start.9 = (bf16[64,896]{1,0:T(8,128)(2,1)S(1)}, bf16[64,896]{1,0:T(8,128)(2,1)S(1)}, u32[]{:S(2)}, u32[]{:S(2)}) collective-permute-start(bf16[64,896]{1,0:T(8,128)(2,1)S(1)} %get-tuple-element.80.refs_6_), channel_id=1, source_target_pairs={{0,2},{1,3},{2,0},{3,1},{4,6},{5,7},{6,4},{7,5},{8,10},{9,11},{10,... | collective-permute-start | bytes 344072 | tf_op jit(solution)/shard_map/ppermute | solution.py:510
  15.5 0.3 collective-permute-done.5.refs_1_
  15.8 2.7 %collective-permute-start.7 = (bf16[48,384]{1,0:T(8,128)(2,1)S(1)}, bf16[48,384]{1,0:T(8,128)(2,1)S(1)}, u32[]{:S(2)}, u32[]{:S(2)}) collective-permute-start(bf16[48,384]{1,0:T(8,128)(2,1)S(1)} %get-tuple-element.72), channel_id=1, source_target_pairs={{0,16},{1,17},{2,18},{3,19},{4,20},{5,21},{6,22},{7,23},{8,24},{9,... | collective-permute-start | bytes 110600 | tf_op jit(solution)/shard_map/ppermute | solution.py:528
  18.5 1.6 %collective-permute-start.6 = (bf16[96,384]{1,0:T(8,128)(2,1)S(1)}, bf16[96,384]{1,0:T(8,128)(2,1)S(1)}, u32[]{:S(2)}, u32[]{:S(2)}) collective-permute-start(bf16[96,384]{1,0:T(8,128)(2,1)S(1)} %get-tuple-element.71), channel_id=1, source_target_pairs={{0,8},{1,25},{2,10},{3,27},{4,12},{5,29},{6,14},{7,31},{8,0},{9,17... | collective-permute-start | bytes 221192 | tf_op jit(solution)/shard_map/ppermute | solution.py:528
  20.1 0.0 collective-permute-done.10.refs_4_.refs_1_
  20.1 1.6 %collective-permute-start.13 = (bf16[64,896]{1,0:T(8,128)(2,1)S(1)}, bf16[64,896]{1,0:T(8,128)(2,1)S(1)}, u32[]{:S(2)}, u32[]{:S(2)}) collective-permute-start(bf16[64,896]{1,0:T(8,128)(2,1)S(1)} %third_grads.1), channel_id=1, source_target_pairs={{0,4},{1,7},{2,6},{3,5},{4,0},{5,3},{6,2},{7,1},{8,12},{9,15},{10,... | collective-permute-start | bytes 344072 | tf_op jit(solution)/shard_map/ppermute | solution.py:514
  21.7 1.1 %near.1 = (f32[256,384]{1,0:T(8,128)S(1)}, f32[256,384]{1,0:T(8,128)S(1)}, f32[256,384]{1,0:T(8,128)S(1)}) custom-call(f32[16,128]{1,0:T(8,128)S(1)} %get-tuple-element.56.refs_0_.refs_1_, bf16[480,1152]{1,0:T(8,128)(2,1)S(1)} %get-tuple-element.59.refs_1_.refs_2_.refs_4_.refs_3_, bf16[256,512]{1,0:T(8,128)(2,1)S(1)} %get-tuple-element.75.refs_2_, ...), custom_call_target="tpu_custom_call" | custom-call | flops 1600000000 | bytes 10000 | tf_op jit(solution)/shard_map/near/pallas_call | solution.py:142
  22.7 0.0 collective-permute-done.7.refs_2_
  22.7 0.1 collective-permute-done.6.refs_1_
  22.9 0.7 %collective-permute-start.8 = (bf16[144,384]{1,0:T(8,128)(2,1)S(1)}, bf16[144,384]{1,0:T(8,128)(2,1)S(1)}, u32[]{:S(2)}, u32[]{:S(2)}) collective-permute-start(bf16[144,384]{1,0:T(8,128)(2,1)S(1)} %layer_sum.1.refs_1_), channel_id=1, source_target_pairs={{0,1},{1,0},{2,3},{3,2},{4,5},{5,4},{6,7},{7,6},{8,9},{9,8},{10,11... | collective-permute-start | bytes 331784 | tf_op jit(solution)/shard_map/ppermute | solution.py:510
  23.6 0.0 collective-permute-done.9.refs_4_
  23.6 0.1 collective-permute-start.12
  23.6 0.5 %key.2 = (f32[256,384]{1,0:T(8,128)S(1)}, f32[256,384]{1,0:T(8,128)S(1)}) custom-call(f32[16,128]{1,0:T(8,128)S(1)} %get-tuple-element.56.refs_0_.refs_1_, f32[256,384]{1,0:T(8,128)S(1)} %get-tuple-element.82.refs_1_, f32[256,384]{1,0:T(8,128)S(1)} %get-tuple-element.83.refs_2_, bf16[480,1152]{1,0:T(8,128)(2,1)S(1)} %get-tuple-element.59.refs_1_.refs_2_.refs_4_.refs_3_, ...), custom_call_target="tpu_custom_call" | custom-call | flops 100000000 | bytes 10000 | tf_op jit(solution)/shard_map/key/pallas_call | solution.py:142
  24.1 0.4 %collective-permute-done.8.refs_2_ = bf16[144,384]{1,0:T(8,128)(2,1)S(1)} collective-permute-done((bf16[144,384]{1,0:T(8,128)(2,1)S(1)}, bf16[144,384]{1,0:T(8,128)(2,1)S(1)}, u32[]{:S(2)}, u32[]{:S(2)}) %collective-permute-start.8) | collective-permute-done | bytes 110624 | tf_op jit(solution)/shard_map/ppermute | solution.py:510
  24.6 0.6 %collective-permute-done.13.refs_6_ = bf16[64,896]{1,0:T(8,128)(2,1)S(1)} collective-permute-done((bf16[64,896]{1,0:T(8,128)(2,1)S(1)}, bf16[64,896]{1,0:T(8,128)(2,1)S(1)}, u32[]{:S(2)}, u32[]{:S(2)}) %collective-permute-start.13) | collective-permute-done | bytes 114720 | tf_op jit(solution)/shard_map/ppermute | solution.py:514
  25.2 0.0 collective-permute-start.14
  25.2 1.5 %collective-permute-start.11 = (bf16[96,384]{1,0:T(8,128)(2,1)S(1)}, bf16[96,384]{1,0:T(8,128)(2,1)S(1)}, u32[]{:S(2)}, u32[]{:S(2)}) collective-permute-start(bf16[96,384]{1,0:T(8,128)(2,1)S(1)} %get-tuple-element.88.refs_3_), channel_id=1, source_target_pairs={{0,4},{1,7},{2,6},{3,5},{4,0},{5,3},{6,2},{7,1},{8,12},{9,15},{10,... | collective-permute-start | bytes 221192 | tf_op jit(solution)/shard_map/ppermute | solution.py:514
  26.6 0.9 %collective-permute-start.15 = (bf16[48,384]{1,0:T(8,128)(2,1)S(1)}, bf16[48,384]{1,0:T(8,128)(2,1)S(1)}, u32[]{:S(2)}, u32[]{:S(2)}) collective-permute-start(bf16[48,384]{1,0:T(8,128)(2,1)S(1)} %get-tuple-element.103), channel_id=1, source_target_pairs={{0,2},{1,3},{2,0},{3,1},{4,6},{5,7},{6,4},{7,5},{8,10},{9,11},{10,... | collective-permute-start | bytes 110600 | tf_op jit(solution)/shard_map/ppermute | solution.py:510
  27.6 0.7 %far.1.refs_0_ = bf16[256,384]{1,0:T(8,128)(2,1)S(1)} custom-call(f32[16,128]{1,0:T(8,128)S(1)} %get-tuple-element.56.refs_0_.refs_1_, f32[256,384]{1,0:T(8,128)S(1)} %get-tuple-element.94.refs_1_, bf16[128,768]{1,0:T(8,128)(2,1)S(1)} %get-tuple-element.95.refs_2_, bf16[64,768]{1,0:T(8,128)(2,1)S(1)} %get-tuple-element.96.refs_3_, ...), custom_call_target="tpu_custom_call" | custom-call | flops 100000000 | bytes 10000 | tf_op jit(solution)/shard_map/far/pallas_call | solution.py:142
  28.3 0.0 collective-permute-done.12.refs_5_
  28.3 0.0 collective-permute-done.14.refs_7_
  28.3 0.8 %key.3 = (bf16[256,384]{1,0:T(8,128)(2,1)S(1)}, bf16[256,384]{1,0:T(8,128)(2,1)S(1)}) custom-call(f32[16,128]{1,0:T(8,128)S(1)} %get-tuple-element.56.refs_0_.refs_1_, f32[256,384]{1,0:T(8,128)S(1)} %get-tuple-element.89.refs_1_, f32[256,384]{1,0:T(8,128)S(1)} %get-tuple-element.90.refs_2_, ...), custom_call_target="tpu_custom_call" | custom-call | flops 100000000 | bytes 10000 | tf_op jit(solution)/shard_map/key/pallas_call | solution.py:142
  29.1 1.0 %collective-permute-done.11.refs_0_ = bf16[96,384]{1,0:T(8,128)(2,1)S(1)} collective-permute-done((bf16[96,384]{1,0:T(8,128)(2,1)S(1)}, bf16[96,384]{1,0:T(8,128)(2,1)S(1)}, u32[]{:S(2)}, u32[]{:S(2)}) %collective-permute-start.11) | collective-permute-done | bytes 73760 | tf_op jit(solution)/shard_map/ppermute | solution.py:514
  30.2 0.9 %collective-permute-done.15.refs_1_ = bf16[48,384]{1,0:T(8,128)(2,1)S(1)} collective-permute-done((bf16[48,384]{1,0:T(8,128)(2,1)S(1)}, bf16[48,384]{1,0:T(8,128)(2,1)S(1)}, u32[]{:S(2)}, u32[]{:S(2)}) %collective-permute-start.15) | collective-permute-done | bytes 36896 | tf_op jit(solution)/shard_map/ppermute | solution.py:510
  31.1 0.1 collective-permute-start.16
  31.2 0.8 %flush.1 = (bf16[256,384]{1,0:T(8,128)(2,1)}, bf16[256,384]{1,0:T(8,128)(2,1)}, bf16[256,384]{1,0:T(8,128)(2,1)}) custom-call(bf16[256,384]{1,0:T(8,128)(2,1)S(1)} %far.1.refs_0_, bf16[256,384]{1,0:T(8,128)(2,1)S(1)} %get-tuple-element.99.refs_1_, bf16[256,384]{1,0:T(8,128)(2,1)S(1)} %get-tuple-element.100.refs_2_), custom_call_target="tpu_custom_call" | custom-call | flops 1 | bytes 10000 | tf_op jit(solution)/shard_map/flush/pallas_call | solution.py:142
  32.0 0.5 %collective-permute-done.16.refs_2_ = bf16[144,384]{1,0:T(8,128)(2,1)S(1)} collective-permute-done((bf16[144,384]{1,0:T(8,128)(2,1)S(1)}, bf16[144,384]{1,0:T(8,128)(2,1)S(1)}, u32[]{:S(2)}, u32[]{:S(2)}) %collective-permute-start.16) | collective-permute-done | bytes 110624 | tf_op jit(solution)/shard_map/ppermute | solution.py:510
  32.5 0.7 %weight_out.1 = f32[96,384]{1,0:T(8,128)} custom-call(s32[1]{0:T(128)} %bitcast.refs_0_, bf16[144,384]{1,0:T(8,128)(2,1)S(1)} %plane_rows.1.refs_1_, bf16[144,384]{1,0:T(8,128)(2,1)S(1)} %collective-permute-done.16.refs_2_, bf16[96,384]{1,0:T(8,128)(2,1)S(1)} %get-tuple-element.88.refs_3_), custom_call_target="tpu_custom_call" | custom-call | flops 1 | bytes 10000 | tf_op jit(solution)/shard_map/weight_out/pallas_call | solution.py:142
  (9 shorter events, 0.1 us)
Async XLA Ops:
  2.3 3.1 %collective-permute-start = (bf16[160,768]{1,0:T(8,128)(2,1)S(1)}, bf16[160,768]{1,0:T(8,128)(2,1)S(1)}, u32[]{:S(2)}, u32[]{:S(2)}) collective-permute-start(bf16[160,768]{1,0:T(8,128)(2,1)S(1)} %get-tuple-element.57.refs_0_), channel_id=1, source_target_pairs={{0,1},{1,0},{2,3},{3,2},{4,5},{5,4},{6,7},{7,6},{8,9},{9,8},{10,11... | collective-permute-start | bytes 737288 | tf_op jit(solution)/shard_map/ppermute | solution.py:510
  2.9 7.0 %collective-permute-start.3 = (bf16[64,768]{1,0:T(8,128)(2,1)S(1)}, bf16[64,768]{1,0:T(8,128)(2,1)S(1)}, u32[]{:S(2)}, u32[]{:S(2)}) collective-permute-start(bf16[64,768]{1,0:T(8,128)(2,1)S(1)} %get-tuple-element.58), channel_id=1, source_target_pairs={{0,2},{1,3},{2,0},{3,1},{4,6},{5,7},{6,4},{7,5},{8,10},{9,11},{10,... | collective-permute-start | bytes 294920 | tf_op jit(solution)/shard_map/ppermute | solution.py:510
  5.5 5.7 %collective-permute-start.1 = (bf16[64,768]{1,0:T(8,128)(2,1)S(1)}, bf16[64,768]{1,0:T(8,128)(2,1)S(1)}, u32[]{:S(2)}, u32[]{:S(2)}) collective-permute-start(bf16[64,768]{1,0:T(8,128)(2,1)S(1)} %third_rows.1), channel_id=1, source_target_pairs={{0,4},{1,7},{2,6},{3,5},{4,0},{5,3},{6,2},{7,1},{8,12},{9,15},{10,... | collective-permute-start | bytes 294920 | tf_op jit(solution)/shard_map/ppermute | solution.py:514
  8.5 0.9 %copy-start = (bf16[256,1536]{1,0:T(8,128)(2,1)}, bf16[256,1536]{1,0:T(8,128)(2,1)S(1)}, u32[]{:S(2)}) copy-start(bf16[256,1536]{1,0:T(8,128)(2,1)S(1)} %get-tuple-element.76.refs_3_) | copy-start | bytes 2359300
  9.9 1.7 %collective-permute-start.4 = (bf16[64,768]{1,0:T(8,128)(2,1)S(1)}, bf16[64,768]{1,0:T(8,128)(2,1)S(1)}, u32[]{:S(2)}, u32[]{:S(2)}) collective-permute-start(bf16[64,768]{1,0:T(8,128)(2,1)S(1)} %collective-permute-done.3.refs_3_.refs_8_), channel_id=1, source_target_pairs={{0,1},{1,0},{2,3},{3,2},{4,5},{5,4},{6,7},{7,6},{8,9},{9,8},{10,11... | collective-permute-start | bytes 294920 | tf_op jit(solution)/shard_map/ppermute | solution.py:510
  11.2 1.3 %collective-permute-start.2 = (bf16[64,768]{1,0:T(8,128)(2,1)S(1)}, bf16[64,768]{1,0:T(8,128)(2,1)S(1)}, u32[]{:S(2)}, u32[]{:S(2)}) collective-permute-start(bf16[64,768]{1,0:T(8,128)(2,1)S(1)} %collective-permute-done.1.refs_5_.refs_10_), channel_id=1, source_target_pairs={{0,1},{1,0},{2,3},{3,2},{4,5},{5,4},{6,7},{7,6},{8,9},{9,8},{10,11... | collective-permute-start | bytes 294920 | tf_op jit(solution)/shard_map/ppermute | solution.py:510
  13.8 7.9 %copy-start.1 = (bf16[256,1536]{1,0:T(8,128)(2,1)S(1)}, bf16[256,1536]{1,0:T(8,128)(2,1)}, u32[]{:S(2)}) copy-start(bf16[256,1536]{1,0:T(8,128)(2,1)} %copy-done) | copy-start | bytes 2359300
  14.0 6.1 %collective-permute-start.10 = (bf16[160,896]{1,0:T(8,128)(2,1)S(1)}, bf16[160,896]{1,0:T(8,128)(2,1)S(1)}, u32[]{:S(2)}, u32[]{:S(2)}) collective-permute-start(bf16[160,896]{1,0:T(8,128)(2,1)S(1)} %get-tuple-element.84.refs_0_.refs_5_), channel_id=1, source_target_pairs={{0,1},{1,0},{2,3},{3,2},{4,5},{5,4},{6,7},{7,6},{8,9},{9,8},{10,11... | collective-permute-start | bytes 860168 | tf_op jit(solution)/shard_map/ppermute | solution.py:510
  14.2 1.6 %collective-permute-start.5 = (bf16[144,384]{1,0:T(8,128)(2,1)S(1)}, bf16[144,384]{1,0:T(8,128)(2,1)S(1)}, u32[]{:S(2)}, u32[]{:S(2)}) collective-permute-start(bf16[144,384]{1,0:T(8,128)(2,1)S(1)} %get-tuple-element.70), channel_id=1, source_target_pairs={{0,1},{1,0},{2,3},{3,2},{4,5},{5,4},{6,7},{7,6},{8,9},{9,8},{10,11... | collective-permute-start | bytes 331784 | tf_op jit(solution)/shard_map/ppermute | solution.py:510
  14.6 9.0 %collective-permute-start.9 = (bf16[64,896]{1,0:T(8,128)(2,1)S(1)}, bf16[64,896]{1,0:T(8,128)(2,1)S(1)}, u32[]{:S(2)}, u32[]{:S(2)}) collective-permute-start(bf16[64,896]{1,0:T(8,128)(2,1)S(1)} %get-tuple-element.80.refs_6_), channel_id=1, source_target_pairs={{0,2},{1,3},{2,0},{3,1},{4,6},{5,7},{6,4},{7,5},{8,10},{9,11},{10,... | collective-permute-start | bytes 344072 | tf_op jit(solution)/shard_map/ppermute | solution.py:510
  15.8 6.9 %collective-permute-start.7 = (bf16[48,384]{1,0:T(8,128)(2,1)S(1)}, bf16[48,384]{1,0:T(8,128)(2,1)S(1)}, u32[]{:S(2)}, u32[]{:S(2)}) collective-permute-start(bf16[48,384]{1,0:T(8,128)(2,1)S(1)} %get-tuple-element.72), channel_id=1, source_target_pairs={{0,16},{1,17},{2,18},{3,19},{4,20},{5,21},{6,22},{7,23},{8,24},{9,... | collective-permute-start | bytes 110600 | tf_op jit(solution)/shard_map/ppermute | solution.py:528
  18.5 4.4 %collective-permute-start.6 = (bf16[96,384]{1,0:T(8,128)(2,1)S(1)}, bf16[96,384]{1,0:T(8,128)(2,1)S(1)}, u32[]{:S(2)}, u32[]{:S(2)}) collective-permute-start(bf16[96,384]{1,0:T(8,128)(2,1)S(1)} %get-tuple-element.71), channel_id=1, source_target_pairs={{0,8},{1,25},{2,10},{3,27},{4,12},{5,29},{6,14},{7,31},{8,0},{9,17... | collective-permute-start | bytes 221192 | tf_op jit(solution)/shard_map/ppermute | solution.py:528
  20.1 5.1 %collective-permute-start.13 = (bf16[64,896]{1,0:T(8,128)(2,1)S(1)}, bf16[64,896]{1,0:T(8,128)(2,1)S(1)}, u32[]{:S(2)}, u32[]{:S(2)}) collective-permute-start(bf16[64,896]{1,0:T(8,128)(2,1)S(1)} %third_grads.1), channel_id=1, source_target_pairs={{0,4},{1,7},{2,6},{3,5},{4,0},{5,3},{6,2},{7,1},{8,12},{9,15},{10,... | collective-permute-start | bytes 344072 | tf_op jit(solution)/shard_map/ppermute | solution.py:514
  22.9 1.6 %collective-permute-start.8 = (bf16[144,384]{1,0:T(8,128)(2,1)S(1)}, bf16[144,384]{1,0:T(8,128)(2,1)S(1)}, u32[]{:S(2)}, u32[]{:S(2)}) collective-permute-start(bf16[144,384]{1,0:T(8,128)(2,1)S(1)} %layer_sum.1.refs_1_), channel_id=1, source_target_pairs={{0,1},{1,0},{2,3},{3,2},{4,5},{5,4},{6,7},{7,6},{8,9},{9,8},{10,11... | collective-permute-start | bytes 331784 | tf_op jit(solution)/shard_map/ppermute | solution.py:510
  23.6 4.8 %collective-permute-start.12 = (bf16[64,896]{1,0:T(8,128)(2,1)S(1)}, bf16[64,896]{1,0:T(8,128)(2,1)S(1)}, u32[]{:S(2)}, u32[]{:S(2)}) collective-permute-start(bf16[64,896]{1,0:T(8,128)(2,1)S(1)} %collective-permute-done.9.refs_4_), channel_id=1, source_target_pairs={{0,1},{1,0},{2,3},{3,2},{4,5},{5,4},{6,7},{7,6},{8,9},{9,8},{10,11... | collective-permute-start | bytes 344072 | tf_op jit(solution)/shard_map/ppermute | solution.py:510
  25.2 3.2 %collective-permute-start.14 = (bf16[64,896]{1,0:T(8,128)(2,1)S(1)}, bf16[64,896]{1,0:T(8,128)(2,1)S(1)}, u32[]{:S(2)}, u32[]{:S(2)}) collective-permute-start(bf16[64,896]{1,0:T(8,128)(2,1)S(1)} %collective-permute-done.13.refs_6_), channel_id=1, source_target_pairs={{0,1},{1,0},{2,3},{3,2},{4,5},{5,4},{6,7},{7,6},{8,9},{9,8},{10,11... | collective-permute-start | bytes 344072 | tf_op jit(solution)/shard_map/ppermute | solution.py:510
  25.2 5.0 %collective-permute-start.11 = (bf16[96,384]{1,0:T(8,128)(2,1)S(1)}, bf16[96,384]{1,0:T(8,128)(2,1)S(1)}, u32[]{:S(2)}, u32[]{:S(2)}) collective-permute-start(bf16[96,384]{1,0:T(8,128)(2,1)S(1)} %get-tuple-element.88.refs_3_), channel_id=1, source_target_pairs={{0,4},{1,7},{2,6},{3,5},{4,0},{5,3},{6,2},{7,1},{8,12},{9,15},{10,... | collective-permute-start | bytes 221192 | tf_op jit(solution)/shard_map/ppermute | solution.py:514
  26.6 4.4 %collective-permute-start.15 = (bf16[48,384]{1,0:T(8,128)(2,1)S(1)}, bf16[48,384]{1,0:T(8,128)(2,1)S(1)}, u32[]{:S(2)}, u32[]{:S(2)}) collective-permute-start(bf16[48,384]{1,0:T(8,128)(2,1)S(1)} %get-tuple-element.103), channel_id=1, source_target_pairs={{0,2},{1,3},{2,0},{3,1},{4,6},{5,7},{6,4},{7,5},{8,10},{9,11},{10,... | collective-permute-start | bytes 110600 | tf_op jit(solution)/shard_map/ppermute | solution.py:510
  31.1 1.4 %collective-permute-start.16 = (bf16[144,384]{1,0:T(8,128)(2,1)S(1)}, bf16[144,384]{1,0:T(8,128)(2,1)S(1)}, u32[]{:S(2)}, u32[]{:S(2)}) collective-permute-start(bf16[144,384]{1,0:T(8,128)(2,1)S(1)} %plane_rows.1.refs_1_), channel_id=1, source_target_pairs={{0,1},{1,0},{2,3},{3,2},{4,5},{5,4},{6,7},{7,6},{8,9},{9,8},{10,11... | collective-permute-start | bytes 331784 | tf_op jit(solution)/shard_map/ppermute | solution.py:510

commit v8 on v7

--- a/solution.py
+++ b/solution.py
@@ -738,8 +738,8 @@
         third_in, _ = lax.optimization_barrier((third_in, weight))
         third_too = traded(third_in, 1)
         sibling_grads = [[View(far_in), View(far_too)], [View(third_in), View(third_too)]]
-        plane_one = split_traded(weight, 2, 3)
-        plane_half = traded(weight_half, 2)
+        plane_one = split_traded(weight, 1, 3)
+        plane_half = traded(weight_half, 4)
         key_grad, value_grad = key_call(2, top, near_sums, sibling_grads, BF)
         plane_one, key_grad, query_grad = lax.optimization_barrier((plane_one, key_grad, query_grad))
         (joint,) = placed(

time: 33.3 us -> 32.6 us (0.979)
  waiting for transfers between devices: 5.25 us -> 4.39 us
    ppermute x12, waiting for transfers between devices: 2.89 us -> 1.92 us  [traded(): lax.ppermute(value, SEQ, [(source, source ^ mask) for source in range(lax...]
    ppermute x12, starting transfers between devices: 7.09 us -> 7.78 us  [traded(): lax.ppermute(value, SEQ, [(source, source ^ mask) for source in range(lax...]
    ppermute x3, starting transfers between devices: 4.6 us -> 4.02 us  [split_traded(): lax.ppermute(value, SEQ, [(source, source ^ 2 * (second if source % 2 els...]
  transfers between devices with their start and end apart: 17 -> 17, of which waited for: 10 -> 9; matrix products, arithmetic and copies ran while one was open for 0% -> 0% of each run, Pallas kernels for 19% -> 19%
where the time goes in v8:
time: 32.6 us; the launch traced here: 32.4 us
  starting transfers between devices  16 us (49%)
  Pallas kernels  10.2 us (31%)
  waiting for transfers between devices  4.39 us (13%)
  local copies, waits for them, and re-layouts  0.98 us (3%)
  between operations  0.79 us (2%)
    pallas_call x18, Pallas kernels, call(): pl.pallas_call(body, out_shape=[jax.ShapeDtypeStruct(shape, kind) for sha...  10.2 us
    ppermute x12, starting transfers between devices, traded(): lax.ppermute(value, SEQ, [(source, source ^ mask) for source in range(lax...  7.78 us
    ppermute x2, starting transfers between devices, layer_traded(): return lax.ppermute(value, axes, pairs)  4.23 us
    ppermute x3, starting transfers between devices, split_traded(): lax.ppermute(value, SEQ, [(source, source ^ 2 * (second if source % 2 els...  4.02 us
    ppermute x3, waiting for transfers between devices, split_traded(): lax.ppermute(value, SEQ, [(source, source ^ 2 * (second if source % 2 els...  2.34 us
    ppermute x12, waiting for transfers between devices, traded(): lax.ppermute(value, SEQ, [(source, source ^ mask) for source in range(lax...  1.92 us
    unnamed x4, local copies, waits for them, and re-layouts  0.9 us
  transfers between devices with their start and end apart: 17, of which 9 were waited for; matrix products, arithmetic and copies ran while one was open for 0% of the time, Pallas kernels for 19%

profile of v8, /device:TPU:0, one launch (start us, length us, event | category | flops | bytes accessed | tf_op | source)
XLA Modules:
  0.0 32.4 jit_solution(2041841972517117741)
XLA Ops:
  0.6 1.7 %pool.1 = (f32[16,128]{1,0:T(8,128)S(1)}, bf16[480,1152]{1,0:T(8,128)(2,1)S(1)}, bf16[160,768]{1,0:T(8,128)(2,1)S(1)}, bf16[64,768]{1,0:T(8,128)(2,1)S(1)}) custom-call(bf16[256,384]{1,0:T(8,128)(2,1)} %bitcast.14, bf16[256,384]{1,0:T(8,128)(2,1)} %bitcast.15, bf16[256,384]{1,0:T(8,128)(2,1)} %bitcast.16, f32[6]{0:T(128)} %refs_3_.2), custom_call_target="tpu_custom_call" | custom-call | flops 1 | bytes 10000 | tf_op jit(solution)/shard_map/pool/pallas_call | solution.py:142
  2.3 0.5 %collective-permute-start = (bf16[160,768]{1,0:T(8,128)(2,1)S(1)}, bf16[160,768]{1,0:T(8,128)(2,1)S(1)}, u32[]{:S(2)}, u32[]{:S(2)}) collective-permute-start(bf16[160,768]{1,0:T(8,128)(2,1)S(1)} %get-tuple-element.57.refs_0_), channel_id=1, source_target_pairs={{0,1},{1,0},{2,3},{3,2},{4,5},{5,4},{6,7},{7,6},{8,9},{9,8},{10,11... | collective-permute-start | bytes 737288 | tf_op jit(solution)/shard_map/ppermute | solution.py:510
  2.9 2.6 %collective-permute-start.3 = (bf16[64,768]{1,0:T(8,128)(2,1)S(1)}, bf16[64,768]{1,0:T(8,128)(2,1)S(1)}, u32[]{:S(2)}, u32[]{:S(2)}) collective-permute-start(bf16[64,768]{1,0:T(8,128)(2,1)S(1)} %get-tuple-element.58), channel_id=1, source_target_pairs={{0,2},{1,3},{2,0},{3,1},{4,6},{5,7},{6,4},{7,5},{8,10},{9,11},{10,... | collective-permute-start | bytes 294920 | tf_op jit(solution)/shard_map/ppermute | solution.py:510
  5.5 0.0 collective-permute-done.refs_1_.refs_3_.refs_7_
  5.5 1.6 %collective-permute-start.1 = (bf16[64,768]{1,0:T(8,128)(2,1)S(1)}, bf16[64,768]{1,0:T(8,128)(2,1)S(1)}, u32[]{:S(2)}, u32[]{:S(2)}) collective-permute-start(bf16[64,768]{1,0:T(8,128)(2,1)S(1)} %third_rows.1), channel_id=1, source_target_pairs={{0,4},{1,7},{2,6},{3,5},{4,0},{5,3},{6,2},{7,1},{8,12},{9,15},{10,... | collective-permute-start | bytes 294920 | tf_op jit(solution)/shard_map/ppermute | solution.py:514
  7.0 1.5 %base.1 = (f32[256,768]{1,0:T(8,128)S(1)}, bf16[256,1536]{1,0:T(8,128)(2,1)S(1)}, bf16[256,768]{1,0:T(8,128)(2,1)S(1)}) custom-call(f32[16,128]{1,0:T(8,128)S(1)} %get-tuple-element.56.refs_0_.refs_1_, bf16[480,1152]{1,0:T(8,128)(2,1)S(1)} %get-tuple-element.59.refs_1_.refs_2_.refs_4_.refs_3_, bf16[256,384]{1,0:T(8,128)(2,1)} %bitcast.13, ...), custom_call_target="tpu_custom_call" | custom-call | flops 100000000 | bytes 10000 | tf_op jit(solution)/shard_map/base/pallas_call | solution.py:142
  8.5 0.9 %copy-done = bf16[256,1536]{1,0:T(8,128)(2,1)} copy-done((bf16[256,1536]{1,0:T(8,128)(2,1)}, bf16[256,1536]{1,0:T(8,128)(2,1)S(1)}, u32[]{:S(2)}) %copy-start) | copy-done | bytes 786456
  9.4 0.4 %level.2 = (bf16[128,768]{1,0:T(8,128)(2,1)S(1)}, f32[256,768]{1,0:T(8,128)S(1)}) custom-call(f32[16,128]{1,0:T(8,128)S(1)} %get-tuple-element.56.refs_0_.refs_1_, f32[256,768]{1,0:T(8,128)S(1)} %get-tuple-element.60.refs_1_, bf16[480,1152]{1,0:T(8,128)(2,1)S(1)} %get-tuple-element.59.refs_1_.refs_2_.refs_4_.refs_3_, ...), custom_call_target="tpu_custom_call" | custom-call | flops 25000000 | bytes 10000 | tf_op jit(solution)/shard_map/level/pallas_call | solution.py:142
  9.8 0.0 collective-permute-done.3.refs_3_.refs_8_
  9.9 0.7 %collective-permute-start.4 = (bf16[64,768]{1,0:T(8,128)(2,1)S(1)}, bf16[64,768]{1,0:T(8,128)(2,1)S(1)}, u32[]{:S(2)}, u32[]{:S(2)}) collective-permute-start(bf16[64,768]{1,0:T(8,128)(2,1)S(1)} %collective-permute-done.3.refs_3_.refs_8_), channel_id=1, source_target_pairs={{0,1},{1,0},{2,3},{3,2},{4,5},{5,4},{6,7},{7,6},{8,9},{9,8},{10,11... | collective-permute-start | bytes 294920 | tf_op jit(solution)/shard_map/ppermute | solution.py:510
  10.6 0.6 %collective-permute-done.1.refs_5_.refs_10_ = bf16[64,768]{1,0:T(8,128)(2,1)S(1)} collective-permute-done((bf16[64,768]{1,0:T(8,128)(2,1)S(1)}, bf16[64,768]{1,0:T(8,128)(2,1)S(1)}, u32[]{:S(2)}, u32[]{:S(2)}) %collective-permute-start.1) | collective-permute-done | bytes 98336 | tf_op jit(solution)/shard_map/ppermute | solution.py:514
  11.2 0.0 collective-permute-start.2
  11.2 0.1 stack.23.refs_0_
  11.3 0.3 collective-permute-done.4.refs_4_.refs_9_
  11.5 0.4 %level.3 = (bf16[64,768]{1,0:T(8,128)(2,1)S(1)}, f32[256,768]{1,0:T(8,128)S(1)}) custom-call(f32[16,128]{1,0:T(8,128)S(1)} %get-tuple-element.56.refs_0_.refs_1_, f32[256,768]{1,0:T(8,128)S(1)} %get-tuple-element.62.refs_1_, bf16[480,1152]{1,0:T(8,128)(2,1)S(1)} %get-tuple-element.59.refs_1_.refs_2_.refs_4_.refs_3_, ...), custom_call_target="tpu_custom_call" | custom-call | flops 25000000 | bytes 10000 | tf_op jit(solution)/shard_map/level/pallas_call | solution.py:142
  11.9 0.6 %collective-permute-done.2.refs_6_.refs_11_ = bf16[64,768]{1,0:T(8,128)(2,1)S(1)} collective-permute-done((bf16[64,768]{1,0:T(8,128)(2,1)S(1)}, bf16[64,768]{1,0:T(8,128)(2,1)S(1)}, u32[]{:S(2)}, u32[]{:S(2)}) %collective-permute-start.2) | collective-permute-done | bytes 98336 | tf_op jit(solution)/shard_map/ppermute | solution.py:510
  12.5 1.3 %forward.1 = (bf16[32,768]{1,0:T(8,128)(2,1)S(1)}, f32[256,384]{1,0:T(8,128)S(1)}, f32[256,384]{1,0:T(8,128)S(1)}, bf16[96,384]{1,0:T(8,128)(2,1)S(1)}, bf16[144...) custom-call(s32[5]{0:T(128)S(1)} %stack.23.refs_0_, f32[16,128]{1,0:T(8,128)S(1)} %get-tuple-element.56.refs_0_.refs_1_, ...), custom_call_target="tpu_custom_call" | custom-call | flops 1 | bytes 10000 | tf_op jit(solution)/shard_map/forward/pallas_call | solution.py:142
  13.8 0.2 grads.1
  14.0 0.2 collective-permute-start.10
  14.2 0.4 %collective-permute-start.5 = (bf16[144,384]{1,0:T(8,128)(2,1)S(1)}, bf16[144,384]{1,0:T(8,128)(2,1)S(1)}, u32[]{:S(2)}, u32[]{:S(2)}) collective-permute-start(bf16[144,384]{1,0:T(8,128)(2,1)S(1)} %get-tuple-element.70), channel_id=1, source_target_pairs={{0,1},{1,0},{2,3},{3,2},{4,5},{5,4},{6,7},{7,6},{8,9},{9,8},{10,11... | collective-permute-start | bytes 331784 | tf_op jit(solution)/shard_map/ppermute | solution.py:510
  14.6 0.9 %collective-permute-start.9 = (bf16[64,896]{1,0:T(8,128)(2,1)S(1)}, bf16[64,896]{1,0:T(8,128)(2,1)S(1)}, u32[]{:S(2)}, u32[]{:S(2)}) collective-permute-start(bf16[64,896]{1,0:T(8,128)(2,1)S(1)} %get-tuple-element.80.refs_6_), channel_id=1, source_target_pairs={{0,2},{1,3},{2,0},{3,1},{4,6},{5,7},{6,4},{7,5},{8,10},{9,11},{10,... | collective-permute-start | bytes 344072 | tf_op jit(solution)/shard_map/ppermute | solution.py:510
  15.5 0.3 collective-permute-done.5.refs_1_
  15.8 2.7 %collective-permute-start.7 = (bf16[48,384]{1,0:T(8,128)(2,1)S(1)}, bf16[48,384]{1,0:T(8,128)(2,1)S(1)}, u32[]{:S(2)}, u32[]{:S(2)}) collective-permute-start(bf16[48,384]{1,0:T(8,128)(2,1)S(1)} %get-tuple-element.72), channel_id=1, source_target_pairs={{0,16},{1,17},{2,18},{3,19},{4,20},{5,21},{6,22},{7,23},{8,24},{9,... | collective-permute-start | bytes 110600 | tf_op jit(solution)/shard_map/ppermute | solution.py:528
  18.5 1.6 %collective-permute-start.6 = (bf16[96,384]{1,0:T(8,128)(2,1)S(1)}, bf16[96,384]{1,0:T(8,128)(2,1)S(1)}, u32[]{:S(2)}, u32[]{:S(2)}) collective-permute-start(bf16[96,384]{1,0:T(8,128)(2,1)S(1)} %get-tuple-element.71), channel_id=1, source_target_pairs={{0,8},{1,25},{2,10},{3,27},{4,12},{5,29},{6,14},{7,31},{8,0},{9,17... | collective-permute-start | bytes 221192 | tf_op jit(solution)/shard_map/ppermute | solution.py:528
  20.1 0.0 collective-permute-done.10.refs_4_.refs_1_
  20.1 1.6 %collective-permute-start.13 = (bf16[64,896]{1,0:T(8,128)(2,1)S(1)}, bf16[64,896]{1,0:T(8,128)(2,1)S(1)}, u32[]{:S(2)}, u32[]{:S(2)}) collective-permute-start(bf16[64,896]{1,0:T(8,128)(2,1)S(1)} %third_grads.1), channel_id=1, source_target_pairs={{0,4},{1,7},{2,6},{3,5},{4,0},{5,3},{6,2},{7,1},{8,12},{9,15},{10,... | collective-permute-start | bytes 344072 | tf_op jit(solution)/shard_map/ppermute | solution.py:514
  21.7 1.1 %near.1 = (f32[256,384]{1,0:T(8,128)S(1)}, f32[256,384]{1,0:T(8,128)S(1)}, f32[256,384]{1,0:T(8,128)S(1)}) custom-call(f32[16,128]{1,0:T(8,128)S(1)} %get-tuple-element.56.refs_0_.refs_1_, bf16[480,1152]{1,0:T(8,128)(2,1)S(1)} %get-tuple-element.59.refs_1_.refs_2_.refs_4_.refs_3_, bf16[256,512]{1,0:T(8,128)(2,1)S(1)} %get-tuple-element.75.refs_2_, ...), custom_call_target="tpu_custom_call" | custom-call | flops 1600000000 | bytes 10000 | tf_op jit(solution)/shard_map/near/pallas_call | solution.py:142
  22.7 0.0 collective-permute-done.7.refs_2_
  22.7 0.1 collective-permute-done.6.refs_1_
  22.9 0.7 %collective-permute-start.8 = (bf16[144,384]{1,0:T(8,128)(2,1)S(1)}, bf16[144,384]{1,0:T(8,128)(2,1)S(1)}, u32[]{:S(2)}, u32[]{:S(2)}) collective-permute-start(bf16[144,384]{1,0:T(8,128)(2,1)S(1)} %layer_sum.1.refs_1_), channel_id=1, source_target_pairs={{0,1},{1,0},{2,3},{3,2},{4,5},{5,4},{6,7},{7,6},{8,9},{9,8},{10,11... | collective-permute-start | bytes 331784 | tf_op jit(solution)/shard_map/ppermute | solution.py:510
  23.6 0.0 collective-permute-done.9.refs_4_
  23.6 0.1 collective-permute-start.12
  23.6 0.5 %key.2 = (f32[256,384]{1,0:T(8,128)S(1)}, f32[256,384]{1,0:T(8,128)S(1)}) custom-call(f32[16,128]{1,0:T(8,128)S(1)} %get-tuple-element.56.refs_0_.refs_1_, f32[256,384]{1,0:T(8,128)S(1)} %get-tuple-element.82.refs_1_, f32[256,384]{1,0:T(8,128)S(1)} %get-tuple-element.83.refs_2_, bf16[480,1152]{1,0:T(8,128)(2,1)S(1)} %get-tuple-element.59.refs_1_.refs_2_.refs_4_.refs_3_, ...), custom_call_target="tpu_custom_call" | custom-call | flops 100000000 | bytes 10000 | tf_op jit(solution)/shard_map/key/pallas_call | solution.py:142
  24.1 0.4 %collective-permute-done.8.refs_2_ = bf16[144,384]{1,0:T(8,128)(2,1)S(1)} collective-permute-done((bf16[144,384]{1,0:T(8,128)(2,1)S(1)}, bf16[144,384]{1,0:T(8,128)(2,1)S(1)}, u32[]{:S(2)}, u32[]{:S(2)}) %collective-permute-start.8) | collective-permute-done | bytes 110624 | tf_op jit(solution)/shard_map/ppermute | solution.py:510
  24.6 0.6 %collective-permute-done.13.refs_6_ = bf16[64,896]{1,0:T(8,128)(2,1)S(1)} collective-permute-done((bf16[64,896]{1,0:T(8,128)(2,1)S(1)}, bf16[64,896]{1,0:T(8,128)(2,1)S(1)}, u32[]{:S(2)}, u32[]{:S(2)}) %collective-permute-start.13) | collective-permute-done | bytes 114720 | tf_op jit(solution)/shard_map/ppermute | solution.py:514
  25.2 0.0 collective-permute-start.14
  25.2 0.9 %collective-permute-start.11 = (bf16[96,384]{1,0:T(8,128)(2,1)S(1)}, bf16[96,384]{1,0:T(8,128)(2,1)S(1)}, u32[]{:S(2)}, u32[]{:S(2)}) collective-permute-start(bf16[96,384]{1,0:T(8,128)(2,1)S(1)} %get-tuple-element.88.refs_3_), channel_id=1, source_target_pairs={{0,2},{1,7},{2,0},{3,5},{4,6},{5,3},{6,4},{7,1},{8,10},{9,15},{10,... | collective-permute-start | bytes 221192 | tf_op jit(solution)/shard_map/ppermute | solution.py:514
  26.1 1.5 %collective-permute-start.15 = (bf16[48,384]{1,0:T(8,128)(2,1)S(1)}, bf16[48,384]{1,0:T(8,128)(2,1)S(1)}, u32[]{:S(2)}, u32[]{:S(2)}) collective-permute-start(bf16[48,384]{1,0:T(8,128)(2,1)S(1)} %get-tuple-element.103), channel_id=1, source_target_pairs={{0,4},{1,5},{2,6},{3,7},{4,0},{5,1},{6,2},{7,3},{8,12},{9,13},{10,... | collective-permute-start | bytes 110600 | tf_op jit(solution)/shard_map/ppermute | solution.py:510
  27.6 0.7 %far.1.refs_0_ = bf16[256,384]{1,0:T(8,128)(2,1)S(1)} custom-call(f32[16,128]{1,0:T(8,128)S(1)} %get-tuple-element.56.refs_0_.refs_1_, f32[256,384]{1,0:T(8,128)S(1)} %get-tuple-element.94.refs_1_, bf16[128,768]{1,0:T(8,128)(2,1)S(1)} %get-tuple-element.95.refs_2_, bf16[64,768]{1,0:T(8,128)(2,1)S(1)} %get-tuple-element.96.refs_3_, ...), custom_call_target="tpu_custom_call" | custom-call | flops 100000000 | bytes 10000 | tf_op jit(solution)/shard_map/far/pallas_call | solution.py:142
  28.3 0.0 collective-permute-done.12.refs_5_
  28.3 0.0 collective-permute-done.14.refs_7_
  28.3 0.8 %key.3 = (bf16[256,384]{1,0:T(8,128)(2,1)S(1)}, bf16[256,384]{1,0:T(8,128)(2,1)S(1)}) custom-call(f32[16,128]{1,0:T(8,128)S(1)} %get-tuple-element.56.refs_0_.refs_1_, f32[256,384]{1,0:T(8,128)S(1)} %get-tuple-element.89.refs_1_, f32[256,384]{1,0:T(8,128)S(1)} %get-tuple-element.90.refs_2_, ...), custom_call_target="tpu_custom_call" | custom-call | flops 100000000 | bytes 10000 | tf_op jit(solution)/shard_map/key/pallas_call | solution.py:142
  29.1 1.2 %collective-permute-done.11.refs_0_ = bf16[96,384]{1,0:T(8,128)(2,1)S(1)} collective-permute-done((bf16[96,384]{1,0:T(8,128)(2,1)S(1)}, bf16[96,384]{1,0:T(8,128)(2,1)S(1)}, u32[]{:S(2)}, u32[]{:S(2)}) %collective-permute-start.11) | collective-permute-done | bytes 73760 | tf_op jit(solution)/shard_map/ppermute | solution.py:514
  30.3 0.0 collective-permute-done.15.refs_1_
  30.3 0.2 collective-permute-start.16
  30.5 0.8 %flush.1 = (bf16[256,384]{1,0:T(8,128)(2,1)}, bf16[256,384]{1,0:T(8,128)(2,1)}, bf16[256,384]{1,0:T(8,128)(2,1)}) custom-call(bf16[256,384]{1,0:T(8,128)(2,1)S(1)} %far.1.refs_0_, bf16[256,384]{1,0:T(8,128)(2,1)S(1)} %get-tuple-element.99.refs_1_, bf16[256,384]{1,0:T(8,128)(2,1)S(1)} %get-tuple-element.100.refs_2_), custom_call_target="tpu_custom_call" | custom-call | flops 1 | bytes 10000 | tf_op jit(solution)/shard_map/flush/pallas_call | solution.py:142
  31.3 0.4 %collective-permute-done.16.refs_2_ = bf16[144,384]{1,0:T(8,128)(2,1)S(1)} collective-permute-done((bf16[144,384]{1,0:T(8,128)(2,1)S(1)}, bf16[144,384]{1,0:T(8,128)(2,1)S(1)}, u32[]{:S(2)}, u32[]{:S(2)}) %collective-permute-start.16) | collective-permute-done | bytes 110624 | tf_op jit(solution)/shard_map/ppermute | solution.py:510
  31.7 0.7 %weight_out.1 = f32[96,384]{1,0:T(8,128)} custom-call(s32[1]{0:T(128)} %bitcast.refs_0_, bf16[144,384]{1,0:T(8,128)(2,1)S(1)} %plane_rows.1.refs_1_, bf16[144,384]{1,0:T(8,128)(2,1)S(1)} %collective-permute-done.16.refs_2_, bf16[96,384]{1,0:T(8,128)(2,1)S(1)} %get-tuple-element.88.refs_3_), custom_call_target="tpu_custom_call" | custom-call | flops 1 | bytes 10000 | tf_op jit(solution)/shard_map/weight_out/pallas_call | solution.py:142
  (9 shorter events, 0.1 us)
Async XLA Ops:
  2.3 3.1 %collective-permute-start = (bf16[160,768]{1,0:T(8,128)(2,1)S(1)}, bf16[160,768]{1,0:T(8,128)(2,1)S(1)}, u32[]{:S(2)}, u32[]{:S(2)}) collective-permute-start(bf16[160,768]{1,0:T(8,128)(2,1)S(1)} %get-tuple-element.57.refs_0_), channel_id=1, source_target_pairs={{0,1},{1,0},{2,3},{3,2},{4,5},{5,4},{6,7},{7,6},{8,9},{9,8},{10,11... | collective-permute-start | bytes 737288 | tf_op jit(solution)/shard_map/ppermute | solution.py:510
  2.9 7.0 %collective-permute-start.3 = (bf16[64,768]{1,0:T(8,128)(2,1)S(1)}, bf16[64,768]{1,0:T(8,128)(2,1)S(1)}, u32[]{:S(2)}, u32[]{:S(2)}) collective-permute-start(bf16[64,768]{1,0:T(8,128)(2,1)S(1)} %get-tuple-element.58), channel_id=1, source_target_pairs={{0,2},{1,3},{2,0},{3,1},{4,6},{5,7},{6,4},{7,5},{8,10},{9,11},{10,... | collective-permute-start | bytes 294920 | tf_op jit(solution)/shard_map/ppermute | solution.py:510
  5.5 5.7 %collective-permute-start.1 = (bf16[64,768]{1,0:T(8,128)(2,1)S(1)}, bf16[64,768]{1,0:T(8,128)(2,1)S(1)}, u32[]{:S(2)}, u32[]{:S(2)}) collective-permute-start(bf16[64,768]{1,0:T(8,128)(2,1)S(1)} %third_rows.1), channel_id=1, source_target_pairs={{0,4},{1,7},{2,6},{3,5},{4,0},{5,3},{6,2},{7,1},{8,12},{9,15},{10,... | collective-permute-start | bytes 294920 | tf_op jit(solution)/shard_map/ppermute | solution.py:514
  8.5 0.9 %copy-start = (bf16[256,1536]{1,0:T(8,128)(2,1)}, bf16[256,1536]{1,0:T(8,128)(2,1)S(1)}, u32[]{:S(2)}) copy-start(bf16[256,1536]{1,0:T(8,128)(2,1)S(1)} %get-tuple-element.76.refs_3_) | copy-start | bytes 2359300
  9.9 1.7 %collective-permute-start.4 = (bf16[64,768]{1,0:T(8,128)(2,1)S(1)}, bf16[64,768]{1,0:T(8,128)(2,1)S(1)}, u32[]{:S(2)}, u32[]{:S(2)}) collective-permute-start(bf16[64,768]{1,0:T(8,128)(2,1)S(1)} %collective-permute-done.3.refs_3_.refs_8_), channel_id=1, source_target_pairs={{0,1},{1,0},{2,3},{3,2},{4,5},{5,4},{6,7},{7,6},{8,9},{9,8},{10,11... | collective-permute-start | bytes 294920 | tf_op jit(solution)/shard_map/ppermute | solution.py:510
  11.2 1.3 %collective-permute-start.2 = (bf16[64,768]{1,0:T(8,128)(2,1)S(1)}, bf16[64,768]{1,0:T(8,128)(2,1)S(1)}, u32[]{:S(2)}, u32[]{:S(2)}) collective-permute-start(bf16[64,768]{1,0:T(8,128)(2,1)S(1)} %collective-permute-done.1.refs_5_.refs_10_), channel_id=1, source_target_pairs={{0,1},{1,0},{2,3},{3,2},{4,5},{5,4},{6,7},{7,6},{8,9},{9,8},{10,11... | collective-permute-start | bytes 294920 | tf_op jit(solution)/shard_map/ppermute | solution.py:510
  13.8 7.9 %copy-start.1 = (bf16[256,1536]{1,0:T(8,128)(2,1)S(1)}, bf16[256,1536]{1,0:T(8,128)(2,1)}, u32[]{:S(2)}) copy-start(bf16[256,1536]{1,0:T(8,128)(2,1)} %copy-done) | copy-start | bytes 2359300
  14.0 6.1 %collective-permute-start.10 = (bf16[160,896]{1,0:T(8,128)(2,1)S(1)}, bf16[160,896]{1,0:T(8,128)(2,1)S(1)}, u32[]{:S(2)}, u32[]{:S(2)}) collective-permute-start(bf16[160,896]{1,0:T(8,128)(2,1)S(1)} %get-tuple-element.84.refs_0_.refs_5_), channel_id=1, source_target_pairs={{0,1},{1,0},{2,3},{3,2},{4,5},{5,4},{6,7},{7,6},{8,9},{9,8},{10,11... | collective-permute-start | bytes 860168 | tf_op jit(solution)/shard_map/ppermute | solution.py:510
  14.2 1.6 %collective-permute-start.5 = (bf16[144,384]{1,0:T(8,128)(2,1)S(1)}, bf16[144,384]{1,0:T(8,128)(2,1)S(1)}, u32[]{:S(2)}, u32[]{:S(2)}) collective-permute-start(bf16[144,384]{1,0:T(8,128)(2,1)S(1)} %get-tuple-element.70), channel_id=1, source_target_pairs={{0,1},{1,0},{2,3},{3,2},{4,5},{5,4},{6,7},{7,6},{8,9},{9,8},{10,11... | collective-permute-start | bytes 331784 | tf_op jit(solution)/shard_map/ppermute | solution.py:510
  14.6 9.0 %collective-permute-start.9 = (bf16[64,896]{1,0:T(8,128)(2,1)S(1)}, bf16[64,896]{1,0:T(8,128)(2,1)S(1)}, u32[]{:S(2)}, u32[]{:S(2)}) collective-permute-start(bf16[64,896]{1,0:T(8,128)(2,1)S(1)} %get-tuple-element.80.refs_6_), channel_id=1, source_target_pairs={{0,2},{1,3},{2,0},{3,1},{4,6},{5,7},{6,4},{7,5},{8,10},{9,11},{10,... | collective-permute-start | bytes 344072 | tf_op jit(solution)/shard_map/ppermute | solution.py:510
  15.8 6.9 %collective-permute-start.7 = (bf16[48,384]{1,0:T(8,128)(2,1)S(1)}, bf16[48,384]{1,0:T(8,128)(2,1)S(1)}, u32[]{:S(2)}, u32[]{:S(2)}) collective-permute-start(bf16[48,384]{1,0:T(8,128)(2,1)S(1)} %get-tuple-element.72), channel_id=1, source_target_pairs={{0,16},{1,17},{2,18},{3,19},{4,20},{5,21},{6,22},{7,23},{8,24},{9,... | collective-permute-start | bytes 110600 | tf_op jit(solution)/shard_map/ppermute | solution.py:528
  18.5 4.4 %collective-permute-start.6 = (bf16[96,384]{1,0:T(8,128)(2,1)S(1)}, bf16[96,384]{1,0:T(8,128)(2,1)S(1)}, u32[]{:S(2)}, u32[]{:S(2)}) collective-permute-start(bf16[96,384]{1,0:T(8,128)(2,1)S(1)} %get-tuple-element.71), channel_id=1, source_target_pairs={{0,8},{1,25},{2,10},{3,27},{4,12},{5,29},{6,14},{7,31},{8,0},{9,17... | collective-permute-start | bytes 221192 | tf_op jit(solution)/shard_map/ppermute | solution.py:528
  20.1 5.1 %collective-permute-start.13 = (bf16[64,896]{1,0:T(8,128)(2,1)S(1)}, bf16[64,896]{1,0:T(8,128)(2,1)S(1)}, u32[]{:S(2)}, u32[]{:S(2)}) collective-permute-start(bf16[64,896]{1,0:T(8,128)(2,1)S(1)} %third_grads.1), channel_id=1, source_target_pairs={{0,4},{1,7},{2,6},{3,5},{4,0},{5,3},{6,2},{7,1},{8,12},{9,15},{10,... | collective-permute-start | bytes 344072 | tf_op jit(solution)/shard_map/ppermute | solution.py:514
  22.9 1.6 %collective-permute-start.8 = (bf16[144,384]{1,0:T(8,128)(2,1)S(1)}, bf16[144,384]{1,0:T(8,128)(2,1)S(1)}, u32[]{:S(2)}, u32[]{:S(2)}) collective-permute-start(bf16[144,384]{1,0:T(8,128)(2,1)S(1)} %layer_sum.1.refs_1_), channel_id=1, source_target_pairs={{0,1},{1,0},{2,3},{3,2},{4,5},{5,4},{6,7},{7,6},{8,9},{9,8},{10,11... | collective-permute-start | bytes 331784 | tf_op jit(solution)/shard_map/ppermute | solution.py:510
  23.6 4.8 %collective-permute-start.12 = (bf16[64,896]{1,0:T(8,128)(2,1)S(1)}, bf16[64,896]{1,0:T(8,128)(2,1)S(1)}, u32[]{:S(2)}, u32[]{:S(2)}) collective-permute-start(bf16[64,896]{1,0:T(8,128)(2,1)S(1)} %collective-permute-done.9.refs_4_), channel_id=1, source_target_pairs={{0,1},{1,0},{2,3},{3,2},{4,5},{5,4},{6,7},{7,6},{8,9},{9,8},{10,11... | collective-permute-start | bytes 344072 | tf_op jit(solution)/shard_map/ppermute | solution.py:510
  25.2 3.2 %collective-permute-start.14 = (bf16[64,896]{1,0:T(8,128)(2,1)S(1)}, bf16[64,896]{1,0:T(8,128)(2,1)S(1)}, u32[]{:S(2)}, u32[]{:S(2)}) collective-permute-start(bf16[64,896]{1,0:T(8,128)(2,1)S(1)} %collective-permute-done.13.refs_6_), channel_id=1, source_target_pairs={{0,1},{1,0},{2,3},{3,2},{4,5},{5,4},{6,7},{7,6},{8,9},{9,8},{10,11... | collective-permute-start | bytes 344072 | tf_op jit(solution)/shard_map/ppermute | solution.py:510
  25.2 5.1 %collective-permute-start.11 = (bf16[96,384]{1,0:T(8,128)(2,1)S(1)}, bf16[96,384]{1,0:T(8,128)(2,1)S(1)}, u32[]{:S(2)}, u32[]{:S(2)}) collective-permute-start(bf16[96,384]{1,0:T(8,128)(2,1)S(1)} %get-tuple-element.88.refs_3_), channel_id=1, source_target_pairs={{0,2},{1,7},{2,0},{3,5},{4,6},{5,3},{6,4},{7,1},{8,10},{9,15},{10,... | collective-permute-start | bytes 221192 | tf_op jit(solution)/shard_map/ppermute | solution.py:514
  26.1 4.2 %collective-permute-start.15 = (bf16[48,384]{1,0:T(8,128)(2,1)S(1)}, bf16[48,384]{1,0:T(8,128)(2,1)S(1)}, u32[]{:S(2)}, u32[]{:S(2)}) collective-permute-start(bf16[48,384]{1,0:T(8,128)(2,1)S(1)} %get-tuple-element.103), channel_id=1, source_target_pairs={{0,4},{1,5},{2,6},{3,7},{4,0},{5,1},{6,2},{7,3},{8,12},{9,13},{10,... | collective-permute-start | bytes 110600 | tf_op jit(solution)/shard_map/ppermute | solution.py:510
  30.3 1.4 %collective-permute-start.16 = (bf16[144,384]{1,0:T(8,128)(2,1)S(1)}, bf16[144,384]{1,0:T(8,128)(2,1)S(1)}, u32[]{:S(2)}, u32[]{:S(2)}) collective-permute-start(bf16[144,384]{1,0:T(8,128)(2,1)S(1)} %plane_rows.1.refs_1_), channel_id=1, source_target_pairs={{0,1},{1,0},{2,3},{3,2},{4,5},{5,4},{6,7},{7,6},{8,9},{9,8},{10,11... | collective-permute-start | bytes 331784 | tf_op jit(solution)/shard_map/ppermute | solution.py:510

commit v9 on v8

--- a/solution.py
+++ b/solution.py
@@ -163,20 +163,24 @@
         copies[which].start()
     rows, width = q_ref.shape
     order = order_matrix(rows, top)
+    current = {}
     for which, ref in ((1, k_ref), (2, v_ref), (0, q_ref)):
         copies[which].wait()
-        current = dot(order, ref[...])
-        columns = slice(which * width, (which + 1) * width)
-        rows_ref[:rows, columns] = current.astype(BF)
-        for height in range(1, top + 1):
-            total = halves_sum(current)
-            rounded = (total if which == 2 else 0.5 * total).astype(BF)
+        current[which] = dot(order, ref[...])
+    for height in range(top + 1):
+        for which in (1, 2, 0):
+            columns = slice(which * width, (which + 1) * width)
+            if height:
+                total = halves_sum(current[which])
+                rounded = (total if which == 2 else 0.5 * total).astype(BF)
+            else:
+                rounded = current[which].astype(BF)
             rows_ref[starts[height] : starts[height] + rounded.shape[0], columns] = rounded
-            if which:
+            if height and which:
                 target, start = places[height - 1]
                 span = slice(start, start + rounded.shape[0])
                 level_refs[target][span, (which - 1) * width : which * width] = rounded
-            current = rounded.astype(F32)
+            current[which] = rounded.astype(F32)
     copies[3].wait()
     fill_factors(scale_ref, factor_ref)
 

time: 32.6 us -> 32.6 us (level)
  no operation moved by 1% of the time
where the time goes in v9:
time: 32.6 us; the launch traced here: 32.5 us
  starting transfers between devices  16 us (49%)
  Pallas kernels  10.3 us (32%)
  waiting for transfers between devices  4.41 us (14%)
  local copies, waits for them, and re-layouts  0.98 us (3%)
  between operations  0.79 us (2%)
    pallas_call x18, Pallas kernels, call(): pl.pallas_call(body, out_shape=[jax.ShapeDtypeStruct(shape, kind) for sha...  10.3 us
    ppermute x12, starting transfers between devices, traded(): lax.ppermute(value, SEQ, [(source, source ^ mask) for source in range(lax...  7.77 us
    ppermute x2, starting transfers between devices, layer_traded(): return lax.ppermute(value, axes, pairs)  4.23 us
    ppermute x3, starting transfers between devices, split_traded(): lax.ppermute(value, SEQ, [(source, source ^ 2 * (second if source % 2 els...  4.02 us
    ppermute x3, waiting for transfers between devices, split_traded(): lax.ppermute(value, SEQ, [(source, source ^ 2 * (second if source % 2 els...  2.36 us
    ppermute x12, waiting for transfers between devices, traded(): lax.ppermute(value, SEQ, [(source, source ^ mask) for source in range(lax...  1.93 us
    unnamed x4, local copies, waits for them, and re-layouts  0.9 us
  transfers between devices with their start and end apart: 17, of which 9 were waited for; matrix products, arithmetic and copies ran while one was open for 0% of the time, Pallas kernels for 19%

profile of v9, /device:TPU:0, one launch (start us, length us, event | category | flops | bytes accessed | tf_op | source)
XLA Modules:
  0.0 32.5 jit_solution(9591082968760659586)
XLA Ops:
  0.6 1.8 %pool.1 = (f32[16,128]{1,0:T(8,128)S(1)}, bf16[480,1152]{1,0:T(8,128)(2,1)S(1)}, bf16[160,768]{1,0:T(8,128)(2,1)S(1)}, bf16[64,768]{1,0:T(8,128)(2,1)S(1)}) custom-call(bf16[256,384]{1,0:T(8,128)(2,1)} %bitcast.14, bf16[256,384]{1,0:T(8,128)(2,1)} %bitcast.15, bf16[256,384]{1,0:T(8,128)(2,1)} %bitcast.16, f32[6]{0:T(128)} %refs_3_.2), custom_call_target="tpu_custom_call" | custom-call | flops 1 | bytes 10000 | tf_op jit(solution)/shard_map/pool/pallas_call | solution.py:142
  2.4 0.5 %collective-permute-start = (bf16[160,768]{1,0:T(8,128)(2,1)S(1)}, bf16[160,768]{1,0:T(8,128)(2,1)S(1)}, u32[]{:S(2)}, u32[]{:S(2)}) collective-permute-start(bf16[160,768]{1,0:T(8,128)(2,1)S(1)} %get-tuple-element.57.refs_0_), channel_id=1, source_target_pairs={{0,1},{1,0},{2,3},{3,2},{4,5},{5,4},{6,7},{7,6},{8,9},{9,8},{10,11... | collective-permute-start | bytes 737288 | tf_op jit(solution)/shard_map/ppermute | solution.py:514
  2.9 2.6 %collective-permute-start.3 = (bf16[64,768]{1,0:T(8,128)(2,1)S(1)}, bf16[64,768]{1,0:T(8,128)(2,1)S(1)}, u32[]{:S(2)}, u32[]{:S(2)}) collective-permute-start(bf16[64,768]{1,0:T(8,128)(2,1)S(1)} %get-tuple-element.58), channel_id=1, source_target_pairs={{0,2},{1,3},{2,0},{3,1},{4,6},{5,7},{6,4},{7,5},{8,10},{9,11},{10,... | collective-permute-start | bytes 294920 | tf_op jit(solution)/shard_map/ppermute | solution.py:514
  5.5 0.0 collective-permute-done.refs_1_.refs_3_.refs_7_
  5.5 1.6 %collective-permute-start.1 = (bf16[64,768]{1,0:T(8,128)(2,1)S(1)}, bf16[64,768]{1,0:T(8,128)(2,1)S(1)}, u32[]{:S(2)}, u32[]{:S(2)}) collective-permute-start(bf16[64,768]{1,0:T(8,128)(2,1)S(1)} %third_rows.1), channel_id=1, source_target_pairs={{0,4},{1,7},{2,6},{3,5},{4,0},{5,3},{6,2},{7,1},{8,12},{9,15},{10,... | collective-permute-start | bytes 294920 | tf_op jit(solution)/shard_map/ppermute | solution.py:518
  7.1 1.5 %base.1 = (f32[256,768]{1,0:T(8,128)S(1)}, bf16[256,1536]{1,0:T(8,128)(2,1)S(1)}, bf16[256,768]{1,0:T(8,128)(2,1)S(1)}) custom-call(f32[16,128]{1,0:T(8,128)S(1)} %get-tuple-element.56.refs_0_.refs_1_, bf16[480,1152]{1,0:T(8,128)(2,1)S(1)} %get-tuple-element.59.refs_1_.refs_2_.refs_4_.refs_3_, bf16[256,384]{1,0:T(8,128)(2,1)} %bitcast.13, ...), custom_call_target="tpu_custom_call" | custom-call | flops 100000000 | bytes 10000 | tf_op jit(solution)/shard_map/base/pallas_call | solution.py:142
  8.6 0.9 %copy-done = bf16[256,1536]{1,0:T(8,128)(2,1)} copy-done((bf16[256,1536]{1,0:T(8,128)(2,1)}, bf16[256,1536]{1,0:T(8,128)(2,1)S(1)}, u32[]{:S(2)}) %copy-start) | copy-done | bytes 786456
  9.5 0.4 %level.2 = (bf16[128,768]{1,0:T(8,128)(2,1)S(1)}, f32[256,768]{1,0:T(8,128)S(1)}) custom-call(f32[16,128]{1,0:T(8,128)S(1)} %get-tuple-element.56.refs_0_.refs_1_, f32[256,768]{1,0:T(8,128)S(1)} %get-tuple-element.60.refs_1_, bf16[480,1152]{1,0:T(8,128)(2,1)S(1)} %get-tuple-element.59.refs_1_.refs_2_.refs_4_.refs_3_, ...), custom_call_target="tpu_custom_call" | custom-call | flops 25000000 | bytes 10000 | tf_op jit(solution)/shard_map/level/pallas_call | solution.py:142
  9.9 0.0 collective-permute-done.3.refs_3_.refs_8_
  9.9 0.7 %collective-permute-start.4 = (bf16[64,768]{1,0:T(8,128)(2,1)S(1)}, bf16[64,768]{1,0:T(8,128)(2,1)S(1)}, u32[]{:S(2)}, u32[]{:S(2)}) collective-permute-start(bf16[64,768]{1,0:T(8,128)(2,1)S(1)} %collective-permute-done.3.refs_3_.refs_8_), channel_id=1, source_target_pairs={{0,1},{1,0},{2,3},{3,2},{4,5},{5,4},{6,7},{7,6},{8,9},{9,8},{10,11... | collective-permute-start | bytes 294920 | tf_op jit(solution)/shard_map/ppermute | solution.py:514
  10.7 0.6 %collective-permute-done.1.refs_5_.refs_10_ = bf16[64,768]{1,0:T(8,128)(2,1)S(1)} collective-permute-done((bf16[64,768]{1,0:T(8,128)(2,1)S(1)}, bf16[64,768]{1,0:T(8,128)(2,1)S(1)}, u32[]{:S(2)}, u32[]{:S(2)}) %collective-permute-start.1) | collective-permute-done | bytes 98336 | tf_op jit(solution)/shard_map/ppermute | solution.py:518
  11.3 0.0 collective-permute-start.2
  11.3 0.1 stack.23.refs_0_
  11.3 0.3 collective-permute-done.4.refs_4_.refs_9_
  11.6 0.4 %level.3 = (bf16[64,768]{1,0:T(8,128)(2,1)S(1)}, f32[256,768]{1,0:T(8,128)S(1)}) custom-call(f32[16,128]{1,0:T(8,128)S(1)} %get-tuple-element.56.refs_0_.refs_1_, f32[256,768]{1,0:T(8,128)S(1)} %get-tuple-element.62.refs_1_, bf16[480,1152]{1,0:T(8,128)(2,1)S(1)} %get-tuple-element.59.refs_1_.refs_2_.refs_4_.refs_3_, ...), custom_call_target="tpu_custom_call" | custom-call | flops 25000000 | bytes 10000 | tf_op jit(solution)/shard_map/level/pallas_call | solution.py:142
  12.0 0.6 %collective-permute-done.2.refs_6_.refs_11_ = bf16[64,768]{1,0:T(8,128)(2,1)S(1)} collective-permute-done((bf16[64,768]{1,0:T(8,128)(2,1)S(1)}, bf16[64,768]{1,0:T(8,128)(2,1)S(1)}, u32[]{:S(2)}, u32[]{:S(2)}) %collective-permute-start.2) | collective-permute-done | bytes 98336 | tf_op jit(solution)/shard_map/ppermute | solution.py:514
  12.6 1.3 %forward.1 = (bf16[32,768]{1,0:T(8,128)(2,1)S(1)}, f32[256,384]{1,0:T(8,128)S(1)}, f32[256,384]{1,0:T(8,128)S(1)}, bf16[96,384]{1,0:T(8,128)(2,1)S(1)}, bf16[144...) custom-call(s32[5]{0:T(128)S(1)} %stack.23.refs_0_, f32[16,128]{1,0:T(8,128)S(1)} %get-tuple-element.56.refs_0_.refs_1_, ...), custom_call_target="tpu_custom_call" | custom-call | flops 1 | bytes 10000 | tf_op jit(solution)/shard_map/forward/pallas_call | solution.py:142
  13.9 0.2 grads.1
  14.1 0.2 collective-permute-start.10
  14.3 0.4 %collective-permute-start.5 = (bf16[144,384]{1,0:T(8,128)(2,1)S(1)}, bf16[144,384]{1,0:T(8,128)(2,1)S(1)}, u32[]{:S(2)}, u32[]{:S(2)}) collective-permute-start(bf16[144,384]{1,0:T(8,128)(2,1)S(1)} %get-tuple-element.70), channel_id=1, source_target_pairs={{0,1},{1,0},{2,3},{3,2},{4,5},{5,4},{6,7},{7,6},{8,9},{9,8},{10,11... | collective-permute-start | bytes 331784 | tf_op jit(solution)/shard_map/ppermute | solution.py:514
  14.6 0.9 %collective-permute-start.9 = (bf16[64,896]{1,0:T(8,128)(2,1)S(1)}, bf16[64,896]{1,0:T(8,128)(2,1)S(1)}, u32[]{:S(2)}, u32[]{:S(2)}) collective-permute-start(bf16[64,896]{1,0:T(8,128)(2,1)S(1)} %get-tuple-element.80.refs_6_), channel_id=1, source_target_pairs={{0,2},{1,3},{2,0},{3,1},{4,6},{5,7},{6,4},{7,5},{8,10},{9,11},{10,... | collective-permute-start | bytes 344072 | tf_op jit(solution)/shard_map/ppermute | solution.py:514
  15.6 0.3 collective-permute-done.5.refs_1_
  15.9 2.6 %collective-permute-start.7 = (bf16[48,384]{1,0:T(8,128)(2,1)S(1)}, bf16[48,384]{1,0:T(8,128)(2,1)S(1)}, u32[]{:S(2)}, u32[]{:S(2)}) collective-permute-start(bf16[48,384]{1,0:T(8,128)(2,1)S(1)} %get-tuple-element.72), channel_id=1, source_target_pairs={{0,16},{1,17},{2,18},{3,19},{4,20},{5,21},{6,22},{7,23},{8,24},{9,... | collective-permute-start | bytes 110600 | tf_op jit(solution)/shard_map/ppermute | solution.py:532
  18.5 1.6 %collective-permute-start.6 = (bf16[96,384]{1,0:T(8,128)(2,1)S(1)}, bf16[96,384]{1,0:T(8,128)(2,1)S(1)}, u32[]{:S(2)}, u32[]{:S(2)}) collective-permute-start(bf16[96,384]{1,0:T(8,128)(2,1)S(1)} %get-tuple-element.71), channel_id=1, source_target_pairs={{0,8},{1,25},{2,10},{3,27},{4,12},{5,29},{6,14},{7,31},{8,0},{9,17... | collective-permute-start | bytes 221192 | tf_op jit(solution)/shard_map/ppermute | solution.py:532
  20.1 0.0 collective-permute-done.10.refs_4_.refs_1_
  20.2 1.6 %collective-permute-start.13 = (bf16[64,896]{1,0:T(8,128)(2,1)S(1)}, bf16[64,896]{1,0:T(8,128)(2,1)S(1)}, u32[]{:S(2)}, u32[]{:S(2)}) collective-permute-start(bf16[64,896]{1,0:T(8,128)(2,1)S(1)} %third_grads.1), channel_id=1, source_target_pairs={{0,4},{1,7},{2,6},{3,5},{4,0},{5,3},{6,2},{7,1},{8,12},{9,15},{10,... | collective-permute-start | bytes 344072 | tf_op jit(solution)/shard_map/ppermute | solution.py:518
  21.7 1.1 %near.1 = (f32[256,384]{1,0:T(8,128)S(1)}, f32[256,384]{1,0:T(8,128)S(1)}, f32[256,384]{1,0:T(8,128)S(1)}) custom-call(f32[16,128]{1,0:T(8,128)S(1)} %get-tuple-element.56.refs_0_.refs_1_, bf16[480,1152]{1,0:T(8,128)(2,1)S(1)} %get-tuple-element.59.refs_1_.refs_2_.refs_4_.refs_3_, bf16[256,512]{1,0:T(8,128)(2,1)S(1)} %get-tuple-element.75.refs_2_, ...), custom_call_target="tpu_custom_call" | custom-call | flops 1600000000 | bytes 10000 | tf_op jit(solution)/shard_map/near/pallas_call | solution.py:142
  22.8 0.0 collective-permute-done.7.refs_2_
  22.8 0.1 collective-permute-done.6.refs_1_
  22.9 0.7 %collective-permute-start.8 = (bf16[144,384]{1,0:T(8,128)(2,1)S(1)}, bf16[144,384]{1,0:T(8,128)(2,1)S(1)}, u32[]{:S(2)}, u32[]{:S(2)}) collective-permute-start(bf16[144,384]{1,0:T(8,128)(2,1)S(1)} %layer_sum.1.refs_1_), channel_id=1, source_target_pairs={{0,1},{1,0},{2,3},{3,2},{4,5},{5,4},{6,7},{7,6},{8,9},{9,8},{10,11... | collective-permute-start | bytes 331784 | tf_op jit(solution)/shard_map/ppermute | solution.py:514
  23.6 0.0 collective-permute-done.9.refs_4_
  23.6 0.1 collective-permute-start.12
  23.7 0.5 %key.2 = (f32[256,384]{1,0:T(8,128)S(1)}, f32[256,384]{1,0:T(8,128)S(1)}) custom-call(f32[16,128]{1,0:T(8,128)S(1)} %get-tuple-element.56.refs_0_.refs_1_, f32[256,384]{1,0:T(8,128)S(1)} %get-tuple-element.82.refs_1_, f32[256,384]{1,0:T(8,128)S(1)} %get-tuple-element.83.refs_2_, bf16[480,1152]{1,0:T(8,128)(2,1)S(1)} %get-tuple-element.59.refs_1_.refs_2_.refs_4_.refs_3_, ...), custom_call_target="tpu_custom_call" | custom-call | flops 100000000 | bytes 10000 | tf_op jit(solution)/shard_map/key/pallas_call | solution.py:142
  24.2 0.4 %collective-permute-done.8.refs_2_ = bf16[144,384]{1,0:T(8,128)(2,1)S(1)} collective-permute-done((bf16[144,384]{1,0:T(8,128)(2,1)S(1)}, bf16[144,384]{1,0:T(8,128)(2,1)S(1)}, u32[]{:S(2)}, u32[]{:S(2)}) %collective-permute-start.8) | collective-permute-done | bytes 110624 | tf_op jit(solution)/shard_map/ppermute | solution.py:514
  24.6 0.6 %collective-permute-done.13.refs_6_ = bf16[64,896]{1,0:T(8,128)(2,1)S(1)} collective-permute-done((bf16[64,896]{1,0:T(8,128)(2,1)S(1)}, bf16[64,896]{1,0:T(8,128)(2,1)S(1)}, u32[]{:S(2)}, u32[]{:S(2)}) %collective-permute-start.13) | collective-permute-done | bytes 114720 | tf_op jit(solution)/shard_map/ppermute | solution.py:518
  25.2 0.0 collective-permute-start.14
  25.2 0.9 %collective-permute-start.11 = (bf16[96,384]{1,0:T(8,128)(2,1)S(1)}, bf16[96,384]{1,0:T(8,128)(2,1)S(1)}, u32[]{:S(2)}, u32[]{:S(2)}) collective-permute-start(bf16[96,384]{1,0:T(8,128)(2,1)S(1)} %get-tuple-element.88.refs_3_), channel_id=1, source_target_pairs={{0,2},{1,7},{2,0},{3,5},{4,6},{5,3},{6,4},{7,1},{8,10},{9,15},{10,... | collective-permute-start | bytes 221192 | tf_op jit(solution)/shard_map/ppermute | solution.py:518
  26.1 1.5 %collective-permute-start.15 = (bf16[48,384]{1,0:T(8,128)(2,1)S(1)}, bf16[48,384]{1,0:T(8,128)(2,1)S(1)}, u32[]{:S(2)}, u32[]{:S(2)}) collective-permute-start(bf16[48,384]{1,0:T(8,128)(2,1)S(1)} %get-tuple-element.103), channel_id=1, source_target_pairs={{0,4},{1,5},{2,6},{3,7},{4,0},{5,1},{6,2},{7,3},{8,12},{9,13},{10,... | collective-permute-start | bytes 110600 | tf_op jit(solution)/shard_map/ppermute | solution.py:514
  27.6 0.7 %far.1.refs_0_ = bf16[256,384]{1,0:T(8,128)(2,1)S(1)} custom-call(f32[16,128]{1,0:T(8,128)S(1)} %get-tuple-element.56.refs_0_.refs_1_, f32[256,384]{1,0:T(8,128)S(1)} %get-tuple-element.94.refs_1_, bf16[128,768]{1,0:T(8,128)(2,1)S(1)} %get-tuple-element.95.refs_2_, bf16[64,768]{1,0:T(8,128)(2,1)S(1)} %get-tuple-element.96.refs_3_, ...), custom_call_target="tpu_custom_call" | custom-call | flops 100000000 | bytes 10000 | tf_op jit(solution)/shard_map/far/pallas_call | solution.py:142
  28.4 0.0 collective-permute-done.12.refs_5_
  28.4 0.0 collective-permute-done.14.refs_7_
  28.4 0.8 %key.3 = (bf16[256,384]{1,0:T(8,128)(2,1)S(1)}, bf16[256,384]{1,0:T(8,128)(2,1)S(1)}) custom-call(f32[16,128]{1,0:T(8,128)S(1)} %get-tuple-element.56.refs_0_.refs_1_, f32[256,384]{1,0:T(8,128)S(1)} %get-tuple-element.89.refs_1_, f32[256,384]{1,0:T(8,128)S(1)} %get-tuple-element.90.refs_2_, ...), custom_call_target="tpu_custom_call" | custom-call | flops 100000000 | bytes 10000 | tf_op jit(solution)/shard_map/key/pallas_call | solution.py:142
  29.2 1.2 %collective-permute-done.11.refs_0_ = bf16[96,384]{1,0:T(8,128)(2,1)S(1)} collective-permute-done((bf16[96,384]{1,0:T(8,128)(2,1)S(1)}, bf16[96,384]{1,0:T(8,128)(2,1)S(1)}, u32[]{:S(2)}, u32[]{:S(2)}) %collective-permute-start.11) | collective-permute-done | bytes 73760 | tf_op jit(solution)/shard_map/ppermute | solution.py:518
  30.4 0.0 collective-permute-done.15.refs_1_
  30.4 0.2 collective-permute-start.16
  30.6 0.8 %flush.1 = (bf16[256,384]{1,0:T(8,128)(2,1)}, bf16[256,384]{1,0:T(8,128)(2,1)}, bf16[256,384]{1,0:T(8,128)(2,1)}) custom-call(bf16[256,384]{1,0:T(8,128)(2,1)S(1)} %far.1.refs_0_, bf16[256,384]{1,0:T(8,128)(2,1)S(1)} %get-tuple-element.99.refs_1_, bf16[256,384]{1,0:T(8,128)(2,1)S(1)} %get-tuple-element.100.refs_2_), custom_call_target="tpu_custom_call" | custom-call | flops 1 | bytes 10000 | tf_op jit(solution)/shard_map/flush/pallas_call | solution.py:142
  31.4 0.4 %collective-permute-done.16.refs_2_ = bf16[144,384]{1,0:T(8,128)(2,1)S(1)} collective-permute-done((bf16[144,384]{1,0:T(8,128)(2,1)S(1)}, bf16[144,384]{1,0:T(8,128)(2,1)S(1)}, u32[]{:S(2)}, u32[]{:S(2)}) %collective-permute-start.16) | collective-permute-done | bytes 110624 | tf_op jit(solution)/shard_map/ppermute | solution.py:514
  31.8 0.7 %weight_out.1 = f32[96,384]{1,0:T(8,128)} custom-call(s32[1]{0:T(128)} %bitcast.refs_0_, bf16[144,384]{1,0:T(8,128)(2,1)S(1)} %plane_rows.1.refs_1_, bf16[144,384]{1,0:T(8,128)(2,1)S(1)} %collective-permute-done.16.refs_2_, bf16[96,384]{1,0:T(8,128)(2,1)S(1)} %get-tuple-element.88.refs_3_), custom_call_target="tpu_custom_call" | custom-call | flops 1 | bytes 10000 | tf_op jit(solution)/shard_map/weight_out/pallas_call | solution.py:142
  (9 shorter events, 0.1 us)
Async XLA Ops:
  2.4 3.1 %collective-permute-start = (bf16[160,768]{1,0:T(8,128)(2,1)S(1)}, bf16[160,768]{1,0:T(8,128)(2,1)S(1)}, u32[]{:S(2)}, u32[]{:S(2)}) collective-permute-start(bf16[160,768]{1,0:T(8,128)(2,1)S(1)} %get-tuple-element.57.refs_0_), channel_id=1, source_target_pairs={{0,1},{1,0},{2,3},{3,2},{4,5},{5,4},{6,7},{7,6},{8,9},{9,8},{10,11... | collective-permute-start | bytes 737288 | tf_op jit(solution)/shard_map/ppermute | solution.py:514
  2.9 7.0 %collective-permute-start.3 = (bf16[64,768]{1,0:T(8,128)(2,1)S(1)}, bf16[64,768]{1,0:T(8,128)(2,1)S(1)}, u32[]{:S(2)}, u32[]{:S(2)}) collective-permute-start(bf16[64,768]{1,0:T(8,128)(2,1)S(1)} %get-tuple-element.58), channel_id=1, source_target_pairs={{0,2},{1,3},{2,0},{3,1},{4,6},{5,7},{6,4},{7,5},{8,10},{9,11},{10,... | collective-permute-start | bytes 294920 | tf_op jit(solution)/shard_map/ppermute | solution.py:514
  5.5 5.7 %collective-permute-start.1 = (bf16[64,768]{1,0:T(8,128)(2,1)S(1)}, bf16[64,768]{1,0:T(8,128)(2,1)S(1)}, u32[]{:S(2)}, u32[]{:S(2)}) collective-permute-start(bf16[64,768]{1,0:T(8,128)(2,1)S(1)} %third_rows.1), channel_id=1, source_target_pairs={{0,4},{1,7},{2,6},{3,5},{4,0},{5,3},{6,2},{7,1},{8,12},{9,15},{10,... | collective-permute-start | bytes 294920 | tf_op jit(solution)/shard_map/ppermute | solution.py:518
  8.6 0.9 %copy-start = (bf16[256,1536]{1,0:T(8,128)(2,1)}, bf16[256,1536]{1,0:T(8,128)(2,1)S(1)}, u32[]{:S(2)}) copy-start(bf16[256,1536]{1,0:T(8,128)(2,1)S(1)} %get-tuple-element.76.refs_3_) | copy-start | bytes 2359300
  9.9 1.7 %collective-permute-start.4 = (bf16[64,768]{1,0:T(8,128)(2,1)S(1)}, bf16[64,768]{1,0:T(8,128)(2,1)S(1)}, u32[]{:S(2)}, u32[]{:S(2)}) collective-permute-start(bf16[64,768]{1,0:T(8,128)(2,1)S(1)} %collective-permute-done.3.refs_3_.refs_8_), channel_id=1, source_target_pairs={{0,1},{1,0},{2,3},{3,2},{4,5},{5,4},{6,7},{7,6},{8,9},{9,8},{10,11... | collective-permute-start | bytes 294920 | tf_op jit(solution)/shard_map/ppermute | solution.py:514
  11.3 1.3 %collective-permute-start.2 = (bf16[64,768]{1,0:T(8,128)(2,1)S(1)}, bf16[64,768]{1,0:T(8,128)(2,1)S(1)}, u32[]{:S(2)}, u32[]{:S(2)}) collective-permute-start(bf16[64,768]{1,0:T(8,128)(2,1)S(1)} %collective-permute-done.1.refs_5_.refs_10_), channel_id=1, source_target_pairs={{0,1},{1,0},{2,3},{3,2},{4,5},{5,4},{6,7},{7,6},{8,9},{9,8},{10,11... | collective-permute-start | bytes 294920 | tf_op jit(solution)/shard_map/ppermute | solution.py:514
  13.9 7.9 %copy-start.1 = (bf16[256,1536]{1,0:T(8,128)(2,1)S(1)}, bf16[256,1536]{1,0:T(8,128)(2,1)}, u32[]{:S(2)}) copy-start(bf16[256,1536]{1,0:T(8,128)(2,1)} %copy-done) | copy-start | bytes 2359300
  14.1 6.1 %collective-permute-start.10 = (bf16[160,896]{1,0:T(8,128)(2,1)S(1)}, bf16[160,896]{1,0:T(8,128)(2,1)S(1)}, u32[]{:S(2)}, u32[]{:S(2)}) collective-permute-start(bf16[160,896]{1,0:T(8,128)(2,1)S(1)} %get-tuple-element.84.refs_0_.refs_5_), channel_id=1, source_target_pairs={{0,1},{1,0},{2,3},{3,2},{4,5},{5,4},{6,7},{7,6},{8,9},{9,8},{10,11... | collective-permute-start | bytes 860168 | tf_op jit(solution)/shard_map/ppermute | solution.py:514
  14.3 1.6 %collective-permute-start.5 = (bf16[144,384]{1,0:T(8,128)(2,1)S(1)}, bf16[144,384]{1,0:T(8,128)(2,1)S(1)}, u32[]{:S(2)}, u32[]{:S(2)}) collective-permute-start(bf16[144,384]{1,0:T(8,128)(2,1)S(1)} %get-tuple-element.70), channel_id=1, source_target_pairs={{0,1},{1,0},{2,3},{3,2},{4,5},{5,4},{6,7},{7,6},{8,9},{9,8},{10,11... | collective-permute-start | bytes 331784 | tf_op jit(solution)/shard_map/ppermute | solution.py:514
  14.6 9.0 %collective-permute-start.9 = (bf16[64,896]{1,0:T(8,128)(2,1)S(1)}, bf16[64,896]{1,0:T(8,128)(2,1)S(1)}, u32[]{:S(2)}, u32[]{:S(2)}) collective-permute-start(bf16[64,896]{1,0:T(8,128)(2,1)S(1)} %get-tuple-element.80.refs_6_), channel_id=1, source_target_pairs={{0,2},{1,3},{2,0},{3,1},{4,6},{5,7},{6,4},{7,5},{8,10},{9,11},{10,... | collective-permute-start | bytes 344072 | tf_op jit(solution)/shard_map/ppermute | solution.py:514
  15.9 6.9 %collective-permute-start.7 = (bf16[48,384]{1,0:T(8,128)(2,1)S(1)}, bf16[48,384]{1,0:T(8,128)(2,1)S(1)}, u32[]{:S(2)}, u32[]{:S(2)}) collective-permute-start(bf16[48,384]{1,0:T(8,128)(2,1)S(1)} %get-tuple-element.72), channel_id=1, source_target_pairs={{0,16},{1,17},{2,18},{3,19},{4,20},{5,21},{6,22},{7,23},{8,24},{9,... | collective-permute-start | bytes 110600 | tf_op jit(solution)/shard_map/ppermute | solution.py:532
  18.5 4.4 %collective-permute-start.6 = (bf16[96,384]{1,0:T(8,128)(2,1)S(1)}, bf16[96,384]{1,0:T(8,128)(2,1)S(1)}, u32[]{:S(2)}, u32[]{:S(2)}) collective-permute-start(bf16[96,384]{1,0:T(8,128)(2,1)S(1)} %get-tuple-element.71), channel_id=1, source_target_pairs={{0,8},{1,25},{2,10},{3,27},{4,12},{5,29},{6,14},{7,31},{8,0},{9,17... | collective-permute-start | bytes 221192 | tf_op jit(solution)/shard_map/ppermute | solution.py:532
  20.2 5.1 %collective-permute-start.13 = (bf16[64,896]{1,0:T(8,128)(2,1)S(1)}, bf16[64,896]{1,0:T(8,128)(2,1)S(1)}, u32[]{:S(2)}, u32[]{:S(2)}) collective-permute-start(bf16[64,896]{1,0:T(8,128)(2,1)S(1)} %third_grads.1), channel_id=1, source_target_pairs={{0,4},{1,7},{2,6},{3,5},{4,0},{5,3},{6,2},{7,1},{8,12},{9,15},{10,... | collective-permute-start | bytes 344072 | tf_op jit(solution)/shard_map/ppermute | solution.py:518
  22.9 1.6 %collective-permute-start.8 = (bf16[144,384]{1,0:T(8,128)(2,1)S(1)}, bf16[144,384]{1,0:T(8,128)(2,1)S(1)}, u32[]{:S(2)}, u32[]{:S(2)}) collective-permute-start(bf16[144,384]{1,0:T(8,128)(2,1)S(1)} %layer_sum.1.refs_1_), channel_id=1, source_target_pairs={{0,1},{1,0},{2,3},{3,2},{4,5},{5,4},{6,7},{7,6},{8,9},{9,8},{10,11... | collective-permute-start | bytes 331784 | tf_op jit(solution)/shard_map/ppermute | solution.py:514
  23.6 4.8 %collective-permute-start.12 = (bf16[64,896]{1,0:T(8,128)(2,1)S(1)}, bf16[64,896]{1,0:T(8,128)(2,1)S(1)}, u32[]{:S(2)}, u32[]{:S(2)}) collective-permute-start(bf16[64,896]{1,0:T(8,128)(2,1)S(1)} %collective-permute-done.9.refs_4_), channel_id=1, source_target_pairs={{0,1},{1,0},{2,3},{3,2},{4,5},{5,4},{6,7},{7,6},{8,9},{9,8},{10,11... | collective-permute-start | bytes 344072 | tf_op jit(solution)/shard_map/ppermute | solution.py:514
  25.2 3.2 %collective-permute-start.14 = (bf16[64,896]{1,0:T(8,128)(2,1)S(1)}, bf16[64,896]{1,0:T(8,128)(2,1)S(1)}, u32[]{:S(2)}, u32[]{:S(2)}) collective-permute-start(bf16[64,896]{1,0:T(8,128)(2,1)S(1)} %collective-permute-done.13.refs_6_), channel_id=1, source_target_pairs={{0,1},{1,0},{2,3},{3,2},{4,5},{5,4},{6,7},{7,6},{8,9},{9,8},{10,11... | collective-permute-start | bytes 344072 | tf_op jit(solution)/shard_map/ppermute | solution.py:514
  25.2 5.1 %collective-permute-start.11 = (bf16[96,384]{1,0:T(8,128)(2,1)S(1)}, bf16[96,384]{1,0:T(8,128)(2,1)S(1)}, u32[]{:S(2)}, u32[]{:S(2)}) collective-permute-start(bf16[96,384]{1,0:T(8,128)(2,1)S(1)} %get-tuple-element.88.refs_3_), channel_id=1, source_target_pairs={{0,2},{1,7},{2,0},{3,5},{4,6},{5,3},{6,4},{7,1},{8,10},{9,15},{10,... | collective-permute-start | bytes 221192 | tf_op jit(solution)/shard_map/ppermute | solution.py:518
  26.1 4.2 %collective-permute-start.15 = (bf16[48,384]{1,0:T(8,128)(2,1)S(1)}, bf16[48,384]{1,0:T(8,128)(2,1)S(1)}, u32[]{:S(2)}, u32[]{:S(2)}) collective-permute-start(bf16[48,384]{1,0:T(8,128)(2,1)S(1)} %get-tuple-element.103), channel_id=1, source_target_pairs={{0,4},{1,5},{2,6},{3,7},{4,0},{5,1},{6,2},{7,3},{8,12},{9,13},{10,... | collective-permute-start | bytes 110600 | tf_op jit(solution)/shard_map/ppermute | solution.py:514
  30.4 1.4 %collective-permute-start.16 = (bf16[144,384]{1,0:T(8,128)(2,1)S(1)}, bf16[144,384]{1,0:T(8,128)(2,1)S(1)}, u32[]{:S(2)}, u32[]{:S(2)}) collective-permute-start(bf16[144,384]{1,0:T(8,128)(2,1)S(1)} %plane_rows.1.refs_1_), channel_id=1, source_target_pairs={{0,1},{1,0},{2,3},{3,2},{4,5},{5,4},{6,7},{7,6},{8,9},{9,8},{10,11... | collective-permute-start | bytes 331784 | tf_op jit(solution)/shard_map/ppermute | solution.py:514
